TPU v7x, 32 devices: a whole 2x2x4 slice. The times are simulated.
32 devices in a mesh: grp: 8 (over y, x, core), cli: 4 (over z).
Axes of the slice: x: 2, y: 2, z: 4, core: 2. Of those that a mesh axis runs over, the one named last changes fastest.
Arguments:
- token_ids: int32 [32, 128], P(('grp', 'cli')), may hold values from 0 to 51199
- target_ids: int32 [32, 128], P(('grp', 'cli')), may hold values from 0 to 51199
- segment_ids: int32 [32, 128], P(('grp', 'cli')), may hold values from 0 to 3, never falling along the last dimension, each value on 1 to 64 neighbouring positions
- chosen: int32 [32], P(('grp', 'cli')), may hold values from 0 to 3, as said below
- table: float32 [4, 51200, 768], P(None, ('grp', 'cli')), may hold values from -0.4375 to 0.4375
- table_momentum: float32 [4, 51200, 768], P(None, ('grp', 'cli')), may hold values from -0.00390625 to 0.00390625
- stack: float32 [4, 9344, 768], P(None, ('grp', 'cli')), may hold values from -0.21875 to 0.21875
- stack_momentum: float32 [4, 9344, 768], P(None, ('grp', 'cli')), may hold values from -0.009765625 to 0.009765625
- vectors: float32 [4, 14, 768], replicated, may hold values from -1 to 1.4
- vector_momentum: float32 [4, 14, 768], replicated, may hold values from -0.0546875 to 0.0546875
Outputs:
- loss: float32 [], replicated
- client_losses: float32 [32, 4], P(('grp', 'cli'))
- table_grad: float32 [4, 51200, 768], P(None, ('grp', 'cli'))
- table_momentum_new: float32 [4, 51200, 768], P(None, ('grp', 'cli'))
- table_new: float32 [4, 51200, 768], P(None, ('grp', 'cli'))
- stack_grad: float32 [4, 9344, 768], P(None, ('grp', 'cli'))
- stack_momentum_new: float32 [4, 9344, 768], P(None, ('grp', 'cli'))
- stack_new: float32 [4, 9344, 768], P(None, ('grp', 'cli'))
- vector_grad: float32 [4, 14, 768], replicated
- vector_momentum_new: float32 [4, 14, 768], replicated
- vector_new: float32 [4, 14, 768], replicated
Inputs may be any that keep to these rules, and one draw needn't show every extreme that they name: Every one of the 4 models is chosen by at least one client.
All inputs are finite; a program needn't handle non-finite values.
Results may differ from a plain program's by a relative error of at most 0.0095.
Values may be sent and summed in bfloat16 or wider, within the bound.
A program may use at most 1 GiB of HBM per device.

v0:
```python
import jax
import jax.numpy as jnp
from jax import lax
from jax.sharding import PartitionSpec as P

HEADS = 12
HEAD_DIM = 64


epsilon = 1e-05
momentum_decay = 0.9
table_rate = 4.0
stack_rate = 4.0
vector_rate = 50.0


def layer_norm(inputs, gain_row, shift_row):
    centred = inputs - jnp.mean(inputs, -1, keepdims=True)
    spread = jnp.mean(centred * centred, -1, keepdims=True)
    return centred * lax.rsqrt(spread + epsilon) * gain_row + shift_row


def project(inputs, matrix):
    return lax.dot_general(
        inputs, matrix, (((1,), (1,)), ((), ())), preferred_element_type=jnp.float32
    )


def product(inputs, matrix):
    return jnp.dot(inputs, matrix, preferred_element_type=jnp.float32)


def outer_rows(left, right):
    return lax.dot_general(
        left, right, (((0,), (0,)), ((), ())), preferred_element_type=jnp.float32
    )


def attend(queries, key_rows, segment_row):
    row_count = queries.shape[0]
    head_shape = (row_count, HEADS, HEAD_DIM)
    scores = jnp.einsum(
        "qhd,khd->hqk",
        queries.reshape(head_shape),
        key_rows.reshape(head_shape),
        preferred_element_type=jnp.float32,
    ) * HEAD_DIM ** (-0.5)
    positions = jnp.arange(row_count)
    allowed = (positions[None, :] <= positions[:, None]) & (
        segment_row[None, :] == segment_row[:, None]
    )
    return jax.nn.softmax(jnp.where(allowed[None], scores, -1e30), axis=-1)


def layer_forward(weights, vector_one, inputs, segment_row):
    model_width = inputs.shape[1]
    row_count = inputs.shape[0]
    normed = layer_norm(inputs, vector_one[0], vector_one[1]).astype(jnp.bfloat16)
    queries = (project(normed, weights[0:model_width]) + vector_one[6]).astype(jnp.bfloat16)
    key_rows = project(normed, weights[model_width : 2 * model_width]).astype(jnp.bfloat16)
    values = (project(normed, weights[2 * model_width : 3 * model_width]) + vector_one[7]).astype(
        jnp.bfloat16
    )
    attention = attend(queries, key_rows, segment_row)
    head_shape = (row_count, HEADS, HEAD_DIM)
    mixture = jnp.einsum(
        "hqk,khd->qhd",
        attention.astype(jnp.bfloat16),
        values.reshape(head_shape),
        preferred_element_type=jnp.float32,
    )
    mixture = mixture.reshape(row_count, model_width).astype(jnp.bfloat16)
    middle = inputs + (project(mixture, weights[3 * model_width : 4 * model_width]) + vector_one[8])
    normed_two = layer_norm(middle, vector_one[2], vector_one[3]).astype(jnp.bfloat16)
    hidden = project(normed_two, weights[4 * model_width : 8 * model_width]) + vector_one[
        10:14
    ].reshape(-1)
    active = jax.nn.gelu(hidden, approximate=True).astype(jnp.bfloat16)
    residual = middle + (
        product(active, weights[8 * model_width : 12 * model_width]) + vector_one[9]
    )
    normed_out = layer_norm(residual, vector_one[4], vector_one[5]).astype(jnp.bfloat16)
    return (
        normed,
        queries,
        key_rows,
        values,
        attention,
        mixture,
        middle,
        normed_two,
        hidden,
        active,
        residual,
        normed_out,
    )


def norm_grad(operand, gain_row, shift_row, cotangent):
    outcome, pullback = jax.vjp(layer_norm, operand, gain_row, shift_row)
    return pullback(cotangent)


def gelu_tanh(hidden):
    return jax.nn.gelu(hidden, approximate=True)


def layer_backward(weights, vector_one, inputs, segment_row, grad_out):
    model_width = inputs.shape[1]
    row_count = inputs.shape[0]
    head_shape = (row_count, HEADS, HEAD_DIM)
    scaling = HEAD_DIM ** (-0.5)
    (
        normed,
        queries,
        key_rows,
        values,
        attention,
        mixture,
        middle,
        normed_two,
        hidden,
        active,
        residual,
        normed_out,
    ) = layer_forward(weights, vector_one, inputs, segment_row)
    d_residual, d_gain_out, d_shift_out = norm_grad(
        residual, vector_one[4], vector_one[5], grad_out
    )
    d_outer = d_residual.astype(jnp.bfloat16)
    d_bias_out = jnp.sum(d_outer.astype(jnp.float32), 0)
    grad_down = outer_rows(active, d_outer)
    d_active = project(d_outer, weights[8 * model_width : 12 * model_width])
    gelu_value, gelu_pull = jax.vjp(gelu_tanh, hidden)
    d_hidden = gelu_pull(d_active)[0].astype(jnp.bfloat16)
    d_bias_hidden = jnp.sum(d_hidden.astype(jnp.float32), 0)
    grad_up = outer_rows(d_hidden, normed_two)
    d_normed_two = product(d_hidden, weights[4 * model_width : 8 * model_width])
    d_middle_norm, d_gain_two, d_shift_two = norm_grad(
        middle, vector_one[2], vector_one[3], d_normed_two
    )
    d_middle = d_residual + d_middle_norm
    d_branch = d_middle.astype(jnp.bfloat16)
    d_bias_branch = jnp.sum(d_branch.astype(jnp.float32), 0)
    grad_mix = outer_rows(d_branch, mixture)
    d_mixture = (
        product(d_branch, weights[3 * model_width : 4 * model_width])
        .astype(jnp.bfloat16)
        .reshape(head_shape)
    )
    d_attention = jnp.einsum(
        "qhd,khd->hqk", d_mixture, values.reshape(head_shape), preferred_element_type=jnp.float32
    )
    d_values = jnp.einsum(
        "hqk,qhd->khd",
        attention.astype(jnp.bfloat16),
        d_mixture,
        preferred_element_type=jnp.float32,
    )
    d_values = d_values.reshape(row_count, model_width).astype(jnp.bfloat16)
    d_scores = (
        attention * (d_attention - jnp.sum(attention * d_attention, -1, keepdims=True))
    ).astype(jnp.bfloat16)
    d_queries = (
        jnp.einsum(
            "hqk,khd->qhd",
            d_scores,
            key_rows.reshape(head_shape),
            preferred_element_type=jnp.float32,
        )
        * scaling
    )
    d_queries = d_queries.reshape(row_count, model_width).astype(jnp.bfloat16)
    d_keys = (
        jnp.einsum(
            "hqk,qhd->khd",
            d_scores,
            queries.reshape(head_shape),
            preferred_element_type=jnp.float32,
        )
        * scaling
    )
    d_keys = d_keys.reshape(row_count, model_width).astype(jnp.bfloat16)
    d_joined = jnp.concatenate([d_queries, d_keys, d_values], axis=1)
    grad_joined = outer_rows(d_joined, normed)
    d_normed = product(d_joined, weights[0 : 3 * model_width])
    d_inputs_norm, d_gain_one, d_shift_one = norm_grad(
        inputs, vector_one[0], vector_one[1], d_normed
    )
    d_inputs = d_middle + d_inputs_norm
    stack_rows = jnp.concatenate([grad_joined, grad_mix, grad_up, grad_down, d_inputs], axis=0)
    bias_query = jnp.sum(d_queries.astype(jnp.float32), 0)
    bias_value = jnp.sum(d_values.astype(jnp.float32), 0)
    vector_rows = jnp.concatenate(
        [
            jnp.stack(
                [
                    d_gain_one,
                    d_shift_one,
                    d_gain_two,
                    d_shift_two,
                    d_gain_out,
                    d_shift_out,
                    bias_query,
                    bias_value,
                    d_bias_branch,
                    d_bias_out,
                ]
            ),
            d_bias_hidden.reshape(4, model_width),
        ],
        axis=0,
    )
    return (stack_rows, vector_rows, d_inputs)


def update(weight, momentum, gradient, step_rate):
    renewed = momentum_decay * momentum + gradient
    return (renewed, weight - step_rate * (gradient + momentum_decay * renewed))


def body(
    token_ids,
    target_ids,
    segment_ids,
    chosen,
    table,
    table_momentum,
    stack,
    stack_momentum,
    vectors,
    vector_momentum,
):
    models = table.shape[0]
    block_rows = table.shape[1]
    model_width = table.shape[2]
    seq_len = token_ids.shape[1]
    devices = lax.axis_size(("grp", "cli"))
    group_size = lax.axis_size("cli")
    device_index = lax.axis_index(("grp", "cli"))
    member_index = lax.axis_index("cli")
    token_row = token_ids[0]
    target_row = target_ids[0]
    segment_row = segment_ids[0]
    model_index = chosen[0]
    model_range = jnp.arange(models, dtype=jnp.int32)
    valid_row = jnp.concatenate(
        [(segment_row[:-1] == segment_row[1:]).astype(jnp.float32), jnp.zeros((1,), jnp.float32)]
    )
    count_own = jnp.sum(valid_row)
    own_choice = (model_range == model_index).astype(jnp.float32)
    client_rows = jnp.where(
        (jnp.arange(devices) == device_index)[:, None], (own_choice * count_own)[None, :], 0.0
    )
    client_rows = lax.psum(client_rows, ("grp", "cli"))
    totals = jnp.sum(client_rows, axis=0)
    model_column = jnp.full((seq_len,), model_index, jnp.int32)
    group_tokens, group_targets, group_valid, group_models = (
        lax.all_gather(token_row, "cli", axis=0, tiled=True),
        lax.all_gather(target_row, "cli", axis=0, tiled=True),
        lax.all_gather(valid_row.astype(jnp.int32), "cli", axis=0, tiled=True),
        lax.all_gather(model_column, "cli", axis=0, tiled=True),
    )
    stack_all = lax.all_gather(stack.astype(jnp.bfloat16), ("grp", "cli"), axis=1, tiled=True)
    table_part = lax.all_gather(table.astype(jnp.bfloat16), "grp", axis=1, tiled=True)
    part_rows = table_part.shape[1]

    def locate(global_ids):
        block_index = global_ids // block_rows
        is_owned = block_index % group_size == member_index
        local_rows = jnp.where(
            is_owned, block_index // group_size * block_rows + global_ids % block_rows, 0
        )
        return (is_owned, local_rows)

    token_owned, token_local = locate(group_tokens)
    target_owned, target_local = locate(group_targets)
    picked = jnp.take(table_part, token_local, axis=1)
    embed_terms = jnp.where(token_owned[None, :, None], picked, jnp.zeros_like(picked)).astype(
        jnp.float32
    )
    embedded = lax.psum_scatter(
        embed_terms.astype(jnp.bfloat16), "cli", scatter_dimension=1, tiled=True
    ).astype(jnp.float32)
    inputs = embedded + stack_all[:, 12 * model_width :, :].astype(jnp.float32)

    def forward_one(element):
        return layer_forward(element[0], element[1], element[2], segment_row)[11]

    normed_outs = lax.map(forward_one, (stack_all, vectors, inputs))
    group_outs = lax.all_gather(normed_outs, "cli", axis=1, tiled=True)

    def head_stats(element):
        outs_one, table_one = element
        logits = project(outs_one, table_one)
        highest = jnp.max(logits, -1)
        exp_total = jnp.sum(jnp.exp(logits - highest[:, None]), -1)
        target_logit = jnp.where(
            target_owned, jnp.take_along_axis(logits, target_local[:, None], axis=1)[:, 0], 0.0
        )
        return (highest, exp_total, target_logit)

    highests, exp_totals, target_logits = lax.map(head_stats, (group_outs, table_part))
    highest_all = lax.pmax(highests, "cli")
    sum_all, target_all = (
        lax.psum((exp_totals * jnp.exp(highests - highest_all)).astype(jnp.bfloat16), "cli").astype(
            jnp.float32
        ),
        lax.psum(target_logits.astype(jnp.bfloat16), "cli").astype(jnp.float32),
    )
    log_totals = highest_all + jnp.log(sum_all)
    token_loss = log_totals - target_all
    own_loss = lax.dynamic_slice_in_dim(token_loss, member_index * seq_len, seq_len, 1)
    client_losses = (jnp.sum(own_loss * valid_row[None, :], axis=1) / count_own)[None, :]
    own_total = jnp.sum(own_choice * totals)
    loss_term = jnp.sum(jnp.sum(own_loss * own_choice[:, None], 0) * valid_row) / own_total
    group_totals = jnp.sum(
        jnp.where(group_models[:, None] == model_range[None, :], totals[None, :], 0.0), axis=1
    )
    token_weight = group_valid.astype(jnp.float32) / group_totals
    vocab_range = jnp.arange(part_rows)

    def head_back(grad_table, block_index):
        block_start = block_index * seq_len
        model_pick = group_models[block_start]
        outs_block = lax.dynamic_slice(
            group_outs, (model_pick, block_start, 0), (1, seq_len, model_width)
        )[0]
        table_one = lax.dynamic_index_in_dim(table_part, model_pick, 0, keepdims=False)
        logits = project(outs_block, table_one)
        lse_block = lax.dynamic_slice(log_totals, (model_pick, block_start), (1, seq_len))[0]
        softmax_rows = jnp.exp(logits - lse_block[:, None])
        target_block = lax.dynamic_slice_in_dim(target_local, block_start, seq_len)
        owned_block = lax.dynamic_slice_in_dim(target_owned, block_start, seq_len)
        weight_block = lax.dynamic_slice_in_dim(token_weight, block_start, seq_len)
        target_hit = (
            (vocab_range[None, :] == target_block[:, None]) & owned_block[:, None]
        ).astype(jnp.float32)
        d_logits = (weight_block[:, None] * (softmax_rows - target_hit)).astype(jnp.bfloat16)
        d_outs = product(d_logits, table_one)
        grad_rows = outer_rows(d_logits, outs_block)
        current = lax.dynamic_index_in_dim(grad_table, model_pick, 0, keepdims=False)
        grad_table = lax.dynamic_update_index_in_dim(grad_table, current + grad_rows, model_pick, 0)
        return (grad_table, d_outs)

    head_init = jnp.zeros((models, part_rows, model_width), jnp.float32)
    grad_table, d_outs = lax.scan(head_back, head_init, jnp.arange(group_size))
    d_final = lax.psum_scatter(
        d_outs.reshape(group_size * seq_len, model_width), "cli", scatter_dimension=0, tiled=True
    )
    stack_one = lax.dynamic_index_in_dim(stack_all, model_index, 0, keepdims=False)
    vector_one = lax.dynamic_index_in_dim(vectors, model_index, 0, keepdims=False)
    inputs_one = lax.dynamic_index_in_dim(inputs, model_index, 0, keepdims=False)
    stack_rows, vector_rows, d_inputs = layer_backward(
        stack_one, vector_one, inputs_one, segment_row, d_final
    )
    group_grads = lax.all_gather(d_inputs.astype(jnp.bfloat16), "cli", axis=0, tiled=True)
    drop_rows = jnp.where(token_owned, token_local, part_rows)
    grad_table = grad_table.at[group_models, drop_rows].add(
        group_grads.astype(jnp.float32), mode="drop"
    )
    table_grad = lax.psum_scatter(
        grad_table.astype(jnp.bfloat16), "grp", scatter_dimension=1, tiled=True
    ).astype(jnp.float32)
    masked = jnp.where((model_range == model_index)[:, None, None], stack_rows[None], 0.0)
    stack_grad = lax.psum_scatter(masked, ("grp", "cli"), scatter_dimension=1, tiled=True)
    vector_masked = jnp.where((model_range == model_index)[:, None, None], vector_rows[None], 0.0)
    vector_grad, loss = lax.psum((vector_masked, loss_term), ("grp", "cli"))
    table_momentum_new, table_new = update(table, table_momentum, table_grad, table_rate)
    stack_momentum_new, stack_new = update(stack, stack_momentum, stack_grad, stack_rate)
    vector_momentum_new, vector_new = update(vectors, vector_momentum, vector_grad, vector_rate)
    return (
        loss,
        client_losses,
        table_grad,
        table_momentum_new,
        table_new,
        stack_grad,
        stack_momentum_new,
        stack_new,
        vector_grad,
        vector_momentum_new,
        vector_new,
    )


def solution(mesh):
    placed = (
        P(("grp", "cli"), None),
        P(("grp", "cli"), None),
        P(("grp", "cli"), None),
        P(("grp", "cli")),
        P(None, ("grp", "cli"), None),
        P(None, ("grp", "cli"), None),
        P(None, ("grp", "cli"), None),
        P(None, ("grp", "cli"), None),
        P(),
        P(),
    )
    return jax.shard_map(
        body,
        mesh=mesh,
        in_specs=placed,
        out_specs=(
            P(),
            P(("grp", "cli"), None),
            P(None, ("grp", "cli"), None),
            P(None, ("grp", "cli"), None),
            P(None, ("grp", "cli"), None),
            P(None, ("grp", "cli"), None),
            P(None, ("grp", "cli"), None),
            P(None, ("grp", "cli"), None),
            P(),
            P(),
            P(),
        ),
        check_vma=False,
    )
```

profile of v0, /device:TPU:0, one launch (start us, length us, event | category | flops | bytes accessed | tf_op | source)
XLA Modules:
  0.0 3884.0 jit_solution(11815534252745579856)
XLA Ops:
  7.2 29.7 copy.117
  40.9 12.6 all-gather
  54.1 338.0 %all-gather.8.cloned.1.call-done = bf16[4,12800,768]{2,0,1:T(4,128)(2,1)} async-done(((bf16[4,1600,768]{2,0,1:T(4,128)(2,1)}), bf16[4,12800,768]{2,0,1:T(4,128)(2,1)}) %all-gather.8.cloned.1.call-update) | async-done | bytes 78643216 | tf_op jit(solution)/shard_map/all_gather | solution.py:265
  392.1 16.9 gather_fusion.1
  409.0 4.4 select_bitcast_fusion
  415.2 290.1 %all-gather.10.cloned.1.call-done = bf16[4,9344,768]{2,0,1:T(4,128)(2,1)} async-done(((bf16[4,292,768]{2,0,1:T(4,128)(2,1)}), bf16[4,9344,768]{2,0,1:T(4,128)(2,1)}) %all-gather.10.cloned.1.call-update) | async-done | bytes 57409552 | tf_op jit(solution)/shard_map/all_gather | solution.py:264
  705.3 38.5 copy.97
  743.9 83.7 %all-reduce.9.cloned.1.call-done = bf16[4,512,768]{2,0,1:T(4,128)(2,1)} async-done(((bf16[4,512,768]{2,0,1:T(4,128)(2,1)}), bf16[4,512,768]{2,0,1:T(4,128)(2,1)}) %all-reduce.9.cloned.1.call-update) | async-done | bytes 3145744
  830.3 68.9 %while.37 = (s32[]{:T(128)}, bf16[4,128,768]{2,1,0:T(8,128)(2,1)}, f32[4,128,768]{2,1,0:T(8,128)S(1)}, f32[4,14,768]{2,0,1:T(4,128)S(1)}, bf16[4,9344,768]{2,1,0...) while((s32[]{:T(128)}, bf16[4,128,768]{2,1,0:T(8,128)(2,1)}, ...), condition=%wide.region_10.11_spmd, body=%wide.region_1.10_spmd.sunk | while | flops 1896827008 | bytes 24394716 | solution.py:290
  840.2 6.3 fusion.286
  857.4 6.3 fusion.286
  874.6 6.3 fusion.286
  891.8 6.3 fusion.286
  901.4 42.1 %psum.37 = f32[32,4]{0,1:T(4,128)S(1)} all-reduce(f32[32,4]{0,1:T(4,128)S(1)} %broadcast_select_fusion.2), channel_id=1, replica_groups=mesh['grp'=8,'cli'=4] {'grp','cli'}, use_global_device_ids=true, to_apply=%region_21.22 | all-reduce | flops 128 | bytes 1024 | tf_op jit(solution)/shard_map/psum | solution.py:255
  943.7 11.3 all-gather.1
  955.0 7.7 all-gather.2
  967.8 51.4 %copy.99 = bf16[4,12800,768]{2,1,0:T(8,128)(2,1)} copy(bf16[4,12800,768]{2,0,1:T(4,128)(2,1)} %all-gather.8.cloned.1.call-done) | data formatting | bytes 157286400 | tf_op jit(solution)/shard_map/while | solution.py:303
  1020.5 167.4 %while.38 = (s32[]{:T(128)}, f32[4,512]{1,0:T(4,128)S(1)}, f32[4,512]{1,0:T(4,128)S(1)}, bf16[4,512]{1,0:T(4,128)(2,1)S(1)}, bf16[4,512,768]{2,1,0:T(8,128)(2,1)...) while((s32[]{:T(128)}, f32[4,512]{1,0:T(4,128)S(1)}, ...), condition=%wide.region_14.15_spmd, body=%wide.region_11.14_spmd.sunk | while | flops 10086000640 | bytes 72927864 | solution.py:303
  1020.5 21.3 fusion.288
  1041.8 10.8 exponential_reduce_fusion.2
  1053.4 8.2 gather_fusion
  1062.4 21.3 fusion.288
  1083.7 10.8 exponential_reduce_fusion.2
  1095.2 8.2 gather_fusion
  1104.2 21.3 fusion.288
  1125.5 10.8 exponential_reduce_fusion.2
  1137.1 8.2 gather_fusion
  1146.1 21.3 fusion.288
  1167.4 10.8 exponential_reduce_fusion.2
  1179.0 8.2 gather_fusion
  1187.9 10.4 pmax.7
  1198.4 8.6 all-reduce.2
  1209.0 9.4 all-gather.3
  1218.4 48.1 %broadcast_in_dim.238 = f32[4,12800,768]{2,1,0:T(8,128)} broadcast(f32[]{:T(128)} %constant.231.clone.1), dimensions={} | broadcast | bytes 157286400 | tf_op jit(solution)/shard_map/broadcast_in_dim | solution.py:346
  1266.5 320.7 %while.39 = (s32[]{:T(128)}, f32[4,12800,768]{2,1,0:T(8,128)}, f32[4,128,768]{2,1,0:T(8,128)}, s32[4]{0:T(128)S(1)}, s32[512]{0:T(512)S(1)}, /*index=5*/f32[512]...) while((s32[]{:T(128)}, f32[4,12800,768]{2,1,0:T(8,128)}, ...), condition=%wide.region_28.29_spmd.clone, body=%wide.region_27.28_spmd.clone.sunk | while | flops 7571046400 | bytes 207235280 | solution.py:347
  1270.3 26.9 constant_dynamic-slice_fusion.30
  1298.9 10.5 fusion.296
  1309.4 28.6 bitcast_dynamic-update-slice_fusion.2
  1338.0 8.8 fusion.297
  1350.5 26.9 constant_dynamic-slice_fusion.30
  1379.1 10.5 fusion.296
  1389.6 28.5 bitcast_dynamic-update-slice_fusion.2
  1418.1 8.8 fusion.297
  1430.7 26.9 constant_dynamic-slice_fusion.30
  1459.2 10.5 fusion.296
  1469.7 28.6 bitcast_dynamic-update-slice_fusion.2
  1498.3 8.8 fusion.297
  1510.9 26.9 constant_dynamic-slice_fusion.30
  1539.4 10.5 fusion.296
  1549.9 28.5 bitcast_dynamic-update-slice_fusion.2
  1578.5 8.8 fusion.297
  1598.1 4.0 fusion.110
  1606.5 15.4 reduce-scatter.3.cloned.1.call-done
  1625.6 5.4 convert_reduce_fusion
  1654.0 9.2 copy-done.2
  1665.3 46.9 %broadcast_select_fusion = f32[4,9344,768]{2,0,1:T(4,128)} fusion(f32[9344,768]{1,0:T(8,128)} %get-tuple-element.391, pred[4]{0:T(512)(128)(4,1)S(1)} %copy-done.60), kind=kLoop, calls=%fused_computation.140 | loop fusion | flops 28704768 | bytes 143523840 | tf_op jit(solution)/shard_map/jit(_where)/select_n | solution.py:365
  1712.8 18.2 all_gather.31
  1731.2 74.8 %scatter_fusion = f32[4,12800,768]{2,1,0:T(8,128)} fusion(f32[4,12800,768]{2,1,0:T(8,128)} %get-tuple-element.154, s32[512]{0:T(512)S(1)} %bitcast.358, f32[512,768]{1,0:T(8,128)S(1)} %convert_element_type.245), kind=kCustom, calls=%fused_computation.2 | custom fusion | flops 393216 | bytes 4722688 | tf_op jit(solution)/shard_map/scatter-add | solution.py:359
  1806.0 77.7 %convert_element_type.246 = bf16[4,12800,768]{2,1,0:T(8,128)(2,1)} convert(f32[4,12800,768]{2,1,0:T(8,128)} %scatter_fusion) | non-fusion elementwise | flops 39321600 | bytes 235929600 | tf_op jit(solution)/shard_map/convert_element_type | solution.py:363
  1886.2 39.6 %psum.38 = f32[]{:T(128)} all-reduce(f32[]{:T(128)S(6)} %div.149), channel_id=1, replica_groups=mesh['grp'=8,'cli'=4] {'grp','cli'}, use_global_device_ids=true, to_apply=%region_24.25 | all-reduce | flops 1 | bytes 8 | tf_op jit(solution)/shard_map/psum | solution.py:368
  1928.7 1469.2 %all-reduce.11.cloned.1.call-done = f32[4,9344,768]{2,0,1:T(4,128)} async-done(((f32[4,9344,768]{2,0,1:T(4,128)}), f32[4,9344,768]{2,0,1:T(4,128)}) %all-reduce.11.cloned.1.call-update) | async-done | bytes 114819088
  3397.9 8.3 multiply_subtract_fusion.1
  3406.2 432.9 %reduce-scatter.5.cloned.1.call-done = bf16[4,1600,768]{2,1,0:T(8,128)(2,1)} async-done(((bf16[4,12800,768]{2,1,0:T(8,128)(2,1)}), bf16[4,1600,768]{2,1,0:T(8,128)(2,1)}) %reduce-scatter.5.cloned.1.call-update) | async-done | bytes 9830416 | tf_op jit(solution)/shard_map/reduce_scatter | solution.py:362
  3839.1 37.0 multiply_subtract_fusion
  (431 shorter events, 127.5 us)
Async XLA Ops:
  7.2 384.9 %all-gather.8.cloned.1.call-start = ((), (), s32[]{:S(2)}) async-start(), calls=%async_computation.2 | async-start | bytes 88473600 | tf_op jit(solution)/shard_map/all_gather | solution.py:265
  36.9 4.0 copy-start.65
  36.9 668.4 %all-gather.10.cloned.1.call-start = ((), (), s32[]{:S(2)}) async-start(), calls=%async_computation.3 | async-start | bytes 59203584 | tf_op jit(solution)/shard_map/all_gather | solution.py:264
  40.9 786.7 %all-reduce.9.cloned.1.call-start = ((), (), s32[]{:S(2)}) async-start(), calls=%async_computation.8 | async-start | bytes 6291456
  409.0 5.0 copy-start.72
  413.4 607.0 %all-gather.12.cloned.1.call-start = ((), (), s32[]{:S(2)}) async-start(), calls=%async_computation.4 | async-start | bytes 3932160 | tf_op jit(solution)/shard_map/all_gather | solution.py:291
  743.8 86.4 %copy-start.6 = (f32[4,14,768]{2,0,1:T(4,128)S(1)}, f32[4,14,768]{2,0,1:T(4,128)}, u32[]{:S(2)}) copy-start(f32[4,14,768]{2,0,1:T(4,128)} %param.24) | copy-start | bytes 516100
  743.9 86.4 %copy-start.19 = (s32[1,128]{1,0:T(1,128)S(1)}, s32[1,128]{1,0:T(1,128)}, u32[]{:S(2)}) copy-start(s32[1,128]{1,0:T(1,128)} %param.18) | copy-start | bytes 1540
  830.3 113.4 %copy-start.66 = (s32[1,128]{1,0:T(1,128)S(1)}, s32[1,128]{1,0:T(1,128)}, u32[]{:S(2)}) copy-start(s32[1,128]{1,0:T(1,128)} %param.17) | copy-start | bytes 1540
  899.2 120.4 %copy-start = (f32[4,128,768]{2,1,0:T(8,128)}, f32[4,128,768]{2,1,0:T(8,128)S(1)}, u32[]{:S(2)}) copy-start(f32[4,128,768]{2,1,0:T(8,128)S(1)} %get-tuple-element.767) | copy-start | bytes 4718596
  899.2 722.6 %reduce-scatter.3.cloned.1.call-start = ((), (), s32[]{:S(2)}) async-start(), calls=%async_computation.5 | async-start | bytes 1966080 | tf_op jit(solution)/shard_map/reduce_scatter | solution.py:348
  943.6 22.2 copy-start.58
  962.7 56.5 %copy-start.25 = (s32[4,1,128]{2,1,0:T(1,128)}, s32[4,1,128]{2,1,0:T(1,128)S(1)}, u32[]{:S(2)}) copy-start(s32[4,1,128]{2,1,0:T(1,128)S(1)} %all-gather.2) | copy-start | bytes 6148
  963.4 56.2 %copy-start.17 = (f32[768]{0:T(1024)}, f32[768]{0:T(1024)S(1)}, u32[]{:S(2)}) copy-start(f32[768]{0:T(1024)S(1)} %get-tuple-element.306) | copy-start | bytes 9220
  963.4 56.2 %copy-start.21 = (f32[768]{0:T(1024)}, f32[768]{0:T(1024)S(1)}, u32[]{:S(2)}) copy-start(f32[768]{0:T(1024)S(1)} %get-tuple-element.305) | copy-start | bytes 9220
  1020.4 187.2 %copy-start.70 = (f32[4]{0:T(128)S(1)}, f32[4]{0:T(128)}, u32[]{:S(2)}) copy-start(f32[4]{0:T(128)} %fusion.185) | copy-start | bytes 52
  1020.4 187.2 %copy-start.71 = (f32[128]{0:T(128)S(1)}, f32[128]{0:T(128)}, u32[]{:S(2)}) copy-start(f32[128]{0:T(128)} %pad_maximum_fusion.3) | copy-start | bytes 1540
  1020.4 187.9 %copy-start.68 = (f32[127]{0:T(128)S(1)}, f32[127]{0:T(128)}, u32[]{:S(2)}) copy-start(f32[127]{0:T(128)} %copy-done.67) | copy-start | bytes 1528
  1020.4 197.9 %copy-start.50 = (f32[512]{0:T(512)S(1)}, f32[512]{0:T(512)}, u32[]{:S(2)}) copy-start(f32[512]{0:T(512)} %select_reduce_fusion) | copy-start | bytes 6148
  1187.9 78.6 %copy-start.27 = (pred[512]{0:T(512)(128)(4,1)}, pred[512]{0:T(512)(128)(4,1)S(1)}, u32[]{:S(2)}) copy-start(pred[512]{0:T(512)(128)(4,1)S(1)} %get-tuple-element.790) | copy-start | bytes 1540
  1218.4 48.1 %copy-start.26 = (s32[4,1,128]{2,1,0:T(1,128)S(1)}, s32[4,1,128]{2,1,0:T(1,128)}, u32[]{:S(2)}) copy-start(s32[4,1,128]{2,1,0:T(1,128)} %copy-done.25) | copy-start | bytes 6148
  1266.5 321.1 %copy-start.5 = (bf16[128,768]{1,0:T(8,128)(2,1)S(1)}, bf16[128,768]{1,0:T(8,128)(2,1)}, u32[]{:S(2)}) copy-start(bf16[128,768]{1,0:T(8,128)(2,1)} %fusion.131) | copy-start | bytes 589828
  1266.5 321.1 %copy-start.33 = (f32[768]{0:T(1024)S(1)}, f32[768]{0:T(1024)}, u32[]{:S(2)}) copy-start(f32[768]{0:T(1024)} %get-tuple-element.304) | copy-start | bytes 9220
  1270.3 28.5 copy-start.28
  1350.5 28.5 copy-start.28
  1430.6 28.5 copy-start.28
  1510.9 28.5 copy-start.28
  1587.3 6.6 copy-start.38
  1587.3 339.6 %all-reduce.7.cloned.1.call-start = ((), (), s32[]{:S(2)}) async-start(), calls=%async_computation.7 | async-start | bytes 344064 | tf_op jit(solution)/shard_map/psum | solution.py:368
  1589.6 6.3 copy-start.15
  1591.6 4.2 copy-start.9
  1595.2 6.9 copy-start.47
  1595.2 2.8 copy-start.20
  1595.2 2.8 copy-start.29
  1595.2 2.8 copy-start.43
  1597.8 37.1 copy-start.45
  1598.0 4.1 copy-start.63
  1598.0 4.1 copy-start.54
  1598.1 4.1 copy-start.57
  1602.2 4.1 copy-start.3
  1602.2 19.6 copy-start.23
  1625.6 5.4 copy-start.55
  1631.0 3.9 copy-start.64
  1635.9 7.1 copy-start.48
  1643.0 2.7 copy-start.8
  1646.9 3.4 copy-start.30
  1646.9 3.4 copy-start.46
  1646.9 3.4 copy-start.56
  1652.1 11.1 copy-start.40
  1652.1 11.1 copy-start.39
  1652.1 11.2 copy-start.35
  1652.1 11.2 copy-start.34
  1652.1 11.3 copy-start.51
  1652.1 11.3 copy-start.37
  1652.1 11.3 copy-start.36
  1652.1 11.3 copy-start.44
  1652.1 11.4 copy-start.60
  1653.7 9.5 copy-start.2
  1664.4 1733.5 %all-reduce.11.cloned.1.call-start = ((), (), s32[]{:S(2)}) async-start(), calls=%async_computation.9 | async-start | bytes 229638144
  1712.2 2126.9 %reduce-scatter.5.cloned.1.call-start = ((), (), s32[]{:S(2)}) async-start(), calls=%async_computation.6 | async-start | bytes 88473600 | tf_op jit(solution)/shard_map/reduce_scatter | solution.py:362
  1883.7 42.1 %copy-start.69 = (f32[4]{0:T(128)S(1)}, f32[4]{0:T(128)}, u32[]{:S(2)}) copy-start(f32[4]{0:T(128)} %get-tuple-element.308) | copy-start | bytes 52
  1883.7 43.2 %copy-start.7 = (f32[4,14,768]{2,0,1:T(4,128)S(1)}, f32[4,14,768]{2,0,1:T(4,128)}, u32[]{:S(2)}) copy-start(f32[4,14,768]{2,0,1:T(4,128)} %param.24) | copy-start | bytes 516100
  1883.7 43.2 %copy-start.16 = (f32[4,14,768]{2,0,1:T(4,128)S(1)}, f32[4,14,768]{2,0,1:T(4,128)}, u32[]{:S(2)}) copy-start(f32[4,14,768]{2,0,1:T(4,128)} %param.25) | copy-start | bytes 516100
  3406.2 469.9 %copy-start.14 = (f32[4,14,768]{2,0,1:T(4,128)S(1)}, f32[4,14,768]{2,0,1:T(4,128)}, u32[]{:S(2)}) copy-start(f32[4,14,768]{2,0,1:T(4,128)} %all-reduce.7.cloned.1.call-done) | copy-start | bytes 516100
  (20 other events, 34.2 us)
Sparse Core Ops, SparseCore 0:
  37.1 355.0 all-gather.7
  395.5 309.8 all-gather.9
  708.3 119.2 all-reduce.8
  899.3 63.4 all-gather.11
  1587.4 34.3 reduce-scatter.2
  1664.5 121.3 all-reduce.6
  1792.3 1605.5 all-reduce.10
  3402.0 437.0 reduce-scatter.4
where the time goes:
time: 3900 us; the launch traced here: 3880 us
  waiting for transfers between devices  2630 us (67%)
  matrix products  378 us (10%)
  local copies, waits for them, and re-layouts  357 us (9%)
  other arithmetic  329 us (8%)
  blocking collectives  160 us (4%)
    unnamed x10, waiting for transfers between devices  1550 us
    reduce_scatter x1, waiting for transfers between devices, body(): lax.psum_scatter(grad_table.astype(jnp.bfloat16), 'grp', scatter_dimensio...  433 us
    all_gather x1, waiting for transfers between devices, body(): lax.all_gather(table.astype(jnp.bfloat16), 'grp', axis=1, tiled=True)  338 us
    all_gather x1, waiting for transfers between devices, body(): lax.all_gather(stack.astype(jnp.bfloat16), ('grp', 'cli'), axis=1, tiled=...  290 us
    dot_general x30, matrix products, project(): lax.dot_general(inputs, matrix, (((1,), (1,)), ((), ())), preferred_eleme...  174 us
    dot_general x8, matrix products, outer_rows(): lax.dot_general(left, right, (((0,), (0,)), ((), ())), preferred_element_...  119 us
    dynamic_slice x4, local copies, waits for them, and re-layouts, head_back(): lax.dynamic_index_in_dim(grad_table, model_pick, 0, keepdims=False)  108 us
  transfers between devices with their start and end apart: 8, of which 6 were waited for; matrix products, arithmetic and copies ran while one was open for 9% of the time, Pallas kernels for 0%

commit v1 on v0

v1 whole, which is shorter than its diff:
```python
import functools

import jax
import jax.numpy as jnp
from jax import lax
from jax.experimental import pallas as pl
from jax.experimental.pallas import tpu as pltpu
from jax.sharding import PartitionSpec as P

HEADS = 12
HEAD_DIM = 64


epsilon = 1e-05
momentum_decay = 0.9
table_rate = 4.0
stack_rate = 4.0
vector_rate = 50.0

ROUND_ROWS = 128
MIB = 1 << 20


def layer_norm(inputs, gain_row, shift_row):
    centred = inputs - jnp.mean(inputs, -1, keepdims=True)
    spread = jnp.mean(centred * centred, -1, keepdims=True)
    return centred * lax.rsqrt(spread + epsilon) * gain_row + shift_row


def project(inputs, matrix):
    return lax.dot_general(
        inputs, matrix, (((1,), (1,)), ((), ())), preferred_element_type=jnp.float32
    )


def product(inputs, matrix):
    return jnp.dot(inputs, matrix, preferred_element_type=jnp.float32)


def outer_rows(left, right):
    return lax.dot_general(
        left, right, (((0,), (0,)), ((), ())), preferred_element_type=jnp.float32
    )


def split_heads(rows, seq_len):
    return rows.reshape(-1, seq_len, HEADS, HEAD_DIM)


def attend(queries, key_rows, segment_rows):
    seq_len = segment_rows.shape[1]
    scores = jnp.einsum(
        "nqhd,nkhd->nhqk",
        split_heads(queries, seq_len),
        split_heads(key_rows, seq_len),
        preferred_element_type=jnp.float32,
    ) * HEAD_DIM ** (-0.5)
    positions = jnp.arange(seq_len)
    allowed = (positions[None, None, :] <= positions[None, :, None]) & (
        segment_rows[:, None, :] == segment_rows[:, :, None]
    )
    return jax.nn.softmax(jnp.where(allowed[:, None], scores, -1e30), axis=-1)


def layer_forward(weights, vector_one, inputs, segment_rows):
    row_count, model_width = inputs.shape
    seq_len = segment_rows.shape[1]
    normed = layer_norm(inputs, vector_one[0], vector_one[1]).astype(jnp.bfloat16)
    queries = (project(normed, weights[0:model_width]) + vector_one[6]).astype(jnp.bfloat16)
    key_rows = project(normed, weights[model_width : 2 * model_width]).astype(jnp.bfloat16)
    values = (project(normed, weights[2 * model_width : 3 * model_width]) + vector_one[7]).astype(
        jnp.bfloat16
    )
    attention = attend(queries, key_rows, segment_rows)
    mixture = jnp.einsum(
        "nhqk,nkhd->nqhd",
        attention.astype(jnp.bfloat16),
        split_heads(values, seq_len),
        preferred_element_type=jnp.float32,
    )
    mixture = mixture.reshape(row_count, model_width).astype(jnp.bfloat16)
    middle = inputs + (project(mixture, weights[3 * model_width : 4 * model_width]) + vector_one[8])
    normed_two = layer_norm(middle, vector_one[2], vector_one[3]).astype(jnp.bfloat16)
    hidden = project(normed_two, weights[4 * model_width : 8 * model_width]) + vector_one[
        10:14
    ].reshape(-1)
    active = jax.nn.gelu(hidden, approximate=True).astype(jnp.bfloat16)
    residual = middle + (
        product(active, weights[8 * model_width : 12 * model_width]) + vector_one[9]
    )
    normed_out = layer_norm(residual, vector_one[4], vector_one[5]).astype(jnp.bfloat16)
    return (
        normed,
        queries,
        key_rows,
        values,
        attention,
        mixture,
        middle,
        normed_two,
        hidden,
        active,
        residual,
        normed_out,
    )


def norm_grad(operand, gain_row, shift_row, cotangent):
    outcome, pullback = jax.vjp(layer_norm, operand, gain_row, shift_row)
    return pullback(cotangent)


def gelu_tanh(hidden):
    return jax.nn.gelu(hidden, approximate=True)


def layer_backward(weights, vector_one, inputs, segment_rows, saved, grad_out):
    row_count, model_width = inputs.shape
    seq_len = segment_rows.shape[1]
    scaling = HEAD_DIM ** (-0.5)
    (
        normed,
        queries,
        key_rows,
        values,
        attention,
        mixture,
        middle,
        normed_two,
        hidden,
        active,
        residual,
        normed_out,
    ) = saved
    d_residual, d_gain_out, d_shift_out = norm_grad(
        residual, vector_one[4], vector_one[5], grad_out
    )
    d_outer = d_residual.astype(jnp.bfloat16)
    d_bias_out = jnp.sum(d_outer.astype(jnp.float32), 0)
    grad_down = outer_rows(active, d_outer)
    d_active = project(d_outer, weights[8 * model_width : 12 * model_width])
    gelu_value, gelu_pull = jax.vjp(gelu_tanh, hidden)
    d_hidden = gelu_pull(d_active)[0].astype(jnp.bfloat16)
    d_bias_hidden = jnp.sum(d_hidden.astype(jnp.float32), 0)
    grad_up = outer_rows(d_hidden, normed_two)
    d_normed_two = product(d_hidden, weights[4 * model_width : 8 * model_width])
    d_middle_norm, d_gain_two, d_shift_two = norm_grad(
        middle, vector_one[2], vector_one[3], d_normed_two
    )
    d_middle = d_residual + d_middle_norm
    d_branch = d_middle.astype(jnp.bfloat16)
    d_bias_branch = jnp.sum(d_branch.astype(jnp.float32), 0)
    grad_mix = outer_rows(d_branch, mixture)
    d_mixture = split_heads(
        product(d_branch, weights[3 * model_width : 4 * model_width]).astype(jnp.bfloat16), seq_len
    )
    d_attention = jnp.einsum(
        "nqhd,nkhd->nhqk", d_mixture, split_heads(values, seq_len), preferred_element_type=jnp.float32
    )
    d_values = jnp.einsum(
        "nhqk,nqhd->nkhd",
        attention.astype(jnp.bfloat16),
        d_mixture,
        preferred_element_type=jnp.float32,
    )
    d_values = d_values.reshape(row_count, model_width).astype(jnp.bfloat16)
    d_scores = (
        attention * (d_attention - jnp.sum(attention * d_attention, -1, keepdims=True))
    ).astype(jnp.bfloat16)
    d_queries = (
        jnp.einsum(
            "nhqk,nkhd->nqhd",
            d_scores,
            split_heads(key_rows, seq_len),
            preferred_element_type=jnp.float32,
        )
        * scaling
    )
    d_queries = d_queries.reshape(row_count, model_width).astype(jnp.bfloat16)
    d_keys = (
        jnp.einsum(
            "nhqk,nqhd->nkhd",
            d_scores,
            split_heads(queries, seq_len),
            preferred_element_type=jnp.float32,
        )
        * scaling
    )
    d_keys = d_keys.reshape(row_count, model_width).astype(jnp.bfloat16)
    d_joined = jnp.concatenate([d_queries, d_keys, d_values], axis=1)
    grad_joined = outer_rows(d_joined, normed)
    d_normed = product(d_joined, weights[0 : 3 * model_width])
    d_inputs_norm, d_gain_one, d_shift_one = norm_grad(
        inputs, vector_one[0], vector_one[1], d_normed
    )
    d_inputs = d_middle + d_inputs_norm
    grad_places = jnp.sum(d_inputs.reshape(-1, seq_len, model_width), axis=0)
    stack_rows = jnp.concatenate(
        [
            piece.astype(jnp.bfloat16)
            for piece in (grad_joined, grad_mix, grad_up, grad_down, grad_places)
        ],
        axis=0,
    )
    bias_query = jnp.sum(d_queries.astype(jnp.float32), 0)
    bias_value = jnp.sum(d_values.astype(jnp.float32), 0)
    vector_rows = jnp.concatenate(
        [
            jnp.stack(
                [
                    d_gain_one,
                    d_shift_one,
                    d_gain_two,
                    d_shift_two,
                    d_gain_out,
                    d_shift_out,
                    bias_query,
                    bias_value,
                    d_bias_branch,
                    d_bias_out,
                ]
            ),
            d_bias_hidden.reshape(4, model_width),
        ],
        axis=0,
    )
    return (stack_rows, vector_rows, d_inputs)


def update(weight, momentum, gradient, step_rate):
    renewed = momentum_decay * momentum + gradient
    return (renewed, weight - step_rate * (gradient + momentum_decay * renewed))


def stats_kernel(outs_ref, table_ref, target_ref, stat_ref):
    logits = project(table_ref[0], outs_ref[0])
    highest = jnp.max(logits, axis=0, keepdims=True)
    total = jnp.sum(jnp.exp(logits - highest), axis=0, keepdims=True)
    rows = lax.broadcasted_iota(jnp.int32, logits.shape, 0)
    hit = jnp.sum(jnp.where(rows == target_ref[0], logits, 0.0), axis=0, keepdims=True)
    stat_ref[0, 0:1, :] = highest + jnp.log(total)
    stat_ref[0, 1:2, :] = hit


def head_stats(outs_all, table_low, target_blocks, groups, members, share):
    blocks, rows, width = outs_all.shape
    part_rows = table_low.shape[1]
    return pl.pallas_call(
        stats_kernel,
        out_shape=jax.ShapeDtypeStruct((blocks, 2, rows), jnp.float32),
        grid=(members, groups),
        in_specs=[
            pl.BlockSpec((1, rows, width), lambda z, g: (g * members + z, 0, 0)),
            pl.BlockSpec((1, part_rows, width), lambda z, g: (z // share, 0, 0)),
            pl.BlockSpec((1, 1, rows), lambda z, g: (g * share + z % share, 0, 0)),
        ],
        out_specs=pl.BlockSpec((1, 2, rows), lambda z, g: (g * members + z, 0, 0)),
        compiler_params=pltpu.CompilerParams(vmem_limit_bytes=56 * MIB),
        cost_estimate=pl.CostEstimate(
            flops=2 * blocks * rows * part_rows * width,
            bytes_accessed=2 * outs_all.size + 2 * table_low.size,
            transcendentals=blocks * rows * part_rows,
        ),
    )(outs_all, table_low, target_blocks)


def back_kernel(
    model_ref, fresh_ref, first_ref, second_ref, a_ref, b_ref, table_ref, info_ref, target_ref, d_outs_ref, grad_ref
):
    step = pl.program_id(0)
    seq_len = a_ref.shape[1]
    outs = jnp.concatenate([a_ref[0], b_ref[0]], axis=0)
    logits = project(table_ref[0], outs)
    rows = lax.broadcasted_iota(jnp.int32, logits.shape, 0)
    soft = jnp.exp(logits - info_ref[0, 0:1, :])
    hit = (rows == target_ref[0]).astype(jnp.float32)
    d_logits = (info_ref[0, 1:2, :] * (soft - hit)).astype(jnp.bfloat16)
    d_outs = outer_rows(d_logits, table_ref[0])
    d_outs_ref[0] = d_outs[:seq_len].astype(d_outs_ref.dtype)
    d_outs_ref[1] = d_outs[seq_len:].astype(d_outs_ref.dtype)
    gain = product(d_logits, outs)

    @pl.when(fresh_ref[step] == 1)
    def start():
        grad_ref[0] = gain

    @pl.when(fresh_ref[step] == 0)
    def more():
        grad_ref[0] += gain


def head_back(outs_pieces, table_low, model_of, fresh, first, second, info, target):
    steps = model_of.shape[0]
    models, part_rows, width = table_low.shape
    seq_len = outs_pieces.shape[1]
    return pl.pallas_call(
        back_kernel,
        out_shape=(
            jax.ShapeDtypeStruct((2 * steps, seq_len, width), jnp.bfloat16),
            jax.ShapeDtypeStruct((models, part_rows, width), jnp.float32),
        ),
        grid_spec=pltpu.PrefetchScalarGridSpec(
            num_scalar_prefetch=4,
            grid=(steps,),
            in_specs=[
                pl.BlockSpec((1, seq_len, width), lambda s, m, f, a, b: (a[s], 0, 0)),
                pl.BlockSpec((1, seq_len, width), lambda s, m, f, a, b: (b[s], 0, 0)),
                pl.BlockSpec((1, part_rows, width), lambda s, m, f, a, b: (m[s], 0, 0)),
                pl.BlockSpec((1, 2, 2 * seq_len), lambda s, m, f, a, b: (s, 0, 0)),
                pl.BlockSpec((1, 1, 2 * seq_len), lambda s, m, f, a, b: (s, 0, 0)),
            ],
            out_specs=(
                pl.BlockSpec((2, seq_len, width), lambda s, m, f, a, b: (s, 0, 0)),
                pl.BlockSpec((1, part_rows, width), lambda s, m, f, a, b: (m[s], 0, 0)),
            ),
        ),
        compiler_params=pltpu.CompilerParams(vmem_limit_bytes=56 * MIB),
        cost_estimate=pl.CostEstimate(
            flops=12 * steps * seq_len * part_rows * width,
            bytes_accessed=4 * steps * seq_len * width * 2 + 6 * table_low.size,
            transcendentals=2 * steps * seq_len * part_rows,
        ),
    )(model_of, fresh, first, second, outs_pieces, outs_pieces, table_low, info, target)


def finish_kernel(
    model_ref, fresh_ref, final_ref, first_ref, second_ref, a_ref, b_ref, ids_ref, head_ref, table_ref, momentum_ref,
    grad_ref, momentum_new_ref, table_new_ref,
):
    tile = pl.program_id(0)
    step = pl.program_id(1)
    tile_rows = grad_ref.shape[1]
    rows = lax.broadcasted_iota(jnp.int32, (tile_rows, ids_ref.shape[2]), 0) + tile * tile_rows
    hits = (rows == ids_ref[0]).astype(jnp.float32).astype(jnp.bfloat16)
    outs = jnp.concatenate([a_ref[0], b_ref[0]], axis=0)
    gain = product(hits, outs)

    @pl.when(fresh_ref[step] == 1)
    def start():
        grad_ref[0] = head_ref[0] + gain

    @pl.when(fresh_ref[step] == 0)
    def more():
        grad_ref[0] += gain

    @pl.when(final_ref[step] == 1)
    def close():
        renewed, fresh_table = update(table_ref[0], momentum_ref[0], grad_ref[0], table_rate)
        momentum_new_ref[0] = renewed
        table_new_ref[0] = fresh_table


def finish_table(d_inputs, head_grad, table, momentum, model_of, fresh, final, first, second, ids):
    steps = model_of.shape[0]
    models, part_rows, width = table.shape
    seq_len = d_inputs.shape[1]
    tile_rows = part_rows // 2
    state = jax.ShapeDtypeStruct(table.shape, jnp.float32)
    piece = pl.BlockSpec((1, tile_rows, width), lambda t, s, m, f, l, a, b: (m[s], t, 0))
    return pl.pallas_call(
        finish_kernel,
        out_shape=(state, state, state),
        grid_spec=pltpu.PrefetchScalarGridSpec(
            num_scalar_prefetch=5,
            grid=(part_rows // tile_rows, steps),
            in_specs=[
                pl.BlockSpec((1, seq_len, width), lambda t, s, m, f, l, a, b: (a[s], 0, 0)),
                pl.BlockSpec((1, seq_len, width), lambda t, s, m, f, l, a, b: (b[s], 0, 0)),
                pl.BlockSpec((1, 1, 2 * seq_len), lambda t, s, m, f, l, a, b: (s, 0, 0)),
                piece,
                piece,
                piece,
            ],
            out_specs=(piece, piece, piece),
        ),
        compiler_params=pltpu.CompilerParams(vmem_limit_bytes=56 * MIB),
        cost_estimate=pl.CostEstimate(
            flops=4 * steps * seq_len * part_rows * width,
            bytes_accessed=24 * table.size,
            transcendentals=0,
        ),
    )(model_of, fresh, final, first, second, d_inputs, d_inputs, ids, head_grad, table, momentum)


def body(
    token_ids,
    target_ids,
    segment_ids,
    chosen,
    table,
    table_momentum,
    stack,
    stack_momentum,
    vectors,
    vector_momentum,
):
    both = ("grp", "cli")
    models, block_rows, model_width = table.shape
    stack_part = stack.shape[1]
    seq_len = token_ids.shape[1]
    groups = lax.axis_size("grp")
    members = lax.axis_size("cli")
    devices = groups * members
    share = members // models
    local = members // share
    device_index = lax.axis_index(both)
    group_index = lax.axis_index("grp")
    member_index = lax.axis_index("cli")
    model_own = member_index // share
    part_own = member_index % share
    model_range = jnp.arange(models, dtype=jnp.int32)

    def per_member(rows):
        return jnp.repeat(rows, share, axis=0) if share > 1 else rows

    stack_low = per_member(stack.astype(jnp.bfloat16))
    stack_turned = lax.all_to_all(stack_low, "cli", 0, 0, tiled=True)
    weights = lax.all_gather(stack_turned, "grp", axis=0, tiled=True).reshape(
        devices * stack_part, model_width
    )

    facts = lax.all_gather(
        jnp.concatenate([token_ids, target_ids, segment_ids, chosen[:, None]], axis=1),
        both,
        axis=0,
        tiled=True,
    )
    tokens = facts[:, :seq_len]
    targets = facts[:, seq_len : 2 * seq_len]
    segments = facts[:, 2 * seq_len : 3 * seq_len]
    choices = facts[:, 3 * seq_len]
    valid = jnp.concatenate(
        [
            (segments[:, :-1] == segments[:, 1:]).astype(jnp.float32),
            jnp.zeros((devices, 1), jnp.float32),
        ],
        axis=1,
    )
    counts = jnp.sum(valid, axis=1)
    choice_table = (choices[:, None] == model_range[None, :]).astype(jnp.float32)
    totals = jnp.sum(choice_table * counts[:, None], axis=0)
    total_of = jnp.sum(choice_table * totals[None, :], axis=1)

    table_low = table.astype(jnp.bfloat16)
    fine = 16 if block_rows % 64 else 64
    coarse = block_rows // fine
    flat_tokens = tokens.reshape(-1)
    high_hot = (
        (flat_tokens // fine)[:, None] == jnp.arange(devices * coarse, dtype=jnp.int32)[None, :]
    ).astype(jnp.bfloat16)
    low_hot = ((flat_tokens % fine)[:, None] == jnp.arange(fine, dtype=jnp.int32)[None, :]).astype(
        jnp.bfloat16
    )
    seen = (outer_rows(high_hot, low_hot) > 0).astype(jnp.float32)
    before = product(
        seen.astype(jnp.bfloat16),
        jnp.triu(jnp.ones((fine, fine), jnp.bfloat16), 1),
    )
    sums = jnp.sum(seen, axis=1).reshape(devices, coarse)
    uniques = jnp.sum(sums, axis=1)
    ahead = jnp.sum(
        jnp.where(
            jnp.arange(coarse)[None, None, :] < jnp.arange(coarse)[None, :, None],
            sums[:, None, :],
            0.0,
        ),
        axis=2,
    )
    places = before + ahead.reshape(-1, 1)
    rounds = jnp.max(jnp.ceil(uniques / ROUND_ROWS)).astype(jnp.int32)
    own_places = lax.dynamic_slice(places, (device_index * coarse, 0), (coarse, fine)).reshape(-1)
    own_seen = lax.dynamic_slice(seen, (device_index * coarse, 0), (coarse, fine)).reshape(-1)
    own_places = jnp.where(own_seen > 0, own_places, -1.0).astype(jnp.int32)
    first_client = group_index * members + part_own * local
    my_tokens = lax.dynamic_slice(tokens, (first_client, 0), (local, seq_len)).reshape(-1)
    my_segments = lax.dynamic_slice(segments, (first_client, 0), (local, seq_len))
    my_choices = lax.dynamic_slice(choices, (first_client,), (local,))
    my_high = (
        (my_tokens // fine)[:, None] == jnp.arange(devices * coarse, dtype=jnp.int32)[None, :]
    ).astype(jnp.bfloat16)
    my_low = (my_tokens % fine)[:, None] == jnp.arange(fine, dtype=jnp.int32)[None, :]
    split_places = jnp.concatenate(
        [jnp.floor(places / 64.0), places - 64.0 * jnp.floor(places / 64.0)], axis=1
    ).astype(jnp.bfloat16)
    picked_places = product(my_high, split_places)
    picked_places = 64.0 * picked_places[:, :fine] + picked_places[:, fine:]
    my_places = jnp.sum(jnp.where(my_low, picked_places, 0.0), axis=1).astype(jnp.int32)
    my_owner = my_tokens // block_rows

    def fetch(round_index, embedded):
        start = round_index * ROUND_ROWS
        wanted = jnp.arange(ROUND_ROWS, dtype=jnp.int32) + start
        pick = (own_places[None, :] == wanted[:, None]).astype(jnp.bfloat16)
        rows = jnp.einsum("ur,krd->kud", pick, table_low, preferred_element_type=jnp.float32)
        rows = per_member(rows.astype(jnp.bfloat16))
        turned = lax.all_to_all(rows, "cli", 0, 0, tiled=True)
        pool = lax.all_gather(turned, "grp", axis=0, tiled=True).reshape(-1, model_width)
        offset = my_places - start
        inside = (offset >= 0) & (offset < ROUND_ROWS)
        found = jnp.take(pool, jnp.where(inside, my_owner * ROUND_ROWS + offset, 0), axis=0)
        return jnp.where(inside[:, None], found.astype(jnp.float32), embedded)

    embedded = fetch(jnp.int32(0), jnp.zeros((local * seq_len, model_width), jnp.float32))
    _, embedded = lax.while_loop(
        lambda carry: carry[0] < rounds,
        lambda carry: (carry[0] + 1, fetch(carry[0], carry[1])),
        (jnp.int32(1), embedded),
    )
    vector_one = lax.dynamic_index_in_dim(vectors, model_own, 0, keepdims=False)
    inputs = embedded + jnp.tile(weights[12 * model_width :].astype(jnp.float32), (local, 1))
    saved = layer_forward(weights, vector_one, inputs, my_segments)
    normed_out = saved[11]

    outs_all = lax.all_gather(normed_out[None], both, axis=0, tiled=True)
    target_local = targets - device_index * block_rows
    target_local = jnp.where((target_local >= 0) & (target_local < block_rows), target_local, -1)
    stats = head_stats(
        outs_all,
        table_low,
        target_local.reshape(groups * share, 1, local * seq_len),
        groups,
        members,
        share,
    )
    shares = lax.all_to_all(stats, both, 0, 0, tiled=True)
    log_total = jax.nn.logsumexp(shares[:, 0], axis=0)
    token_loss = log_total - jnp.sum(shares[:, 1], axis=0)
    everything = lax.all_gather(
        jnp.stack([log_total, token_loss])[None], both, axis=0, tiled=True
    )
    everything = (
        everything.reshape(groups, models, share, 2, local, seq_len)
        .transpose(3, 1, 0, 2, 4, 5)
        .reshape(2, models, devices, seq_len)
    )
    all_losses = jnp.sum(everything[1] * valid[None], axis=2)
    loss = jnp.sum(choice_table.T * all_losses / total_of[None, :])
    client_losses = lax.dynamic_slice(
        (all_losses / counts[None, :]).T, (device_index, 0), (1, models)
    )
    chosen_total = jnp.sum(choice_table.T[:, :, None] * everything[0], axis=0)

    numbers = jnp.sum(choice_table, axis=0)
    padded = 2.0 * jnp.ceil(numbers / 2.0)
    offsets = jnp.cumsum(padded) - padded
    earlier = (
        jnp.arange(devices)[None, :] < jnp.arange(devices)[:, None]
    ) & (choices[None, :] == choices[:, None])
    slot_of = jnp.sum(choice_table * offsets[None, :], axis=1) + jnp.sum(
        earlier.astype(jnp.float32), axis=1
    )
    slots = devices + models
    steps = slots // 2
    at_slot = jnp.arange(slots)[:, None] == slot_of.astype(jnp.int32)[None, :]
    filled = jnp.any(at_slot, axis=1)
    client_at = jnp.sum(jnp.where(at_slot, jnp.arange(devices)[None, :], 0), axis=1).astype(
        jnp.int32
    )
    step_start = 2.0 * jnp.arange(steps)
    model_of = (
        jnp.sum((step_start[:, None] >= offsets[None, :]).astype(jnp.int32), axis=1) - 1
    ).astype(jnp.int32)
    fresh = jnp.concatenate(
        [jnp.ones((1,), jnp.int32), (model_of[1:] != model_of[:-1]).astype(jnp.int32)]
    )
    final = jnp.concatenate(
        [(model_of[1:] != model_of[:-1]).astype(jnp.int32), jnp.ones((1,), jnp.int32)]
    )
    within = client_at % members
    piece_at = (
        (client_at // members * members + jnp.repeat(model_of, 2) * share + within // local) * local
        + within % local
    ).astype(jnp.int32)
    weight_rows = valid / total_of[:, None]
    slot_log = jnp.where(filled[:, None], jnp.take(chosen_total, client_at, axis=0), 1e30)
    slot_weight = jnp.where(filled[:, None], jnp.take(weight_rows, client_at, axis=0), 0.0)
    slot_info = jnp.stack(
        [slot_log.reshape(steps, 2 * seq_len), slot_weight.reshape(steps, 2 * seq_len)], axis=1
    )
    slot_target = jnp.where(filled[:, None], jnp.take(target_local, client_at, axis=0), -1)
    d_slots, head_grad = head_back(
        outs_all.reshape(-1, seq_len, model_width),
        table_low,
        model_of,
        fresh,
        piece_at[0::2],
        piece_at[1::2],
        slot_info,
        slot_target.reshape(steps, 1, 2 * seq_len),
    )
    d_outs = jnp.take(d_slots, slot_of.astype(jnp.int32), axis=0)
    d_group = lax.psum_scatter(
        d_outs.reshape(devices * seq_len, model_width), "grp", scatter_dimension=0, tiled=True
    )
    d_group = lax.psum(d_group, "cli").reshape(members, seq_len, model_width)
    d_mine = lax.dynamic_slice(
        d_group, (part_own * local, 0, 0), (local, seq_len, model_width)
    ).astype(jnp.float32)
    d_final = jnp.where((my_choices == model_own)[:, None, None], d_mine, 0.0).reshape(
        local * seq_len, model_width
    )
    stack_rows, vector_rows, d_inputs = layer_backward(
        weights, vector_one, inputs, my_segments, saved, d_final
    )
    d_wide = d_inputs.astype(jnp.bfloat16)
    if share > 1:
        d_wide = lax.dynamic_update_slice(
            jnp.zeros((members * seq_len, model_width), jnp.bfloat16),
            d_wide,
            (part_own * local * seq_len, 0),
        )
    d_client = lax.psum_scatter(d_wide, "cli", scatter_dimension=0, tiled=True)
    d_all = lax.all_gather(d_client[None], both, axis=0, tiled=True)

    stack_sum = lax.psum_scatter(stack_rows, "grp", scatter_dimension=0, tiled=True)
    stack_back = lax.all_to_all(
        stack_sum.reshape(members, stack_part, model_width), "cli", 0, 0, tiled=True
    ).astype(jnp.float32)
    stack_grad = jnp.sum(
        stack_back.reshape(models, share, stack_part, model_width), axis=1
    )
    vector_masked = jnp.where((model_range == model_own)[:, None, None], vector_rows[None], 0.0)
    vector_grad = lax.psum(vector_masked, both)

    token_local = tokens - device_index * block_rows
    token_local = jnp.where((token_local >= 0) & (token_local < block_rows), token_local, -1)
    slot_token = jnp.where(filled[:, None], jnp.take(token_local, client_at, axis=0), -1)
    table_grad, table_momentum_new, table_new = finish_table(
        d_all,
        head_grad,
        table,
        table_momentum,
        model_of,
        fresh,
        final,
        client_at[0::2],
        client_at[1::2],
        slot_token.reshape(steps, 1, 2 * seq_len),
    )
    stack_momentum_new, stack_new = update(stack, stack_momentum, stack_grad, stack_rate)
    vector_momentum_new, vector_new = update(vectors, vector_momentum, vector_grad, vector_rate)
    return (
        loss,
        client_losses,
        table_grad,
        table_momentum_new,
        table_new,
        stack_grad,
        stack_momentum_new,
        stack_new,
        vector_grad,
        vector_momentum_new,
        vector_new,
    )


def solution(mesh):
    rows = P(("grp", "cli"), None)
    parts = P(None, ("grp", "cli"), None)
    return jax.shard_map(
        body,
        mesh=mesh,
        in_specs=(rows, rows, rows, P(("grp", "cli")), parts, parts, parts, parts, P(), P()),
        out_specs=(P(), rows, parts, parts, parts, parts, parts, parts, P(), P(), P()),
        check_vma=False,
    )
```

time: 3900 us -> 1290 us (0.33)
  waiting for transfers between devices: 2630 us -> 645 us
  matrix products: 378 us -> 80.9 us
  local copies, waits for them, and re-layouts: 357 us -> 70.3 us
  other arithmetic: 329 us -> 43.3 us
  Pallas kernels: 0 us -> 216 us
    unnamed x10 -> x9, waiting for transfers between devices: 1550 us -> 0.15 us
    all_gather x3 -> x4, waiting for transfers between devices: 628 us -> 291 us  [the longest x1 150 us: body(): outs_all = lax.all_gather(normed_out[None], both, axis=0, tiled=True)]
    reduce_scatter x2 -> x3, waiting for transfers between devices: 448 us -> 167 us  [the longest x1 106 us: body(): lax.psum_scatter(stack_rows, 'grp', scatter_dimension=0, tiled=True)]
    pallas_call x0 -> x3, Pallas kernels: none -> 216 us  [the longest x1 74.1 us: head_back(): pl.pallas_call(back_kernel, out_shape=(jax.ShapeDtypeStruct((2 * steps, s...]
    psum x1 -> x2, waiting for transfers between devices: 0.01 us -> 182 us  [the longest x1 136 us: body(): vector_grad = lax.psum(vector_masked, both)]
    dot_general x30 -> x6, matrix products: 174 us -> 23.2 us  [project(): lax.dot_general(inputs, matrix, (((1,), (1,)), ((), ())), preferred_eleme...]
    dynamic_slice x24 -> x0, local copies, waits for them, and re-layouts: 116 us -> none  [the longest x4 108 us: head_back(): lax.dynamic_index_in_dim(grad_table, model_pick, 0, keepdims=False)]
    dot_general x8 -> x5, matrix products: 119 us -> 25 us  [outer_rows(): lax.dot_general(left, right, (((0,), (0,)), ((), ())), preferred_element_...]
  transfers between devices with their start and end apart: 8 -> 11, of which waited for: 6 -> 9; matrix products, arithmetic and copies ran while one was open for 9% -> 4% of each run, Pallas kernels for 0% -> 5%
where the time goes in v1:
time: 1290 us; the launch traced here: 1280 us
  waiting for transfers between devices  645 us (50%)
  Pallas kernels  216 us (17%)
  blocking collectives  197 us (15%)
  matrix products  80.9 us (6%)
  local copies, waits for them, and re-layouts  70.3 us (5%)
  other arithmetic  43.3 us (3%)
  between operations  16.5 us (1%)
    all_gather x1, waiting for transfers between devices, body(): outs_all = lax.all_gather(normed_out[None], both, axis=0, tiled=True)  150 us
    psum x1, waiting for transfers between devices, body(): vector_grad = lax.psum(vector_masked, both)  136 us
    reduce_scatter x1, waiting for transfers between devices, body(): lax.psum_scatter(stack_rows, 'grp', scatter_dimension=0, tiled=True)  106 us
    pallas_call x1, Pallas kernels, head_back(): pl.pallas_call(back_kernel, out_shape=(jax.ShapeDtypeStruct((2 * steps, s...  74.1 us
    all_gather x1, waiting for transfers between devices, body(): d_all = lax.all_gather(d_client[None], both, axis=0, tiled=True)  72.7 us
    pallas_call x1, Pallas kernels, head_stats(): pl.pallas_call(stats_kernel, out_shape=jax.ShapeDtypeStruct((blocks, 2, r...  72.5 us
    all_gather x1, blocking collectives, body(): lax.all_gather(jnp.concatenate([token_ids, target_ids, segment_ids, chose...  70.1 us
    pallas_call x1, Pallas kernels, finish_table(): pl.pallas_call(finish_kernel, out_shape=(state, state, state), grid_spec=...  69.4 us
  transfers between devices with their start and end apart: 11, of which 9 were waited for; matrix products, arithmetic and copies ran while one was open for 4% of the time, Pallas kernels for 5%

profile of v1, /device:TPU:0, one launch (start us, length us, event | category | flops | bytes accessed | tf_op | source)
XLA Modules:
  0.0 1277.7 jit_solution(12242085703940469650)
XLA Ops:
  8.6 70.1 %all-gather.3 = s32[32,1,385]{2,1,0:T(1,128)S(1)} all-gather(s32[1,1,385]{2,1,0:T(1,128)S(1)} %add_bitcast_fusion), channel_id=1, replica_groups=mesh['grp'=8,'cli'=4] {'grp','cli'}, dimensions={0}, use_global_device_ids=true | all-gather | bytes 50820 | tf_op jit(solution)/shard_map/all_gather | solution.py:422
  78.8 2.6 fusion.137
  82.2 7.5 convert_element_type.248.table_ref
  89.6 1.8 fusion.43
  91.4 2.1 copy-done
  93.5 18.9 %all_to_all.26 = bf16[4,128,768]{2,1,0:T(8,128)(2,1)} all-to-all(bf16[4,128,768]{2,1,0:T(8,128)(2,1)S(1)} %fusion.43), channel_id=1, replica_groups=mesh['grp'=8,'cli'=4] {'cli'}, dimensions={0} | all-to-all | bytes 1572864 | tf_op jit(solution)/shard_map/all_to_all | solution.py:496
  112.5 2.5 copy.260
  115.0 43.0 %all_to_all.27 = bf16[4,292,768]{2,1,0:T(8,128)(2,1)} all-to-all(bf16[4,292,768]{2,1,0:T(8,128)(2,1)S(1)} %copy.260), channel_id=1, replica_groups=mesh['grp'=8,'cli'=4] {'cli'}, dimensions={0} | all-to-all | bytes 3588096 | tf_op jit(solution)/shard_map/all_to_all | solution.py:417
  160.2 1.0 fusion.99
  161.3 0.8 constant_dynamic-slice_fusion.1
  162.4 6.8 gather_fusion.1
  169.5 68.2 %all-gather.13.cloned.1.call-done = bf16[32,292,768]{2,1,0:T(8,128)(2,1)} async-done(((bf16[4,292,768]{2,1,0:T(8,128)(2,1)}), bf16[32,292,768]{2,1,0:T(8,128)(2,1)}) %all-gather.13.cloned.1.call-update) | async-done | bytes 14352400 | tf_op jit(solution)/shard_map/all_gather | solution.py:418
  237.7 16.8 %reshape.770 = bf16[9344,768]{1,0:T(8,128)(2,1)} reshape(bf16[32,292,768]{2,1,0:T(8,128)(2,1)} %all-gather.13.cloned.1.call-done) | data formatting | bytes 28704768 | tf_op jit(solution)/shard_map/reshape | solution.py:418
  254.5 1.0 slice_convert_fusion
  256.4 1.5 add_convert_fusion.4
  257.9 2.4 convolution_convert_fusion.6
  260.3 2.1 add_convert_fusion.2
  262.9 2.3 add_convert_fusion.3
  266.8 1.3 fusion.138
  268.7 1.0 copy-done.10
  270.7 2.2 fusion.139
  273.3 5.0 fusion.24
  278.3 8.7 fusion.140
  287.3 1.2 add_convert_fusion
  293.3 150.1 %all-gather.15.cloned.1.call-done = bf16[16384,768]{1,0:T(8,128)(2,1)} async-done(((bf16[512,768]{1,0:T(8,128)(2,1)}), bf16[16384,768]{1,0:T(8,128)(2,1)}) %all-gather.15.cloned.1.call-update) | async-done | bytes 25165840 | tf_op jit(solution)/shard_map/all_gather | solution.py:514
  443.3 72.5 %shard_map.185 = f32[32,2,512]{2,1,0:T(2,128)} custom-call(bf16[32,512,768]{2,1,0:T(8,128)(2,1)} %bitcast.244, bf16[4,1600,768]{2,1,0:T(8,128)(2,1)} %get-tuple-element.339, s32[8,1,512]{2,1,0:T(1,128)} %bitcast.223), custom_call_target="tpu_custom_call" | custom-call | flops 40265318400 | bytes 34996224 | tf_op jit(solution)/shard_map/pallas_call | solution.py:248
  515.9 2.8 all-to-all-start.3
  522.0 5.1 all-to-all-done.3
  527.3 65.0 %all-gather.4 = f32[32,2,512]{2,1,0:T(2,128)S(1)} all-gather(f32[1,2,512]{2,1,0:T(2,128)S(1)} %maximum_bitcast_fusion), channel_id=3, replica_groups=mesh['grp'=8,'cli'=4] {'grp','cli'}, dimensions={0}, use_global_device_ids=true | all-gather | bytes 135168 | tf_op jit(solution)/shard_map/all_gather | solution.py:528
  594.7 74.1 %shard_map.186 = (bf16[36,128,768]{2,1,0:T(8,128)(2,1)}, f32[4,1600,768]{2,1,0:T(8,128)}) custom-call(s32[18]{0:T(128)} %copy-done.49, s32[18]{0:T(128)} %get-tuple-element.217.fresh_ref, s32[18]{0:T(128)} %slice.167.first_ref, s32[18]{0:T(128)} %slice.168.second_ref, bf16[128,128,768]{2,1,0:T(8,128)(2,1)} %bitcast.245, bf16[128,128,768]{2,1,0:T(8,128)(2,1)} %bitcast.246, ...), custom_call_target="tpu_custom_call" | custom-call | flops 33973862400 | bytes 43646976 | tf_op jit(solution)/shard_map/pallas_call | solution.py:296
  668.8 6.8 gather_fusion.2
  675.6 7.4 bitcast_select_fusion
  683.1 59.4 %reduce-scatter.4.cloned.1.call-done = bf16[512,768]{1,0:T(8,128)(2,1)} async-done(((bf16[4096,768]{1,0:T(8,128)(2,1)}), bf16[512,768]{1,0:T(8,128)(2,1)}) %reduce-scatter.4.cloned.1.call-update) | async-done | bytes 786448 | tf_op jit(solution)/shard_map/reduce_scatter | solution.py:592
  742.7 45.7 %all-reduce.4.cloned.1.call-done = bf16[512,768]{1,0:T(8,128)(2,1)} async-done(((bf16[512,768]{1,0:T(8,128)(2,1)}), bf16[512,768]{1,0:T(8,128)(2,1)}) %all-reduce.4.cloned.1.call-update) | async-done | bytes 786448 | tf_op jit(solution)/shard_map/psum | solution.py:595
  788.5 1.9 multiply_reduce_fusion.1
  791.5 9.3 convert_reduce_fusion
  800.8 6.4 multiply_reduce_fusion.2
  808.1 2.9 convolution_convert_fusion.5
  811.1 2.3 copy.189
  813.4 2.6 reshape.780
  816.0 3.6 convert_reduce_fusion.3
  819.6 0.8 multiply_reduce_fusion
  820.5 1.0 multiply_convert_fusion.1
  821.5 1.2 fusion.45
  825.6 1.0 copy-done.2
  826.7 4.6 multiply_reduce_fusion.3
  831.3 3.8 fusion.17
  835.1 0.8 fusion.131
  835.9 1.2 fusion.130
  837.6 3.0 fusion.38
  840.6 7.0 fusion.16
  847.6 8.7 fusion.15
  858.3 1.8 reduce-scatter.6.cloned.1.call-done
  860.0 105.7 %reduce-scatter.8.cloned.1.call-done = bf16[1168,768]{1,0:T(8,128)(2,1)} async-done(((bf16[9344,768]{1,0:T(8,128)(2,1)}), bf16[1168,768]{1,0:T(8,128)(2,1)}) %reduce-scatter.8.cloned.1.call-update) | async-done | bytes 1794064 | tf_op jit(solution)/shard_map/reduce_scatter | solution.py:615
  965.7 2.6 reshape.783
  968.3 4.9 all-to-all-start.4
  976.6 136.1 %all-reduce.6.cloned.1.call-done = f32[4,14,768]{2,0,1:T(4,128)} async-done(((f32[4,14,768]{2,0,1:T(4,128)}), f32[4,14,768]{2,0,1:T(4,128)}) %all-reduce.6.cloned.1.call-update) | async-done | bytes 172048 | tf_op jit(solution)/shard_map/psum | solution.py:623
  1112.7 1.8 multiply_subtract_fusion.1
  1114.5 72.7 %all-gather.17.cloned.1.call-done = bf16[4096,768]{1,0:T(8,128)(2,1)} async-done(((bf16[128,768]{1,0:T(8,128)(2,1)}), bf16[4096,768]{1,0:T(8,128)(2,1)}) %all-gather.17.cloned.1.call-update) | async-done | bytes 6291472 | tf_op jit(solution)/shard_map/all_gather | solution.py:613
  1187.1 69.4 %shard_map.187 = (f32[4,1600,768]{2,1,0:T(8,128)}, f32[4,1600,768]{2,1,0:T(8,128)}, f32[4,1600,768]{2,1,0:T(8,128)}) custom-call(s32[18]{0:T(128)} %copy-done.49, s32[18]{0:T(128)} %get-tuple-element.217.fresh_ref, s32[18]{0:T(128)} %get-tuple-element.216.final_ref, s32[18]{0:T(128)} %slice.165.first_ref, s32[18]{0:T(128)} %slice.166.second_ref, ...), custom_call_target="tpu_custom_call" | custom-call | flops 11324620800 | bytes 117964800 | tf_op jit(solution)/shard_map/pallas_call | solution.py:360
  1256.6 4.8 multiply_subtract_fusion
  1261.4 3.2 copy.205
  1264.6 3.2 copy.204
  1267.8 2.5 copy.203
  (264 shorter events, 31.0 us)
Async XLA Ops:
  7.2 155.2 %all-gather.11.cloned.1.call-start = ((), (), s32[]{:S(2)}) async-start(), calls=%async_computation.8 | async-start | bytes 7077888 | tf_op jit(solution)/shard_map/all_gather | solution.py:497
  89.6 3.9 copy-start
  112.4 125.3 %all-gather.13.cloned.1.call-start = ((), (), s32[]{:S(2)}) async-start(), calls=%async_computation.9 | async-start | bytes 16367616 | tf_op jit(solution)/shard_map/all_gather | solution.py:418
  159.5 131.6 %copy-start.12 = (s32[32,128]{1,0:T(8,128)}, s32[32,128]{1,0:T(8,128)S(1)}, u32[]{:S(2)}) copy-start(s32[32,128]{1,0:T(8,128)S(1)} %get-tuple-element.202) | copy-start | bytes 49156
  161.2 95.1 %copy-start.25 = (f32[768]{0:T(1024)}, f32[768]{0:T(1024)S(1)}, u32[]{:S(2)}) copy-start(f32[768]{0:T(1024)S(1)} %get-tuple-element.145) | copy-start | bytes 9220
  161.2 112.0 %copy-start.34 = (f32[768]{0:T(1024)}, f32[768]{0:T(1024)S(1)}, u32[]{:S(2)}) copy-start(f32[768]{0:T(1024)S(1)} %get-tuple-element.140) | copy-start | bytes 9220
  161.2 112.0 %copy-start.45 = (f32[768]{0:T(1024)}, f32[768]{0:T(1024)S(1)}, u32[]{:S(2)}) copy-start(f32[768]{0:T(1024)S(1)} %get-tuple-element.139) | copy-start | bytes 9220
  162.2 116.1 %copy-start.36 = (f32[1,4,768]{2,0,1:T(1,128)}, f32[1,4,768]{2,0,1:T(1,128)S(1)}, u32[]{:S(2)}) copy-start(f32[1,4,768]{2,0,1:T(1,128)S(1)} %constant_dynamic-slice_fusion.1) | copy-start | bytes 36868
  255.7 2.2 copy-start.1
  255.7 187.6 %all-gather.15.cloned.1.call-start = ((), (), s32[]{:S(2)}) async-start(), calls=%async_computation.15 | async-start | bytes 25952256 | tf_op jit(solution)/shard_map/all_gather | solution.py:514
  256.0 1.9 copy-start.27
  256.3 3.9 copy-start.31
  256.3 3.9 copy-start.29
  257.9 4.5 copy-start.14
  265.7 2.5 copy-start.16
  268.1 1.7 copy-start.10
  268.1 2.5 copy-start.13
  270.4 2.5 copy-start.8
  272.9 5.4 copy-start.5
  273.2 5.0 copy-start.39
  278.2 8.7 copy-start.52
  288.7 227.1 %copy-start.41 = (f32[32]{0:T(128)}, f32[32]{0:T(128)S(1)}, u32[]{:S(2)}) copy-start(f32[32]{0:T(128)S(1)} %fusion.95) | copy-start | bytes 388
  289.3 226.5 %copy-start.49 = (s32[18]{0:T(128)}, s32[18]{0:T(128)S(1)}, u32[]{:S(2)}) copy-start(s32[18]{0:T(128)S(1)} %broadcast_add_fusion.model_ref) | copy-start | bytes 220
  289.7 226.1 %copy-start.43 = (f32[32]{0:T(128)}, f32[32]{0:T(128)S(1)}, u32[]{:S(2)}) copy-start(f32[32]{0:T(128)S(1)} %get-tuple-element.152) | copy-start | bytes 388
  289.8 226.0 %copy-start.50 = (s32[36]{0:T(128)}, s32[36]{0:T(128)S(1)}, u32[]{:S(2)}) copy-start(s32[36]{0:T(128)S(1)} %select_reduce_fusion.1) | copy-start | bytes 436
  290.5 230.3 %copy-start.38 = (s32[1024]{0:T(1024)}, s32[1024]{0:T(1024)S(1)}, u32[]{:S(2)}) copy-start(s32[1024]{0:T(1024)S(1)} %get-tuple-element.240) | copy-start | bytes 12292
  291.7 224.1 %copy-start.47 = (pred[36]{0:T(512)(128)(4,1)}, pred[36]{0:T(512)(128)(4,1)S(1)}, u32[]{:S(2)}) copy-start(pred[36]{0:T(512)(128)(4,1)S(1)} %fusion.88) | copy-start | bytes 112
  291.8 224.1 %copy-start.48 = (pred[36]{0:T(512)(128)(4,1)}, pred[36]{0:T(512)(128)(4,1)S(1)}, u32[]{:S(2)}) copy-start(pred[36]{0:T(512)(128)(4,1)S(1)} %compare_and_fusion.3) | copy-start | bytes 112
  515.9 11.2 all-to-all-start.3
  518.6 223.8 %reduce-scatter.4.cloned.1.call-start = ((), (), s32[]{:S(2)}) async-start(), calls=%async_computation.10 | async-start | bytes 7077888 | tf_op jit(solution)/shard_map/reduce_scatter | solution.py:592
  668.8 6.8 copy-start.33
  683.0 105.5 %all-reduce.4.cloned.1.call-start = ((), (), s32[]{:S(2)}) async-start(), calls=%async_computation.11 | async-start | bytes 1572864 | tf_op jit(solution)/shard_map/psum | solution.py:595
  742.5 117.5 %reduce-scatter.6.cloned.1.call-start = ((), (), s32[]{:S(2)}) async-start(), calls=%async_computation.12 | async-start | bytes 983040 | tf_op jit(solution)/shard_map/reduce_scatter | solution.py:612
  788.5 2.0 copy-start.9
  790.5 1.0 copy-start.37
  791.4 9.3 copy-start.19
  791.4 9.3 copy-start.6
  791.4 9.3 copy-start.35
  791.5 9.3 copy-start.40
  800.7 6.4 copy-start.53
  816.0 3.6 copy-start.11
  816.0 3.6 copy-start.17
  816.0 3.6 copy-start.18
  825.2 1.4 copy-start.2
  825.2 1.5 copy-start.4
  825.2 1.5 copy-start.26
  825.3 1.4 copy-start.28
  825.3 1.4 copy-start.30
  826.7 4.6 copy-start.15
  831.3 3.8 copy-start.32
  837.1 3.5 copy-start.7
  837.2 3.5 copy-start.46
  837.2 128.5 %reduce-scatter.8.cloned.1.call-start = ((), (), s32[]{:S(2)}) async-start(), calls=%async_computation.13 | async-start | bytes 16146432 | tf_op jit(solution)/shard_map/reduce_scatter | solution.py:615
  840.6 7.0 copy-start.20
  857.0 255.7 %all-reduce.6.cloned.1.call-start = ((), (), s32[]{:S(2)}) async-start(), calls=%async_computation.14 | async-start | bytes 344064 | tf_op jit(solution)/shard_map/psum | solution.py:623
  858.2 328.9 %all-gather.17.cloned.1.call-start = ((), (), s32[]{:S(2)}) async-start(), calls=%async_computation.16 | async-start | bytes 6488064 | tf_op jit(solution)/shard_map/all_gather | solution.py:613
  968.3 5.0 copy-start.51
  968.3 6.2 copy-start.44
  968.3 6.3 copy-start.24
  968.3 7.0 copy-start.42
  968.3 144.4 %copy-start.22 = (f32[4,14,768]{2,0,1:T(4,128)S(1)}, f32[4,14,768]{2,0,1:T(4,128)}, u32[]{:S(2)}) copy-start(f32[4,14,768]{2,0,1:T(4,128)} %param.24) | copy-start | bytes 516100
  968.3 144.4 %copy-start.23 = (f32[4,14,768]{2,0,1:T(4,128)S(1)}, f32[4,14,768]{2,0,1:T(4,128)}, u32[]{:S(2)}) copy-start(f32[4,14,768]{2,0,1:T(4,128)} %param.25) | copy-start | bytes 516100
  968.3 288.3 %all-to-all-start.4 = ((bf16[4,292,768]{2,1,0:T(8,128)(2,1)}), bf16[4,292,768]{2,1,0:T(8,128)(2,1)S(1)}, u32[]{:S(2)}, u32[]{:S(2)}) async-start(bf16[4,292,768]{2,1,0:T(8,128)(2,1)} %reshape.783), calls=%async_computation.7 | async-start | bytes 3637248 | tf_op jit(solution)/shard_map/all_to_all | solution.py:616
  1267.8 2.5 copy-start.21
  (1 other events, 0.9 us)
Sparse Core Ops, SparseCore 0:
  112.6 42.7 all-gather.10
  158.2 79.4 all-gather.12
  288.6 154.6 all-gather.14
  683.2 59.2 reduce-scatter.3
  744.8 43.6 all-reduce.3
  837.3 22.6 reduce-scatter.5
  864.7 101.0 reduce-scatter.7
  971.8 140.8 all-reduce.5
  1115.6 71.5 all-gather.16

commit v2 on v1

--- a/solution.py
+++ b/solution.py
@@ -227,6 +227,12 @@
     return (stack_rows, vector_rows, d_inputs)
 
 
+def share_all(rows, axes, size):
+    return lax.all_to_all(
+        jnp.broadcast_to(rows[None], (size,) + rows.shape), axes, 0, 0, tiled=True
+    )
+
+
 def update(weight, momentum, gradient, step_rate):
     renewed = momentum_decay * momentum + gradient
     return (renewed, weight - step_rate * (gradient + momentum_decay * renewed))
@@ -265,10 +271,23 @@
 
 
 def back_kernel(
-    model_ref, fresh_ref, first_ref, second_ref, a_ref, b_ref, table_ref, info_ref, target_ref, d_outs_ref, grad_ref
+    model_ref, fresh_ref, first_ref, second_ref, place_ref, a_ref, b_ref, table_ref, info_ref, target_ref, d_outs_ref,
+    grad_ref, held, sems,
 ):
     step = pl.program_id(0)
+    steps = pl.num_programs(0)
     seq_len = a_ref.shape[1]
+    slot = lax.rem(step, 2)
+
+    def leave(which, where, half):
+        return pltpu.make_async_copy(
+            held.at[which, half], d_outs_ref.at[where], sems.at[which, half]
+        )
+
+    @pl.when(step >= 2)
+    def reuse():
+        leave(slot, 0, 0).wait()
+        leave(slot, 0, 1).wait()
     outs = jnp.concatenate([a_ref[0], b_ref[0]], axis=0)
     logits = project(table_ref[0], outs)
     rows = lax.broadcasted_iota(jnp.int32, logits.shape, 0)
@@ -276,8 +295,10 @@
     hit = (rows == target_ref[0]).astype(jnp.float32)
     d_logits = (info_ref[0, 1:2, :] * (soft - hit)).astype(jnp.bfloat16)
     d_outs = outer_rows(d_logits, table_ref[0])
-    d_outs_ref[0] = d_outs[:seq_len].astype(d_outs_ref.dtype)
-    d_outs_ref[1] = d_outs[seq_len:].astype(d_outs_ref.dtype)
+    held[slot, 0] = d_outs[:seq_len].astype(held.dtype)
+    held[slot, 1] = d_outs[seq_len:].astype(held.dtype)
+    leave(slot, place_ref[2 * step], 0).start()
+    leave(slot, place_ref[2 * step + 1], 1).start()
     gain = product(d_logits, outs)
 
     @pl.when(fresh_ref[step] == 1)
@@ -288,8 +309,14 @@
     def more():
         grad_ref[0] += gain
 
-
-def head_back(outs_pieces, table_low, model_of, fresh, first, second, info, target):
+    @pl.when(step == steps - 1)
+    def drain():
+        for which in range(2):
+            leave(which, 0, 0).wait()
+            leave(which, 0, 1).wait()
+
+
+def head_back(outs_pieces, table_low, model_of, fresh, first, second, place, info, target):
     steps = model_of.shape[0]
     models, part_rows, width = table_low.shape
     seq_len = outs_pieces.shape[1]
@@ -300,19 +327,23 @@
             jax.ShapeDtypeStruct((models, part_rows, width), jnp.float32),
         ),
         grid_spec=pltpu.PrefetchScalarGridSpec(
-            num_scalar_prefetch=4,
+            num_scalar_prefetch=5,
             grid=(steps,),
             in_specs=[
-                pl.BlockSpec((1, seq_len, width), lambda s, m, f, a, b: (a[s], 0, 0)),
-                pl.BlockSpec((1, seq_len, width), lambda s, m, f, a, b: (b[s], 0, 0)),
-                pl.BlockSpec((1, part_rows, width), lambda s, m, f, a, b: (m[s], 0, 0)),
-                pl.BlockSpec((1, 2, 2 * seq_len), lambda s, m, f, a, b: (s, 0, 0)),
-                pl.BlockSpec((1, 1, 2 * seq_len), lambda s, m, f, a, b: (s, 0, 0)),
+                pl.BlockSpec((1, seq_len, width), lambda s, m, f, a, b, p: (a[s], 0, 0)),
+                pl.BlockSpec((1, seq_len, width), lambda s, m, f, a, b, p: (b[s], 0, 0)),
+                pl.BlockSpec((1, part_rows, width), lambda s, m, f, a, b, p: (m[s], 0, 0)),
+                pl.BlockSpec((1, 2, 2 * seq_len), lambda s, m, f, a, b, p: (s, 0, 0)),
+                pl.BlockSpec((1, 1, 2 * seq_len), lambda s, m, f, a, b, p: (s, 0, 0)),
             ],
             out_specs=(
-                pl.BlockSpec((2, seq_len, width), lambda s, m, f, a, b: (s, 0, 0)),
-                pl.BlockSpec((1, part_rows, width), lambda s, m, f, a, b: (m[s], 0, 0)),
+                pl.BlockSpec(memory_space=pl.ANY),
+                pl.BlockSpec((1, part_rows, width), lambda s, m, f, a, b, p: (m[s], 0, 0)),
             ),
+            scratch_shapes=[
+                pltpu.VMEM((2, 2, seq_len, width), jnp.bfloat16),
+                pltpu.SemaphoreType.DMA((2, 2)),
+            ],
         ),
         compiler_params=pltpu.CompilerParams(vmem_limit_bytes=56 * MIB),
         cost_estimate=pl.CostEstimate(
@@ -320,7 +351,7 @@
             bytes_accessed=4 * steps * seq_len * width * 2 + 6 * table_low.size,
             transcendentals=2 * steps * seq_len * part_rows,
         ),
-    )(model_of, fresh, first, second, outs_pieces, outs_pieces, table_low, info, target)
+    )(model_of, fresh, first, second, place, outs_pieces, outs_pieces, table_low, info, target)
 
 
 def finish_kernel(
@@ -419,11 +450,8 @@
         devices * stack_part, model_width
     )
 
-    facts = lax.all_gather(
-        jnp.concatenate([token_ids, target_ids, segment_ids, chosen[:, None]], axis=1),
-        both,
-        axis=0,
-        tiled=True,
+    facts = share_all(
+        jnp.concatenate([token_ids[0], target_ids[0], segment_ids[0], chosen]), both, devices
     )
     tokens = facts[:, :seq_len]
     targets = facts[:, seq_len : 2 * seq_len]
@@ -525,9 +553,7 @@
     shares = lax.all_to_all(stats, both, 0, 0, tiled=True)
     log_total = jax.nn.logsumexp(shares[:, 0], axis=0)
     token_loss = log_total - jnp.sum(shares[:, 1], axis=0)
-    everything = lax.all_gather(
-        jnp.stack([log_total, token_loss])[None], both, axis=0, tiled=True
-    )
+    everything = share_all(jnp.stack([log_total, token_loss]), both, devices)
     everything = (
         everything.reshape(groups, models, share, 2, local, seq_len)
         .transpose(3, 1, 0, 2, 4, 5)
@@ -578,19 +604,23 @@
         [slot_log.reshape(steps, 2 * seq_len), slot_weight.reshape(steps, 2 * seq_len)], axis=1
     )
     slot_target = jnp.where(filled[:, None], jnp.take(target_local, client_at, axis=0), -1)
-    d_slots, head_grad = head_back(
+    spare = devices + jnp.cumsum(1 - filled.astype(jnp.int32)) - 1
+    d_outs, head_grad = head_back(
         outs_all.reshape(-1, seq_len, model_width),
         table_low,
         model_of,
         fresh,
         piece_at[0::2],
         piece_at[1::2],
+        jnp.where(filled, client_at, spare).astype(jnp.int32),
         slot_info,
         slot_target.reshape(steps, 1, 2 * seq_len),
     )
-    d_outs = jnp.take(d_slots, slot_of.astype(jnp.int32), axis=0)
     d_group = lax.psum_scatter(
-        d_outs.reshape(devices * seq_len, model_width), "grp", scatter_dimension=0, tiled=True
+        d_outs[:devices].reshape(devices * seq_len, model_width),
+        "grp",
+        scatter_dimension=0,
+        tiled=True,
     )
     d_group = lax.psum(d_group, "cli").reshape(members, seq_len, model_width)
     d_mine = lax.dynamic_slice(
@@ -619,8 +649,14 @@
     stack_grad = jnp.sum(
         stack_back.reshape(models, share, stack_part, model_width), axis=1
     )
-    vector_masked = jnp.where((model_range == model_own)[:, None, None], vector_rows[None], 0.0)
-    vector_grad = lax.psum(vector_masked, both)
+    vector_piece = vector_rows.size // groups
+    vector_part = jnp.sum(
+        lax.all_to_all(vector_rows.reshape(groups, vector_piece), "grp", 0, 0, tiled=True), axis=0
+    )
+    vector_grad = jnp.sum(
+        share_all(vector_part, both, devices).reshape(groups, models, share, vector_piece), axis=2
+    )
+    vector_grad = vector_grad.transpose(1, 0, 2).reshape(vectors.shape)
 
     token_local = tokens - device_index * block_rows
     token_local = jnp.where((token_local >= 0) & (token_local < block_rows), token_local, -1)

time: 1290 us -> 1050 us (0.81)
  waiting for transfers between devices: 645 us -> 518 us
  blocking collectives: 197 us -> 76.3 us
    psum x1 -> x0, waiting for transfers between devices: 136 us -> none  [body(): vector_grad = lax.psum(vector_masked, both)]
    all_gather x2 -> x0, blocking collectives: 135 us -> none  [the longest x1 70.1 us: body(): lax.all_gather(jnp.concatenate([token_ids, target_ids, segment_ids, chose...]
  transfers between devices with their start and end apart: 11 -> 13, of which waited for: 9 -> 10; matrix products, arithmetic and copies ran while one was open for 4% -> 5% of each run, Pallas kernels for 5% -> 7%
where the time goes in v2:
time: 1050 us; the launch traced here: 1040 us
  waiting for transfers between devices  518 us (49%)
  Pallas kernels  216 us (21%)
  matrix products  84.5 us (8%)
  blocking collectives  76.3 us (7%)
  local copies, waits for them, and re-layouts  72.1 us (7%)
  other arithmetic  37.3 us (4%)
  starting transfers between devices  20.9 us (2%)
  between operations  16.9 us (2%)
    all_gather x1, waiting for transfers between devices, body(): outs_all = lax.all_gather(normed_out[None], both, axis=0, tiled=True)  152 us
    reduce_scatter x1, waiting for transfers between devices, body(): lax.psum_scatter(stack_rows, 'grp', scatter_dimension=0, tiled=True)  93.5 us
    all_gather x1, waiting for transfers between devices, body(): d_all = lax.all_gather(d_client[None], both, axis=0, tiled=True)  78.5 us
    pallas_call x1, Pallas kernels, head_back(): pl.pallas_call(back_kernel, out_shape=(jax.ShapeDtypeStruct((2 * steps, s...  73.9 us
    pallas_call x1, Pallas kernels, head_stats(): pl.pallas_call(stats_kernel, out_shape=jax.ShapeDtypeStruct((blocks, 2, r...  72.5 us
    pallas_call x1, Pallas kernels, finish_table(): pl.pallas_call(finish_kernel, out_shape=(state, state, state), grid_spec=...  69.5 us
    all_gather x1, waiting for transfers between devices, body(): lax.all_gather(stack_turned, 'grp', axis=0, tiled=True)  66.6 us
    reduce_scatter x1, waiting for transfers between devices, body(): lax.psum_scatter(d_outs[:devices].reshape(devices * seq_len, model_width)...  59 us
  transfers between devices with their start and end apart: 13, of which 10 were waited for; matrix products, arithmetic and copies ran while one was open for 5% of the time, Pallas kernels for 7%

profile of v2, /device:TPU:0, one launch (start us, length us, event | category | flops | bytes accessed | tf_op | source)
XLA Modules:
  0.0 1042.3 jit_solution(6548415072471664896)
XLA Ops:
  7.9 11.5 %convert_element_type.246.table_ref = bf16[4,1600,768]{2,1,0:T(8,128)(2,1)} convert(f32[4,1600,768]{2,1,0:T(8,128)} %table_ref.1) | non-fusion elementwise | flops 4915200 | bytes 29491200 | tf_op jit(solution)/shard_map/convert_element_type | solution.py:472
  20.0 7.3 all-to-all-start.1
  27.4 7.4 all-to-all-done.1
  34.9 2.6 fusion.137
  38.3 5.6 fusion.43
  43.9 23.3 %all_to_all.55 = bf16[4,128,768]{2,1,0:T(8,128)(2,1)} all-to-all(bf16[4,128,768]{2,1,0:T(8,128)(2,1)S(1)} %fusion.43), channel_id=1, replica_groups=mesh['grp'=8,'cli'=4] {'cli'}, dimensions={0} | all-to-all | bytes 1572864 | tf_op jit(solution)/shard_map/all_to_all | solution.py:524
  67.2 2.5 copy.374
  69.8 44.6 %all_to_all.56 = bf16[4,292,768]{2,1,0:T(8,128)(2,1)} all-to-all(bf16[4,292,768]{2,1,0:T(8,128)(2,1)S(1)} %copy.374), channel_id=1, replica_groups=mesh['grp'=8,'cli'=4] {'cli'}, dimensions={0} | all-to-all | bytes 3588096 | tf_op jit(solution)/shard_map/all_to_all | solution.py:448
  114.4 1.0 fusion.100
  115.4 0.8 constant_dynamic-slice_fusion.1
  119.3 6.8 gather_fusion.1
  126.4 66.6 %all-gather.10.cloned.1.call-done = bf16[32,292,768]{2,1,0:T(8,128)(2,1)} async-done(((bf16[4,292,768]{2,1,0:T(8,128)(2,1)}), bf16[32,292,768]{2,1,0:T(8,128)(2,1)}) %all-gather.10.cloned.1.call-update) | async-done | bytes 14352400 | tf_op jit(solution)/shard_map/all_gather | solution.py:449
  193.0 16.8 %reshape.791 = bf16[9344,768]{1,0:T(8,128)(2,1)} reshape(bf16[32,292,768]{2,1,0:T(8,128)(2,1)} %all-gather.10.cloned.1.call-done) | data formatting | bytes 28704768 | tf_op jit(solution)/shard_map/reshape | solution.py:449
  209.8 1.0 slice_convert_fusion
  211.6 1.5 add_convert_fusion.4
  213.2 2.4 convolution_convert_fusion.6
  215.5 2.1 add_convert_fusion.2
  218.1 2.3 add_convert_fusion.3
  222.0 1.3 fusion.138
  224.0 1.0 copy-done.9
  225.9 2.2 fusion.139
  228.5 5.0 fusion.24
  233.5 8.7 fusion.140
  242.6 1.2 add_convert_fusion
  246.4 152.2 %all-gather.12.cloned.1.call-done = bf16[16384,768]{1,0:T(8,128)(2,1)} async-done(((bf16[512,768]{1,0:T(8,128)(2,1)}), bf16[16384,768]{1,0:T(8,128)(2,1)}) %all-gather.12.cloned.1.call-update) | async-done | bytes 25165840 | tf_op jit(solution)/shard_map/all_gather | solution.py:542
  398.6 72.5 %shard_map.185 = f32[32,2,512]{2,1,0:T(2,128)} custom-call(bf16[32,512,768]{2,1,0:T(8,128)(2,1)} %bitcast.244, bf16[4,1600,768]{2,1,0:T(8,128)(2,1)} %get-tuple-element.335, s32[8,1,512]{2,1,0:T(1,128)} %bitcast.219), custom_call_target="tpu_custom_call" | custom-call | flops 40265318400 | bytes 34996224 | tf_op jit(solution)/shard_map/pallas_call | solution.py:254
  471.1 2.8 all-to-all-start.4
  475.2 7.1 all-to-all-done.4
  483.2 2.6 all-to-all-start.5
  489.3 4.9 all-to-all-done.5
  496.7 73.9 %shard_map.186 = (bf16[36,128,768]{2,1,0:T(8,128)(2,1)}, f32[4,1600,768]{2,1,0:T(8,128)}) custom-call(s32[18]{0:T(128)} %copy-done.49, s32[18]{0:T(128)} %get-tuple-element.227.fresh_ref, s32[18]{0:T(128)} %slice.170.first_ref, s32[18]{0:T(128)} %slice.171.second_ref, s32[36]{0:T(128)} %get-tuple-element.225.place_ref, bf16[128,128,768]{2,1,0:T(8,128)(2,1)} %bitcast.245, ...), custom_call_target="tpu_custom_call" | custom-call | flops 33973862400 | bytes 43646976 | tf_op jit(solution)/shard_map/pallas_call | solution.py:323
  570.6 6.1 slice.173
  576.9 59.0 %reduce-scatter.4.cloned.1.call-done = bf16[512,768]{1,0:T(8,128)(2,1)} async-done(((bf16[4096,768]{1,0:T(8,128)(2,1)}), bf16[512,768]{1,0:T(8,128)(2,1)}) %reduce-scatter.4.cloned.1.call-update) | async-done | bytes 786448 | tf_op jit(solution)/shard_map/reduce_scatter | solution.py:619
  636.1 45.8 %all-reduce.3.cloned.1.call-done = bf16[512,768]{1,0:T(8,128)(2,1)} async-done(((bf16[512,768]{1,0:T(8,128)(2,1)}), bf16[512,768]{1,0:T(8,128)(2,1)}) %all-reduce.3.cloned.1.call-update) | async-done | bytes 786448 | tf_op jit(solution)/shard_map/psum | solution.py:625
  681.9 1.9 multiply_reduce_fusion.1
  685.3 9.1 convert_reduce_fusion
  694.4 6.4 multiply_reduce_fusion.2
  701.8 2.9 convolution_convert_fusion.5
  704.7 2.3 copy.285
  707.0 2.6 reshape.802
  709.7 3.5 convert_reduce_fusion.3
  713.3 0.8 multiply_reduce_fusion
  714.1 1.0 multiply_convert_fusion.1
  715.1 1.2 fusion.45
  719.3 1.0 copy-done.1
  720.3 4.6 multiply_reduce_fusion.3
  724.9 3.8 fusion.17
  728.7 0.8 fusion.131
  729.5 1.2 fusion.130
  731.3 3.0 fusion.38
  734.2 7.0 fusion.16
  741.2 8.7 fusion.15
  750.7 2.9 reduce-scatter.6.cloned.1.call-done
  754.1 8.4 all_to_all.57
  763.2 2.6 all-to-all-start.8
  765.8 93.5 %reduce-scatter.8.cloned.1.call-done = bf16[1168,768]{1,0:T(8,128)(2,1)} async-done(((bf16[9344,768]{1,0:T(8,128)(2,1)}), bf16[1168,768]{1,0:T(8,128)(2,1)}) %reduce-scatter.8.cloned.1.call-update) | async-done | bytes 1794064 | tf_op jit(solution)/shard_map/reduce_scatter | solution.py:645
  859.4 2.6 reshape.805
  862.0 4.9 all-to-all-start.6
  873.6 78.5 %all-gather.14.cloned.1.call-done = bf16[4096,768]{1,0:T(8,128)(2,1)} async-done(((bf16[128,768]{1,0:T(8,128)(2,1)}), bf16[4096,768]{1,0:T(8,128)(2,1)}) %all-gather.14.cloned.1.call-update) | async-done | bytes 6291472 | tf_op jit(solution)/shard_map/all_gather | solution.py:643
  952.1 69.5 %shard_map.187 = (f32[4,1600,768]{2,1,0:T(8,128)}, f32[4,1600,768]{2,1,0:T(8,128)}, f32[4,1600,768]{2,1,0:T(8,128)}) custom-call(s32[18]{0:T(128)} %copy-done.49, s32[18]{0:T(128)} %get-tuple-element.227.fresh_ref, s32[18]{0:T(128)} %get-tuple-element.226.final_ref, s32[18]{0:T(128)} %slice.168.first_ref, s32[18]{0:T(128)} %slice.169.second_ref, ...), custom_call_target="tpu_custom_call" | custom-call | flops 11324620800 | bytes 117964800 | tf_op jit(solution)/shard_map/pallas_call | solution.py:391
  1021.6 4.8 multiply_subtract_fusion
  1026.4 3.2 copy.304
  1029.6 3.2 copy.303
  1032.8 2.5 copy.302
  (287 shorter events, 34.7 us)
Async XLA Ops:
  7.8 11.5 %copy-start.52 = (s32[1,128]{1,0:T(1,128)S(1)}, s32[1,128]{1,0:T(1,128)}, u32[]{:S(2)}) copy-start(s32[1,128]{1,0:T(1,128)} %param.18) | copy-start | bytes 1540
  7.8 11.5 %copy-start.53 = (s32[1,128]{1,0:T(1,128)S(1)}, s32[1,128]{1,0:T(1,128)}, u32[]{:S(2)}) copy-start(s32[1,128]{1,0:T(1,128)} %param.17) | copy-start | bytes 1540
  7.9 11.5 %copy-start.54 = (s32[1,128]{1,0:T(1,128)S(1)}, s32[1,128]{1,0:T(1,128)}, u32[]{:S(2)}) copy-start(s32[1,128]{1,0:T(1,128)} %param.16) | copy-start | bytes 1540
  20.0 14.8 %all-to-all-start.1 = ((s32[32,1,385]{2,1,0:T(1,128)}), s32[32,1,385]{2,1,0:T(1,128)S(1)}, u32[]{:S(2)}, u32[]{:S(2)}) async-start(s32[32,1,385]{2,1,0:T(1,128)} %broadcast_in_dim.282), calls=%async_computation.1 | async-start | bytes 131072 | tf_op jit(solution)/shard_map/all_to_all | solution.py:231
  27.3 91.9 %all-gather.8.cloned.1.call-start = ((), (), s32[]{:S(2)}) async-start(), calls=%async_computation.12 | async-start | bytes 7077888 | tf_op jit(solution)/shard_map/all_gather | solution.py:525
  67.2 125.8 %all-gather.10.cloned.1.call-start = ((), (), s32[]{:S(2)}) async-start(), calls=%async_computation.13 | async-start | bytes 16367616 | tf_op jit(solution)/shard_map/all_gather | solution.py:449
  115.4 96.2 %copy-start.22 = (f32[768]{0:T(1024)}, f32[768]{0:T(1024)S(1)}, u32[]{:S(2)}) copy-start(f32[768]{0:T(1024)S(1)} %get-tuple-element.156) | copy-start | bytes 9220
  115.4 113.1 %copy-start.34 = (f32[768]{0:T(1024)}, f32[768]{0:T(1024)S(1)}, u32[]{:S(2)}) copy-start(f32[768]{0:T(1024)S(1)} %get-tuple-element.151) | copy-start | bytes 9220
  115.4 113.1 %copy-start.46 = (f32[768]{0:T(1024)}, f32[768]{0:T(1024)S(1)}, u32[]{:S(2)}) copy-start(f32[768]{0:T(1024)S(1)} %get-tuple-element.150) | copy-start | bytes 9220
  116.2 117.3 %copy-start.36 = (f32[1,4,768]{2,0,1:T(1,128)}, f32[1,4,768]{2,0,1:T(1,128)S(1)}, u32[]{:S(2)}) copy-start(f32[1,4,768]{2,0,1:T(1,128)S(1)} %constant_dynamic-slice_fusion.1) | copy-start | bytes 36868
  211.0 2.2 copy-start
  211.0 187.6 %all-gather.12.cloned.1.call-start = ((), (), s32[]{:S(2)}) async-start(), calls=%async_computation.18 | async-start | bytes 25952256 | tf_op jit(solution)/shard_map/all_gather | solution.py:542
  211.2 1.9 copy-start.24
  211.6 1.6 copy-start.32
  211.6 1.6 copy-start.28
  213.2 4.5 copy-start.13
  220.9 2.5 copy-start.15
  223.4 1.7 copy-start.9
  223.4 1.7 copy-start.26
  223.4 2.5 copy-start.12
  225.7 2.5 copy-start.7
  228.2 5.4 copy-start.4
  228.5 5.0 copy-start.39
  233.5 8.7 copy-start.55
  244.6 226.5 %copy-start.30 = (s32[8,4]{0,1:T(4,128)}, s32[8,4]{0,1:T(4,128)S(1)}, u32[]{:S(2)}) copy-start(s32[8,4]{0,1:T(4,128)S(1)} %copy.264) | copy-start | bytes 388
  244.7 241.1 %copy-start.49 = (s32[18]{0:T(128)}, s32[18]{0:T(128)S(1)}, u32[]{:S(2)}) copy-start(s32[18]{0:T(128)S(1)} %broadcast_add_fusion.model_ref) | copy-start | bytes 220
  245.2 225.9 %copy-start.43 = (f32[32]{0:T(128)}, f32[32]{0:T(128)S(1)}, u32[]{:S(2)}) copy-start(f32[32]{0:T(128)S(1)} %get-tuple-element.163) | copy-start | bytes 388
  245.3 229.8 %copy-start.45 = (pred[36]{0:T(512)(128)(4,1)}, pred[36]{0:T(512)(128)(4,1)S(1)}, u32[]{:S(2)}) copy-start(pred[36]{0:T(512)(128)(4,1)S(1)} %fusion.89) | copy-start | bytes 112
  245.7 225.4 %copy-start.50 = (s32[36]{0:T(128)}, s32[36]{0:T(128)S(1)}, u32[]{:S(2)}) copy-start(s32[36]{0:T(128)S(1)} %select_reduce_fusion.1) | copy-start | bytes 436
  245.7 229.4 %copy-start.48 = (pred[36]{0:T(512)(128)(4,1)}, pred[36]{0:T(512)(128)(4,1)S(1)}, u32[]{:S(2)}) copy-start(pred[36]{0:T(512)(128)(4,1)S(1)} %compare_and_fusion.3) | copy-start | bytes 112
  398.6 75.3 %copy-start.11 = (s32[32,128]{1,0:T(8,128)S(1)}, s32[32,128]{1,0:T(8,128)}, u32[]{:S(2)}) copy-start(s32[32,128]{1,0:T(8,128)} %get-tuple-element.211) | copy-start | bytes 49156
  471.1 11.2 %all-to-all-start.4 = ((f32[32,2,512]{2,1,0:T(2,128)}), f32[32,2,512]{2,1,0:T(2,128)S(1)}, u32[]{:S(2)}, u32[]{:S(2)}) async-start(f32[32,2,512]{2,1,0:T(2,128)} %shard_map.185), calls=%async_computation.4 | async-start | bytes 262144 | tf_op jit(solution)/shard_map/all_to_all | solution.py:553
  473.9 15.3 %copy-start.38 = (s32[1024]{0:T(1024)}, s32[1024]{0:T(1024)S(1)}, u32[]{:S(2)}) copy-start(s32[1024]{0:T(1024)S(1)} %pad_clamp_fusion.1) | copy-start | bytes 12292
  483.2 11.0 %all-to-all-start.5 = ((f32[32,2,512]{2,1,0:T(2,128)}), f32[32,2,512]{2,1,0:T(2,128)S(1)}, u32[]{:S(2)}, u32[]{:S(2)}) async-start(f32[32,2,512]{2,1,0:T(2,128)} %broadcast_in_dim.301), calls=%async_computation.5 | async-start | bytes 262144 | tf_op jit(solution)/shard_map/all_to_all | solution.py:231
  485.8 150.0 %reduce-scatter.4.cloned.1.call-start = ((), (), s32[]{:S(2)}) async-start(), calls=%async_computation.14 | async-start | bytes 7077888 | tf_op jit(solution)/shard_map/reduce_scatter | solution.py:619
  576.8 105.1 %all-reduce.3.cloned.1.call-start = ((), (), s32[]{:S(2)}) async-start(), calls=%async_computation.15 | async-start | bytes 1572864 | tf_op jit(solution)/shard_map/psum | solution.py:625
  635.8 117.8 %reduce-scatter.6.cloned.1.call-start = ((), (), s32[]{:S(2)}) async-start(), calls=%async_computation.16 | async-start | bytes 983040 | tf_op jit(solution)/shard_map/reduce_scatter | solution.py:642
  681.9 2.0 copy-start.8
  684.8 9.6 copy-start.18
  685.3 9.1 copy-start.5
  685.3 9.1 copy-start.35
  685.3 9.1 copy-start.40
  694.3 6.4 copy-start.56
  704.7 4.9 copy-start.27
  709.6 3.6 copy-start.10
  709.6 3.6 copy-start.16
  709.7 3.6 copy-start.17
  718.8 1.5 copy-start.3
  718.9 1.5 copy-start.23
  720.3 4.6 copy-start.14
  724.9 3.8 copy-start.33
  730.8 3.5 copy-start.6
  730.8 3.5 copy-start.47
  730.8 128.6 %reduce-scatter.8.cloned.1.call-start = ((), (), s32[]{:S(2)}) async-start(), calls=%async_computation.17 | async-start | bytes 16146432 | tf_op jit(solution)/shard_map/reduce_scatter | solution.py:645
  734.2 7.0 copy-start.19
  750.6 201.5 %all-gather.14.cloned.1.call-start = ((), (), s32[]{:S(2)}) async-start(), calls=%async_computation.19 | async-start | bytes 6488064 | tf_op jit(solution)/shard_map/all_gather | solution.py:643
  763.2 98.7 %all-to-all-start.8 = ((f32[32,1,1344]{2,1,0:T(1,128)}), f32[32,1,1344]{2,1,0:T(1,128)S(1)}, u32[]{:S(2)}, u32[]{:S(2)}) async-start(f32[32,1,1344]{2,1,0:T(1,128)} %broadcast_in_dim.319), calls=%async_computation.11 | async-start | bytes 360448 | tf_op jit(solution)/shard_map/all_to_all | solution.py:231
  861.9 5.0 copy-start.51
  861.9 6.3 copy-start.44
  861.9 7.2 copy-start.42
  861.9 8.0 copy-start.31
  861.9 10.0 copy-start.20
  862.0 10.0 copy-start.21
  862.0 159.6 %all-to-all-start.6 = ((bf16[4,292,768]{2,1,0:T(8,128)(2,1)}), bf16[4,292,768]{2,1,0:T(8,128)(2,1)S(1)}, u32[]{:S(2)}, u32[]{:S(2)}) async-start(bf16[4,292,768]{2,1,0:T(8,128)(2,1)} %reshape.805), calls=%async_computation.9 | async-start | bytes 3637248 | tf_op jit(solution)/shard_map/all_to_all | solution.py:646
  (6 other events, 6.4 us)
Sparse Core Ops, SparseCore 0:
  67.3 43.1 all-gather.7
  114.5 78.3 all-gather.9
  243.9 154.6 all-gather.11
  576.9 58.8 reduce-scatter.3
  638.2 43.6 all-reduce.2
  730.9 22.6 reduce-scatter.5
  758.2 101.0 reduce-scatter.7
  862.2 89.8 all-gather.13

commit v3 on v2

--- a/solution.py
+++ b/solution.py
@@ -18,7 +18,10 @@
 vector_rate = 50.0
 
 ROUND_ROWS = 128
+SLAB_STEP = 32
 MIB = 1 << 20
+POOL_BYTES = 32 * MIB
+MESH = pl.DeviceIdType.MESH
 
 
 def layer_norm(inputs, gain_row, shift_row):
@@ -236,6 +239,411 @@
 def update(weight, momentum, gradient, step_rate):
     renewed = momentum_decay * momentum + gradient
     return (renewed, weight - step_rate * (gradient + momentum_decay * renewed))
+
+
+def flipped(value, offset, size):
+    bit = 1
+    while bit < size:
+        digit = lax.rem(lax.div(offset, bit), 2)
+        value = value + digit * bit * (1 - 2 * lax.rem(lax.div(value, bit), 2))
+        bit *= 2
+    return value
+
+
+class Place:
+    def __init__(self, groups, members):
+        self.groups, self.members = groups, members
+        self.ys = 2
+        self.xs = groups // 4
+        self.grp = lax.axis_index("grp")
+        self.cli = lax.axis_index("cli")
+        self.core = lax.rem(self.grp, 2)
+        self.x = lax.rem(lax.div(self.grp, 2), self.xs)
+        self.y = lax.div(self.grp, 2 * self.xs)
+
+    def group(self, jx=0, jy=0, jc=0):
+        x = flipped(self.x, jx, self.xs)
+        y = flipped(self.y, jy, self.ys)
+        core = self.core + jc * (1 - 2 * self.core)
+        return (y * self.xs + x) * 2 + core
+
+    def block(self, jx, jy, level, jc=0):
+        return self.group(jx, jy, jc) * self.members + level
+
+    def peer(self, jx=0, jy=0, jc=0):
+        return (self.group(jx, jy, jc), self.cli)
+
+    def level(self, level):
+        return (self.grp, level)
+
+    def nearest(self, i):
+        z, last = self.cli, self.members - 1
+        low = jnp.where(2 * z < last, 1, 0)
+        sign = 2 * low - 1
+        margin = low * z + (1 - low) * (last - z)
+        step = lax.div(i + 1, 2)
+        odd = lax.rem(i, 2)
+        near = z + sign * step * (2 * odd - 1)
+        far = z + sign * (i - margin)
+        return jnp.where(i <= 2 * margin, near, far)
+
+
+def greet(place):
+    barrier = pltpu.get_barrier_semaphore()
+    peers = [place.peer(jx=j) for j in range(1, place.xs)] + [place.peer(jy=j) for j in range(1, place.ys)]
+    peers.append(place.peer(jc=1))
+    peers += [place.level(lax.rem(place.cli + j, place.members)) for j in range(1, place.members)]
+    for peer in peers:
+        pl.semaphore_signal(barrier, inc=1, device_id=peer, device_id_type=MESH)
+    pl.semaphore_wait(barrier, len(peers))
+
+
+def spread_sems(groups, members, pieces):
+    xs, ys, items = groups // 4, 2, members * pieces
+    dma = pltpu.SemaphoreType.DMA
+    shapes = [(items,)] * 3 + [(items, xs)] * 2 + [(items, ys)] * 2 + [(items, xs, ys)] * 6
+    return [dma] + [dma(shape) for shape in shapes]
+
+
+def spread_body(place, chain, pieces, src, out, sems, consume, ready=None):
+    (own_sem, z_up, z_down, z_recv, x_send, x_recv, y_send, y_recv, k_send, k_recv, p_send, p_recv,
+     c_send, c_recv) = sems
+    xs, ys, members = place.xs, place.ys, place.members
+    items = members * pieces
+    size = out.shape[1] // pieces
+    z = place.cli
+    partner = z + 1 - 2 * lax.rem(z, 2)
+    inner_x, inner_y = range(1, xs), range(1, ys)
+
+    def move(source, target, send, recv, device):
+        return pltpu.make_async_remote_copy(
+            src_ref=source, dst_ref=target, send_sem=send, recv_sem=recv, device_id=device, device_id_type=MESH
+        )
+
+    class Item:
+        def __init__(self, k):
+            self.level = place.nearest(lax.div(k, pieces))
+            self.piece = lax.rem(k, pieces)
+            self.slot = self.level * pieces + self.piece
+            self.even = lax.rem(self.piece, 2) == 0
+            self.mine = lax.rem(self.level + z, 2) == 0 if chain else self.level >= 0
+            self.rows = pl.ds(self.piece * size, size)
+
+        def part(self, jx, jy, level=None):
+            return out.at[place.block(jx, jy, self.level if level is None else level), self.rows]
+
+        def here(self, own):
+            return src.at[z if not chain else 0, self.rows] if own else self.part(0, 0)
+
+        def up(self, own=False):
+            return move(self.here(own), self.part(0, 0), z_up.at[self.slot], z_recv.at[self.slot], place.level(z + 1))
+
+        def down(self, own=False):
+            return move(self.here(own), self.part(0, 0), z_down.at[self.slot], z_recv.at[self.slot], place.level(z - 1))
+
+        def straight(self):
+            return move(
+                src.at[self.level, self.rows], self.part(0, 0, z), z_up.at[self.slot],
+                z_recv.at[z * pieces + self.piece], place.level(self.level),
+            )
+
+        def landed(self):
+            part = self.part(0, 0)
+            return move(part, part, z_up.at[self.slot], z_recv.at[self.slot], place.level(partner))
+
+        def to_x(self, jx, own=False):
+            return move(self.here(own), self.part(0, 0), x_send.at[self.slot, jx], x_recv.at[self.slot, jx], place.peer(jx=jx))
+
+        def to_y(self, jy, own=False):
+            return move(self.here(own), self.part(0, 0), y_send.at[self.slot, jy], y_recv.at[self.slot, jy], place.peer(jy=jy))
+
+        def corner_a(self, jx, jy):
+            part = self.part(jx, 0)
+            return move(part, part, k_send.at[self.slot, jx, jy], k_recv.at[self.slot, jx, jy], place.peer(jy=jy))
+
+        def corner_b(self, jx, jy):
+            part = self.part(0, jy)
+            return move(part, part, k_send.at[self.slot, jx, jy], k_recv.at[self.slot, jx, jy], place.peer(jx=jx))
+
+        def corner_z(self, jx, jy):
+            part = self.part(jx, jy)
+            return move(part, part, p_send.at[self.slot, jx, jy], p_recv.at[self.slot, jx, jy], place.level(partner))
+
+        def to_core(self, jx, jy, own=False):
+            part = self.part(jx, jy)
+            return move(self.here(True) if own else part, part, c_send.at[self.slot, jx, jy], c_recv.at[self.slot, jx, jy], place.peer(jc=1))
+
+    own = pltpu.make_async_copy(src.at[z if not chain else 0], out.at[place.block(0, 0, z)], own_sem)
+    own.start()
+    if not chain:
+        for piece in range(pieces):
+            Item(pieces + piece).straight().start()
+
+    def columns(k):
+        item = Item(k)
+        level = item.level
+
+        @pl.when(k < pieces)
+        def mine_first():
+            if chain:
+                @pl.when(z + 1 < members)
+                def onward():
+                    item.up(True).start()
+
+                @pl.when(z > 0)
+                def back():
+                    item.down(True).start()
+
+            for jx in inner_x:
+                item.to_x(jx, True).start()
+            for jy in inner_y:
+                item.to_y(jy, True).start()
+            item.to_core(0, 0, True).start()
+
+        @pl.when(k >= pieces)
+        def arrive():
+            item.landed().wait_recv()
+            if chain:
+                @pl.when((level < z) & (z + 1 < members))
+                def onward():
+                    item.up().start()
+
+                @pl.when((level > z) & (z > 0))
+                def back():
+                    item.down().start()
+            else:
+                @pl.when(k + pieces < items)
+                def following():
+                    Item(k + pieces).straight().start()
+
+            for jx in inner_x:
+                item.to_x(jx).start()
+            for jy in inner_y:
+                item.to_y(jy).start()
+            item.to_core(0, 0).start()
+
+    def edges(k):
+        item = Item(k)
+        for jx in inner_x:
+            item.to_x(jx).wait_recv()
+
+            @pl.when(item.mine & item.even)
+            def pass_a():
+                for jy in inner_y:
+                    item.corner_a(jx, jy).start()
+
+            item.to_core(jx, 0).start()
+        for jy in inner_y:
+            item.to_y(jy).wait_recv()
+
+            @pl.when(item.mine & jnp.logical_not(item.even))
+            def pass_b():
+                for jx in inner_x:
+                    item.corner_b(jx, jy).start()
+
+            item.to_core(0, jy).start()
+
+    def corners(k):
+        item = Item(k)
+
+        @pl.when(item.mine)
+        def mine_now():
+            for jx in inner_x:
+                for jy in inner_y:
+                    item.corner_a(jx, jy).wait_recv()
+                    if chain:
+                        item.corner_z(jx, jy).start()
+                    item.to_core(jx, jy).start()
+
+    def handed(k):
+        item = Item(k)
+
+        @pl.when(jnp.logical_not(item.mine))
+        def from_partner():
+            for jx in inner_x:
+                for jy in inner_y:
+                    item.corner_z(jx, jy).wait_recv()
+                    item.to_core(jx, jy).start()
+
+    spots = xs * ys
+    lag_edge, lag_corner = (2, 4) if chain else (1, 3)
+    lag_handed = pieces + 6 if chain else lag_corner
+    lag_end = lag_handed + 1
+
+    def tick(t, carry):
+        @pl.when(t < items)
+        def arrivals():
+            columns(t)
+
+        @pl.when((t >= lag_edge) & (t < items + lag_edge))
+        def sides():
+            edges(t - lag_edge)
+
+        @pl.when((t >= lag_corner) & (t < items + lag_corner))
+        def far():
+            corners(t - lag_corner)
+
+        if chain:
+            @pl.when((t >= lag_handed) & (t < items + lag_handed))
+            def others():
+                handed(t - lag_handed)
+
+        def visit(e, carry):
+            jc = lax.div(e, spots)
+            spot = lax.rem(e, spots)
+            jx, jy = lax.rem(spot, xs), lax.div(spot, xs)
+            far = jnp.minimum(jx, 1) + jnp.minimum(jy, 1)
+            lag = jnp.where(far == 0, 1, jnp.where(far == 1, lag_edge + 1, lag_end))
+            k = t - lag
+
+            @pl.when((k >= 0) & (k < items))
+            def valid():
+                item = Item(k)
+
+                @pl.when(jc == 1)
+                def shared():
+                    item.to_core(jx, jy).wait_recv()
+
+                if consume is not None:
+                    consume(place.block(jx, jy, item.level, jc), item.level, item.piece)
+
+            return carry
+
+        return lax.fori_loop(0, 2 * spots, visit, carry)
+
+    if ready is not None:
+        own.wait()
+        ready()
+    lax.fori_loop(0, items + lag_end, tick, 0)
+
+    def close(k, carry):
+        item = Item(k)
+        level = item.level
+        if chain:
+            @pl.when((level <= z) & (z + 1 < members))
+            def onward():
+                item.up().wait_send()
+
+            @pl.when((level >= z) & (z > 0))
+            def back():
+                item.down().wait_send()
+        else:
+            @pl.when(k >= pieces)
+            def sent():
+                item.straight().wait_send()
+
+        for jx in inner_x:
+            item.to_x(jx).wait_send()
+        for jy in inner_y:
+            item.to_y(jy).wait_send()
+        for jx in range(xs):
+            for jy in range(ys):
+                item.to_core(jx, jy).wait_send()
+
+        @pl.when(item.mine)
+        def mine_done():
+            for jx in inner_x:
+                for jy in inner_y:
+                    item.corner_a(jx, jy).wait_send()
+                    if chain:
+                        item.corner_z(jx, jy).wait_send()
+
+        return carry
+
+    lax.fori_loop(0, items, close, 0)
+    if ready is None:
+        own.wait()
+
+
+def spread_kernel(groups, members, chain, pieces, src, out, *sems):
+    place = Place(groups, members)
+    greet(place)
+    spread_body(place, chain, pieces, src, out, sems, None)
+
+
+def spread(src, groups, members, collective_id, chain, pieces):
+    count, rows, width = src.shape
+    return pl.pallas_call(
+        functools.partial(spread_kernel, groups, members, chain, pieces),
+        out_shape=jax.ShapeDtypeStruct((groups * members, rows, width), src.dtype),
+        in_specs=[pl.BlockSpec(memory_space=pl.ANY)],
+        out_specs=pl.BlockSpec(memory_space=pl.ANY),
+        scratch_shapes=spread_sems(groups, members, pieces),
+        compiler_params=pltpu.CompilerParams(collective_id=collective_id, has_side_effects=True),
+        cost_estimate=pl.CostEstimate(
+            flops=0, bytes_accessed=4 * groups * members * rows * width, transcendentals=0
+        ),
+    )(src)
+
+
+def score_kernel(groups, members, share, pieces, src, table, target, out, stat, *rest):
+    part, pool, part_sem, out_sems = rest[:4]
+    sems = rest[4:]
+    place = Place(groups, members)
+    load_table = pltpu.make_async_copy(table, part, part_sem)
+    load_table.start()
+    greet(place)
+    rows = pool.shape[1]
+    size = rows // pieces
+
+    def keep(block, piece):
+        here = pl.ds(pl.multiple_of(piece * size, size), size)
+        return pltpu.make_async_copy(pool.at[block, here], out.at[block, here], out_sems.at[block, piece])
+
+    def consume(block, level, piece):
+        keep(block, piece).start()
+        here = pl.ds(pl.multiple_of(piece * size, size), size)
+        model = lax.div(level, share)
+        logits = project(part[model], pool[block, here])
+        highest = jnp.max(logits, axis=0, keepdims=True)
+        total = jnp.sum(jnp.exp(logits - highest), axis=0, keepdims=True)
+        tokens = lax.broadcasted_iota(jnp.int32, logits.shape, 0)
+        wanted = target[lax.div(block, members) * share + lax.rem(level, share), :, here]
+        hit = jnp.sum(jnp.where(tokens == wanted, logits, 0.0), axis=0, keepdims=True)
+        stat[block, 0:1, here] = highest + jnp.log(total)
+        stat[block, 1:2, here] = hit
+
+    spread_body(place, True, pieces, src, pool, sems, consume, load_table.wait)
+
+    def close(block, carry):
+        for piece in range(pieces):
+            keep(block, piece).wait()
+        return carry
+
+    lax.fori_loop(0, groups * members, close, 0)
+
+
+def spread_score(src, table_low, target_blocks, groups, members, share, collective_id, pieces=2):
+    _, rows, width = src.shape
+    blocks = groups * members
+    return pl.pallas_call(
+        functools.partial(score_kernel, groups, members, share, pieces),
+        out_shape=(
+            jax.ShapeDtypeStruct((blocks, rows, width), src.dtype),
+            jax.ShapeDtypeStruct((blocks, 2, rows), jnp.float32),
+        ),
+        in_specs=[
+            pl.BlockSpec(memory_space=pl.ANY),
+            pl.BlockSpec(memory_space=pl.ANY),
+            pl.BlockSpec(memory_space=pltpu.VMEM),
+        ],
+        out_specs=(pl.BlockSpec(memory_space=pl.ANY), pl.BlockSpec(memory_space=pltpu.VMEM)),
+        scratch_shapes=[
+            pltpu.VMEM(table_low.shape, table_low.dtype),
+            pltpu.VMEM((blocks, rows, width), src.dtype),
+            pltpu.SemaphoreType.DMA,
+            pltpu.SemaphoreType.DMA((blocks, pieces)),
+        ]
+        + spread_sems(groups, members, pieces),
+        compiler_params=pltpu.CompilerParams(
+            collective_id=collective_id, has_side_effects=True, vmem_limit_bytes=60 * MIB
+        ),
+        cost_estimate=pl.CostEstimate(
+            flops=2 * blocks * rows * table_low.shape[1] * width,
+            bytes_accessed=2 * blocks * rows * width * 2,
+            transcendentals=blocks * rows * table_low.shape[1],
+        ),
+    )(src, table_low, target_blocks)
 
 
 def stats_kernel(outs_ref, table_ref, target_ref, stat_ref):
@@ -444,11 +852,8 @@
     def per_member(rows):
         return jnp.repeat(rows, share, axis=0) if share > 1 else rows
 
-    stack_low = per_member(stack.astype(jnp.bfloat16))
-    stack_turned = lax.all_to_all(stack_low, "cli", 0, 0, tiled=True)
-    weights = lax.all_gather(stack_turned, "grp", axis=0, tiled=True).reshape(
-        devices * stack_part, model_width
-    )
+    slab = -(-(stack_part + ROUND_ROWS) // SLAB_STEP) * SLAB_STEP
+    round_rows = slab - stack_part
 
     facts = share_all(
         jnp.concatenate([token_ids[0], target_ids[0], segment_ids[0], chosen]), both, devices
@@ -495,7 +900,7 @@
         axis=2,
     )
     places = before + ahead.reshape(-1, 1)
-    rounds = jnp.max(jnp.ceil(uniques / ROUND_ROWS)).astype(jnp.int32)
+    rounds = jnp.max(jnp.ceil(uniques / round_rows)).astype(jnp.int32)
     own_places = lax.dynamic_slice(places, (device_index * coarse, 0), (coarse, fine)).reshape(-1)
     own_seen = lax.dynamic_slice(seen, (device_index * coarse, 0), (coarse, fine)).reshape(-1)
     own_places = jnp.where(own_seen > 0, own_places, -1.0).astype(jnp.int32)
@@ -515,41 +920,50 @@
     my_places = jnp.sum(jnp.where(my_low, picked_places, 0.0), axis=1).astype(jnp.int32)
     my_owner = my_tokens // block_rows
 
-    def fetch(round_index, embedded):
-        start = round_index * ROUND_ROWS
-        wanted = jnp.arange(ROUND_ROWS, dtype=jnp.int32) + start
+    def offered(start):
+        wanted = jnp.arange(round_rows, dtype=jnp.int32) + start
         pick = (own_places[None, :] == wanted[:, None]).astype(jnp.bfloat16)
         rows = jnp.einsum("ur,krd->kud", pick, table_low, preferred_element_type=jnp.float32)
-        rows = per_member(rows.astype(jnp.bfloat16))
-        turned = lax.all_to_all(rows, "cli", 0, 0, tiled=True)
-        pool = lax.all_gather(turned, "grp", axis=0, tiled=True).reshape(-1, model_width)
+        return rows.astype(jnp.bfloat16)
+
+    def taken(pool, lead, start, embedded):
         offset = my_places - start
-        inside = (offset >= 0) & (offset < ROUND_ROWS)
-        found = jnp.take(pool, jnp.where(inside, my_owner * ROUND_ROWS + offset, 0), axis=0)
+        inside = (offset >= 0) & (offset < round_rows)
+        at = my_owner * (lead + round_rows) + lead + offset
+        found = jnp.take(pool.reshape(-1, model_width), jnp.where(inside, at, 0), axis=0)
         return jnp.where(inside[:, None], found.astype(jnp.float32), embedded)
 
-    embedded = fetch(jnp.int32(0), jnp.zeros((local * seq_len, model_width), jnp.float32))
+    def another(carry):
+        index, embedded = carry
+        start = index * round_rows
+        turned = lax.all_to_all(per_member(offered(start)), "cli", 0, 0, tiled=True)
+        pool = lax.all_gather(turned, "grp", axis=0, tiled=True)
+        return (index + 1, taken(pool, 0, start, embedded))
+
+    slabs = jnp.concatenate([stack.astype(jnp.bfloat16), offered(0)], axis=1)
+    pool = spread(per_member(slabs), groups, members, 1, False, 2)
+    weights = pool[:, :stack_part].reshape(devices * stack_part, model_width)
+    embedded = taken(
+        pool, stack_part, 0, jnp.zeros((local * seq_len, model_width), jnp.float32)
+    )
     _, embedded = lax.while_loop(
-        lambda carry: carry[0] < rounds,
-        lambda carry: (carry[0] + 1, fetch(carry[0], carry[1])),
-        (jnp.int32(1), embedded),
+        lambda carry: carry[0] < rounds, another, (jnp.int32(1), embedded)
     )
     vector_one = lax.dynamic_index_in_dim(vectors, model_own, 0, keepdims=False)
     inputs = embedded + jnp.tile(weights[12 * model_width :].astype(jnp.float32), (local, 1))
     saved = layer_forward(weights, vector_one, inputs, my_segments)
     normed_out = saved[11]
 
-    outs_all = lax.all_gather(normed_out[None], both, axis=0, tiled=True)
     target_local = targets - device_index * block_rows
     target_local = jnp.where((target_local >= 0) & (target_local < block_rows), target_local, -1)
-    stats = head_stats(
-        outs_all,
-        table_low,
-        target_local.reshape(groups * share, 1, local * seq_len),
-        groups,
-        members,
-        share,
-    )
+    target_blocks = target_local.reshape(groups * share, 1, local * seq_len)
+    if devices * normed_out.size * 2 <= POOL_BYTES:
+        outs_all, stats = spread_score(
+            normed_out[None], table_low, target_blocks, groups, members, share, 2
+        )
+    else:
+        outs_all = spread(normed_out[None], groups, members, 2, True, 2)
+        stats = head_stats(outs_all, table_low, target_blocks, groups, members, share)
     shares = lax.all_to_all(stats, both, 0, 0, tiled=True)
     log_total = jax.nn.logsumexp(shares[:, 0], axis=0)
     token_loss = log_total - jnp.sum(shares[:, 1], axis=0)
@@ -639,8 +1053,11 @@
             d_wide,
             (part_own * local * seq_len, 0),
         )
-    d_client = lax.psum_scatter(d_wide, "cli", scatter_dimension=0, tiled=True)
-    d_all = lax.all_gather(d_client[None], both, axis=0, tiled=True)
+    d_turned = lax.all_to_all(
+        d_wide.reshape(members, seq_len, model_width), "cli", 0, 0, tiled=True
+    )
+    d_client = jnp.sum(d_turned.astype(jnp.float32), axis=0, keepdims=True).astype(jnp.bfloat16)
+    d_all = spread(d_client, groups, members, 3, True, 2)
 
     stack_sum = lax.psum_scatter(stack_rows, "grp", scatter_dimension=0, tiled=True)
     stack_back = lax.all_to_all(

time: 1050 us -> 945 us (0.900)
  waiting for transfers between devices: 518 us -> 200 us
  Pallas kernels: 216 us -> 451 us
  blocking collectives: 76.3 us -> 19.4 us
  local copies, waits for them, and re-layouts: 72.1 us -> 89 us
    all_gather x4 -> x0, waiting for transfers between devices: 297 us -> none  [the longest x1 152 us: body(): outs_all = lax.all_gather(normed_out[None], both, axis=0, tiled=True)]
    pallas_call x1 -> x3, Pallas kernels: 72.5 us -> 308 us  [the longest x2 178 us: spread(): pl.pallas_call(functools.partial(spread_kernel, groups, members, chain, p...]
    all_to_all x2 -> x1, blocking collectives: 67.9 us -> 11.1 us  [share_all(): lax.all_to_all(jnp.broadcast_to(rows[None], (size,) + rows.shape), axes,...]
    reduce_scatter x1, waiting for transfers between devices: 93.5 us -> 77.6 us  [body(): lax.psum_scatter(stack_rows, 'grp', scatter_dimension=0, tiled=True)]
    slice x0 -> x1, local copies, waits for them, and re-layouts: none -> 10.7 us  [body(): weights = pool[:, :stack_part].reshape(devices * stack_part, model_width)]
  transfers between devices with their start and end apart: 13 -> 8, of which waited for: 10 -> 6; matrix products, arithmetic and copies ran while one was open for 5% -> 2% of each run, Pallas kernels for 7% -> 15%
where the time goes in v3:
time: 945 us; the launch traced here: 933 us
  Pallas kernels  451 us (48%)
  waiting for transfers between devices  200 us (21%)
  local copies, waits for them, and re-layouts  89 us (9%)
  matrix products  85.8 us (9%)
  other arithmetic  46.1 us (5%)
  starting transfers between devices  22 us (2%)
  blocking collectives  19.4 us (2%)
  between operations  18.5 us (2%)
    pallas_call x2, Pallas kernels, spread(): pl.pallas_call(functools.partial(spread_kernel, groups, members, chain, p...  178 us
    pallas_call x1, Pallas kernels, spread_score(): pl.pallas_call(functools.partial(score_kernel, groups, members, share, pi...  130 us
    reduce_scatter x1, waiting for transfers between devices, body(): lax.psum_scatter(stack_rows, 'grp', scatter_dimension=0, tiled=True)  77.6 us
    pallas_call x1, Pallas kernels, head_back(): pl.pallas_call(back_kernel, out_shape=(jax.ShapeDtypeStruct((2 * steps, s...  73.9 us
    pallas_call x1, Pallas kernels, finish_table(): pl.pallas_call(finish_kernel, out_shape=(state, state, state), grid_spec=...  69.4 us
    reduce_scatter x1, waiting for transfers between devices, body(): lax.psum_scatter(d_outs[:devices].reshape(devices * seq_len, model_width)...  58.7 us
    psum x1, waiting for transfers between devices, body(): d_group = lax.psum(d_group, 'cli').reshape(members, seq_len, model_width)  45 us
    dot_general x5, matrix products, outer_rows(): lax.dot_general(left, right, (((0,), (0,)), ((), ())), preferred_element_...  25.5 us
  transfers between devices with their start and end apart: 8, of which 6 were waited for; matrix products, arithmetic and copies ran while one was open for 2% of the time, Pallas kernels for 15%

profile of v3, /device:TPU:0, one launch (start us, length us, event | category | flops | bytes accessed | tf_op | source)
XLA Modules:
  0.0 932.5 jit_solution(6741177550723374376)
XLA Ops:
  9.3 2.6 convert_element_type.248
  12.2 11.5 %convert_element_type.251.table.table_ref = bf16[4,1600,768]{2,1,0:T(8,128)(2,1)} convert(f32[4,1600,768]{2,1,0:T(8,128)} %table_ref.1) | non-fusion elementwise | flops 4915200 | bytes 29491200 | tf_op jit(solution)/shard_map/convert_element_type | solution.py:877
  23.7 1.4 constant_dynamic-slice_fusion.1
  25.1 1.6 fusion.101
  27.4 7.3 all-to-all-start.1
  34.7 7.5 all-to-all-done.1
  44.7 2.6 fusion.138
  53.8 5.7 fusion.43
  59.5 1.8 pad_maximum_fusion.src
  61.4 108.5 %shard_map.185 = bf16[32,448,768]{2,1,0:T(8,128)(2,1)} custom-call(bf16[4,448,768]{2,1,0:T(8,128)(2,1)} %pad_maximum_fusion.src), custom_call_target="tpu_custom_call" | custom-call | bytes 44040192 | tf_op jit(solution)/shard_map/pallas_call | solution.py:566
  169.9 10.7 %slice.144 = bf16[32,292,768]{2,1,0:T(8,128)(2,1)} slice(bf16[32,448,768]{2,1,0:T(8,128)(2,1)} %shard_map.185), slice={[0:32], [0:292], [0:768]} | slice | bytes 28704768 | tf_op jit(solution)/shard_map/slice | solution.py:945
  180.6 16.8 %reshape.806 = bf16[9344,768]{1,0:T(8,128)(2,1)} reshape(bf16[32,292,768]{2,1,0:T(8,128)(2,1)} %slice.144) | data formatting | bytes 28704768 | tf_op jit(solution)/shard_map/reshape | solution.py:945
  197.4 1.0 slice_convert_fusion
  198.4 12.8 %gather_fusion.1 = bf16[512,768]{1,0:T(8,128)(2,1)S(1)} fusion(bf16[14336,768]{1,0:T(8,128)(2,1)} %bitcast.206, s32[1024]{0:T(1024)S(1)} %pad_clamp_fusion.2), kind=kCustom, calls=%fused_computation.5 | custom fusion | bytes 1574912 | tf_op jit(solution)/shard_map/jit(_take)/gather | solution.py:933
  212.3 1.5 add_convert_fusion.4
  213.8 3.2 convolution_convert_fusion.7
  217.1 2.1 add_convert_fusion.2
  219.8 2.1 add_convert_fusion.3
  224.3 1.3 fusion.139
  226.3 1.0 copy-done.9
  228.2 2.2 fusion.140
  230.8 4.9 fusion.24
  235.8 8.7 fusion.141
  244.8 1.2 fusion.57.src
  246.1 130.2 %shard_map.186 = (bf16[32,512,768]{2,1,0:T(8,128)(2,1)}, f32[32,2,512]{2,1,0:T(2,128)}) custom-call(bf16[1,512,768]{2,1,0:T(8,128)(2,1)} %fusion.57.src, bf16[4,1600,768]{2,1,0:T(8,128)(2,1)} %get-tuple-element.342, s32[8,1,512]{2,1,0:T(1,128)} %bitcast.215), custom_call_target="tpu_custom_call" | custom-call | flops 40265318400 | bytes 50331648 | tf_op jit(solution)/shard_map/pallas_call | solution.py:619
  376.3 3.6 all-to-all-start.2
  381.7 6.6 all-to-all-done.2
  389.2 2.6 all-to-all-start.3
  395.2 5.1 all-to-all-done.3
  402.6 73.9 %shard_map.187 = (bf16[36,128,768]{2,1,0:T(8,128)(2,1)}, f32[4,1600,768]{2,1,0:T(8,128)}) custom-call(s32[18]{0:T(128)} %copy-done.63, s32[18]{0:T(128)} %get-tuple-element.231.fresh_ref, s32[18]{0:T(128)} %slice.174.first_ref, s32[18]{0:T(128)} %slice.175.second_ref, s32[36]{0:T(128)} %get-tuple-element.229.place_ref, bf16[128,128,768]{2,1,0:T(8,128)(2,1)} %bitcast.241, ...), custom_call_target="tpu_custom_call" | custom-call | flops 33973862400 | bytes 43646976 | tf_op jit(solution)/shard_map/pallas_call | solution.py:731
  476.5 6.1 slice.177
  482.8 58.7 %reduce-scatter.3.cloned.1.call-done = bf16[512,768]{1,0:T(8,128)(2,1)} async-done(((bf16[4096,768]{1,0:T(8,128)(2,1)}), bf16[512,768]{1,0:T(8,128)(2,1)}) %reduce-scatter.3.cloned.1.call-update) | async-done | bytes 786448 | tf_op jit(solution)/shard_map/reduce_scatter | solution.py:1033
  541.6 0.8 fusion.117
  542.4 45.0 %all-reduce.3.cloned.1.call-done = bf16[512,768]{1,0:T(8,128)(2,1)} async-done(((bf16[512,768]{1,0:T(8,128)(2,1)}), bf16[512,768]{1,0:T(8,128)(2,1)}) %all-reduce.3.cloned.1.call-update) | async-done | bytes 786448 | tf_op jit(solution)/shard_map/psum | solution.py:1039
  587.4 1.9 multiply_reduce_fusion.1
  590.8 9.1 convert_reduce_fusion
  599.9 6.4 multiply_reduce_fusion.2
  607.3 2.9 convolution_convert_fusion.6
  610.2 2.3 copy.286
  612.5 2.6 reshape.817
  615.2 3.5 convert_reduce_fusion.3
  618.8 0.8 multiply_reduce_fusion
  619.6 1.0 multiply_convert_fusion.1
  620.6 1.2 fusion.45
  624.8 1.0 copy-done.1
  625.9 4.6 multiply_reduce_fusion.3
  630.4 3.8 fusion.17
  635.0 1.2 fusion.131
  636.3 3.5 fusion.38
  639.8 7.0 fusion.16
  646.8 8.7 fusion.15
  656.6 8.4 all_to_all.50
  665.2 11.1 %all_to_all.51 = f32[32,1,1344]{2,1,0:T(1,128)S(1)} all-to-all(f32[32,1,1344]{2,1,0:T(1,128)S(1)} %broadcast_in_dim.316), channel_id=1, replica_groups=mesh['grp'=8,'cli'=4] {'grp','cli'}, dimensions={0} | all-to-all | bytes 344064 | tf_op jit(solution)/shard_map/all_to_all | solution.py:234
  676.2 3.5 all-to-all-start.4
  679.7 77.6 %reduce-scatter.5.cloned.1.call-done = bf16[1168,768]{1,0:T(8,128)(2,1)} async-done(((bf16[9344,768]{1,0:T(8,128)(2,1)}), bf16[1168,768]{1,0:T(8,128)(2,1)}) %reduce-scatter.5.cloned.1.call-update) | async-done | bytes 1794064 | tf_op jit(solution)/shard_map/reduce_scatter | solution.py:1062
  757.3 2.6 reshape.821
  759.9 4.9 all-to-all-start.5
  771.6 0.8 reduce_sum.530
  772.4 69.1 %shard_map.188.a_ref.b_ref = bf16[32,128,768]{2,1,0:T(8,128)(2,1)} custom-call(bf16[1,128,768]{2,1,0:T(8,128)(2,1)} %bitcast.217), custom_call_target="tpu_custom_call" | custom-call | bytes 12582912 | tf_op jit(solution)/shard_map/pallas_call | solution.py:566
  841.6 69.4 %shard_map.189 = (f32[4,1600,768]{2,1,0:T(8,128)}, f32[4,1600,768]{2,1,0:T(8,128)}, f32[4,1600,768]{2,1,0:T(8,128)}) custom-call(s32[18]{0:T(128)} %copy-done.63, s32[18]{0:T(128)} %get-tuple-element.231.fresh_ref, s32[18]{0:T(128)} %get-tuple-element.230.final_ref, s32[18]{0:T(128)} %slice.172.first_ref, s32[18]{0:T(128)} %slice.173.second_ref, ...), custom_call_target="tpu_custom_call" | custom-call | flops 11324620800 | bytes 117964800 | tf_op jit(solution)/shard_map/pallas_call | solution.py:799
  911.0 4.8 copy_subtract_fusion
  915.9 3.2 copy.305
  919.1 3.2 copy.304
  922.2 2.5 copy.303
  (309 shorter events, 38.7 us)
Async XLA Ops:
  12.2 12.9 %copy-start.68 = (s32[1,128]{1,0:T(1,128)S(1)}, s32[1,128]{1,0:T(1,128)}, u32[]{:S(2)}) copy-start(s32[1,128]{1,0:T(1,128)} %param.18) | copy-start | bytes 1540
  12.2 12.9 %copy-start.69 = (s32[1,128]{1,0:T(1,128)S(1)}, s32[1,128]{1,0:T(1,128)}, u32[]{:S(2)}) copy-start(s32[1,128]{1,0:T(1,128)} %param.17) | copy-start | bytes 1540
  12.2 12.9 %copy-start.70 = (s32[1,128]{1,0:T(1,128)S(1)}, s32[1,128]{1,0:T(1,128)}, u32[]{:S(2)}) copy-start(s32[1,128]{1,0:T(1,128)} %param.16) | copy-start | bytes 1540
  26.7 185.5 %copy-start.28 = (f32[768]{0:T(1024)}, f32[768]{0:T(1024)S(1)}, u32[]{:S(2)}) copy-start(f32[768]{0:T(1024)S(1)} %get-tuple-element.160) | copy-start | bytes 9220
  27.4 14.8 %all-to-all-start.1 = ((s32[32,1,385]{2,1,0:T(1,128)}), s32[32,1,385]{2,1,0:T(1,128)S(1)}, u32[]{:S(2)}, u32[]{:S(2)}) async-start(s32[32,1,385]{2,1,0:T(1,128)} %broadcast_in_dim.280), calls=%async_computation.1 | async-start | bytes 131072 | tf_op jit(solution)/shard_map/all_to_all | solution.py:234
  42.3 8.0 copy-start.25
  43.7 6.6 copy-start.50
  43.8 5.8 copy-start.52
  43.9 5.0 copy-start.65
  49.0 10.6 %copy-start.63 = (s32[18]{0:T(128)}, s32[18]{0:T(128)S(1)}, u32[]{:S(2)}) copy-start(s32[18]{0:T(128)S(1)} %broadcast_add_fusion.model_ref) | copy-start | bytes 220
  198.4 13.8 %copy-start.2 = (f32[128,768]{1,0:T(8,128)}, f32[128,768]{1,0:T(8,128)S(1)}, u32[]{:S(2)}) copy-start(f32[128,768]{1,0:T(8,128)S(1)} %slice_convert_fusion) | copy-start | bytes 1179652
  211.6 2.2 copy-start
  211.8 2.0 copy-start.30
  213.8 5.8 copy-start.15
  213.8 3.3 copy-start.59
  223.0 2.6 copy-start.17
  225.7 2.5 copy-start.14
  225.7 2.5 copy-start.57
  227.9 2.5 copy-start.7
  228.2 2.6 copy-start.42
  228.2 2.6 copy-start.54
  230.4 5.4 copy-start.4
  230.8 5.0 copy-start.46
  230.8 5.0 copy-start.44
  230.8 5.0 copy-start.56
  235.8 8.7 copy-start.71
  246.0 133.9 %copy-start.53 = (pred[36]{0:T(512)(128)(4,1)S(1)}, pred[36]{0:T(512)(128)(4,1)}, u32[]{:S(2)}) copy-start(pred[36]{0:T(512)(128)(4,1)} %copy-done.52) | copy-start | bytes 112
  246.0 133.9 %copy-start.60 = (s32[36]{0:T(128)S(1)}, s32[36]{0:T(128)}, u32[]{:S(2)}) copy-start(s32[36]{0:T(128)} %reshape.813) | copy-start | bytes 436
  246.0 133.9 %copy-start.61 = (s32[36]{0:T(128)S(1)}, s32[36]{0:T(128)}, u32[]{:S(2)}) copy-start(s32[36]{0:T(128)} %add_reduce_fusion) | copy-start | bytes 436
  246.0 133.9 %copy-start.66 = (s32[36]{0:T(128)S(1)}, s32[36]{0:T(128)}, u32[]{:S(2)}) copy-start(s32[36]{0:T(128)} %copy-done.65) | copy-start | bytes 436
  246.1 134.4 %copy-start.12 = (s32[32,128]{1,0:T(8,128)S(1)}, s32[32,128]{1,0:T(8,128)}, u32[]{:S(2)}) copy-start(s32[32,128]{1,0:T(8,128)} %get-tuple-element.215) | copy-start | bytes 49156
  246.1 135.0 %copy-start.11 = (s32[32,128]{1,0:T(8,128)S(1)}, s32[32,128]{1,0:T(8,128)}, u32[]{:S(2)}) copy-start(s32[32,128]{1,0:T(8,128)} %get-tuple-element.212) | copy-start | bytes 49156
  246.1 135.6 %copy-start.62 = (pred[36]{0:T(512)(128)(4,1)S(1)}, pred[36]{0:T(512)(128)(4,1)}, u32[]{:S(2)}) copy-start(pred[36]{0:T(512)(128)(4,1)} %compare_and_fusion.3) | copy-start | bytes 112
  246.1 145.8 %copy-start.64 = (s32[18]{0:T(128)S(1)}, s32[18]{0:T(128)}, u32[]{:S(2)}) copy-start(s32[18]{0:T(128)} %copy-done.63) | copy-start | bytes 220
  246.1 147.1 %copy-start.34 = (f32[4,8,4]{1,2,0:T(4,128)S(1)}, f32[4,8,4]{1,2,0:T(4,128)}, u32[]{:S(2)}) copy-start(f32[4,8,4]{1,2,0:T(4,128)} %fusion.98) | copy-start | bytes 1540
  246.1 147.2 %copy-start.13 = (f32[32,128]{1,0:T(8,128)S(1)}, f32[32,128]{1,0:T(8,128)}, u32[]{:S(2)}) copy-start(f32[32,128]{1,0:T(8,128)} %fusion.94) | copy-start | bytes 49156
  246.1 149.0 %copy-start.26 = (pred[32,127]{1,0:T(8,128)(4,1)S(1)}, pred[32,127]{1,0:T(8,128)(4,1)}, u32[]{:S(2)}) copy-start(pred[32,127]{1,0:T(8,128)(4,1)} %copy-done.25) | copy-start | bytes 12196
  376.3 12.0 %all-to-all-start.2 = ((f32[32,2,512]{2,1,0:T(2,128)}), f32[32,2,512]{2,1,0:T(2,128)S(1)}, u32[]{:S(2)}, u32[]{:S(2)}) async-start(f32[32,2,512]{2,1,0:T(2,128)} %get-tuple-element.59), calls=%async_computation.2 | async-start | bytes 262144 | tf_op jit(solution)/shard_map/all_to_all | solution.py:967
  389.2 11.0 %all-to-all-start.3 = ((f32[32,2,512]{2,1,0:T(2,128)}), f32[32,2,512]{2,1,0:T(2,128)S(1)}, u32[]{:S(2)}, u32[]{:S(2)}) async-start(f32[32,2,512]{2,1,0:T(2,128)} %broadcast_in_dim.299), calls=%async_computation.3 | async-start | bytes 262144 | tf_op jit(solution)/shard_map/all_to_all | solution.py:234
  391.8 149.7 %reduce-scatter.3.cloned.1.call-start = ((), (), s32[]{:S(2)}) async-start(), calls=%async_computation.10 | async-start | bytes 7077888 | tf_op jit(solution)/shard_map/reduce_scatter | solution.py:1033
  482.7 104.7 %all-reduce.3.cloned.1.call-start = ((), (), s32[]{:S(2)}) async-start(), calls=%async_computation.11 | async-start | bytes 1572864 | tf_op jit(solution)/shard_map/psum | solution.py:1039
  541.5 215.8 %reduce-scatter.5.cloned.1.call-start = ((), (), s32[]{:S(2)}) async-start(), calls=%async_computation.12 | async-start | bytes 16146432 | tf_op jit(solution)/shard_map/reduce_scatter | solution.py:1062
  590.3 9.6 %copy-start.21 = (bf16[512,768]{1,0:T(8,128)(2,1)}, bf16[512,768]{1,0:T(8,128)(2,1)S(1)}, u32[]{:S(2)}) copy-start(bf16[512,768]{1,0:T(8,128)(2,1)S(1)} %get-tuple-element.187) | copy-start | bytes 2359300
  590.8 9.1 copy-start.5
  590.8 9.1 copy-start.43
  590.8 9.1 copy-start.47
  599.9 6.4 copy-start.72
  610.2 4.9 copy-start.33
  615.2 3.6 copy-start.10
  615.2 3.6 copy-start.18
  615.2 3.6 copy-start.20
  625.9 4.6 copy-start.16
  630.4 3.8 copy-start.40
  636.3 3.5 copy-start.6
  636.3 3.5 copy-start.55
  639.8 7.0 copy-start.22
  676.2 83.7 %all-to-all-start.4 = ((bf16[4,128,768]{2,1,0:T(8,128)(2,1)}), bf16[4,128,768]{2,1,0:T(8,128)(2,1)S(1)}, u32[]{:S(2)}, u32[]{:S(2)}) async-start(bf16[4,128,768]{2,1,0:T(8,128)(2,1)} %bitcast.35), calls=%async_computation.5 | async-start | bytes 1572864 | tf_op jit(solution)/shard_map/all_to_all | solution.py:1056
  759.9 5.0 copy-start.67
  759.9 6.3 copy-start.51
  759.9 7.3 copy-start.49
  759.9 8.0 copy-start.38
  759.9 10.1 %copy-start.23 = (f32[4,14,768]{2,0,1:T(4,128)S(1)}, f32[4,14,768]{2,0,1:T(4,128)}, u32[]{:S(2)}) copy-start(f32[4,14,768]{2,0,1:T(4,128)} %param.24) | copy-start | bytes 516100
  759.9 10.0 %copy-start.24 = (f32[4,14,768]{2,0,1:T(4,128)S(1)}, f32[4,14,768]{2,0,1:T(4,128)}, u32[]{:S(2)}) copy-start(f32[4,14,768]{2,0,1:T(4,128)} %param.25) | copy-start | bytes 516100
  759.9 151.1 %all-to-all-start.5 = ((bf16[4,292,768]{2,1,0:T(8,128)(2,1)}), bf16[4,292,768]{2,1,0:T(8,128)(2,1)S(1)}, u32[]{:S(2)}, u32[]{:S(2)}) async-start(bf16[4,292,768]{2,1,0:T(8,128)(2,1)} %reshape.821), calls=%async_computation.7 | async-start | bytes 3637248 | tf_op jit(solution)/shard_map/all_to_all | solution.py:1063
  (17 other events, 21.8 us)
Sparse Core Ops, SparseCore 1:
  482.8 58.6 reduce-scatter.2
  543.8 43.5 all-reduce.2
  656.3 100.9 reduce-scatter.4

commit v4 on v3

--- a/solution.py
+++ b/solution.py
@@ -1,4 +1,5 @@
 import functools
+import math
 
 import jax
 import jax.numpy as jnp
@@ -676,6 +677,55 @@
             transcendentals=blocks * rows * part_rows,
         ),
     )(outs_all, table_low, target_blocks)
+
+
+def unpack_kernel(start, part, at_ref, pool_ref, weights_ref, rows_ref):
+    step = pl.program_id(0)
+    owners, slab, width = pool_ref.shape
+    weights_ref[...] = jnp.concatenate([pool_ref[j, :part] for j in range(owners)], axis=0)
+    columns = lax.broadcasted_iota(jnp.int32, (at_ref.shape[0], slab - start), 1) + start
+    found = jnp.zeros(rows_ref.shape, jnp.float32)
+    for j in range(owners):
+        at = at_ref[...] - (step * owners + j) * slab
+        hits = (columns == at).astype(jnp.float32).astype(jnp.bfloat16)
+        found = found + product(hits, pool_ref[j, start:])
+
+    @pl.when(step == 0)
+    def begin():
+        rows_ref[...] = found
+
+    @pl.when(step > 0)
+    def more():
+        rows_ref[...] += found
+
+
+def unpack(pool, part, at):
+    devices, slab, width = pool.shape
+    owners = 8 // math.gcd(part, 8)
+    start = part // 16 * 16
+    tokens = at.shape[0]
+    return pl.pallas_call(
+        functools.partial(unpack_kernel, start, part),
+        out_shape=(
+            jax.ShapeDtypeStruct((devices * part, width), pool.dtype),
+            jax.ShapeDtypeStruct((tokens, width), jnp.float32),
+        ),
+        grid=(devices // owners,),
+        in_specs=[
+            pl.BlockSpec((tokens, 1), lambda i: (0, 0)),
+            pl.BlockSpec((owners, slab, width), lambda i: (i, 0, 0)),
+        ],
+        out_specs=(
+            pl.BlockSpec((owners * part, width), lambda i: (i, 0)),
+            pl.BlockSpec((tokens, width), lambda i: (0, 0)),
+        ),
+        compiler_params=pltpu.CompilerParams(vmem_limit_bytes=40 * MIB),
+        cost_estimate=pl.CostEstimate(
+            flops=2 * devices * tokens * (slab - start) * width,
+            bytes_accessed=4 * pool.size,
+            transcendentals=0,
+        ),
+    )(at, pool)
 
 
 def back_kernel(
@@ -926,26 +976,24 @@
         rows = jnp.einsum("ur,krd->kud", pick, table_low, preferred_element_type=jnp.float32)
         return rows.astype(jnp.bfloat16)
 
-    def taken(pool, lead, start, embedded):
+    def inside(start):
         offset = my_places - start
-        inside = (offset >= 0) & (offset < round_rows)
-        at = my_owner * (lead + round_rows) + lead + offset
-        found = jnp.take(pool.reshape(-1, model_width), jnp.where(inside, at, 0), axis=0)
-        return jnp.where(inside[:, None], found.astype(jnp.float32), embedded)
+        return ((offset >= 0) & (offset < round_rows), offset)
 
     def another(carry):
         index, embedded = carry
         start = index * round_rows
         turned = lax.all_to_all(per_member(offered(start)), "cli", 0, 0, tiled=True)
-        pool = lax.all_gather(turned, "grp", axis=0, tiled=True)
-        return (index + 1, taken(pool, 0, start, embedded))
+        pool = lax.all_gather(turned, "grp", axis=0, tiled=True).reshape(-1, model_width)
+        here, offset = inside(start)
+        found = jnp.take(pool, jnp.where(here, my_owner * round_rows + offset, 0), axis=0)
+        return (index + 1, jnp.where(here[:, None], found.astype(jnp.float32), embedded))
 
     slabs = jnp.concatenate([stack.astype(jnp.bfloat16), offered(0)], axis=1)
     pool = spread(per_member(slabs), groups, members, 1, False, 2)
-    weights = pool[:, :stack_part].reshape(devices * stack_part, model_width)
-    embedded = taken(
-        pool, stack_part, 0, jnp.zeros((local * seq_len, model_width), jnp.float32)
-    )
+    here, offset = inside(0)
+    at = jnp.where(here, my_owner * slab + stack_part + offset, -1)
+    weights, embedded = unpack(pool, stack_part, at[:, None])
     _, embedded = lax.while_loop(
         lambda carry: carry[0] < rounds, another, (jnp.int32(1), embedded)
     )
@@ -1036,7 +1084,11 @@
         scatter_dimension=0,
         tiled=True,
     )
-    d_group = lax.psum(d_group, "cli").reshape(members, seq_len, model_width)
+    d_level = lax.all_to_all(
+        d_group.reshape(members, seq_len, model_width), "cli", 0, 0, tiled=True
+    )
+    d_level = jnp.sum(d_level.astype(jnp.float32), axis=0).astype(jnp.bfloat16)
+    d_group = share_all(d_level, "cli", members)
     d_mine = lax.dynamic_slice(
         d_group, (part_own * local, 0, 0), (local, seq_len, model_width)
     ).astype(jnp.float32)
@@ -1060,12 +1112,6 @@
     d_all = spread(d_client, groups, members, 3, True, 2)
 
     stack_sum = lax.psum_scatter(stack_rows, "grp", scatter_dimension=0, tiled=True)
-    stack_back = lax.all_to_all(
-        stack_sum.reshape(members, stack_part, model_width), "cli", 0, 0, tiled=True
-    ).astype(jnp.float32)
-    stack_grad = jnp.sum(
-        stack_back.reshape(models, share, stack_part, model_width), axis=1
-    )
     vector_piece = vector_rows.size // groups
     vector_part = jnp.sum(
         lax.all_to_all(vector_rows.reshape(groups, vector_piece), "grp", 0, 0, tiled=True), axis=0
@@ -1090,6 +1136,11 @@
         client_at[1::2],
         slot_token.reshape(steps, 1, 2 * seq_len),
     )
+    stack_sum, table_grad = lax.optimization_barrier((stack_sum, table_grad))
+    stack_back = lax.all_to_all(
+        stack_sum.reshape(members, stack_part, model_width), "cli", 0, 0, tiled=True
+    ).astype(jnp.float32)
+    stack_grad = jnp.sum(stack_back.reshape(models, share, stack_part, model_width), axis=1)
     stack_momentum_new, stack_new = update(stack, stack_momentum, stack_grad, stack_rate)
     vector_momentum_new, vector_new = update(vectors, vector_momentum, vector_grad, vector_rate)
     return (

time: 945 us -> 883 us (0.934)
  waiting for transfers between devices: 200 us -> 153 us
  local copies, waits for them, and re-layouts: 89 us -> 61.7 us
  blocking collectives: 19.4 us -> 32 us
  matrix products: 85.8 us -> 75.5 us
  Pallas kernels: 451 us -> 461 us
    reduce_scatter x1, waiting for transfers between devices: 77.6 us -> 0.01 us  [body(): lax.psum_scatter(stack_rows, 'grp', scatter_dimension=0, tiled=True)]
    psum x1 -> x0, waiting for transfers between devices: 45 us -> none  [body(): d_group = lax.psum(d_group, 'cli').reshape(members, seq_len, model_width)]
    all_to_all x1, waiting for transfers between devices: 0.01 us -> 38.5 us  [body(): lax.all_to_all(stack_sum.reshape(members, stack_part, model_width), 'cli'...]
    pallas_call x0 -> x1, Pallas kernels: none -> 19.1 us  [unpack(): pl.pallas_call(functools.partial(unpack_kernel, start, part), out_shape=(...]
    all_to_all x2 -> x4, waiting for transfers between devices: 12.5 us -> 30.9 us  [share_all(): lax.all_to_all(jnp.broadcast_to(rows[None], (size,) + rows.shape), axes,...]
    all_to_all x1, waiting for transfers between devices: 0.01 us -> 18.3 us  [body(): lax.all_to_all(d_wide.reshape(members, seq_len, model_width), 'cli', 0, 0...]
    reshape x1 -> x0, local copies, waits for them, and re-layouts: 16.8 us -> none  [body(): weights = pool[:, :stack_part].reshape(devices * stack_part, model_width)]
    all_to_all x1, blocking collectives: 11.1 us -> 24.6 us  [body(): lax.all_to_all(d_group.reshape(members, seq_len, model_width), 'cli', 0,...]
  transfers between devices with their start and end apart: 8 -> 9, of which waited for: 6 -> 7; matrix products, arithmetic and copies ran while one was open for 2% -> 2% of each run, Pallas kernels for 15% -> 15%
where the time goes in v4:
time: 883 us; the launch traced here: 873 us
  Pallas kernels  461 us (52%)
  waiting for transfers between devices  153 us (17%)
  matrix products  75.5 us (9%)
  local copies, waits for them, and re-layouts  61.7 us (7%)
  other arithmetic  44.7 us (5%)
  blocking collectives  32 us (4%)
  starting transfers between devices  27.1 us (3%)
  between operations  18.4 us (2%)
    pallas_call x2, Pallas kernels, spread(): pl.pallas_call(functools.partial(spread_kernel, groups, members, chain, p...  168 us
    pallas_call x1, Pallas kernels, spread_score(): pl.pallas_call(functools.partial(score_kernel, groups, members, share, pi...  130 us
    pallas_call x1, Pallas kernels, head_back(): pl.pallas_call(back_kernel, out_shape=(jax.ShapeDtypeStruct((2 * steps, s...  73.7 us
    pallas_call x1, Pallas kernels, finish_table(): pl.pallas_call(finish_kernel, out_shape=(state, state, state), grid_spec=...  69.6 us
    reduce_scatter x1, waiting for transfers between devices, body(): lax.psum_scatter(d_outs[:devices].reshape(devices * seq_len, model_width)...  58.8 us
    all_to_all x1, waiting for transfers between devices, body(): lax.all_to_all(stack_sum.reshape(members, stack_part, model_width), 'cli'...  38.5 us
    all_to_all x4, waiting for transfers between devices, share_all(): lax.all_to_all(jnp.broadcast_to(rows[None], (size,) + rows.shape), axes,...  30.9 us
    all_to_all x1, blocking collectives, body(): lax.all_to_all(d_group.reshape(members, seq_len, model_width), 'cli', 0,...  24.6 us
  transfers between devices with their start and end apart: 9, of which 7 were waited for; matrix products, arithmetic and copies ran while one was open for 2% of the time, Pallas kernels for 15%

profile of v4, /device:TPU:0, one launch (start us, length us, event | category | flops | bytes accessed | tf_op | source)
XLA Modules:
  0.0 873.4 jit_solution(16397930030180199147)
XLA Ops:
  8.7 2.6 convert_element_type.242
  11.6 11.5 %convert_element_type.245.table.table_ref = bf16[4,1600,768]{2,1,0:T(8,128)(2,1)} convert(f32[4,1600,768]{2,1,0:T(8,128)} %table_ref.1) | non-fusion elementwise | flops 4915200 | bytes 29491200 | tf_op jit(solution)/shard_map/convert_element_type | solution.py:927
  23.1 1.4 constant_dynamic-slice_fusion.1
  24.5 1.6 fusion.104
  26.8 7.3 all-to-all-start.1
  34.1 7.5 all-to-all-done.1
  48.6 2.6 fusion.142
  54.3 5.7 fusion.42
  60.0 1.8 pad_maximum_fusion.src
  61.9 108.5 %shard_map.185.pool_ref = bf16[32,448,768]{2,1,0:T(8,128)(2,1)} custom-call(bf16[4,448,768]{2,1,0:T(8,128)(2,1)} %pad_maximum_fusion.src), custom_call_target="tpu_custom_call" | custom-call | bytes 44040192 | tf_op jit(solution)/shard_map/pallas_call | solution.py:567
  170.5 19.1 %shard_map.186 = (bf16[9344,768]{1,0:T(8,128)(2,1)S(1)}, f32[512,768]{1,0:T(8,128)S(1)}) custom-call(s32[512,1]{1,0:T(8,128)S(1)} %fusion.78.at_ref, bf16[32,448,768]{2,1,0:T(8,128)(2,1)} %shard_map.185.pool_ref), custom_call_target="tpu_custom_call" | custom-call | flops 4026531840 | bytes 44040192 | tf_op jit(solution)/shard_map/pallas_call | solution.py:707
  189.6 5.3 copy-done
  196.0 1.5 add_convert_fusion.4
  197.5 3.2 convolution_convert_fusion.7
  200.8 2.1 add_convert_fusion.2
  203.5 2.2 add_convert_fusion.3
  206.0 1.1 reshape.785
  207.1 1.2 copy.314
  208.2 2.2 reshape.787
  214.6 1.1 slice-done.2
  215.6 1.4 slice-done.3
  218.8 2.7 fusion.24
  221.6 4.1 fusion.145
  226.0 1.2 fusion.56.src
  227.3 130.3 %shard_map.187 = (bf16[32,512,768]{2,1,0:T(8,128)(2,1)}, f32[32,2,512]{2,1,0:T(2,128)}) custom-call(bf16[1,512,768]{2,1,0:T(8,128)(2,1)} %fusion.56.src, bf16[4,1600,768]{2,1,0:T(8,128)(2,1)} %get-tuple-element.348, s32[8,1,512]{2,1,0:T(1,128)} %bitcast.220), custom_call_target="tpu_custom_call" | custom-call | flops 40265318400 | bytes 50331648 | tf_op jit(solution)/shard_map/pallas_call | solution.py:620
  357.7 3.6 all-to-all-start.2
  363.1 6.6 all-to-all-done.2
  370.6 2.6 all-to-all-start.3
  376.4 5.2 all-to-all-done.3
  383.3 73.7 %shard_map.188 = (bf16[36,128,768]{2,1,0:T(8,128)(2,1)}, f32[4,1600,768]{2,1,0:T(8,128)}) custom-call(s32[18]{0:T(128)} %copy-done.61, s32[18]{0:T(128)} %get-tuple-element.235.fresh_ref, s32[18]{0:T(128)} %slice.168.first_ref, s32[18]{0:T(128)} %slice.169.second_ref, s32[36]{0:T(128)} %get-tuple-element.237.place_ref, bf16[128,128,768]{2,1,0:T(8,128)(2,1)} %bitcast.247, ...), custom_call_target="tpu_custom_call" | custom-call | flops 33973862400 | bytes 43646976 | tf_op jit(solution)/shard_map/pallas_call | solution.py:781
  457.0 6.1 slice.171
  463.2 58.8 %reduce-scatter.3.cloned.1.call-done = bf16[512,768]{1,0:T(8,128)(2,1)} async-done(((bf16[4096,768]{1,0:T(8,128)(2,1)}), bf16[512,768]{1,0:T(8,128)(2,1)}) %reduce-scatter.3.cloned.1.call-update) | async-done | bytes 786448 | tf_op jit(solution)/shard_map/reduce_scatter | solution.py:1081
  521.9 24.6 %all_to_all.60 = bf16[4,128,768]{2,1,0:T(8,128)(2,1)S(1)} all-to-all(bf16[4,128,768]{2,1,0:T(8,128)(2,1)} %bitcast.224), channel_id=1, replica_groups=mesh['grp'=8,'cli'=4] {'cli'}, dimensions={0} | all-to-all | bytes 1572864 | tf_op jit(solution)/shard_map/all_to_all | solution.py:1087
  547.6 3.5 all-to-all-start.5
  552.0 18.3 %all-to-all-done.5 = bf16[4,128,768]{2,1,0:T(8,128)(2,1)S(1)} async-done(((bf16[4,128,768]{2,1,0:T(8,128)(2,1)}), bf16[4,128,768]{2,1,0:T(8,128)(2,1)S(1)}, u32[]{:S(2)}, u32[]{:S(2)}) %all-to-all-start.5) | async-done | bytes 786464 | tf_op jit(solution)/shard_map/all_to_all | solution.py:235
  572.1 9.2 %convert_reduce_fusion = (f32[3072]{0:T(1024)S(1)}, bf16[512,3072]{1,0:T(8,128)(2,1)S(1)}) fusion(f32[512,3072]{1,0:T(8,128)} %copy-done.68, f32[3072]{0:T(1024)S(1)} %bitcast.237, bf16[512,768]{1,0:T(8,128)(2,1)S(1)} %get-tuple-element.194, bf16[9344,768]{1,0:T(8,128)(2,1)} %copy-done), kind=kOutput, calls=%fused_computation.32 | convolution fusion | flops 2452091904 | bytes 14966784 | tf_op jit(solution)/shard_map/dot_general | solution.py:35
  581.3 6.4 multiply_reduce_fusion.1
  588.7 2.9 convolution_convert_fusion.6
  591.6 2.3 copy.328
  593.9 2.8 reshape.797
  596.8 3.6 convert_reduce_fusion.3
  601.2 1.0 multiply_convert_fusion.1
  602.3 1.2 fusion.44
  606.5 1.0 copy-done.2
  607.5 4.6 multiply_reduce_fusion.2
  612.1 3.8 fusion.17
  616.7 1.7 fusion.135
  618.4 1.5 reduce_sum.543
  619.9 3.3 fusion.37
  623.2 4.7 fusion.16
  627.9 8.7 fusion.15
  637.8 7.4 all_to_all.61
  645.2 3.6 all-to-all-start.6
  650.7 18.3 %all-to-all-done.6 = bf16[4,128,768]{2,1,0:T(8,128)(2,1)S(1)} async-done(((bf16[4,128,768]{2,1,0:T(8,128)(2,1)}), bf16[4,128,768]{2,1,0:T(8,128)(2,1)S(1)}, u32[]{:S(2)}, u32[]{:S(2)}) %all-to-all-start.6) | async-done | bytes 786464 | tf_op jit(solution)/shard_map/all_to_all | solution.py:1108
  669.7 2.6 all-to-all-start.9
  673.1 59.5 %shard_map.189.a_ref.b_ref = bf16[32,128,768]{2,1,0:T(8,128)(2,1)} custom-call(bf16[1,128,768]{2,1,0:T(8,128)(2,1)} %bitcast.222), custom_call_target="tpu_custom_call" | custom-call | bytes 12582912 | tf_op jit(solution)/shard_map/pallas_call | solution.py:567
  732.6 69.6 %shard_map.190 = (f32[4,1600,768]{2,1,0:T(8,128)}, f32[4,1600,768]{2,1,0:T(8,128)}, f32[4,1600,768]{2,1,0:T(8,128)}) custom-call(s32[18]{0:T(128)} %copy-done.61, s32[18]{0:T(128)} %get-tuple-element.235.fresh_ref, s32[18]{0:T(128)} %get-tuple-element.234.final_ref, s32[18]{0:T(128)} %slice.173.first_ref, s32[18]{0:T(128)} %slice.174.second_ref, ...), custom_call_target="tpu_custom_call" | custom-call | flops 11324620800 | bytes 117964800 | tf_op jit(solution)/shard_map/pallas_call | solution.py:849
  802.2 2.6 reshape.801
  804.8 3.9 all-to-all-start.7
  813.6 38.5 %all-to-all-done.7 = bf16[4,292,768]{2,1,0:T(8,128)(2,1)S(1)} async-done(((bf16[4,292,768]{2,1,0:T(8,128)(2,1)}), bf16[4,292,768]{2,1,0:T(8,128)(2,1)S(1)}, u32[]{:S(2)}, u32[]{:S(2)}) %all-to-all-start.7) | async-done | bytes 1794080 | tf_op jit(solution)/shard_map/all_to_all | solution.py:1140
  852.1 4.8 copy_subtract_fusion
  856.9 3.2 copy.347
  860.1 3.2 copy.346
  863.3 2.5 copy.345
  (316 shorter events, 44.6 us)
Async XLA Ops:
  11.6 12.9 %copy-start.65 = (s32[1,128]{1,0:T(1,128)S(1)}, s32[1,128]{1,0:T(1,128)}, u32[]{:S(2)}) copy-start(s32[1,128]{1,0:T(1,128)} %param.18) | copy-start | bytes 1540
  11.6 12.9 %copy-start.66 = (s32[1,128]{1,0:T(1,128)S(1)}, s32[1,128]{1,0:T(1,128)}, u32[]{:S(2)}) copy-start(s32[1,128]{1,0:T(1,128)} %param.17) | copy-start | bytes 1540
  11.6 12.9 %copy-start.67 = (s32[1,128]{1,0:T(1,128)S(1)}, s32[1,128]{1,0:T(1,128)}, u32[]{:S(2)}) copy-start(s32[1,128]{1,0:T(1,128)} %param.16) | copy-start | bytes 1540
  26.8 14.8 %all-to-all-start.1 = ((s32[32,1,385]{2,1,0:T(1,128)}), s32[32,1,385]{2,1,0:T(1,128)S(1)}, u32[]{:S(2)}, u32[]{:S(2)}) async-start(s32[32,1,385]{2,1,0:T(1,128)} %broadcast_in_dim.263), calls=%async_computation.1 | async-start | bytes 131072 | tf_op jit(solution)/shard_map/all_to_all | solution.py:235
  41.7 6.8 copy-start.28
  42.5 5.9 copy-start.47
  43.1 8.0 copy-start.49
  43.2 7.9 copy-start.51
  43.3 7.9 copy-start.63
  189.6 5.4 copy-start
  195.2 2.3 copy-start.1
  195.8 4.9 copy-start.41
  195.8 4.9 copy-start.36
  197.5 5.8 copy-start.18
  197.5 3.3 copy-start.57
  203.3 7.3 copy-start.5
  206.0 4.4 copy-start.40
  207.1 7.5 slice-start
  210.6 4.0 slice-start.1
  211.3 4.3 slice-start.2
  213.0 4.1 slice-start.3
  213.0 4.5 copy-start.17
  213.0 4.5 copy-start.55
  214.5 3.9 copy-start.11
  218.4 3.1 copy-start.9
  218.8 2.8 copy-start.46
  218.8 2.8 copy-start.54
  221.5 4.2 copy-start.68
  221.6 4.4 copy-start.32
  221.6 4.4 copy-start.43
  227.2 134.0 %copy-start.52 = (pred[36]{0:T(512)(128)(4,1)S(1)}, pred[36]{0:T(512)(128)(4,1)}, u32[]{:S(2)}) copy-start(pred[36]{0:T(512)(128)(4,1)} %copy-done.51) | copy-start | bytes 112
  227.2 134.0 %copy-start.58 = (s32[36]{0:T(128)S(1)}, s32[36]{0:T(128)}, u32[]{:S(2)}) copy-start(s32[36]{0:T(128)} %reshape.791) | copy-start | bytes 436
  227.2 134.0 %copy-start.59 = (s32[36]{0:T(128)S(1)}, s32[36]{0:T(128)}, u32[]{:S(2)}) copy-start(s32[36]{0:T(128)} %add_reduce_fusion) | copy-start | bytes 436
  227.2 134.0 %copy-start.64 = (s32[36]{0:T(128)S(1)}, s32[36]{0:T(128)}, u32[]{:S(2)}) copy-start(s32[36]{0:T(128)} %copy-done.63) | copy-start | bytes 436
  227.2 134.6 %copy-start.16 = (s32[32,128]{1,0:T(8,128)S(1)}, s32[32,128]{1,0:T(8,128)}, u32[]{:S(2)}) copy-start(s32[32,128]{1,0:T(8,128)} %get-tuple-element.222) | copy-start | bytes 49156
  227.2 135.1 %copy-start.15 = (s32[32,128]{1,0:T(8,128)S(1)}, s32[32,128]{1,0:T(8,128)}, u32[]{:S(2)}) copy-start(s32[32,128]{1,0:T(8,128)} %get-tuple-element.219) | copy-start | bytes 49156
  227.3 135.7 %copy-start.60 = (pred[36]{0:T(512)(128)(4,1)S(1)}, pred[36]{0:T(512)(128)(4,1)}, u32[]{:S(2)}) copy-start(pred[36]{0:T(512)(128)(4,1)} %compare_and_fusion.3) | copy-start | bytes 112
  227.3 145.9 %copy-start.62 = (s32[18]{0:T(128)S(1)}, s32[18]{0:T(128)}, u32[]{:S(2)}) copy-start(s32[18]{0:T(128)} %copy-done.61) | copy-start | bytes 220
  227.3 147.2 %copy-start.35 = (f32[4,8,4]{1,2,0:T(4,128)S(1)}, f32[4,8,4]{1,2,0:T(4,128)}, u32[]{:S(2)}) copy-start(f32[4,8,4]{1,2,0:T(4,128)} %fusion.101) | copy-start | bytes 1540
  227.3 147.3 %copy-start.14 = (f32[32,128]{1,0:T(8,128)S(1)}, f32[32,128]{1,0:T(8,128)}, u32[]{:S(2)}) copy-start(f32[32,128]{1,0:T(8,128)} %fusion.97) | copy-start | bytes 49156
  227.3 149.1 %copy-start.29 = (pred[32,127]{1,0:T(8,128)(4,1)S(1)}, pred[32,127]{1,0:T(8,128)(4,1)}, u32[]{:S(2)}) copy-start(pred[32,127]{1,0:T(8,128)(4,1)} %copy-done.28) | copy-start | bytes 12196
  357.7 12.0 %all-to-all-start.2 = ((f32[32,2,512]{2,1,0:T(2,128)}), f32[32,2,512]{2,1,0:T(2,128)S(1)}, u32[]{:S(2)}, u32[]{:S(2)}) async-start(f32[32,2,512]{2,1,0:T(2,128)} %get-tuple-element.65), calls=%async_computation.2 | async-start | bytes 262144 | tf_op jit(solution)/shard_map/all_to_all | solution.py:1015
  370.6 11.0 %all-to-all-start.3 = ((f32[32,2,512]{2,1,0:T(2,128)}), f32[32,2,512]{2,1,0:T(2,128)S(1)}, u32[]{:S(2)}, u32[]{:S(2)}) async-start(f32[32,2,512]{2,1,0:T(2,128)} %broadcast_in_dim.278), calls=%async_computation.3 | async-start | bytes 262144 | tf_op jit(solution)/shard_map/all_to_all | solution.py:235
  373.1 148.8 %reduce-scatter.3.cloned.1.call-start = ((), (), s32[]{:S(2)}) async-start(), calls=%async_computation.12 | async-start | bytes 7077888 | tf_op jit(solution)/shard_map/reduce_scatter | solution.py:1081
  547.6 22.6 %all-to-all-start.5 = ((bf16[4,128,768]{2,1,0:T(8,128)(2,1)}), bf16[4,128,768]{2,1,0:T(8,128)(2,1)S(1)}, u32[]{:S(2)}, u32[]{:S(2)}) async-start(bf16[4,128,768]{2,1,0:T(8,128)(2,1)} %broadcast_in_dim.287), calls=%async_computation.6 | async-start | bytes 1572864 | tf_op jit(solution)/shard_map/all_to_all | solution.py:235
  551.1 251.1 %reduce-scatter.5.cloned.1.call-start = ((), (), s32[]{:S(2)}) async-start(), calls=%async_computation.13 | async-start | bytes 16146432 | tf_op jit(solution)/shard_map/reduce_scatter | solution.py:1114
  572.0 9.3 %copy-start.24 = (bf16[512,768]{1,0:T(8,128)(2,1)}, bf16[512,768]{1,0:T(8,128)(2,1)S(1)}, u32[]{:S(2)}) copy-start(bf16[512,768]{1,0:T(8,128)(2,1)S(1)} %get-tuple-element.194) | copy-start | bytes 2359300
  572.0 9.3 %copy-start.10 = (f32[512,768]{1,0:T(8,128)S(1)}, f32[512,768]{1,0:T(8,128)}, u32[]{:S(2)}) copy-start(f32[512,768]{1,0:T(8,128)} %copy-done.9) | copy-start | bytes 4718596
  581.3 6.4 copy-start.69
  596.7 3.6 copy-start.13
  596.7 3.6 copy-start.21
  596.7 3.6 copy-start.23
  607.5 4.6 copy-start.19
  612.1 3.8 copy-start.42
  619.9 3.3 copy-start.70
  623.2 4.7 copy-start.25
  645.2 23.7 %all-to-all-start.6 = ((bf16[4,128,768]{2,1,0:T(8,128)(2,1)}), bf16[4,128,768]{2,1,0:T(8,128)(2,1)S(1)}, u32[]{:S(2)}, u32[]{:S(2)}) async-start(bf16[4,128,768]{2,1,0:T(8,128)(2,1)} %bitcast.35), calls=%async_computation.8 | async-start | bytes 1572864 | tf_op jit(solution)/shard_map/all_to_all | solution.py:1108
  669.7 135.1 %all-to-all-start.9 = ((f32[32,1,1344]{2,1,0:T(1,128)}), f32[32,1,1344]{2,1,0:T(1,128)S(1)}, u32[]{:S(2)}, u32[]{:S(2)}) async-start(f32[32,1,1344]{2,1,0:T(1,128)} %broadcast_in_dim.295), calls=%async_computation.11 | async-start | bytes 360448 | tf_op jit(solution)/shard_map/all_to_all | solution.py:235
  804.8 4.0 copy-start.50
  804.8 4.3 copy-start.48
  804.8 5.1 copy-start.39
  804.8 7.1 copy-start.26
  804.8 7.1 copy-start.27
  804.8 47.2 %all-to-all-start.7 = ((bf16[4,292,768]{2,1,0:T(8,128)(2,1)}), bf16[4,292,768]{2,1,0:T(8,128)(2,1)S(1)}, u32[]{:S(2)}, u32[]{:S(2)}) async-start(bf16[4,292,768]{2,1,0:T(8,128)(2,1)} %reshape.801), calls=%async_computation.9 | async-start | bytes 3637248 | tf_op jit(solution)/shard_map/all_to_all | solution.py:1140
  (20 other events, 25.3 us)
Sparse Core Ops, SparseCore 1:
  463.3 58.6 reduce-scatter.2
  637.4 122.7 reduce-scatter.4

commit v5 on v4

--- a/solution.py
+++ b/solution.py
@@ -18,8 +18,9 @@
 stack_rate = 4.0
 vector_rate = 50.0
 
-ROUND_ROWS = 128
-SLAB_STEP = 32
+ROUND_ROWS = 104
+SLAB_STEP = 16
+TILE = 400
 MIB = 1 << 20
 POOL_BYTES = 32 * MIB
 MESH = pl.DeviceIdType.MESH
@@ -577,6 +578,10 @@
     )(src)
 
 
+def tile_of(part_rows):
+    return TILE if part_rows % TILE == 0 else part_rows
+
+
 def score_kernel(groups, members, share, pieces, src, table, target, out, stat, *rest):
     part, pool, part_sem, out_sems = rest[:4]
     sems = rest[4:]
@@ -595,14 +600,24 @@
         keep(block, piece).start()
         here = pl.ds(pl.multiple_of(piece * size, size), size)
         model = lax.div(level, share)
-        logits = project(part[model], pool[block, here])
-        highest = jnp.max(logits, axis=0, keepdims=True)
-        total = jnp.sum(jnp.exp(logits - highest), axis=0, keepdims=True)
-        tokens = lax.broadcasted_iota(jnp.int32, logits.shape, 0)
         wanted = target[lax.div(block, members) * share + lax.rem(level, share), :, here]
-        hit = jnp.sum(jnp.where(tokens == wanted, logits, 0.0), axis=0, keepdims=True)
-        stat[block, 0:1, here] = highest + jnp.log(total)
-        stat[block, 1:2, here] = hit
+        outs = pool[block, here]
+        part_rows = part.shape[1]
+        tile = tile_of(part_rows)
+        marks = lax.broadcasted_iota(jnp.int32, (tile, size), 0)
+        tops, totals, hits = [], [], []
+        for first in range(0, part_rows, tile):
+            logits = project(part[model, pl.ds(first, tile)], outs)
+            hit = jnp.where(marks == wanted - first, logits, 0.0).reshape(-1, 8, size)
+            hits.append(jnp.sum(hit, axis=0))
+            logits = logits.reshape(-1, 8, size)
+            top = jnp.max(logits, axis=0)
+            tops.append(top)
+            totals.append(jnp.sum(jnp.exp(logits - top[None]), axis=0))
+        highest = jnp.max(functools.reduce(jnp.maximum, tops), axis=0, keepdims=True)
+        total = sum(t * jnp.exp(m - highest) for t, m in zip(totals, tops))
+        stat[block, 0:1, here] = highest + jnp.log(jnp.sum(total, axis=0, keepdims=True))
+        stat[block, 1:2, here] = jnp.sum(sum(hits), axis=0, keepdims=True)
 
     spread_body(place, True, pieces, src, pool, sems, consume, load_table.wait)
 
@@ -747,25 +762,27 @@
         leave(slot, 0, 0).wait()
         leave(slot, 0, 1).wait()
     outs = jnp.concatenate([a_ref[0], b_ref[0]], axis=0)
-    logits = project(table_ref[0], outs)
-    rows = lax.broadcasted_iota(jnp.int32, logits.shape, 0)
-    soft = jnp.exp(logits - info_ref[0, 0:1, :])
-    hit = (rows == target_ref[0]).astype(jnp.float32)
-    d_logits = (info_ref[0, 1:2, :] * (soft - hit)).astype(jnp.bfloat16)
-    d_outs = outer_rows(d_logits, table_ref[0])
+    @pl.when(fresh_ref[step] == 1)
+    def start():
+        grad_ref[...] = jnp.zeros_like(grad_ref)
+
+    part_rows = table_ref.shape[1]
+    size = tile_of(part_rows)
+    d_outs = jnp.zeros((2 * seq_len, outs.shape[1]), jnp.float32)
+    for first_row in range(0, part_rows, size):
+        here = pl.ds(first_row, size)
+        table_rows = table_ref[0, here]
+        logits = project(table_rows, outs)
+        rows = lax.broadcasted_iota(jnp.int32, logits.shape, 0) + first_row
+        soft = jnp.exp(logits - info_ref[0, 0:1, :])
+        soft = jnp.where(rows == target_ref[0], soft - 1.0, soft)
+        d_logits = (info_ref[0, 1:2, :] * soft).astype(jnp.bfloat16)
+        d_outs = d_outs + outer_rows(d_logits, table_rows)
+        grad_ref[0, here] += product(d_logits, outs)
     held[slot, 0] = d_outs[:seq_len].astype(held.dtype)
     held[slot, 1] = d_outs[seq_len:].astype(held.dtype)
     leave(slot, place_ref[2 * step], 0).start()
     leave(slot, place_ref[2 * step + 1], 1).start()
-    gain = product(d_logits, outs)
-
-    @pl.when(fresh_ref[step] == 1)
-    def start():
-        grad_ref[0] = gain
-
-    @pl.when(fresh_ref[step] == 0)
-    def more():
-        grad_ref[0] += gain
 
     @pl.when(step == steps - 1)
     def drain():
@@ -813,10 +830,11 @@
 
 
 def finish_kernel(
-    model_ref, fresh_ref, final_ref, first_ref, second_ref, a_ref, b_ref, ids_ref, head_ref, table_ref, momentum_ref,
-    grad_ref, momentum_new_ref, table_new_ref,
+    first_tile, model_ref, fresh_ref, final_ref, first_ref, second_ref, a_ref, b_ref, ids_ref, head_ref, table_ref,
+    momentum_ref, *rest,
 ):
-    tile = pl.program_id(0)
+    grad_ref, momentum_new_ref, table_new_ref = rest[-3:]
+    tile = pl.program_id(0) + first_tile
     step = pl.program_id(1)
     tile_rows = grad_ref.shape[1]
     rows = lax.broadcasted_iota(jnp.int32, (tile_rows, ids_ref.shape[2]), 0) + tile * tile_rows
@@ -839,19 +857,20 @@
         table_new_ref[0] = fresh_table
 
 
-def finish_table(d_inputs, head_grad, table, momentum, model_of, fresh, final, first, second, ids):
+def finish_table(d_inputs, head_grad, table, momentum, schedule, ids, first_tile, tiles, earlier):
+    model_of, fresh, final, first, second = schedule
     steps = model_of.shape[0]
     models, part_rows, width = table.shape
     seq_len = d_inputs.shape[1]
     tile_rows = part_rows // 2
     state = jax.ShapeDtypeStruct(table.shape, jnp.float32)
-    piece = pl.BlockSpec((1, tile_rows, width), lambda t, s, m, f, l, a, b: (m[s], t, 0))
+    piece = pl.BlockSpec((1, tile_rows, width), lambda t, s, m, f, l, a, b: (m[s], t + first_tile, 0))
     return pl.pallas_call(
-        finish_kernel,
+        functools.partial(finish_kernel, first_tile),
         out_shape=(state, state, state),
         grid_spec=pltpu.PrefetchScalarGridSpec(
             num_scalar_prefetch=5,
-            grid=(part_rows // tile_rows, steps),
+            grid=(tiles, steps),
             in_specs=[
                 pl.BlockSpec((1, seq_len, width), lambda t, s, m, f, l, a, b: (a[s], 0, 0)),
                 pl.BlockSpec((1, seq_len, width), lambda t, s, m, f, l, a, b: (b[s], 0, 0)),
@@ -859,16 +878,18 @@
                 piece,
                 piece,
                 piece,
-            ],
+            ]
+            + [pl.BlockSpec(memory_space=pl.ANY)] * len(earlier),
             out_specs=(piece, piece, piece),
         ),
+        input_output_aliases={11 + i: i for i in range(len(earlier))},
         compiler_params=pltpu.CompilerParams(vmem_limit_bytes=56 * MIB),
         cost_estimate=pl.CostEstimate(
-            flops=4 * steps * seq_len * part_rows * width,
-            bytes_accessed=24 * table.size,
+            flops=4 * steps * seq_len * tiles * tile_rows * width,
+            bytes_accessed=24 * models * tiles * tile_rows * width,
             transcendentals=0,
         ),
-    )(model_of, fresh, final, first, second, d_inputs, d_inputs, ids, head_grad, table, momentum)
+    )(*schedule, d_inputs, d_inputs, ids, head_grad, table, momentum, *earlier)
 
 
 def body(
@@ -1124,22 +1145,16 @@
     token_local = tokens - device_index * block_rows
     token_local = jnp.where((token_local >= 0) & (token_local < block_rows), token_local, -1)
     slot_token = jnp.where(filled[:, None], jnp.take(token_local, client_at, axis=0), -1)
-    table_grad, table_momentum_new, table_new = finish_table(
-        d_all,
-        head_grad,
-        table,
-        table_momentum,
-        model_of,
-        fresh,
-        final,
-        client_at[0::2],
-        client_at[1::2],
-        slot_token.reshape(steps, 1, 2 * seq_len),
-    )
-    stack_sum, table_grad = lax.optimization_barrier((stack_sum, table_grad))
+    schedule = (model_of, fresh, final, client_at[0::2], client_at[1::2])
+    slot_token = slot_token.reshape(steps, 1, 2 * seq_len)
+    upper = finish_table(d_all, head_grad, table, table_momentum, schedule, slot_token, 0, 1, ())
+    stack_sum, upper = lax.optimization_barrier((stack_sum, upper))
     stack_back = lax.all_to_all(
         stack_sum.reshape(members, stack_part, model_width), "cli", 0, 0, tiled=True
     ).astype(jnp.float32)
+    table_grad, table_momentum_new, table_new = finish_table(
+        d_all, head_grad, table, table_momentum, schedule, slot_token, 1, 1, upper
+    )
     stack_grad = jnp.sum(stack_back.reshape(models, share, stack_part, model_width), axis=1)
     stack_momentum_new, stack_new = update(stack, stack_momentum, stack_grad, stack_rate)
     vector_momentum_new, vector_new = update(vectors, vector_momentum, vector_grad, vector_rate)

time: 883 us -> 814 us (0.922)
  waiting for transfers between devices: 153 us -> 115 us
  Pallas kernels: 461 us -> 439 us
    all_to_all x1, waiting for transfers between devices: 38.5 us -> 1.2 us  [body(): lax.all_to_all(stack_sum.reshape(members, stack_part, model_width), 'cli'...]
    pallas_call x2, Pallas kernels: 168 us -> 151 us  [spread(): pl.pallas_call(functools.partial(spread_kernel, groups, members, chain, p...]
    pallas_call x1 -> x2, Pallas kernels: 69.6 us -> 73.5 us  [finish_table(): pl.pallas_call(functools.partial(finish_kernel, first_tile), out_shape=(s...]
    unnamed x162 -> x110, local copies, waits for them, and re-layouts: 23 us -> 23.3 us
  transfers between devices with their start and end apart: 9 -> 9, of which waited for: 7 -> 7; matrix products, arithmetic and copies ran while one was open for 2% -> 2% of each run, Pallas kernels for 15% -> 17%
where the time goes in v5:
time: 814 us; the launch traced here: 805 us
  Pallas kernels  439 us (54%)
  waiting for transfers between devices  115 us (14%)
  matrix products  71.4 us (9%)
  local copies, waits for them, and re-layouts  61.3 us (8%)
  other arithmetic  39.8 us (5%)
  blocking collectives  32 us (4%)
  starting transfers between devices  27.6 us (3%)
  between operations  18.2 us (2%)
    pallas_call x2, Pallas kernels, spread(): pl.pallas_call(functools.partial(spread_kernel, groups, members, chain, p...  151 us
    pallas_call x1, Pallas kernels, spread_score(): pl.pallas_call(functools.partial(score_kernel, groups, members, share, pi...  127 us
    pallas_call x2, Pallas kernels, finish_table(): pl.pallas_call(functools.partial(finish_kernel, first_tile), out_shape=(s...  73.5 us
    pallas_call x1, Pallas kernels, head_back(): pl.pallas_call(back_kernel, out_shape=(jax.ShapeDtypeStruct((2 * steps, s...  69.2 us
    reduce_scatter x1, waiting for transfers between devices, body(): lax.psum_scatter(d_outs[:devices].reshape(devices * seq_len, model_width)...  58.8 us
    all_to_all x4, waiting for transfers between devices, share_all(): lax.all_to_all(jnp.broadcast_to(rows[None], (size,) + rows.shape), axes,...  30.9 us
    all_to_all x1, blocking collectives, body(): lax.all_to_all(d_group.reshape(members, seq_len, model_width), 'cli', 0,...  24.6 us
    unnamed x110, local copies, waits for them, and re-layouts  23.3 us
  transfers between devices with their start and end apart: 9, of which 7 were waited for; matrix products, arithmetic and copies ran while one was open for 2% of the time, Pallas kernels for 17%

profile of v5, /device:TPU:0, one launch (start us, length us, event | category | flops | bytes accessed | tf_op | source)
XLA Modules:
  0.0 804.6 jit_solution(1182055661432932499)
XLA Ops:
  8.7 11.5 %convert_element_type.245.table.table_ref = bf16[4,1600,768]{2,1,0:T(8,128)(2,1)} convert(f32[4,1600,768]{2,1,0:T(8,128)} %table_ref.3) | non-fusion elementwise | flops 4915200 | bytes 29491200 | tf_op jit(solution)/shard_map/convert_element_type | solution.py:948
  20.2 2.6 convert_element_type.242
  24.0 1.0 fusion.104
  25.6 7.3 all-to-all-start.1
  32.9 7.5 all-to-all-done.1
  42.9 2.6 fusion.142
  47.7 5.3 fusion.44
  53.0 1.6 pad_maximum_fusion.src
  54.7 91.7 %shard_map.185.pool_ref = bf16[32,400,768]{2,1,0:T(8,128)(2,1)} custom-call(bf16[4,400,768]{2,1,0:T(8,128)(2,1)} %pad_maximum_fusion.src), custom_call_target="tpu_custom_call" | custom-call | bytes 39321600 | tf_op jit(solution)/shard_map/pallas_call | solution.py:568
  147.8 18.5 %shard_map.186 = (bf16[9344,768]{1,0:T(8,128)(2,1)S(1)}, f32[512,768]{1,0:T(8,128)S(1)}) custom-call(s32[512,1]{1,0:T(8,128)S(1)} %fusion.78.at_ref, bf16[32,400,768]{2,1,0:T(8,128)(2,1)} %shard_map.185.pool_ref), custom_call_target="tpu_custom_call" | custom-call | flops 2818572288 | bytes 39321600 | tf_op jit(solution)/shard_map/pallas_call | solution.py:722
  166.3 5.3 copy-done
  172.5 1.5 add_convert_fusion.4
  174.1 2.4 convolution_convert_fusion.6
  176.5 2.1 add_convert_fusion.3
  178.9 1.1 reshape.785
  180.4 3.2 add_convert_fusion.2
  183.7 2.4 copy.316
  186.1 2.1 reshape.786
  192.5 1.0 slice-done.2
  193.6 1.3 slice-done.3
  195.2 0.9 fusion.144
  196.5 2.7 fusion.24
  199.3 4.1 fusion.145
  203.7 1.2 fusion.54.src
  204.9 126.7 %shard_map.187 = (bf16[32,512,768]{2,1,0:T(8,128)(2,1)}, f32[32,2,512]{2,1,0:T(2,128)}) custom-call(bf16[1,512,768]{2,1,0:T(8,128)(2,1)} %fusion.54.src, bf16[4,1600,768]{2,1,0:T(8,128)(2,1)} %get-tuple-element.350, s32[8,1,512]{2,1,0:T(1,128)} %bitcast.220), custom_call_target="tpu_custom_call" | custom-call | flops 40265318400 | bytes 50331648 | tf_op jit(solution)/shard_map/pallas_call | solution.py:635
  331.6 3.6 all-to-all-start.2
  337.8 5.9 all-to-all-done.2
  344.6 2.6 all-to-all-start.3
  350.5 5.1 all-to-all-done.3
  357.3 69.2 %shard_map.188 = (bf16[36,128,768]{2,1,0:T(8,128)(2,1)}, f32[4,1600,768]{2,1,0:T(8,128)}) custom-call(s32[18]{0:T(128)} %copy-done.36, s32[18]{0:T(128)} %get-tuple-element.248.fresh_ref, s32[18]{0:T(128)} %slice.170.first_ref, s32[18]{0:T(128)} %slice.171.second_ref, s32[36]{0:T(128)} %get-tuple-element.246.place_ref, bf16[128,128,768]{2,1,0:T(8,128)(2,1)} %bitcast.247, ...), custom_call_target="tpu_custom_call" | custom-call | flops 33973862400 | bytes 43646976 | tf_op jit(solution)/shard_map/pallas_call | solution.py:798
  426.6 6.1 slice.173
  432.7 58.8 %reduce-scatter.3.cloned.1.call-done = bf16[512,768]{1,0:T(8,128)(2,1)} async-done(((bf16[4096,768]{1,0:T(8,128)(2,1)}), bf16[512,768]{1,0:T(8,128)(2,1)}) %reduce-scatter.3.cloned.1.call-update) | async-done | bytes 786448 | tf_op jit(solution)/shard_map/reduce_scatter | solution.py:1102
  491.5 24.6 %all_to_all.60 = bf16[4,128,768]{2,1,0:T(8,128)(2,1)S(1)} all-to-all(bf16[4,128,768]{2,1,0:T(8,128)(2,1)} %bitcast.224), channel_id=1, replica_groups=mesh['grp'=8,'cli'=4] {'cli'}, dimensions={0} | all-to-all | bytes 1572864 | tf_op jit(solution)/shard_map/all_to_all | solution.py:1108
  517.2 3.5 all-to-all-start.5
  521.5 18.2 %all-to-all-done.5 = bf16[4,128,768]{2,1,0:T(8,128)(2,1)S(1)} async-done(((bf16[4,128,768]{2,1,0:T(8,128)(2,1)}), bf16[4,128,768]{2,1,0:T(8,128)(2,1)S(1)}, u32[]{:S(2)}, u32[]{:S(2)}) %all-to-all-start.5) | async-done | bytes 786464 | tf_op jit(solution)/shard_map/all_to_all | solution.py:236
  541.6 9.2 %convert_reduce_fusion = (f32[3072]{0:T(1024)S(1)}, bf16[512,3072]{1,0:T(8,128)(2,1)S(1)}) fusion(f32[512,3072]{1,0:T(8,128)} %copy-done.40, f32[3072]{0:T(1024)S(1)} %bitcast.237, bf16[512,768]{1,0:T(8,128)(2,1)S(1)} %get-tuple-element.204, bf16[9344,768]{1,0:T(8,128)(2,1)} %copy-done), kind=kOutput, calls=%fused_computation.32 | convolution fusion | flops 2452091904 | bytes 14966784 | tf_op jit(solution)/shard_map/dot_general | solution.py:36
  550.9 6.4 multiply_reduce_fusion.1
  558.2 2.9 convolution_convert_fusion.5
  561.1 2.3 copy.331
  563.4 2.6 reshape.797
  566.1 3.4 multiply_reduce_fusion
  569.4 1.0 multiply_convert_fusion.1
  571.7 1.2 fusion.43
  572.9 1.3 convert_reduce_fusion.3
  577.0 4.6 multiply_reduce_fusion.2
  581.6 3.8 fusion.17
  586.5 1.9 fusion.37
  588.8 5.1 fusion.16
  593.9 5.6 fusion.15
  599.6 1.2 fusion.135
  602.0 7.5 all_to_all.61
  609.4 3.6 all-to-all-start.6
  615.0 18.2 %all-to-all-done.6 = bf16[4,128,768]{2,1,0:T(8,128)(2,1)S(1)} async-done(((bf16[4,128,768]{2,1,0:T(8,128)(2,1)}), bf16[4,128,768]{2,1,0:T(8,128)(2,1)S(1)}, u32[]{:S(2)}, u32[]{:S(2)}) %all-to-all-start.6) | async-done | bytes 786464 | tf_op jit(solution)/shard_map/all_to_all | solution.py:1129
  633.9 2.6 all-to-all-start.9
  637.4 59.5 %shard_map.189.a_ref.b_ref = bf16[32,128,768]{2,1,0:T(8,128)(2,1)} custom-call(bf16[1,128,768]{2,1,0:T(8,128)(2,1)} %bitcast.222), custom_call_target="tpu_custom_call" | custom-call | bytes 12582912 | tf_op jit(solution)/shard_map/pallas_call | solution.py:568
  696.9 36.9 %shard_map.190 = (f32[4,1600,768]{2,1,0:T(8,128)}, f32[4,1600,768]{2,1,0:T(8,128)}, f32[4,1600,768]{2,1,0:T(8,128)}) custom-call(s32[18]{0:T(128)} %copy-done.36, s32[18]{0:T(128)} %get-tuple-element.248.fresh_ref, s32[18]{0:T(128)} %get-tuple-element.247.final_ref, s32[18]{0:T(128)} %slice.168.first_ref, s32[18]{0:T(128)} %slice.169.second_ref, ...), custom_call_target="tpu_custom_call" | custom-call | flops 5662310400 | bytes 58982400 | tf_op jit(solution)/shard_map/pallas_call | solution.py:868
  733.8 2.6 reshape.801
  736.4 4.3 all-to-all-start.7
  745.5 36.5 %shard_map.191 = (f32[4,1600,768]{2,1,0:T(8,128)}, f32[4,1600,768]{2,1,0:T(8,128)}, f32[4,1600,768]{2,1,0:T(8,128)}) custom-call(s32[18]{0:T(128)} %copy-done.36, s32[18]{0:T(128)} %get-tuple-element.248.fresh_ref, s32[18]{0:T(128)} %get-tuple-element.247.final_ref, ...), custom_call_target="tpu_custom_call", output_to_operand_aliasing={{0}: (11, {}), {1}: (12, {}), {2}: (13, {})} | custom-call | flops 5662310400 | bytes 58982400 | tf_op jit(solution)/shard_map/pallas_call | solution.py:868
  782.0 1.2 all-to-all-done.7
  783.2 4.8 copy_subtract_fusion
  788.1 3.2 copy.349
  791.3 3.2 copy.350
  794.5 2.5 copy.348
  (266 shorter events, 41.9 us)
Async XLA Ops:
  22.8 1.1 copy-start.37
  22.8 1.1 copy-start.38
  22.8 1.1 copy-start.39
  24.9 147.6 %copy-start.26 = (f32[768]{0:T(1024)}, f32[768]{0:T(1024)S(1)}, u32[]{:S(2)}) copy-start(f32[768]{0:T(1024)S(1)} %get-tuple-element.177) | copy-start | bytes 9220
  25.6 14.8 %all-to-all-start.1 = ((s32[32,1,385]{2,1,0:T(1,128)}), s32[32,1,385]{2,1,0:T(1,128)S(1)}, u32[]{:S(2)}, u32[]{:S(2)}) async-start(s32[32,1,385]{2,1,0:T(1,128)} %broadcast_in_dim.263), calls=%async_computation.1 | async-start | bytes 131072 | tf_op jit(solution)/shard_map/all_to_all | solution.py:236
  42.3 3.2 copy-start.34
  166.3 5.4 copy-start
  171.7 0.8 copy-start.3
  171.9 2.1 copy-start.1
  172.1 1.9 copy-start.28
  172.5 3.9 copy-start.32
  172.5 3.9 copy-start.30
  174.1 4.5 copy-start.17
  178.8 1.6 copy-start.18
  180.4 7.8 copy-start.5
  183.7 8.8 %slice-start = ((s8[14352384]{0:T(1024)(128)(4,1)}), s8[1769472]{0:T(1024)(128)(4,1)S(1)}, s32[]{:S(2)}) async-start(s8[14352384]{0:T(1024)(128)(4,1)} %bitcast.210), calls=%async_computation.15 | async-start | bytes 3538944
  188.2 0.9 copy-start.7
  188.2 4.3 slice-start.1
  189.2 1.7 copy-start.20
  189.3 4.3 slice-start.2
  190.2 1.7 copy-start.13
  190.9 3.9 slice-start.3
  190.9 4.3 copy-start.16
  192.5 3.7 copy-start.11
  196.2 3.1 copy-start.9
  199.2 4.1 copy-start.40
  204.9 131.6 %copy-start.15 = (s32[32,128]{1,0:T(8,128)S(1)}, s32[32,128]{1,0:T(8,128)}, u32[]{:S(2)}) copy-start(s32[32,128]{1,0:T(8,128)} %get-tuple-element.232) | copy-start | bytes 49156
  331.6 12.1 %all-to-all-start.2 = ((f32[32,2,512]{2,1,0:T(2,128)}), f32[32,2,512]{2,1,0:T(2,128)S(1)}, u32[]{:S(2)}, u32[]{:S(2)}) async-start(f32[32,2,512]{2,1,0:T(2,128)} %get-tuple-element.70), calls=%async_computation.2 | async-start | bytes 262144 | tf_op jit(solution)/shard_map/all_to_all | solution.py:1036
  335.5 21.9 %copy-start.36 = (s32[18]{0:T(128)}, s32[18]{0:T(128)S(1)}, u32[]{:S(2)}) copy-start(s32[18]{0:T(128)S(1)} %broadcast_add_fusion.model_ref) | copy-start | bytes 220
  344.6 11.0 %all-to-all-start.3 = ((f32[32,2,512]{2,1,0:T(2,128)}), f32[32,2,512]{2,1,0:T(2,128)S(1)}, u32[]{:S(2)}, u32[]{:S(2)}) async-start(f32[32,2,512]{2,1,0:T(2,128)} %broadcast_in_dim.278), calls=%async_computation.3 | async-start | bytes 262144 | tf_op jit(solution)/shard_map/all_to_all | solution.py:236
  347.2 144.3 %reduce-scatter.3.cloned.1.call-start = ((), (), s32[]{:S(2)}) async-start(), calls=%async_computation.12 | async-start | bytes 7077888 | tf_op jit(solution)/shard_map/reduce_scatter | solution.py:1102
  517.2 22.6 %all-to-all-start.5 = ((bf16[4,128,768]{2,1,0:T(8,128)(2,1)}), bf16[4,128,768]{2,1,0:T(8,128)(2,1)S(1)}, u32[]{:S(2)}, u32[]{:S(2)}) async-start(bf16[4,128,768]{2,1,0:T(8,128)(2,1)} %broadcast_in_dim.287), calls=%async_computation.6 | async-start | bytes 1572864 | tf_op jit(solution)/shard_map/all_to_all | solution.py:236
  520.7 213.1 %reduce-scatter.5.cloned.1.call-start = ((), (), s32[]{:S(2)}) async-start(), calls=%async_computation.13 | async-start | bytes 16146432 | tf_op jit(solution)/shard_map/reduce_scatter | solution.py:1135
  541.6 9.3 %copy-start.22 = (bf16[512,768]{1,0:T(8,128)(2,1)}, bf16[512,768]{1,0:T(8,128)(2,1)S(1)}, u32[]{:S(2)}) copy-start(bf16[512,768]{1,0:T(8,128)(2,1)S(1)} %get-tuple-element.204) | copy-start | bytes 2359300
  541.6 9.3 %copy-start.10 = (f32[512,768]{1,0:T(8,128)S(1)}, f32[512,768]{1,0:T(8,128)}, u32[]{:S(2)}) copy-start(f32[512,768]{1,0:T(8,128)} %copy-done.9) | copy-start | bytes 4718596
  550.8 6.4 copy-start.41
  566.1 3.4 copy-start.14
  569.4 1.1 copy-start.6
  570.6 1.1 copy-start.8
  571.7 1.2 copy-start.21
  575.5 1.4 copy-start.2
  575.6 1.5 copy-start.4
  575.6 1.5 copy-start.27
  575.6 1.4 copy-start.29
  575.6 1.4 copy-start.31
  577.0 4.6 copy-start.19
  581.6 3.8 copy-start.33
  585.4 1.1 copy-start.12
  585.4 8.5 %slice-start.4 = ((s8[6291456]{0:T(1024)(128)(4,1)}), s8[4194304]{0:T(1024)(128)(4,1)S(1)}, s32[]{:S(2)}) async-start(s8[6291456]{0:T(1024)(128)(4,1)} %bitcast.249), calls=%async_computation.19 | async-start | bytes 8388608
  586.2 2.6 copy-start.42
  588.8 5.1 copy-start.23
  588.8 5.1 slice-start.5
  609.4 23.7 %all-to-all-start.6 = ((bf16[4,128,768]{2,1,0:T(8,128)(2,1)}), bf16[4,128,768]{2,1,0:T(8,128)(2,1)S(1)}, u32[]{:S(2)}, u32[]{:S(2)}) async-start(bf16[4,128,768]{2,1,0:T(8,128)(2,1)} %bitcast.34), calls=%async_computation.7 | async-start | bytes 1572864 | tf_op jit(solution)/shard_map/all_to_all | solution.py:1129
  633.9 102.4 %all-to-all-start.9 = ((f32[32,1,1344]{2,1,0:T(1,128)}), f32[32,1,1344]{2,1,0:T(1,128)S(1)}, u32[]{:S(2)}, u32[]{:S(2)}) async-start(f32[32,1,1344]{2,1,0:T(1,128)} %broadcast_in_dim.295), calls=%async_computation.11 | async-start | bytes 360448 | tf_op jit(solution)/shard_map/all_to_all | solution.py:236
  736.4 4.7 copy-start.35
  736.4 7.5 copy-start.24
  736.4 7.5 copy-start.25
  736.4 46.9 %all-to-all-start.7 = ((bf16[4,292,768]{2,1,0:T(8,128)(2,1)}), bf16[4,292,768]{2,1,0:T(8,128)(2,1)S(1)}, u32[]{:S(2)}, u32[]{:S(2)}) async-start(bf16[4,292,768]{2,1,0:T(8,128)(2,1)} %reshape.801), calls=%async_computation.9 | async-start | bytes 3637248 | tf_op jit(solution)/shard_map/all_to_all | solution.py:1152
Sparse Core Ops, SparseCore 1:
  432.8 58.6 reduce-scatter.2
  601.6 122.7 reduce-scatter.4

commit v6 on v5

--- a/solution.py
+++ b/solution.py
@@ -694,6 +694,140 @@
     )(outs_all, table_low, target_blocks)
 
 
+def collect_kernel(groups, members, source, out, work, from_core, from_x, from_y, then_y, then_x, from_z, *sems):
+    (load_sem, core_send, core_recv, x_send, x_recv, y_send, y_recv, yy_send, yy_recv, xx_send, xx_recv, z_send,
+     z_recv, g_send, g_recv) = sems
+    place = Place(groups, members)
+    greet(place)
+    xs, ys = place.xs, place.ys
+    half = members // 2
+    upper, lower = pl.ds(0, half), pl.ds(half, half)
+    z = place.cli
+    order = sorted(
+        ((jx, jy) for jx in range(xs) for jy in range(ys)), key=lambda spot: -(spot[0] > 0) - (spot[1] > 0)
+    )
+    started = []
+
+    def send(source_ref, target_ref, send_sem, recv_sem, device):
+        copy = pltpu.make_async_remote_copy(
+            src_ref=source_ref, dst_ref=target_ref, send_sem=send_sem, recv_sem=recv_sem, device_id=device,
+            device_id_type=MESH,
+        )
+        copy.start()
+        started.append(copy)
+
+    def arrival(target_ref, send_sem, recv_sem, device):
+        pltpu.make_async_remote_copy(
+            src_ref=target_ref, dst_ref=target_ref, send_sem=send_sem, recv_sem=recv_sem, device_id=device,
+            device_id_type=MESH,
+        ).wait_recv()
+
+    def spot_of(jx, jy):
+        return jy * xs + jx
+
+    def add(ref, others):
+        total = ref[...].astype(jnp.float32)
+        for other in others:
+            total = total + other[...].astype(jnp.float32)
+        ref[...] = total.astype(ref.dtype)
+
+    for jx, jy in order:
+        k = spot_of(jx, jy)
+        send(
+            source.at[pl.ds(place.group(jx, jy, 1) * members, members)], from_core.at[k], core_send.at[k],
+            core_recv.at[k], place.peer(jc=1),
+        )
+    loads = {}
+    for jx, jy in order:
+        k = spot_of(jx, jy)
+        loads[k] = pltpu.make_async_copy(
+            source.at[pl.ds(place.group(jx, jy, 0) * members, members)], work.at[k], load_sem.at[k]
+        )
+        loads[k].start()
+    for jx, jy in order:
+        k = spot_of(jx, jy)
+        loads[k].wait()
+        arrival(from_core.at[k], core_send.at[k], core_recv.at[k], place.peer(jc=1))
+        add(work.at[k], [from_core.at[k]])
+        if jx:
+            send(work.at[k, upper], from_x.at[jx, jy], x_send.at[jx, jy], x_recv.at[jx, jy], place.peer(jx=jx))
+        if jy:
+            send(work.at[k, lower], from_y.at[jx, jy], y_send.at[jx, jy], y_recv.at[jx, jy], place.peer(jy=jy))
+    for jy in reversed(range(ys)):
+        k = spot_of(0, jy)
+        for jx in range(1, xs):
+            arrival(from_x.at[jx, jy], x_send.at[jx, jy], x_recv.at[jx, jy], place.peer(jx=jx))
+        add(work.at[k, upper], [from_x.at[jx, jy] for jx in range(1, xs)])
+        if jy:
+            send(work.at[k, upper], then_y.at[jy], yy_send.at[jy], yy_recv.at[jy], place.peer(jy=jy))
+    for jx in reversed(range(xs)):
+        k = spot_of(jx, 0)
+        for jy in range(1, ys):
+            arrival(from_y.at[jx, jy], y_send.at[jx, jy], y_recv.at[jx, jy], place.peer(jy=jy))
+        add(work.at[k, lower], [from_y.at[jx, jy] for jy in range(1, ys)])
+        if jx:
+            send(work.at[k, lower], then_x.at[jx], xx_send.at[jx], xx_recv.at[jx], place.peer(jx=jx))
+    own = work.at[0]
+    for jy in range(1, ys):
+        arrival(then_y.at[jy], yy_send.at[jy], yy_recv.at[jy], place.peer(jy=jy))
+    add(own.at[upper], [then_y.at[jy] for jy in range(1, ys)])
+    for jx in range(1, xs):
+        arrival(then_x.at[jx], xx_send.at[jx], xx_recv.at[jx], place.peer(jx=jx))
+    add(own.at[lower], [then_x.at[jx] for jx in range(1, xs)])
+
+    for j in range(1, members):
+        level = lax.rem(z + j, members)
+        send(own.at[level], from_z.at[j], z_send.at[j], z_recv.at[j], place.level(level))
+    total = work[0, z].astype(jnp.float32)
+    for j in range(1, members):
+        arrival(from_z.at[j], z_send.at[j], z_recv.at[j], place.level(lax.rem(z + members - j, members)))
+        total = total + from_z[j].astype(jnp.float32)
+    out[z] = total.astype(out.dtype)
+    for j in range(1, members):
+        send(out.at[z], out.at[z], g_send.at[j], g_recv.at[j], place.level(lax.rem(z + j, members)))
+    for j in range(1, members):
+        level = lax.rem(z + members - j, members)
+        arrival(out.at[level], g_send.at[j], g_recv.at[j], place.level(level))
+    for copy in started:
+        copy.wait_send()
+
+
+def collect(parts, groups, members, collective_id):
+    _, seq_len, width = parts.shape
+    xs, ys, half = groups // 4, 2, members // 2
+    dma = pltpu.SemaphoreType.DMA
+
+    def held(*shape):
+        return pltpu.VMEM(shape + (seq_len, width), parts.dtype)
+
+    return pl.pallas_call(
+        functools.partial(collect_kernel, groups, members),
+        out_shape=jax.ShapeDtypeStruct((members, seq_len, width), parts.dtype),
+        in_specs=[pl.BlockSpec(memory_space=pl.ANY)],
+        out_specs=pl.BlockSpec(memory_space=pltpu.VMEM),
+        scratch_shapes=[
+            held(xs * ys, members),
+            held(xs * ys, members),
+            held(xs, ys, half),
+            held(xs, ys, half),
+            held(ys, half),
+            held(xs, half),
+            held(members),
+        ]
+        + [dma((xs * ys,))] * 3
+        + [dma((xs, ys))] * 4
+        + [dma((ys,))] * 2
+        + [dma((xs,))] * 2
+        + [dma((members,))] * 4,
+        compiler_params=pltpu.CompilerParams(
+            collective_id=collective_id, has_side_effects=True, vmem_limit_bytes=56 * MIB
+        ),
+        cost_estimate=pl.CostEstimate(
+            flops=0, bytes_accessed=4 * groups * members * seq_len * width, transcendentals=0
+        ),
+    )(parts)
+
+
 def unpack_kernel(start, part, at_ref, pool_ref, weights_ref, rows_ref):
     step = pl.program_id(0)
     owners, slab, width = pool_ref.shape
@@ -830,66 +964,51 @@
 
 
 def finish_kernel(
-    first_tile, model_ref, fresh_ref, final_ref, first_ref, second_ref, a_ref, b_ref, ids_ref, head_ref, table_ref,
-    momentum_ref, *rest,
+    first_model, start_ref, first_ref, second_ref, d_ref, ids_ref, head_ref, table_ref, momentum_ref, *rest
 ):
     grad_ref, momentum_new_ref, table_new_ref = rest[-3:]
-    tile = pl.program_id(0) + first_tile
-    step = pl.program_id(1)
+    model = pl.program_id(0) + first_model
     tile_rows = grad_ref.shape[1]
-    rows = lax.broadcasted_iota(jnp.int32, (tile_rows, ids_ref.shape[2]), 0) + tile * tile_rows
-    hits = (rows == ids_ref[0]).astype(jnp.float32).astype(jnp.bfloat16)
-    outs = jnp.concatenate([a_ref[0], b_ref[0]], axis=0)
-    gain = product(hits, outs)
-
-    @pl.when(fresh_ref[step] == 1)
-    def start():
-        grad_ref[0] = head_ref[0] + gain
-
-    @pl.when(fresh_ref[step] == 0)
-    def more():
-        grad_ref[0] += gain
-
-    @pl.when(final_ref[step] == 1)
-    def close():
-        renewed, fresh_table = update(table_ref[0], momentum_ref[0], grad_ref[0], table_rate)
-        momentum_new_ref[0] = renewed
-        table_new_ref[0] = fresh_table
-
-
-def finish_table(d_inputs, head_grad, table, momentum, schedule, ids, first_tile, tiles, earlier):
-    model_of, fresh, final, first, second = schedule
-    steps = model_of.shape[0]
+    tokens = ids_ref.shape[2]
+    rows = lax.broadcasted_iota(jnp.int32, (tile_rows, tokens), 0) + pl.program_id(1) * tile_rows
+    grad_ref[0] = head_ref[0]
+
+    def pair(step, carry):
+        hits = (rows == ids_ref[step]).astype(jnp.float32).astype(jnp.bfloat16)
+        outs = jnp.concatenate([d_ref[first_ref[step]], d_ref[second_ref[step]]], axis=0)
+        grad_ref[0] += product(hits, outs)
+        return carry
+
+    lax.fori_loop(start_ref[model], start_ref[model + 1], pair, 0)
+    renewed, fresh_table = update(table_ref[0], momentum_ref[0], grad_ref[0], table_rate)
+    momentum_new_ref[0] = renewed
+    table_new_ref[0] = fresh_table
+
+
+def finish_table(d_inputs, head_grad, table, momentum, schedule, ids, first_model, count, earlier):
     models, part_rows, width = table.shape
-    seq_len = d_inputs.shape[1]
-    tile_rows = part_rows // 2
+    tile_rows = tile_of(part_rows)
     state = jax.ShapeDtypeStruct(table.shape, jnp.float32)
-    piece = pl.BlockSpec((1, tile_rows, width), lambda t, s, m, f, l, a, b: (m[s], t + first_tile, 0))
+    piece = pl.BlockSpec((1, tile_rows, width), lambda m, t, *_: (m + first_model, t, 0))
+    whole = pl.BlockSpec(memory_space=pltpu.VMEM)
     return pl.pallas_call(
-        functools.partial(finish_kernel, first_tile),
+        functools.partial(finish_kernel, first_model),
         out_shape=(state, state, state),
         grid_spec=pltpu.PrefetchScalarGridSpec(
-            num_scalar_prefetch=5,
-            grid=(tiles, steps),
-            in_specs=[
-                pl.BlockSpec((1, seq_len, width), lambda t, s, m, f, l, a, b: (a[s], 0, 0)),
-                pl.BlockSpec((1, seq_len, width), lambda t, s, m, f, l, a, b: (b[s], 0, 0)),
-                pl.BlockSpec((1, 1, 2 * seq_len), lambda t, s, m, f, l, a, b: (s, 0, 0)),
-                piece,
-                piece,
-                piece,
-            ]
+            num_scalar_prefetch=3,
+            grid=(count, part_rows // tile_rows),
+            in_specs=[whole, whole, piece, piece, piece]
             + [pl.BlockSpec(memory_space=pl.ANY)] * len(earlier),
             out_specs=(piece, piece, piece),
         ),
-        input_output_aliases={11 + i: i for i in range(len(earlier))},
+        input_output_aliases={8 + i: i for i in range(len(earlier))},
         compiler_params=pltpu.CompilerParams(vmem_limit_bytes=56 * MIB),
         cost_estimate=pl.CostEstimate(
-            flops=4 * steps * seq_len * tiles * tile_rows * width,
-            bytes_accessed=24 * models * tiles * tile_rows * width,
+            flops=2 * d_inputs.size * part_rows * count // models,
+            bytes_accessed=24 * count * part_rows * width,
             transcendentals=0,
         ),
-    )(*schedule, d_inputs, d_inputs, ids, head_grad, table, momentum, *earlier)
+    )(*schedule, d_inputs, ids, head_grad, table, momentum, *earlier)
 
 
 def body(
@@ -1072,9 +1191,6 @@
     fresh = jnp.concatenate(
         [jnp.ones((1,), jnp.int32), (model_of[1:] != model_of[:-1]).astype(jnp.int32)]
     )
-    final = jnp.concatenate(
-        [(model_of[1:] != model_of[:-1]).astype(jnp.int32), jnp.ones((1,), jnp.int32)]
-    )
     within = client_at % members
     piece_at = (
         (client_at // members * members + jnp.repeat(model_of, 2) * share + within // local) * local
@@ -1099,17 +1215,7 @@
         slot_info,
         slot_target.reshape(steps, 1, 2 * seq_len),
     )
-    d_group = lax.psum_scatter(
-        d_outs[:devices].reshape(devices * seq_len, model_width),
-        "grp",
-        scatter_dimension=0,
-        tiled=True,
-    )
-    d_level = lax.all_to_all(
-        d_group.reshape(members, seq_len, model_width), "cli", 0, 0, tiled=True
-    )
-    d_level = jnp.sum(d_level.astype(jnp.float32), axis=0).astype(jnp.bfloat16)
-    d_group = share_all(d_level, "cli", members)
+    d_group = collect(d_outs, groups, members, 4)
     d_mine = lax.dynamic_slice(
         d_group, (part_own * local, 0, 0), (local, seq_len, model_width)
     ).astype(jnp.float32)
@@ -1130,32 +1236,43 @@
         d_wide.reshape(members, seq_len, model_width), "cli", 0, 0, tiled=True
     )
     d_client = jnp.sum(d_turned.astype(jnp.float32), axis=0, keepdims=True).astype(jnp.bfloat16)
-    d_all = spread(d_client, groups, members, 3, True, 2)
-
-    stack_sum = lax.psum_scatter(stack_rows, "grp", scatter_dimension=0, tiled=True)
     vector_piece = vector_rows.size // groups
     vector_part = jnp.sum(
         lax.all_to_all(vector_rows.reshape(groups, vector_piece), "grp", 0, 0, tiled=True), axis=0
     )
-    vector_grad = jnp.sum(
-        share_all(vector_part, both, devices).reshape(groups, models, share, vector_piece), axis=2
-    )
+    vector_parts = share_all(vector_part, both, devices)
+    d_client, vector_parts = lax.optimization_barrier((d_client, vector_parts))
+    d_all = spread(d_client, groups, members, 3, True, 2)
+
+    middle = model_width // 2
+    stack_left = lax.psum_scatter(stack_rows[:, :middle], "grp", scatter_dimension=0, tiled=True)
+    stack_right = lax.psum_scatter(stack_rows[:, middle:], "grp", scatter_dimension=0, tiled=True)
+    vector_grad = jnp.sum(vector_parts.reshape(groups, models, share, vector_piece), axis=2)
     vector_grad = vector_grad.transpose(1, 0, 2).reshape(vectors.shape)
 
     token_local = tokens - device_index * block_rows
     token_local = jnp.where((token_local >= 0) & (token_local < block_rows), token_local, -1)
     slot_token = jnp.where(filled[:, None], jnp.take(token_local, client_at, axis=0), -1)
-    schedule = (model_of, fresh, final, client_at[0::2], client_at[1::2])
+    pair_start = jnp.concatenate([offsets, jnp.sum(padded)[None]]) / 2.0
+    schedule = (pair_start.astype(jnp.int32), client_at[0::2], client_at[1::2])
     slot_token = slot_token.reshape(steps, 1, 2 * seq_len)
-    upper = finish_table(d_all, head_grad, table, table_momentum, schedule, slot_token, 0, 1, ())
-    stack_sum, upper = lax.optimization_barrier((stack_sum, upper))
-    stack_back = lax.all_to_all(
-        stack_sum.reshape(members, stack_part, model_width), "cli", 0, 0, tiled=True
-    ).astype(jnp.float32)
-    table_grad, table_momentum_new, table_new = finish_table(
-        d_all, head_grad, table, table_momentum, schedule, slot_token, 1, 1, upper
-    )
-    stack_grad = jnp.sum(stack_back.reshape(models, share, stack_part, model_width), axis=1)
+    lead = models // 2
+
+    def to_owner(rows):
+        back = lax.all_to_all(
+            rows.reshape(members, stack_part, rows.shape[1]), "cli", 0, 0, tiled=True
+        ).astype(jnp.float32)
+        return jnp.sum(back.reshape(models, share, stack_part, rows.shape[1]), axis=1)
+
+    states = finish_table(d_all, head_grad, table, table_momentum, schedule, slot_token, 0, lead, ())
+    stack_left, states = lax.optimization_barrier((stack_left, states))
+    grad_left = to_owner(stack_left)
+    states = finish_table(
+        d_all, head_grad, table, table_momentum, schedule, slot_token, lead, models - lead, states
+    )
+    stack_right, states, grad_left = lax.optimization_barrier((stack_right, states, grad_left))
+    table_grad, table_momentum_new, table_new = states
+    stack_grad = jnp.concatenate([grad_left, to_owner(stack_right)], axis=2)
     stack_momentum_new, stack_new = update(stack, stack_momentum, stack_grad, stack_rate)
     vector_momentum_new, vector_new = update(vectors, vector_momentum, vector_grad, vector_rate)
     return (

time: 814 us -> 793 us (0.974)
  waiting for transfers between devices: 115 us -> 53.3 us
  Pallas kernels: 439 us -> 478 us
  local copies, waits for them, and re-layouts: 61.3 us -> 73.1 us
  blocking collectives: 32 us -> 23.3 us
    reduce_scatter x2, waiting for transfers between devices: 58.8 us -> 0.03 us  [the longest x1 0.03 us: body(): lax.psum_scatter(stack_rows[:, middle:], 'grp', scatter_dimension=0, tile...]
    pallas_call x2 -> x3, Pallas kernels: 73.5 us -> 127 us  [the longest x1 66.7 us: collect(): pl.pallas_call(functools.partial(collect_kernel, groups, members), out_sh...]
    all_to_all x4 -> x2, waiting for transfers between devices: 30.9 us -> 12.5 us  [share_all(): lax.all_to_all(jnp.broadcast_to(rows[None], (size,) + rows.shape), axes,...]
    all_to_all x1 -> x2, waiting for transfers between devices: 1.2 us -> 17.4 us  [to_owner(): lax.all_to_all(rows.reshape(members, stack_part, rows.shape[1]), 'cli', 0...]
    pallas_call x2, Pallas kernels: 151 us -> 136 us  [spread(): pl.pallas_call(functools.partial(spread_kernel, groups, members, chain, p...]
    all_to_all x1, blocking collectives: 24.6 us -> 16 us  [share_all(): lax.all_to_all(jnp.broadcast_to(rows[None], (size,) + rows.shape), axes,...]
    unnamed x110 -> x125, local copies, waits for them, and re-layouts: 23.3 us -> 31.2 us
  transfers between devices with their start and end apart: 9 -> 8, of which waited for: 7 -> 5; matrix products, arithmetic and copies ran while one was open for 2% -> 2% of each run, Pallas kernels for 17% -> 13%
where the time goes in v6:
time: 793 us; the launch traced here: 784 us
  Pallas kernels  478 us (60%)
  local copies, waits for them, and re-layouts  73.1 us (9%)
  matrix products  64.7 us (8%)
  waiting for transfers between devices  53.3 us (7%)
  other arithmetic  46.8 us (6%)
  starting transfers between devices  26.6 us (3%)
  blocking collectives  23.3 us (3%)
  between operations  18.4 us (2%)
    pallas_call x2, Pallas kernels, spread(): pl.pallas_call(functools.partial(spread_kernel, groups, members, chain, p...  136 us
    pallas_call x1, Pallas kernels, spread_score(): pl.pallas_call(functools.partial(score_kernel, groups, members, share, pi...  127 us
    pallas_call x1, Pallas kernels, head_back(): pl.pallas_call(back_kernel, out_shape=(jax.ShapeDtypeStruct((2 * steps, s...  69.2 us
    pallas_call x1, Pallas kernels, collect(): pl.pallas_call(functools.partial(collect_kernel, groups, members), out_sh...  66.7 us
    pallas_call x2, Pallas kernels, finish_table(): pl.pallas_call(functools.partial(finish_kernel, first_model), out_shape=(...  60.5 us
    unnamed x125, local copies, waits for them, and re-layouts  31.2 us
    dot_general x6, matrix products, project(): lax.dot_general(inputs, matrix, (((1,), (1,)), ((), ())), preferred_eleme...  19.9 us
    dot_general x6, matrix products, product(): return jnp.dot(inputs, matrix, preferred_element_type=jnp.float32)  18.9 us
  transfers between devices with their start and end apart: 8, of which 5 were waited for; matrix products, arithmetic and copies ran while one was open for 2% of the time, Pallas kernels for 13%

profile of v6, /device:TPU:0, one launch (start us, length us, event | category | flops | bytes accessed | tf_op | source)
XLA Modules:
  0.0 784.1 jit_solution(4542904669451158420)
XLA Ops:
  8.7 11.5 %convert_element_type.255.table.table_ref = bf16[4,1600,768]{2,1,0:T(8,128)(2,1)} convert(f32[4,1600,768]{2,1,0:T(8,128)} %table_ref.3) | non-fusion elementwise | flops 4915200 | bytes 29491200 | tf_op jit(solution)/shard_map/convert_element_type | solution.py:1067
  20.2 2.6 convert_element_type.252
  25.6 7.3 all-to-all-start.1
  32.9 7.5 all-to-all-done.1
  42.9 2.6 fusion.145
  47.7 5.3 fusion.44
  53.0 1.6 pad_maximum_fusion.1.src
  54.7 91.7 %shard_map.185.pool_ref = bf16[32,400,768]{2,1,0:T(8,128)(2,1)} custom-call(bf16[4,400,768]{2,1,0:T(8,128)(2,1)} %pad_maximum_fusion.1.src), custom_call_target="tpu_custom_call" | custom-call | bytes 39321600 | tf_op jit(solution)/shard_map/pallas_call | solution.py:568
  147.8 18.5 %shard_map.186 = (bf16[9344,768]{1,0:T(8,128)(2,1)S(1)}, f32[512,768]{1,0:T(8,128)S(1)}) custom-call(s32[512,1]{1,0:T(8,128)S(1)} %fusion.78.at_ref, bf16[32,400,768]{2,1,0:T(8,128)(2,1)} %shard_map.185.pool_ref), custom_call_target="tpu_custom_call" | custom-call | flops 2818572288 | bytes 39321600 | tf_op jit(solution)/shard_map/pallas_call | solution.py:856
  166.3 5.3 copy-done
  172.5 1.5 add_convert_fusion.4
  174.1 2.4 convolution_convert_fusion.6
  176.5 2.1 add_convert_fusion.3
  178.9 1.1 reshape.777
  180.4 3.2 add_convert_fusion.2
  183.7 2.4 copy.317
  186.1 2.1 reshape.778
  192.5 1.0 slice-done.2
  193.6 1.3 slice-done.3
  196.5 2.7 fusion.24
  199.3 4.1 fusion.148
  203.7 1.2 fusion.54.src
  204.9 126.7 %shard_map.187 = (bf16[32,512,768]{2,1,0:T(8,128)(2,1)}, f32[32,2,512]{2,1,0:T(2,128)}) custom-call(bf16[1,512,768]{2,1,0:T(8,128)(2,1)} %fusion.54.src, bf16[4,1600,768]{2,1,0:T(8,128)(2,1)} %get-tuple-element.367, s32[8,1,512]{2,1,0:T(1,128)} %bitcast.221), custom_call_target="tpu_custom_call" | custom-call | flops 40265318400 | bytes 50331648 | tf_op jit(solution)/shard_map/pallas_call | solution.py:635
  331.6 3.6 all-to-all-start.2
  337.8 5.9 all-to-all-done.2
  344.6 2.6 all-to-all-start.3
  350.5 5.1 all-to-all-done.3
  357.9 69.2 %shard_map.188 = (bf16[36,128,768]{2,1,0:T(8,128)(2,1)}, f32[4,1600,768]{2,1,0:T(8,128)}) custom-call(s32[18]{0:T(128)} %copy-done.41, s32[18]{0:T(128)} %add_convert_fusion.6.fresh_ref, s32[18]{0:T(128)} %slice.169.first_ref, s32[18]{0:T(128)} %slice.170.second_ref, s32[36]{0:T(128)} %get-tuple-element.264.place_ref, bf16[128,128,768]{2,1,0:T(8,128)(2,1)} %bitcast.248, ...), custom_call_target="tpu_custom_call" | custom-call | flops 33973862400 | bytes 43646976 | tf_op jit(solution)/shard_map/pallas_call | solution.py:932
  427.2 66.7 %shard_map.189 = bf16[4,128,768]{2,1,0:T(8,128)(2,1)} custom-call(bf16[36,128,768]{2,1,0:T(8,128)(2,1)} %get-tuple-element.79.source), custom_call_target="tpu_custom_call" | custom-call | bytes 12582912 | tf_op jit(solution)/shard_map/pallas_call | solution.py:803
  493.9 1.4 fusion.136
  497.5 8.5 %convert_reduce_fusion = (f32[3072]{0:T(1024)S(1)}, bf16[512,3072]{1,0:T(8,128)(2,1)S(1)}) fusion(f32[512,3072]{1,0:T(8,128)S(1)} %bitcast.251, f32[3072]{0:T(1024)S(1)} %bitcast.238, bf16[512,768]{1,0:T(8,128)(2,1)S(1)} %get-tuple-element.218, bf16[9344,768]{1,0:T(8,128)(2,1)} %copy-done), kind=kOutput, calls=%fused_computation.32 | convolution fusion | flops 2452091904 | bytes 14966784 | tf_op jit(solution)/shard_map/dot_general | solution.py:36
  506.1 6.3 multiply_reduce_fusion.1
  513.3 2.9 convolution_convert_fusion.5
  516.3 2.3 copy.332
  518.6 2.4 reshape.787
  521.0 3.3 multiply_reduce_fusion
  526.6 1.2 fusion.43
  527.8 1.3 convert_reduce_fusion.3
  531.6 2.0 fusion.17
  533.7 4.6 multiply_reduce_fusion.2
  539.2 1.0 copy-done.47
  540.3 3.4 fusion.16
  543.8 4.1 fusion.15
  548.7 4.5 copy-done.3
  553.2 1.2 fusion.137
  555.2 10.4 %fusion.143 = (bf16[9344,384]{1,0:T(8,128)(2,1)}, bf16[9344,384]{1,0:T(8,128)(2,1)}) fusion(bf16[9344,768]{1,0:T(8,128)(2,1)} %convert_dynamic-update-slice_fusion), kind=kLoop, calls=%fused_computation.337 | loop fusion | bytes 28704768 | tf_op jit(solution)/shard_map/slice | solution.py:1248
  566.7 7.3 all_to_all.58
  574.1 16.0 %all_to_all.59 = f32[32,1,1344]{2,1,0:T(1,128)S(1)} all-to-all(f32[32,1,1344]{2,1,0:T(1,128)S(1)} %broadcast_in_dim.292), channel_id=1, replica_groups=mesh['grp'=8,'cli'=4] {'grp','cli'}, dimensions={0} | all-to-all | bytes 344064 | tf_op jit(solution)/shard_map/all_to_all | solution.py:236
  590.1 3.5 all-to-all-start.4
  595.5 1.1 fusion.126.start_ref
  596.6 16.9 %all-to-all-done.4 = bf16[4,128,768]{2,1,0:T(8,128)(2,1)S(1)} async-done(((bf16[4,128,768]{2,1,0:T(8,128)(2,1)}), bf16[4,128,768]{2,1,0:T(8,128)(2,1)S(1)}, u32[]{:S(2)}, u32[]{:S(2)}) %all-to-all-start.4) | async-done | bytes 786464 | tf_op jit(solution)/shard_map/all_to_all | solution.py:1235
  614.4 44.3 %shard_map.190.d_ref = bf16[32,128,768]{2,1,0:T(8,128)(2,1)} custom-call(bf16[1,128,768]{2,1,0:T(8,128)(2,1)} %bitcast.223), custom_call_target="tpu_custom_call" | custom-call | bytes 12582912 | tf_op jit(solution)/shard_map/pallas_call | solution.py:568
  658.7 30.5 %shard_map.191 = (f32[4,1600,768]{2,1,0:T(8,128)}, f32[4,1600,768]{2,1,0:T(8,128)}, f32[4,1600,768]{2,1,0:T(8,128)}) custom-call(s32[5]{0:T(128)} %fusion.126.start_ref, s32[18]{0:T(128)} %slice.174.first_ref, s32[18]{0:T(128)} %slice.175.second_ref, bf16[32,128,768]{2,1,0:T(8,128)(2,1)} %shard_map.190.d_ref, s32[18,1,256]{2,1,0:T(1,128)} %reshape.797.ids_ref, ...), custom_call_target="tpu_custom_call" | custom-call | flops 5033164800 | bytes 58982400 | tf_op jit(solution)/shard_map/pallas_call | solution.py:994
  689.2 2.3 reshape.798
  691.5 4.1 all-to-all-start.7
  695.7 30.0 %shard_map.192 = (f32[4,1600,768]{2,1,0:T(8,128)}, f32[4,1600,768]{2,1,0:T(8,128)}, f32[4,1600,768]{2,1,0:T(8,128)}) custom-call(s32[5]{0:T(128)} %fusion.126.start_ref, s32[18]{0:T(128)} %slice.174.first_ref, s32[18]{0:T(128)} %slice.175.second_ref, ...), custom_call_target="tpu_custom_call", output_to_operand_aliasing={{0}: (8, {}), {1}: (9, {}), {2}: (10, {})} | custom-call | flops 5033164800 | bytes 58982400 | tf_op jit(solution)/shard_map/pallas_call | solution.py:994
  725.9 2.3 reshape.799
  728.2 5.3 all-to-all-start.8
  738.8 17.4 %all-to-all-done.8 = bf16[4,292,384]{2,1,0:T(8,128)(2,1)S(1)} async-done(((bf16[4,292,384]{2,1,0:T(8,128)(2,1)}), bf16[4,292,384]{2,1,0:T(8,128)(2,1)S(1)}, u32[]{:S(2)}, u32[]{:S(2)}) %all-to-all-start.8) | async-done | bytes 897056 | tf_op jit(solution)/shard_map/all_to_all | solution.py:1262
  756.2 1.3 convert_element_type.307
  757.5 7.3 copy_subtract_fusion
  764.8 5.2 copy.349
  770.0 3.2 copy.350
  773.2 3.2 copy.351
  (282 shorter events, 44.2 us)
Async XLA Ops:
  22.8 1.1 copy-start.42
  22.8 1.1 copy-start.43
  22.8 1.1 copy-start.44
  24.9 147.6 %copy-start.27 = (f32[768]{0:T(1024)}, f32[768]{0:T(1024)S(1)}, u32[]{:S(2)}) copy-start(f32[768]{0:T(1024)S(1)} %get-tuple-element.191) | copy-start | bytes 9220
  25.6 14.8 %all-to-all-start.1 = ((s32[32,1,385]{2,1,0:T(1,128)}), s32[32,1,385]{2,1,0:T(1,128)S(1)}, u32[]{:S(2)}, u32[]{:S(2)}) async-start(s32[32,1,385]{2,1,0:T(1,128)} %broadcast_in_dim.260), calls=%async_computation.1 | async-start | bytes 131072 | tf_op jit(solution)/shard_map/all_to_all | solution.py:236
  41.7 3.8 copy-start.37
  42.7 293.2 %copy-start.39 = (f32[32]{0:T(128)}, f32[32]{0:T(128)S(1)}, u32[]{:S(2)}) copy-start(f32[32]{0:T(128)S(1)} %get-tuple-element.198) | copy-start | bytes 388
  166.3 5.4 copy-start
  171.7 0.8 copy-start.4
  171.9 2.1 copy-start.1
  172.1 1.9 copy-start.29
  172.5 3.9 copy-start.35
  172.5 3.9 copy-start.31
  174.1 4.5 copy-start.18
  178.8 1.6 copy-start.19
  180.4 7.8 copy-start.6
  183.7 8.8 %slice-start = ((s8[14352384]{0:T(1024)(128)(4,1)}), s8[1769472]{0:T(1024)(128)(4,1)S(1)}, s32[]{:S(2)}) async-start(s8[14352384]{0:T(1024)(128)(4,1)} %bitcast.212), calls=%async_computation.14 | async-start | bytes 3538944
  188.2 0.9 copy-start.8
  188.2 4.3 slice-start.1
  189.2 1.7 copy-start.21
  189.3 4.3 slice-start.2
  190.2 1.7 copy-start.14
  190.9 3.9 slice-start.3
  190.9 4.3 copy-start.17
  192.5 3.7 copy-start.12
  196.2 3.1 copy-start.10
  199.2 4.1 copy-start.45
  204.9 131.7 %copy-start.16 = (s32[32,128]{1,0:T(8,128)S(1)}, s32[32,128]{1,0:T(8,128)}, u32[]{:S(2)}) copy-start(s32[32,128]{1,0:T(8,128)} %get-tuple-element.249) | copy-start | bytes 49156
  331.6 12.0 %all-to-all-start.2 = ((f32[32,2,512]{2,1,0:T(2,128)}), f32[32,2,512]{2,1,0:T(2,128)S(1)}, u32[]{:S(2)}, u32[]{:S(2)}) async-start(f32[32,2,512]{2,1,0:T(2,128)} %get-tuple-element.77), calls=%async_computation.2 | async-start | bytes 262144 | tf_op jit(solution)/shard_map/all_to_all | solution.py:1155
  335.4 1.8 copy-start.33
  335.5 22.5 %copy-start.41 = (s32[18]{0:T(128)}, s32[18]{0:T(128)S(1)}, u32[]{:S(2)}) copy-start(s32[18]{0:T(128)S(1)} %broadcast_add_fusion.model_ref) | copy-start | bytes 220
  344.6 11.0 %all-to-all-start.3 = ((f32[32,2,512]{2,1,0:T(2,128)}), f32[32,2,512]{2,1,0:T(2,128)S(1)}, u32[]{:S(2)}, u32[]{:S(2)}) async-start(f32[32,2,512]{2,1,0:T(2,128)} %broadcast_in_dim.275), calls=%async_computation.3 | async-start | bytes 262144 | tf_op jit(solution)/shard_map/all_to_all | solution.py:236
  347.2 342.0 %reduce-scatter.5.cloned.1.call-start = ((), (), s32[]{:S(2)}) async-start(), calls=%async_computation.12 | async-start | bytes 8073216 | tf_op jit(solution)/shard_map/reduce_scatter | solution.py:1248
  427.2 69.7 %slice-start.4 = ((s8[6291456]{0:T(1024)(128)(4,1)}), s8[2097152]{0:T(1024)(128)(4,1)S(1)}, s32[]{:S(2)}) async-start(s8[6291456]{0:T(1024)(128)(4,1)} %bitcast.250), calls=%async_computation.18 | async-start | bytes 4194304
  495.3 2.2 slice-start.5
  496.8 9.2 %copy-start.23 = (bf16[512,768]{1,0:T(8,128)(2,1)}, bf16[512,768]{1,0:T(8,128)(2,1)S(1)}, u32[]{:S(2)}) copy-start(bf16[512,768]{1,0:T(8,128)(2,1)S(1)} %get-tuple-element.218) | copy-start | bytes 2359300
  497.5 8.5 %copy-start.11 = (f32[512,768]{1,0:T(8,128)S(1)}, f32[512,768]{1,0:T(8,128)}, u32[]{:S(2)}) copy-start(f32[512,768]{1,0:T(8,128)} %copy-done.10) | copy-start | bytes 4718596
  506.0 6.4 copy-start.46
  521.0 3.4 copy-start.15
  524.4 1.1 copy-start.7
  525.5 1.1 copy-start.9
  526.6 1.2 copy-start.22
  530.5 1.1 copy-start.20
  531.6 2.0 copy-start.2
  531.6 2.0 copy-start.5
  531.6 2.0 copy-start.28
  531.6 2.1 copy-start.30
  531.6 2.1 copy-start.32
  533.7 4.7 copy-start.13
  533.7 10.0 %slice-start.6 = ((s8[6291456]{0:T(1024)(128)(4,1)}), s8[2097152]{0:T(1024)(128)(4,1)S(1)}, s32[]{:S(2)}) async-start(s8[6291456]{0:T(1024)(128)(4,1)} %bitcast.252), calls=%async_computation.20 | async-start | bytes 4194304
  538.4 1.9 copy-start.47
  540.3 3.5 copy-start.24
  540.3 3.5 slice-start.7
  543.8 4.1 copy-start.36
  547.9 5.4 copy-start.3
  565.6 160.2 %reduce-scatter.3.cloned.1.call-start = ((), (), s32[]{:S(2)}) async-start(), calls=%async_computation.11 | async-start | bytes 8073216 | tf_op jit(solution)/shard_map/reduce_scatter | solution.py:1249
  590.1 23.5 %all-to-all-start.4 = ((bf16[4,128,768]{2,1,0:T(8,128)(2,1)}), bf16[4,128,768]{2,1,0:T(8,128)(2,1)S(1)}, u32[]{:S(2)}, u32[]{:S(2)}) async-start(bf16[4,128,768]{2,1,0:T(8,128)(2,1)} %bitcast.34), calls=%async_computation.5 | async-start | bytes 1572864 | tf_op jit(solution)/shard_map/all_to_all | solution.py:1235
  691.5 34.1 %all-to-all-start.7 = ((bf16[4,292,384]{2,1,0:T(8,128)(2,1)}), bf16[4,292,384]{2,1,0:T(8,128)(2,1)S(1)}, u32[]{:S(2)}, u32[]{:S(2)}) async-start(bf16[4,292,384]{2,1,0:T(8,128)(2,1)} %reshape.798), calls=%async_computation.9 | async-start | bytes 1818624 | tf_op jit(solution)/shard_map/all_to_all | solution.py:1262
  725.8 7.7 copy-start.40
  725.8 7.9 %copy-start.26 = (f32[4,8,4]{2,0,1:T(4,128)S(1)}, f32[4,8,4]{2,0,1:T(4,128)}, u32[]{:S(2)}) copy-start(f32[4,8,4]{2,0,1:T(4,128)} %get-tuple-element.194) | copy-start | bytes 1540
  725.8 8.0 %copy-start.38 = (f32[32]{0:T(128)S(1)}, f32[32]{0:T(128)}, u32[]{:S(2)}) copy-start(f32[32]{0:T(128)} %copy-done.37) | copy-start | bytes 388
  725.8 8.8 %copy-start.34 = (s32[8,4]{0,1:T(4,128)S(1)}, s32[8,4]{0,1:T(4,128)}, u32[]{:S(2)}) copy-start(s32[8,4]{0,1:T(4,128)} %copy-done.33) | copy-start | bytes 388
  725.9 10.3 %copy-start.25 = (f32[4,14,768]{2,0,1:T(4,128)S(1)}, f32[4,14,768]{2,0,1:T(4,128)}, u32[]{:S(2)}) copy-start(f32[4,14,768]{2,0,1:T(4,128)} %param.24) | copy-start | bytes 516100
  728.2 28.0 %all-to-all-start.8 = ((bf16[4,292,384]{2,1,0:T(8,128)(2,1)}), bf16[4,292,384]{2,1,0:T(8,128)(2,1)S(1)}, u32[]{:S(2)}, u32[]{:S(2)}) async-start(bf16[4,292,384]{2,1,0:T(8,128)(2,1)} %reshape.799), calls=%async_computation.10 | async-start | bytes 1818624 | tf_op jit(solution)/shard_map/all_to_all | solution.py:1262
Sparse Core Ops, SparseCore 1:
  565.7 78.9 reduce-scatter.4
  648.0 66.7 reduce-scatter.2

commit v7 on v6

--- a/solution.py
+++ b/solution.py
@@ -21,6 +21,7 @@
 ROUND_ROWS = 104
 SLAB_STEP = 16
 TILE = 400
+LANES = 128
 MIB = 1 << 20
 POOL_BYTES = 32 * MIB
 MESH = pl.DeviceIdType.MESH
@@ -142,12 +143,10 @@
     )
     d_outer = d_residual.astype(jnp.bfloat16)
     d_bias_out = jnp.sum(d_outer.astype(jnp.float32), 0)
-    grad_down = outer_rows(active, d_outer)
     d_active = project(d_outer, weights[8 * model_width : 12 * model_width])
     gelu_value, gelu_pull = jax.vjp(gelu_tanh, hidden)
     d_hidden = gelu_pull(d_active)[0].astype(jnp.bfloat16)
     d_bias_hidden = jnp.sum(d_hidden.astype(jnp.float32), 0)
-    grad_up = outer_rows(d_hidden, normed_two)
     d_normed_two = product(d_hidden, weights[4 * model_width : 8 * model_width])
     d_middle_norm, d_gain_two, d_shift_two = norm_grad(
         middle, vector_one[2], vector_one[3], d_normed_two
@@ -155,7 +154,6 @@
     d_middle = d_residual + d_middle_norm
     d_branch = d_middle.astype(jnp.bfloat16)
     d_bias_branch = jnp.sum(d_branch.astype(jnp.float32), 0)
-    grad_mix = outer_rows(d_branch, mixture)
     d_mixture = split_heads(
         product(d_branch, weights[3 * model_width : 4 * model_width]).astype(jnp.bfloat16), seq_len
     )
@@ -193,20 +191,27 @@
     )
     d_keys = d_keys.reshape(row_count, model_width).astype(jnp.bfloat16)
     d_joined = jnp.concatenate([d_queries, d_keys, d_values], axis=1)
-    grad_joined = outer_rows(d_joined, normed)
     d_normed = product(d_joined, weights[0 : 3 * model_width])
     d_inputs_norm, d_gain_one, d_shift_one = norm_grad(
         inputs, vector_one[0], vector_one[1], d_normed
     )
     d_inputs = d_middle + d_inputs_norm
     grad_places = jnp.sum(d_inputs.reshape(-1, seq_len, model_width), axis=0)
-    stack_rows = jnp.concatenate(
-        [
-            piece.astype(jnp.bfloat16)
-            for piece in (grad_joined, grad_mix, grad_up, grad_down, grad_places)
-        ],
-        axis=0,
-    )
+    pairs = (
+        (d_joined, normed),
+        (d_branch, mixture),
+        (d_hidden, normed_two),
+        (active, d_outer),
+    )
+    half = model_width // 2
+    stack_halves = [
+        jnp.concatenate(
+            [outer_rows(left, right[:, cut]).astype(jnp.bfloat16) for left, right in pairs]
+            + [grad_places[:, cut].astype(jnp.bfloat16)],
+            axis=0,
+        )
+        for cut in (slice(0, half), slice(half, model_width))
+    ]
     bias_query = jnp.sum(d_queries.astype(jnp.float32), 0)
     bias_value = jnp.sum(d_values.astype(jnp.float32), 0)
     vector_rows = jnp.concatenate(
@@ -229,7 +234,7 @@
         ],
         axis=0,
     )
-    return (stack_rows, vector_rows, d_inputs)
+    return (stack_halves, vector_rows, d_inputs)
 
 
 def share_all(rows, axes, size):
@@ -580,6 +585,82 @@
 
 def tile_of(part_rows):
     return TILE if part_rows % TILE == 0 else part_rows
+
+
+def opening_kernel(groups, members, facts_ref, table_ref, facts_out, low_ref, own_sem, send_sems, recv_sems):
+    devices = groups * members
+    tiles = pl.num_programs(1)
+    step = pl.program_id(0) * tiles + pl.program_id(1)
+    last = pl.num_programs(0) * tiles - 1
+    me = lax.axis_index("grp") * members + lax.axis_index("cli")
+
+    def other(j):
+        return lax.rem(me + j, devices)
+
+    def place(device):
+        return (lax.div(device, members), lax.rem(device, members))
+
+    def give(j):
+        return pltpu.make_async_remote_copy(
+            src_ref=facts_ref, dst_ref=facts_out.at[me], send_sem=send_sems.at[j], recv_sem=recv_sems.at[j],
+            device_id=place(other(j)), device_id_type=MESH,
+        )
+
+    own = pltpu.make_async_copy(facts_ref, facts_out.at[me], own_sem)
+
+    @pl.when(step == 0)
+    def begin():
+        barrier = pltpu.get_barrier_semaphore()
+
+        def hello(j, carry):
+            pl.semaphore_signal(barrier, inc=1, device_id=place(other(j)), device_id_type=MESH)
+            return carry
+
+        def start(j, carry):
+            give(j).start()
+            return carry
+
+        own.start()
+        lax.fori_loop(1, devices, hello, 0)
+        pl.semaphore_wait(barrier, devices - 1)
+        lax.fori_loop(1, devices, start, 0)
+
+    low_ref[...] = table_ref[...].astype(low_ref.dtype)
+
+    @pl.when(step == last)
+    def end():
+        def finish(j, carry):
+            give(j).wait_send()
+            pltpu.make_async_remote_copy(
+                src_ref=facts_ref, dst_ref=facts_out.at[lax.rem(me + devices - j, devices)],
+                send_sem=send_sems.at[j], recv_sem=recv_sems.at[j], device_id=place(other(j)), device_id_type=MESH,
+            ).wait_recv()
+            return carry
+
+        lax.fori_loop(1, devices, finish, 0)
+        own.wait()
+
+
+def opening(facts, table, groups, members, collective_id):
+    devices = groups * members
+    models, part_rows, width = table.shape
+    tile_rows = tile_of(part_rows)
+    piece = pl.BlockSpec((1, tile_rows, width), lambda m, t: (m, t, 0))
+    anywhere = pl.BlockSpec(memory_space=pl.ANY)
+    dma = pltpu.SemaphoreType.DMA
+    return pl.pallas_call(
+        functools.partial(opening_kernel, groups, members),
+        out_shape=(
+            jax.ShapeDtypeStruct((devices,) + facts.shape, facts.dtype),
+            jax.ShapeDtypeStruct(table.shape, jnp.bfloat16),
+        ),
+        grid=(models, part_rows // tile_rows),
+        in_specs=[anywhere, piece],
+        out_specs=(anywhere, piece),
+        scratch_shapes=[dma, dma((devices,)), dma((devices,))],
+        compiler_params=pltpu.CompilerParams(collective_id=collective_id, has_side_effects=True),
+        cost_estimate=pl.CostEstimate(flops=0, bytes_accessed=6 * table.size, transcendentals=0),
+    )(facts, table)
 
 
 def score_kernel(groups, members, share, pieces, src, table, target, out, stat, *rest):
@@ -701,7 +782,6 @@
     greet(place)
     xs, ys = place.xs, place.ys
     half = members // 2
-    upper, lower = pl.ds(0, half), pl.ds(half, half)
     z = place.cli
     order = sorted(
         ((jx, jy) for jx in range(xs) for jy in range(ys)), key=lambda spot: -(spot[0] > 0) - (spot[1] > 0)
@@ -722,66 +802,82 @@
             device_id_type=MESH,
         ).wait_recv()
 
-    def spot_of(jx, jy):
-        return jy * xs + jx
-
     def add(ref, others):
         total = ref[...].astype(jnp.float32)
         for other in others:
             total = total + other[...].astype(jnp.float32)
         ref[...] = total.astype(ref.dtype)
 
-    for jx, jy in order:
-        k = spot_of(jx, jy)
-        send(
-            source.at[pl.ds(place.group(jx, jy, 1) * members, members)], from_core.at[k], core_send.at[k],
-            core_recv.at[k], place.peer(jc=1),
-        )
+    def clients(p):
+        return (p, p + half)
+
+    spots = [(jy * xs + jx, jx, jy) for jx, jy in order]
     loads = {}
-    for jx, jy in order:
-        k = spot_of(jx, jy)
-        loads[k] = pltpu.make_async_copy(
-            source.at[pl.ds(place.group(jx, jy, 0) * members, members)], work.at[k], load_sem.at[k]
-        )
-        loads[k].start()
-    for jx, jy in order:
-        k = spot_of(jx, jy)
-        loads[k].wait()
-        arrival(from_core.at[k], core_send.at[k], core_recv.at[k], place.peer(jc=1))
-        add(work.at[k], [from_core.at[k]])
-        if jx:
-            send(work.at[k, upper], from_x.at[jx, jy], x_send.at[jx, jy], x_recv.at[jx, jy], place.peer(jx=jx))
-        if jy:
-            send(work.at[k, lower], from_y.at[jx, jy], y_send.at[jx, jy], y_recv.at[jx, jy], place.peer(jy=jy))
-    for jy in reversed(range(ys)):
-        k = spot_of(0, jy)
+    for p in range(half):
+        for k, jx, jy in spots:
+            for c in clients(p):
+                send(
+                    source.at[place.group(jx, jy, 1) * members + c], from_core.at[k, c], core_send.at[k, c],
+                    core_recv.at[k, c], place.peer(jc=1),
+                )
+                loads[k, c] = pltpu.make_async_copy(
+                    source.at[place.group(jx, jy, 0) * members + c], work.at[k, c], load_sem.at[k, c]
+                )
+                loads[k, c].start()
+    for p in range(half):
+        a, b = clients(p)
+        for k, jx, jy in spots:
+            for c in (a, b):
+                loads[k, c].wait()
+                arrival(from_core.at[k, c], core_send.at[k, c], core_recv.at[k, c], place.peer(jc=1))
+                add(work.at[k, c], [from_core.at[k, c]])
+            if jx:
+                send(work.at[k, a], from_x.at[p, jx, jy], x_send.at[p, jx, jy], x_recv.at[p, jx, jy], place.peer(jx=jx))
+            if jy:
+                send(work.at[k, b], from_y.at[p, jx, jy], y_send.at[p, jx, jy], y_recv.at[p, jx, jy], place.peer(jy=jy))
+
+    def second(p):
+        a, b = clients(p)
+        for jy in reversed(range(ys)):
+            k = jy * xs
+            for jx in range(1, xs):
+                arrival(from_x.at[p, jx, jy], x_send.at[p, jx, jy], x_recv.at[p, jx, jy], place.peer(jx=jx))
+            add(work.at[k, a], [from_x.at[p, jx, jy] for jx in range(1, xs)])
+            if jy:
+                send(work.at[k, a], then_y.at[p, jy], yy_send.at[p, jy], yy_recv.at[p, jy], place.peer(jy=jy))
+        for jx in reversed(range(xs)):
+            for jy in range(1, ys):
+                arrival(from_y.at[p, jx, jy], y_send.at[p, jx, jy], y_recv.at[p, jx, jy], place.peer(jy=jy))
+            add(work.at[jx, b], [from_y.at[p, jx, jy] for jy in range(1, ys)])
+            if jx:
+                send(work.at[jx, b], then_x.at[p, jx], xx_send.at[p, jx], xx_recv.at[p, jx], place.peer(jx=jx))
+
+    def third(p):
+        a, b = clients(p)
+        for jy in range(1, ys):
+            arrival(then_y.at[p, jy], yy_send.at[p, jy], yy_recv.at[p, jy], place.peer(jy=jy))
+        add(work.at[0, a], [then_y.at[p, jy] for jy in range(1, ys)])
         for jx in range(1, xs):
-            arrival(from_x.at[jx, jy], x_send.at[jx, jy], x_recv.at[jx, jy], place.peer(jx=jx))
-        add(work.at[k, upper], [from_x.at[jx, jy] for jx in range(1, xs)])
-        if jy:
-            send(work.at[k, upper], then_y.at[jy], yy_send.at[jy], yy_recv.at[jy], place.peer(jy=jy))
-    for jx in reversed(range(xs)):
-        k = spot_of(jx, 0)
-        for jy in range(1, ys):
-            arrival(from_y.at[jx, jy], y_send.at[jx, jy], y_recv.at[jx, jy], place.peer(jy=jy))
-        add(work.at[k, lower], [from_y.at[jx, jy] for jy in range(1, ys)])
-        if jx:
-            send(work.at[k, lower], then_x.at[jx], xx_send.at[jx], xx_recv.at[jx], place.peer(jx=jx))
-    own = work.at[0]
-    for jy in range(1, ys):
-        arrival(then_y.at[jy], yy_send.at[jy], yy_recv.at[jy], place.peer(jy=jy))
-    add(own.at[upper], [then_y.at[jy] for jy in range(1, ys)])
-    for jx in range(1, xs):
-        arrival(then_x.at[jx], xx_send.at[jx], xx_recv.at[jx], place.peer(jx=jx))
-    add(own.at[lower], [then_x.at[jx] for jx in range(1, xs)])
-
-    for j in range(1, members):
-        level = lax.rem(z + j, members)
-        send(own.at[level], from_z.at[j], z_send.at[j], z_recv.at[j], place.level(level))
+            arrival(then_x.at[p, jx], xx_send.at[p, jx], xx_recv.at[p, jx], place.peer(jx=jx))
+        add(work.at[0, b], [then_x.at[p, jx] for jx in range(1, xs)])
+        for c in (a, b):
+            @pl.when(z != c)
+            def give():
+                pltpu.make_async_remote_copy(
+                    src_ref=work.at[0, c], dst_ref=from_z.at[z], send_sem=z_send.at[c], recv_sem=z_recv.at[z],
+                    device_id=place.level(c), device_id_type=MESH,
+                ).start()
+
+    for p in range(half + 1):
+        if p < half:
+            second(p)
+        if p:
+            third(p - 1)
     total = work[0, z].astype(jnp.float32)
     for j in range(1, members):
-        arrival(from_z.at[j], z_send.at[j], z_recv.at[j], place.level(lax.rem(z + members - j, members)))
-        total = total + from_z[j].astype(jnp.float32)
+        level = lax.rem(z + members - j, members)
+        arrival(from_z.at[level], z_send.at[level], z_recv.at[level], place.level(level))
+        total = total + from_z[level].astype(jnp.float32)
     out[z] = total.astype(out.dtype)
     for j in range(1, members):
         send(out.at[z], out.at[z], g_send.at[j], g_recv.at[j], place.level(lax.rem(z + j, members)))
@@ -790,6 +886,13 @@
         arrival(out.at[level], g_send.at[j], g_recv.at[j], place.level(level))
     for copy in started:
         copy.wait_send()
+    for c in range(members):
+        @pl.when(z != c)
+        def given():
+            pltpu.make_async_remote_copy(
+                src_ref=work.at[0, c], dst_ref=from_z.at[z], send_sem=z_send.at[c], recv_sem=z_recv.at[z],
+                device_id=place.level(c), device_id_type=MESH,
+            ).wait_send()
 
 
 def collect(parts, groups, members, collective_id):
@@ -808,16 +911,16 @@
         scratch_shapes=[
             held(xs * ys, members),
             held(xs * ys, members),
-            held(xs, ys, half),
-            held(xs, ys, half),
-            held(ys, half),
-            held(xs, half),
+            held(half, xs, ys),
+            held(half, xs, ys),
+            held(half, ys),
+            held(half, xs),
             held(members),
         ]
-        + [dma((xs * ys,))] * 3
-        + [dma((xs, ys))] * 4
-        + [dma((ys,))] * 2
-        + [dma((xs,))] * 2
+        + [dma((xs * ys, members))] * 3
+        + [dma((half, xs, ys))] * 4
+        + [dma((half, ys))] * 2
+        + [dma((half, xs))] * 2
         + [dma((members,))] * 4,
         compiler_params=pltpu.CompilerParams(
             collective_id=collective_id, has_side_effects=True, vmem_limit_bytes=56 * MIB
@@ -1045,9 +1148,10 @@
     slab = -(-(stack_part + ROUND_ROWS) // SLAB_STEP) * SLAB_STEP
     round_rows = slab - stack_part
 
-    facts = share_all(
-        jnp.concatenate([token_ids[0], target_ids[0], segment_ids[0], chosen]), both, devices
-    )
+    facts = jnp.concatenate([token_ids[0], target_ids[0], segment_ids[0], chosen])
+    facts = jnp.pad(facts, (0, -facts.size % LANES))[None]
+    facts, table_low = opening(facts, table, groups, members, 5)
+    facts = facts[:, 0]
     tokens = facts[:, :seq_len]
     targets = facts[:, seq_len : 2 * seq_len]
     segments = facts[:, 2 * seq_len : 3 * seq_len]
@@ -1064,7 +1168,6 @@
     totals = jnp.sum(choice_table * counts[:, None], axis=0)
     total_of = jnp.sum(choice_table * totals[None, :], axis=1)
 
-    table_low = table.astype(jnp.bfloat16)
     fine = 16 if block_rows % 64 else 64
     coarse = block_rows // fine
     flat_tokens = tokens.reshape(-1)
@@ -1222,7 +1325,7 @@
     d_final = jnp.where((my_choices == model_own)[:, None, None], d_mine, 0.0).reshape(
         local * seq_len, model_width
     )
-    stack_rows, vector_rows, d_inputs = layer_backward(
+    stack_halves, vector_rows, d_inputs = layer_backward(
         weights, vector_one, inputs, my_segments, saved, d_final
     )
     d_wide = d_inputs.astype(jnp.bfloat16)
@@ -1240,15 +1343,13 @@
     vector_part = jnp.sum(
         lax.all_to_all(vector_rows.reshape(groups, vector_piece), "grp", 0, 0, tiled=True), axis=0
     )
+    d_all = spread(d_client, groups, members, 3, True, 2)
+    d_all, vector_part = lax.optimization_barrier((d_all, vector_part))
     vector_parts = share_all(vector_part, both, devices)
-    d_client, vector_parts = lax.optimization_barrier((d_client, vector_parts))
-    d_all = spread(d_client, groups, members, 3, True, 2)
-
-    middle = model_width // 2
-    stack_left = lax.psum_scatter(stack_rows[:, :middle], "grp", scatter_dimension=0, tiled=True)
-    stack_right = lax.psum_scatter(stack_rows[:, middle:], "grp", scatter_dimension=0, tiled=True)
-    vector_grad = jnp.sum(vector_parts.reshape(groups, models, share, vector_piece), axis=2)
-    vector_grad = vector_grad.transpose(1, 0, 2).reshape(vectors.shape)
+
+    stack_left, stack_right = (
+        lax.psum_scatter(rows, "grp", scatter_dimension=0, tiled=True) for rows in stack_halves
+    )
 
     token_local = tokens - device_index * block_rows
     token_local = jnp.where((token_local >= 0) & (token_local < block_rows), token_local, -1)
@@ -1265,7 +1366,7 @@
         return jnp.sum(back.reshape(models, share, stack_part, rows.shape[1]), axis=1)
 
     states = finish_table(d_all, head_grad, table, table_momentum, schedule, slot_token, 0, lead, ())
-    stack_left, states = lax.optimization_barrier((stack_left, states))
+    stack_left, states, vector_parts = lax.optimization_barrier((stack_left, states, vector_parts))
     grad_left = to_owner(stack_left)
     states = finish_table(
         d_all, head_grad, table, table_momentum, schedule, slot_token, lead, models - lead, states
@@ -1273,6 +1374,8 @@
     stack_right, states, grad_left = lax.optimization_barrier((stack_right, states, grad_left))
     table_grad, table_momentum_new, table_new = states
     stack_grad = jnp.concatenate([grad_left, to_owner(stack_right)], axis=2)
+    vector_grad = jnp.sum(vector_parts.reshape(groups, models, share, vector_piece), axis=2)
+    vector_grad = vector_grad.transpose(1, 0, 2).reshape(vectors.shape)
     stack_momentum_new, stack_new = update(stack, stack_momentum, stack_grad, stack_rate)
     vector_momentum_new, vector_new = update(vectors, vector_momentum, vector_grad, vector_rate)
     return (

time: 793 us -> 790 us (level)
  Pallas kernels: 478 us -> 504 us
  matrix products: 64.7 us -> 81.2 us
  blocking collectives: 23.3 us -> 7.48 us
  local copies, waits for them, and re-layouts: 73.1 us -> 61.1 us
  waiting for transfers between devices: 53.3 us -> 41.9 us
  other arithmetic: 46.8 us -> 38.7 us
    pallas_call x0 -> x1, Pallas kernels: none -> 23.6 us  [opening(): pl.pallas_call(functools.partial(opening_kernel, groups, members), out_sh...]
    all_to_all x1 -> x0, blocking collectives: 16 us -> none  [share_all(): lax.all_to_all(jnp.broadcast_to(rows[None], (size,) + rows.shape), axes,...]
    dot_general x5 -> x9, matrix products: 13 us -> 27.5 us  [outer_rows(): lax.dot_general(left, right, (((0,), (0,)), ((), ())), preferred_element_...]
    convert_element_type x1, other arithmetic: 11.5 us -> 0.32 us  [layer_forward(): layer_norm(middle, vector_one[2], vector_one[3]).astype(jnp.bfloat16)]
    slice x1 -> x0, local copies, waits for them, and re-layouts: 10.4 us -> none  [body(): stack_rows[:, :middle]]
    all_to_all x2, waiting for transfers between devices: 12.5 us -> 3.77 us  [share_all(): lax.all_to_all(jnp.broadcast_to(rows[None], (size,) + rows.shape), axes,...]
    unnamed x125 -> x126, local copies, waits for them, and re-layouts: 31.2 us -> 29.9 us
  transfers between devices with their start and end apart: 8 -> 8, of which waited for: 5 -> 4; matrix products, arithmetic and copies ran while one was open for 2% -> 3% of each run, Pallas kernels for 13% -> 14%
where the time goes in v7:
time: 790 us; the launch traced here: 782 us
  Pallas kernels  504 us (64%)
  matrix products  81.2 us (10%)
  local copies, waits for them, and re-layouts  61.1 us (8%)
  waiting for transfers between devices  41.9 us (5%)
  other arithmetic  38.7 us (5%)
  starting transfers between devices  28.9 us (4%)
  between operations  18.2 us (2%)
    pallas_call x2, Pallas kernels, spread(): pl.pallas_call(functools.partial(spread_kernel, groups, members, chain, p...  142 us
    pallas_call x1, Pallas kernels, spread_score(): pl.pallas_call(functools.partial(score_kernel, groups, members, share, pi...  129 us
    pallas_call x1, Pallas kernels, head_back(): pl.pallas_call(back_kernel, out_shape=(jax.ShapeDtypeStruct((2 * steps, s...  69.2 us
    pallas_call x2, Pallas kernels, finish_table(): pl.pallas_call(functools.partial(finish_kernel, first_model), out_shape=(...  60.7 us
    pallas_call x1, Pallas kernels, collect(): pl.pallas_call(functools.partial(collect_kernel, groups, members), out_sh...  60.4 us
    unnamed x126, local copies, waits for them, and re-layouts  29.9 us
    dot_general x9, matrix products, outer_rows(): lax.dot_general(left, right, (((0,), (0,)), ((), ())), preferred_element_...  27.5 us
    pallas_call x1, Pallas kernels, opening(): pl.pallas_call(functools.partial(opening_kernel, groups, members), out_sh...  23.6 us
  transfers between devices with their start and end apart: 8, of which 4 were waited for; matrix products, arithmetic and copies ran while one was open for 3% of the time, Pallas kernels for 14%

profile of v7, /device:TPU:0, one launch (start us, length us, event | category | flops | bytes accessed | tf_op | source)
XLA Modules:
  0.0 781.9 jit_solution(13261407930988950670)
XLA Ops:
  10.0 23.6 %shard_map.185 = (s32[32,1,512]{2,1,0:T(1,128)}, bf16[4,1600,768]{2,1,0:T(8,128)(2,1)}) custom-call(s32[1,512]{1,0:T(1,128)} %bitcast.250, f32[4,1600,768]{2,1,0:T(8,128)} %table_ref.5), custom_call_target="tpu_custom_call" | custom-call | bytes 29491200 | tf_op jit(solution)/shard_map/pallas_call | solution.py:651
  35.2 2.6 convert_element_type.251
  38.4 2.6 fusion.152
  44.0 1.7 fusion.35
  45.8 5.3 fusion.48
  51.2 1.6 pad_maximum_fusion.1.src
  52.8 91.3 %shard_map.186.pool_ref = bf16[32,400,768]{2,1,0:T(8,128)(2,1)} custom-call(bf16[4,400,768]{2,1,0:T(8,128)(2,1)} %pad_maximum_fusion.1.src), custom_call_target="tpu_custom_call" | custom-call | bytes 39321600 | tf_op jit(solution)/shard_map/pallas_call | solution.py:573
  144.3 18.5 %shard_map.187 = (bf16[9344,768]{1,0:T(8,128)(2,1)S(1)}, f32[512,768]{1,0:T(8,128)S(1)}) custom-call(s32[512,1]{1,0:T(8,128)S(1)} %fusion.86.at_ref, bf16[32,400,768]{2,1,0:T(8,128)(2,1)} %shard_map.186.pool_ref), custom_call_target="tpu_custom_call" | custom-call | flops 2818572288 | bytes 39321600 | tf_op jit(solution)/shard_map/pallas_call | solution.py:959
  162.9 5.3 copy-done
  171.4 1.5 add_convert_fusion.4
  173.0 2.4 convolution_convert_fusion.8
  175.4 2.1 add_convert_fusion.2
  177.9 2.6 add_convert_fusion.3
  181.9 1.2 copy.318
  183.0 2.1 reshape.773
  189.3 1.2 slice-done.2
  190.5 1.4 slice-done.3
  193.8 5.6 multiply_convert_fusion
  199.5 2.7 fusion.155
  202.5 1.2 fusion.58.src
  203.7 129.4 %shard_map.188 = (bf16[32,512,768]{2,1,0:T(8,128)(2,1)}, f32[32,2,512]{2,1,0:T(2,128)}) custom-call(bf16[1,512,768]{2,1,0:T(8,128)(2,1)} %fusion.58.src, bf16[4,1600,768]{2,1,0:T(8,128)(2,1)} %get-tuple-element.375, s32[8,1,512]{2,1,0:T(1,128)} %bitcast.228), custom_call_target="tpu_custom_call" | custom-call | flops 40265318400 | bytes 50331648 | tf_op jit(solution)/shard_map/pallas_call | solution.py:716
  333.2 2.8 all-to-all-start.1
  340.9 3.5 all-to-all-done.1
  345.3 2.6 all-to-all-start.2
  352.5 3.8 all-to-all-done.2
  358.6 69.2 %shard_map.189 = (bf16[36,128,768]{2,1,0:T(8,128)(2,1)}, f32[4,1600,768]{2,1,0:T(8,128)}) custom-call(s32[18]{0:T(128)} %copy-done.45, s32[18]{0:T(128)} %add_convert_fusion.6.fresh_ref, s32[18]{0:T(128)} %slice.195.first_ref, s32[18]{0:T(128)} %slice.196.second_ref, s32[36]{0:T(128)} %get-tuple-element.270.place_ref, bf16[128,128,768]{2,1,0:T(8,128)(2,1)} %bitcast.257, ...), custom_call_target="tpu_custom_call" | custom-call | flops 33973862400 | bytes 43646976 | tf_op jit(solution)/shard_map/pallas_call | solution.py:1035
  427.8 60.4 %shard_map.190 = bf16[4,128,768]{2,1,0:T(8,128)(2,1)} custom-call(bf16[36,128,768]{2,1,0:T(8,128)(2,1)} %get-tuple-element.84.source), custom_call_target="tpu_custom_call" | custom-call | bytes 12582912 | tf_op jit(solution)/shard_map/pallas_call | solution.py:906
  488.2 1.4 fusion.142
  491.8 8.1 %convert_reduce_fusion = (f32[3072]{0:T(1024)S(1)}, bf16[512,3072]{1,0:T(8,128)(2,1)S(1)}) fusion(f32[512,3072]{1,0:T(8,128)S(1)} %bitcast.260, f32[3072]{0:T(1024)S(1)} %bitcast.247, bf16[512,768]{1,0:T(8,128)(2,1)S(1)} %get-tuple-element.224, bf16[9344,768]{1,0:T(8,128)(2,1)} %copy-done), kind=kOutput, calls=%fused_computation.32 | convolution fusion | flops 2452091904 | bytes 14966784 | tf_op jit(solution)/shard_map/dot_general | solution.py:37
  500.0 6.4 multiply_reduce_fusion.1
  508.3 2.9 convolution_convert_fusion.7
  511.2 2.3 copy.332
  513.5 2.8 reshape.781
  516.4 3.5 convert_reduce_fusion.3
  521.9 1.2 fusion.47
  527.1 4.6 multiply_reduce_fusion.2
  531.7 2.7 fusion.17
  534.4 2.6 fusion.20
  537.9 1.8 fusion.145
  539.7 1.6 reduce_sum.543
  541.3 2.9 fusion.44
  544.2 5.3 fusion.16
  549.5 3.4 fusion.15
  552.8 1.4 fusion.45
  554.3 3.3 fusion.19
  557.5 3.3 fusion.18
  562.6 7.5 all_to_all.49
  570.1 8.7 %all-to-all-start.3 = ((bf16[4,128,768]{2,1,0:T(8,128)(2,1)}), bf16[4,128,768]{2,1,0:T(8,128)(2,1)S(1)}, u32[]{:S(2)}, u32[]{:S(2)}) async-start(bf16[4,128,768]{2,1,0:T(8,128)(2,1)} %bitcast.35), calls=%async_computation.4 | async-start | bytes 1572864 | tf_op jit(solution)/shard_map/all_to_all | solution.py:1338
  580.7 1.2 fusion.134.start_ref
  582.0 16.8 %all-to-all-done.3 = bf16[4,128,768]{2,1,0:T(8,128)(2,1)S(1)} async-done(((bf16[4,128,768]{2,1,0:T(8,128)(2,1)}), bf16[4,128,768]{2,1,0:T(8,128)(2,1)S(1)}, u32[]{:S(2)}, u32[]{:S(2)}) %all-to-all-start.3) | async-done | bytes 786464 | tf_op jit(solution)/shard_map/all_to_all | solution.py:1338
  599.6 51.0 %shard_map.191.d_ref = bf16[32,128,768]{2,1,0:T(8,128)(2,1)} custom-call(bf16[1,128,768]{2,1,0:T(8,128)(2,1)} %bitcast.230), custom_call_target="tpu_custom_call" | custom-call | bytes 12582912 | tf_op jit(solution)/shard_map/pallas_call | solution.py:573
  651.4 4.0 all-to-all-start.5
  655.4 30.4 %shard_map.192 = (f32[4,1600,768]{2,1,0:T(8,128)}, f32[4,1600,768]{2,1,0:T(8,128)}, f32[4,1600,768]{2,1,0:T(8,128)}) custom-call(s32[5]{0:T(128)} %fusion.134.start_ref, s32[18]{0:T(128)} %slice.204.first_ref, s32[18]{0:T(128)} %slice.205.second_ref, bf16[32,128,768]{2,1,0:T(8,128)(2,1)} %shard_map.191.d_ref, s32[18,1,256]{2,1,0:T(1,128)} %reshape.791.ids_ref, ...), custom_call_target="tpu_custom_call" | custom-call | flops 5033164800 | bytes 58982400 | tf_op jit(solution)/shard_map/pallas_call | solution.py:1097
  685.9 2.3 reshape.792
  688.2 5.2 all-to-all-start.6
  693.4 30.3 %shard_map.193 = (f32[4,1600,768]{2,1,0:T(8,128)}, f32[4,1600,768]{2,1,0:T(8,128)}, f32[4,1600,768]{2,1,0:T(8,128)}) custom-call(s32[5]{0:T(128)} %fusion.134.start_ref, s32[18]{0:T(128)} %slice.204.first_ref, s32[18]{0:T(128)} %slice.205.second_ref, ...), custom_call_target="tpu_custom_call", output_to_operand_aliasing={{0}: (8, {}), {1}: (9, {}), {2}: (10, {})} | custom-call | flops 5033164800 | bytes 58982400 | tf_op jit(solution)/shard_map/pallas_call | solution.py:1097
  723.8 2.3 reshape.793
  726.1 5.3 all-to-all-start.7
  736.7 17.2 %all-to-all-done.7 = bf16[4,292,384]{2,1,0:T(8,128)(2,1)S(1)} async-done(((bf16[4,292,384]{2,1,0:T(8,128)(2,1)}), bf16[4,292,384]{2,1,0:T(8,128)(2,1)S(1)}, u32[]{:S(2)}, u32[]{:S(2)}) %all-to-all-start.7) | async-done | bytes 897056 | tf_op jit(solution)/shard_map/all_to_all | solution.py:1363
  753.9 1.3 convert_element_type.308
  755.3 7.3 copy_subtract_fusion
  762.6 5.2 copy.351
  767.8 3.2 copy.350
  771.0 3.2 copy.349
  (285 shorter events, 51.3 us)
Async XLA Ops:
  162.8 5.4 copy-start
  168.2 3.2 copy-start.5
  168.5 4.5 copy-start.1
  168.7 4.3 copy-start.33
  169.0 0.6 copy-start.39
  169.1 6.3 copy-start.35
  171.4 3.9 copy-start.31
  173.0 4.5 copy-start.17
  177.9 7.4 copy-start.7
  181.9 7.4 slice-start
  185.2 0.9 copy-start.9
  185.3 3.9 slice-start.1
  186.1 1.6 copy-start.19
  186.1 4.4 slice-start.2
  187.0 1.7 copy-start.13
  187.7 4.2 slice-start.3
  187.7 4.6 copy-start.16
  189.2 3.9 copy-start.11
  193.2 6.3 copy-start.3
  193.8 5.6 copy-start.23
  199.5 2.7 copy-start.46
  203.7 135.9 %copy-start.15 = (s32[32,128]{1,0:T(8,128)S(1)}, s32[32,128]{1,0:T(8,128)}, u32[]{:S(2)}) copy-start(s32[32,128]{1,0:T(8,128)} %get-tuple-element.255) | copy-start | bytes 49156
  203.7 145.7 %copy-start.12 = (bf16[4,128,12,64]{1,0,3,2:T(4,128)(2,1)S(1)}, bf16[4,128,12,64]{1,0,3,2:T(4,128)(2,1)}, u32[]{:S(2)}) copy-start(bf16[4,128,12,64]{1,0,3,2:T(4,128)(2,1)} %copy-done.11) | copy-start | bytes 2359300
  333.2 11.2 %all-to-all-start.1 = ((f32[32,2,512]{2,1,0:T(2,128)}), f32[32,2,512]{2,1,0:T(2,128)S(1)}, u32[]{:S(2)}, u32[]{:S(2)}) async-start(f32[32,2,512]{2,1,0:T(2,128)} %get-tuple-element.82), calls=%async_computation.1 | async-start | bytes 262144 | tf_op jit(solution)/shard_map/all_to_all | solution.py:1258
  336.3 1.3 copy-start.41
  337.5 0.5 copy-start.43
  337.9 20.7 %copy-start.45 = (s32[18]{0:T(128)}, s32[18]{0:T(128)S(1)}, u32[]{:S(2)}) copy-start(s32[18]{0:T(128)S(1)} %broadcast_add_fusion.model_ref) | copy-start | bytes 220
  338.0 0.6 copy-start.37
  345.3 11.0 %all-to-all-start.2 = ((f32[32,2,512]{2,1,0:T(2,128)}), f32[32,2,512]{2,1,0:T(2,128)S(1)}, u32[]{:S(2)}, u32[]{:S(2)}) async-start(f32[32,2,512]{2,1,0:T(2,128)} %broadcast_in_dim.272), calls=%async_computation.2 | async-start | bytes 262144 | tf_op jit(solution)/shard_map/all_to_all | solution.py:241
  347.9 338.0 %reduce-scatter.5.cloned.1.call-start = ((), (), s32[]{:S(2)}) async-start(), calls=%async_computation.11 | async-start | bytes 8073216 | tf_op jit(solution)/shard_map/reduce_scatter | solution.py:1351
  427.8 63.3 %slice-start.4 = ((s8[6291456]{0:T(1024)(128)(4,1)}), s8[2097152]{0:T(1024)(128)(4,1)S(1)}, s32[]{:S(2)}) async-start(s8[6291456]{0:T(1024)(128)(4,1)} %bitcast.259), calls=%async_computation.17 | async-start | bytes 4194304
  489.6 2.2 slice-start.5
  491.1 8.8 %copy-start.25 = (bf16[512,768]{1,0:T(8,128)(2,1)}, bf16[512,768]{1,0:T(8,128)(2,1)S(1)}, u32[]{:S(2)}) copy-start(bf16[512,768]{1,0:T(8,128)(2,1)S(1)} %get-tuple-element.224) | copy-start | bytes 2359300
  491.8 8.2 %copy-start.4 = (f32[512,768]{1,0:T(8,128)S(1)}, f32[512,768]{1,0:T(8,128)}, u32[]{:S(2)}) copy-start(f32[512,768]{1,0:T(8,128)} %copy-done.3) | copy-start | bytes 4718596
  500.0 6.4 copy-start.48
  507.4 0.9 copy-start.27
  516.3 3.6 copy-start.14
  516.3 3.6 copy-start.20
  516.3 3.6 copy-start.22
  520.8 1.1 copy-start.8
  521.9 1.2 copy-start.10
  525.6 1.4 copy-start.2
  525.7 1.5 copy-start.6
  525.7 1.5 copy-start.32
  525.7 1.4 copy-start.34
  525.7 1.4 copy-start.36
  527.1 4.6 copy-start.18
  534.4 2.6 copy-start.40
  539.7 4.5 copy-start.24
  544.2 5.3 copy-start.26
  544.2 5.3 copy-start.47
  549.4 3.4 copy-start.21
  549.4 3.4 copy-start.28
  549.4 4.8 copy-start.49
  561.6 162.2 %reduce-scatter.3.cloned.1.call-start = ((), (), s32[]{:S(2)}) async-start(), calls=%async_computation.10 | async-start | bytes 8073216 | tf_op jit(solution)/shard_map/reduce_scatter | solution.py:1351
  570.1 28.7 %all-to-all-start.3 = ((bf16[4,128,768]{2,1,0:T(8,128)(2,1)}), bf16[4,128,768]{2,1,0:T(8,128)(2,1)S(1)}, u32[]{:S(2)}, u32[]{:S(2)}) async-start(bf16[4,128,768]{2,1,0:T(8,128)(2,1)} %bitcast.35), calls=%async_computation.4 | async-start | bytes 1572864 | tf_op jit(solution)/shard_map/all_to_all | solution.py:1338
  651.4 34.5 %all-to-all-start.5 = ((f32[32,1,1344]{2,1,0:T(1,128)}), f32[32,1,1344]{2,1,0:T(1,128)S(1)}, u32[]{:S(2)}, u32[]{:S(2)}) async-start(f32[32,1,1344]{2,1,0:T(1,128)} %broadcast_in_dim.289), calls=%async_computation.7 | async-start | bytes 360448 | tf_op jit(solution)/shard_map/all_to_all | solution.py:241
  688.2 35.4 %all-to-all-start.6 = ((bf16[4,292,384]{2,1,0:T(8,128)(2,1)}), bf16[4,292,384]{2,1,0:T(8,128)(2,1)S(1)}, u32[]{:S(2)}, u32[]{:S(2)}) async-start(bf16[4,292,384]{2,1,0:T(8,128)(2,1)} %reshape.792), calls=%async_computation.8 | async-start | bytes 1818624 | tf_op jit(solution)/shard_map/all_to_all | solution.py:1363
  723.8 7.7 copy-start.44
  723.8 7.8 %copy-start.30 = (f32[4,8,4]{2,0,1:T(4,128)S(1)}, f32[4,8,4]{2,0,1:T(4,128)}, u32[]{:S(2)}) copy-start(f32[4,8,4]{2,0,1:T(4,128)} %get-tuple-element.200) | copy-start | bytes 1540
  723.8 8.0 %copy-start.42 = (f32[32]{0:T(128)S(1)}, f32[32]{0:T(128)}, u32[]{:S(2)}) copy-start(f32[32]{0:T(128)} %copy-done.41) | copy-start | bytes 388
  723.8 8.7 %copy-start.38 = (s32[8,4]{0,1:T(4,128)S(1)}, s32[8,4]{0,1:T(4,128)}, u32[]{:S(2)}) copy-start(s32[8,4]{0,1:T(4,128)} %copy-done.37) | copy-start | bytes 388
  723.8 10.3 %copy-start.29 = (f32[4,14,768]{2,0,1:T(4,128)S(1)}, f32[4,14,768]{2,0,1:T(4,128)}, u32[]{:S(2)}) copy-start(f32[4,14,768]{2,0,1:T(4,128)} %param.24) | copy-start | bytes 516100
  726.1 27.8 %all-to-all-start.7 = ((bf16[4,292,384]{2,1,0:T(8,128)(2,1)}), bf16[4,292,384]{2,1,0:T(8,128)(2,1)S(1)}, u32[]{:S(2)}, u32[]{:S(2)}) async-start(bf16[4,292,384]{2,1,0:T(8,128)(2,1)} %reshape.793), calls=%async_computation.9 | async-start | bytes 1818624 | tf_op jit(solution)/shard_map/all_to_all | solution.py:1363
Sparse Core Ops, SparseCore 1:
  561.7 86.5 reduce-scatter.4
  651.6 65.0 reduce-scatter.2

commit v8 on v7

--- a/solution.py
+++ b/solution.py
@@ -203,15 +203,6 @@
         (d_hidden, normed_two),
         (active, d_outer),
     )
-    half = model_width // 2
-    stack_halves = [
-        jnp.concatenate(
-            [outer_rows(left, right[:, cut]).astype(jnp.bfloat16) for left, right in pairs]
-            + [grad_places[:, cut].astype(jnp.bfloat16)],
-            axis=0,
-        )
-        for cut in (slice(0, half), slice(half, model_width))
-    ]
     bias_query = jnp.sum(d_queries.astype(jnp.float32), 0)
     bias_value = jnp.sum(d_values.astype(jnp.float32), 0)
     vector_rows = jnp.concatenate(
@@ -234,7 +225,7 @@
         ],
         axis=0,
     )
-    return (stack_halves, vector_rows, d_inputs)
+    return (pairs, grad_places, vector_rows, d_inputs)
 
 
 def share_all(rows, axes, size):
@@ -616,13 +607,16 @@
             pl.semaphore_signal(barrier, inc=1, device_id=place(other(j)), device_id_type=MESH)
             return carry
 
+        own.start()
+        lax.fori_loop(1, devices, hello, 0)
+
+    @pl.when(step == last // 2)
+    def exchange():
         def start(j, carry):
             give(j).start()
             return carry
 
-        own.start()
-        lax.fori_loop(1, devices, hello, 0)
-        pl.semaphore_wait(barrier, devices - 1)
+        pl.semaphore_wait(pltpu.get_barrier_semaphore(), devices - 1)
         lax.fori_loop(1, devices, start, 0)
 
     low_ref[...] = table_ref[...].astype(low_ref.dtype)
@@ -1325,7 +1319,7 @@
     d_final = jnp.where((my_choices == model_own)[:, None, None], d_mine, 0.0).reshape(
         local * seq_len, model_width
     )
-    stack_halves, vector_rows, d_inputs = layer_backward(
+    pairs, grad_places, vector_rows, d_inputs = layer_backward(
         weights, vector_one, inputs, my_segments, saved, d_final
     )
     d_wide = d_inputs.astype(jnp.bfloat16)
@@ -1335,20 +1329,23 @@
             d_wide,
             (part_own * local * seq_len, 0),
         )
+    d_wide, pairs, vector_rows = lax.optimization_barrier((d_wide, pairs, vector_rows))
     d_turned = lax.all_to_all(
         d_wide.reshape(members, seq_len, model_width), "cli", 0, 0, tiled=True
     )
+    stack_rows = jnp.concatenate(
+        [outer_rows(left, right).astype(jnp.bfloat16) for left, right in pairs]
+        + [grad_places.astype(jnp.bfloat16)],
+        axis=0,
+    )
+    stack_rows, d_turned = lax.optimization_barrier((stack_rows, d_turned))
+    stack_sum = lax.psum_scatter(stack_rows, "grp", scatter_dimension=0, tiled=True)
     d_client = jnp.sum(d_turned.astype(jnp.float32), axis=0, keepdims=True).astype(jnp.bfloat16)
+    d_all = spread(d_client, groups, members, 3, True, 2)
+    d_all, vector_rows = lax.optimization_barrier((d_all, vector_rows))
     vector_piece = vector_rows.size // groups
-    vector_part = jnp.sum(
-        lax.all_to_all(vector_rows.reshape(groups, vector_piece), "grp", 0, 0, tiled=True), axis=0
-    )
-    d_all = spread(d_client, groups, members, 3, True, 2)
-    d_all, vector_part = lax.optimization_barrier((d_all, vector_part))
-    vector_parts = share_all(vector_part, both, devices)
-
-    stack_left, stack_right = (
-        lax.psum_scatter(rows, "grp", scatter_dimension=0, tiled=True) for rows in stack_halves
+    vector_part = lax.all_to_all(
+        vector_rows.reshape(groups, vector_piece), "grp", 0, 0, tiled=True
     )
 
     token_local = tokens - device_index * block_rows
@@ -1359,21 +1356,17 @@
     slot_token = slot_token.reshape(steps, 1, 2 * seq_len)
     lead = models // 2
 
-    def to_owner(rows):
-        back = lax.all_to_all(
-            rows.reshape(members, stack_part, rows.shape[1]), "cli", 0, 0, tiled=True
-        ).astype(jnp.float32)
-        return jnp.sum(back.reshape(models, share, stack_part, rows.shape[1]), axis=1)
-
     states = finish_table(d_all, head_grad, table, table_momentum, schedule, slot_token, 0, lead, ())
-    stack_left, states, vector_parts = lax.optimization_barrier((stack_left, states, vector_parts))
-    grad_left = to_owner(stack_left)
-    states = finish_table(
+    stack_sum, states, vector_part = lax.optimization_barrier((stack_sum, states, vector_part))
+    stack_back = lax.all_to_all(
+        stack_sum.reshape(members, stack_part, model_width), "cli", 0, 0, tiled=True
+    ).astype(jnp.float32)
+    stack_grad = jnp.sum(stack_back.reshape(models, share, stack_part, model_width), axis=1)
+    table_grad, table_momentum_new, table_new = finish_table(
         d_all, head_grad, table, table_momentum, schedule, slot_token, lead, models - lead, states
     )
-    stack_right, states, grad_left = lax.optimization_barrier((stack_right, states, grad_left))
-    table_grad, table_momentum_new, table_new = states
-    stack_grad = jnp.concatenate([grad_left, to_owner(stack_right)], axis=2)
+    stack_grad, vector_part = lax.optimization_barrier((stack_grad, vector_part))
+    vector_parts = share_all(jnp.sum(vector_part, axis=0), both, devices)
     vector_grad = jnp.sum(vector_parts.reshape(groups, models, share, vector_piece), axis=2)
     vector_grad = vector_grad.transpose(1, 0, 2).reshape(vectors.shape)
     stack_momentum_new, stack_new = update(stack, stack_momentum, stack_grad, stack_rate)

time: 790 us -> 764 us (0.967)
  Pallas kernels: 504 us -> 490 us
    reduce_scatter x2 -> x1, waiting for transfers between devices: 0.05 us -> 24.2 us  [body(): lax.psum_scatter(stack_rows, 'grp', scatter_dimension=0, tiled=True)]
    all_to_all x1, waiting for transfers between devices: 16.8 us -> 3.14 us  [body(): lax.all_to_all(d_wide.reshape(members, seq_len, model_width), 'cli', 0, 0...]
    dot_general x9 -> x5, matrix products: 27.5 us -> 18.3 us  [outer_rows(): lax.dot_general(left, right, (((0,), (0,)), ((), ())), preferred_element_...]
    unnamed x126 -> x120, local copies, waits for them, and re-layouts: 29.9 us -> 27.3 us
  transfers between devices with their start and end apart: 8 -> 7, of which waited for: 4 -> 5; matrix products, arithmetic and copies ran while one was open for 3% -> 6% of each run, Pallas kernels for 14% -> 13%
where the time goes in v8:
time: 764 us; the launch traced here: 755 us
  Pallas kernels  490 us (64%)
  matrix products  75.4 us (10%)
  local copies, waits for them, and re-layouts  61 us (8%)
  waiting for transfers between devices  46.7 us (6%)
  other arithmetic  36.9 us (5%)
  starting transfers between devices  26.4 us (3%)
  between operations  18.1 us (2%)
    pallas_call x2, Pallas kernels, spread(): pl.pallas_call(functools.partial(spread_kernel, groups, members, chain, p...  139 us
    pallas_call x1, Pallas kernels, spread_score(): pl.pallas_call(functools.partial(score_kernel, groups, members, share, pi...  127 us
    pallas_call x1, Pallas kernels, head_back(): pl.pallas_call(back_kernel, out_shape=(jax.ShapeDtypeStruct((2 * steps, s...  69.3 us
    pallas_call x1, Pallas kernels, collect(): pl.pallas_call(functools.partial(collect_kernel, groups, members), out_sh...  60.4 us
    pallas_call x2, Pallas kernels, finish_table(): pl.pallas_call(functools.partial(finish_kernel, first_model), out_shape=(...  58.5 us
    unnamed x120, local copies, waits for them, and re-layouts  27.3 us
    reduce_scatter x1, waiting for transfers between devices, body(): lax.psum_scatter(stack_rows, 'grp', scatter_dimension=0, tiled=True)  24.2 us
    dot_general x6, matrix products, project(): lax.dot_general(inputs, matrix, (((1,), (1,)), ((), ())), preferred_eleme...  21.9 us
  transfers between devices with their start and end apart: 7, of which 5 were waited for; matrix products, arithmetic and copies ran while one was open for 6% of the time, Pallas kernels for 13%

profile of v8, /device:TPU:0, one launch (start us, length us, event | category | flops | bytes accessed | tf_op | source)
XLA Modules:
  0.0 754.8 jit_solution(5701813072329725716)
XLA Ops:
  10.0 18.1 %shard_map.185 = (s32[32,1,512]{2,1,0:T(1,128)}, bf16[4,1600,768]{2,1,0:T(8,128)(2,1)}) custom-call(s32[1,512]{1,0:T(1,128)} %bitcast.250, f32[4,1600,768]{2,1,0:T(8,128)} %table_ref.5), custom_call_target="tpu_custom_call" | custom-call | bytes 29491200 | tf_op jit(solution)/shard_map/pallas_call | solution.py:645
  29.6 2.6 convert_element_type.237
  32.9 2.6 fusion.140
  38.4 1.7 fusion.32
  40.3 5.3 fusion.44
  45.6 1.6 pad_maximum_fusion.src
  47.3 99.9 %shard_map.186.pool_ref = bf16[32,400,768]{2,1,0:T(8,128)(2,1)} custom-call(bf16[4,400,768]{2,1,0:T(8,128)(2,1)} %pad_maximum_fusion.src), custom_call_target="tpu_custom_call" | custom-call | bytes 39321600 | tf_op jit(solution)/shard_map/pallas_call | solution.py:564
  147.3 18.5 %shard_map.187 = (bf16[9344,768]{1,0:T(8,128)(2,1)S(1)}, f32[512,768]{1,0:T(8,128)S(1)}) custom-call(s32[512,1]{1,0:T(8,128)S(1)} %fusion.74.at_ref, bf16[32,400,768]{2,1,0:T(8,128)(2,1)} %shard_map.186.pool_ref), custom_call_target="tpu_custom_call" | custom-call | flops 2818572288 | bytes 39321600 | tf_op jit(solution)/shard_map/pallas_call | solution.py:953
  165.8 5.3 copy-done
  174.4 1.5 add_convert_fusion.4
  175.9 2.4 convolution_convert_fusion.6
  178.3 2.1 add_convert_fusion.2
  180.9 2.6 add_convert_fusion.3
  183.8 1.1 reshape.766
  184.8 1.2 copy.317
  186.0 2.1 reshape.768
  192.2 1.2 slice-done.2
  193.4 1.4 slice-done.3
  196.8 5.6 multiply_convert_fusion
  202.4 2.7 fusion.143
  205.5 1.2 fusion.54.src
  206.7 126.5 %shard_map.188 = (bf16[32,512,768]{2,1,0:T(8,128)(2,1)}, f32[32,2,512]{2,1,0:T(2,128)}) custom-call(bf16[1,512,768]{2,1,0:T(8,128)(2,1)} %fusion.54.src, bf16[4,1600,768]{2,1,0:T(8,128)(2,1)} %get-tuple-element.389, s32[8,1,512]{2,1,0:T(1,128)} %bitcast.229), custom_call_target="tpu_custom_call" | custom-call | flops 40265318400 | bytes 50331648 | tf_op jit(solution)/shard_map/pallas_call | solution.py:710
  333.2 3.6 all-to-all-start.1
  341.2 4.1 all-to-all-done.1
  346.2 2.7 all-to-all-start.2
  353.3 4.0 all-to-all-done.2
  359.1 69.3 %shard_map.189 = (bf16[36,128,768]{2,1,0:T(8,128)(2,1)}, f32[4,1600,768]{2,1,0:T(8,128)}) custom-call(s32[18]{0:T(128)} %copy-done.42, s32[18]{0:T(128)} %add_convert_fusion.6.fresh_ref, s32[18]{0:T(128)} %slice.165.first_ref, s32[18]{0:T(128)} %slice.166.second_ref, s32[36]{0:T(128)} %get-tuple-element.284.place_ref, bf16[128,128,768]{2,1,0:T(8,128)(2,1)} %bitcast.257, ...), custom_call_target="tpu_custom_call" | custom-call | flops 33973862400 | bytes 43646976 | tf_op jit(solution)/shard_map/pallas_call | solution.py:1029
  428.4 60.4 %shard_map.190 = bf16[4,128,768]{2,1,0:T(8,128)(2,1)} custom-call(bf16[36,128,768]{2,1,0:T(8,128)(2,1)} %get-tuple-element.93.source), custom_call_target="tpu_custom_call" | custom-call | bytes 12582912 | tf_op jit(solution)/shard_map/pallas_call | solution.py:900
  488.7 1.4 fusion.130
  492.3 8.3 %convert_reduce_fusion = (f32[3072]{0:T(1024)S(1)}, bf16[512,3072]{1,0:T(8,128)(2,1)S(1)}) fusion(f32[512,3072]{1,0:T(8,128)S(1)} %bitcast.260, f32[3072]{0:T(1024)S(1)} %bitcast.247, bf16[512,768]{1,0:T(8,128)(2,1)S(1)} %get-tuple-element.101, bf16[9344,768]{1,0:T(8,128)(2,1)} %copy-done), kind=kOutput, calls=%fused_computation.32 | convolution fusion | flops 2452091904 | bytes 14966784 | tf_op jit(solution)/shard_map/dot_general | solution.py:37
  500.7 6.4 multiply_reduce_fusion.1
  509.0 2.9 convolution_convert_fusion.5
  511.9 2.3 copy.331
  514.2 2.4 reshape.776
  516.6 4.3 convert_reduce_fusion.3
  523.0 2.1 fusion.43
  525.0 1.4 convert_reduce_fusion.4
  526.6 2.6 copy.342
  529.4 1.8 copy.336
  531.1 1.8 copy.339
  534.4 5.3 multiply_reduce_fusion.2
  540.6 1.8 fusion.133
  542.4 1.7 reduce_sum.551
  544.2 8.8 %all-to-all-start.3 = ((bf16[4,128,768]{2,1,0:T(8,128)(2,1)}), bf16[4,128,768]{2,1,0:T(8,128)(2,1)S(1)}, u32[]{:S(2)}, u32[]{:S(2)}) async-start(bf16[4,128,768]{2,1,0:T(8,128)(2,1)} %bitcast.222), calls=%async_computation.3 | async-start | bytes 1572864 | tf_op jit(solution)/shard_map/all_to_all | solution.py:1333
  553.4 5.0 fusion.17
  558.5 1.8 fusion.37
  560.3 4.4 fusion.16
  564.7 4.4 fusion.15
  569.8 3.1 all-to-all-done.3
  574.8 1.2 fusion.122.start_ref
  576.9 38.9 %shard_map.191.d_ref = bf16[32,128,768]{2,1,0:T(8,128)(2,1)} custom-call(bf16[1,128,768]{2,1,0:T(8,128)(2,1)} %bitcast.231), custom_call_target="tpu_custom_call" | custom-call | bytes 12582912 | tf_op jit(solution)/shard_map/pallas_call | solution.py:564
  616.5 3.3 all-to-all-start.4
  619.8 29.3 %shard_map.192 = (f32[4,1600,768]{2,1,0:T(8,128)}, f32[4,1600,768]{2,1,0:T(8,128)}, f32[4,1600,768]{2,1,0:T(8,128)}) custom-call(s32[5]{0:T(128)} %fusion.122.start_ref, s32[18]{0:T(128)} %slice.161.first_ref, s32[18]{0:T(128)} %slice.162.second_ref, bf16[32,128,768]{2,1,0:T(8,128)(2,1)} %shard_map.191.d_ref, s32[18,1,256]{2,1,0:T(1,128)} %reshape.786.ids_ref, ...), custom_call_target="tpu_custom_call" | custom-call | flops 5033164800 | bytes 58982400 | tf_op jit(solution)/shard_map/pallas_call | solution.py:1091
  649.1 24.2 %reduce-scatter.2.cloned.1.call-done = bf16[1168,768]{1,0:T(8,128)(2,1)} async-done(((bf16[9344,768]{1,0:T(8,128)(2,1)}), bf16[1168,768]{1,0:T(8,128)(2,1)}) %reduce-scatter.2.cloned.1.call-update) | async-done | bytes 1794064 | tf_op jit(solution)/shard_map/reduce_scatter | solution.py:1342
  673.3 2.6 reshape.787
  675.9 4.6 all-to-all-start.5
  682.2 29.2 %shard_map.193 = (f32[4,1600,768]{2,1,0:T(8,128)}, f32[4,1600,768]{2,1,0:T(8,128)}, f32[4,1600,768]{2,1,0:T(8,128)}) custom-call(s32[5]{0:T(128)} %fusion.122.start_ref, s32[18]{0:T(128)} %slice.161.first_ref, s32[18]{0:T(128)} %slice.162.second_ref, ...), custom_call_target="tpu_custom_call", output_to_operand_aliasing={{0}: (8, {}), {1}: (9, {}), {2}: (10, {})} | custom-call | flops 5033164800 | bytes 58982400 | tf_op jit(solution)/shard_map/pallas_call | solution.py:1091
  711.4 11.2 %all-to-all-done.5 = bf16[4,292,768]{2,1,0:T(8,128)(2,1)S(1)} async-done(((bf16[4,292,768]{2,1,0:T(8,128)(2,1)}), bf16[4,292,768]{2,1,0:T(8,128)(2,1)S(1)}, u32[]{:S(2)}, u32[]{:S(2)}) %all-to-all-start.5) | async-done | bytes 1794080 | tf_op jit(solution)/shard_map/all_to_all | solution.py:1361
  722.6 2.0 convert_element_type.290
  725.5 2.9 all-to-all-start.6
  728.4 6.0 copy_subtract_fusion
  734.4 3.2 copy.348
  737.6 3.2 copy.350
  740.8 3.2 copy.349
  (270 shorter events, 45.9 us)
Async XLA Ops:
  165.8 5.4 copy-start
  171.2 3.2 copy-start.6
  171.4 4.5 copy-start.1
  171.6 4.3 copy-start.36
  172.0 0.6 copy-start.40
  172.0 6.3 copy-start.38
  174.4 3.9 copy-start.34
  175.9 4.5 copy-start.21
  180.9 7.4 copy-start.8
  184.8 7.4 slice-start
  188.1 0.9 copy-start.10
  188.3 3.9 slice-start.1
  189.0 1.6 copy-start.22
  189.0 4.4 slice-start.2
  189.9 1.7 copy-start.17
  190.6 4.2 slice-start.3
  190.6 4.6 copy-start.20
  192.2 3.9 copy-start.14
  196.1 6.3 copy-start.4
  196.8 5.6 copy-start.26
  202.4 2.7 copy-start.43
  206.7 133.3 %copy-start.19 = (s32[32,128]{1,0:T(8,128)S(1)}, s32[32,128]{1,0:T(8,128)}, u32[]{:S(2)}) copy-start(s32[32,128]{1,0:T(8,128)} %get-tuple-element.270) | copy-start | bytes 49156
  206.7 143.6 %copy-start.15 = (bf16[4,128,12,64]{1,0,3,2:T(4,128)(2,1)S(1)}, bf16[4,128,12,64]{1,0,3,2:T(4,128)(2,1)}, u32[]{:S(2)}) copy-start(bf16[4,128,12,64]{1,0,3,2:T(4,128)(2,1)} %copy-done.14) | copy-start | bytes 2359300
  333.2 12.1 %all-to-all-start.1 = ((f32[32,2,512]{2,1,0:T(2,128)}), f32[32,2,512]{2,1,0:T(2,128)S(1)}, u32[]{:S(2)}, u32[]{:S(2)}) async-start(f32[32,2,512]{2,1,0:T(2,128)} %get-tuple-element.91), calls=%async_computation.1 | async-start | bytes 262144 | tf_op jit(solution)/shard_map/all_to_all | solution.py:1252
  338.8 20.3 %copy-start.42 = (s32[18]{0:T(128)}, s32[18]{0:T(128)S(1)}, u32[]{:S(2)}) copy-start(s32[18]{0:T(128)S(1)} %broadcast_add_fusion.model_ref) | copy-start | bytes 220
  346.2 11.1 %all-to-all-start.2 = ((f32[32,2,512]{2,1,0:T(2,128)}), f32[32,2,512]{2,1,0:T(2,128)S(1)}, u32[]{:S(2)}, u32[]{:S(2)}) async-start(f32[32,2,512]{2,1,0:T(2,128)} %broadcast_in_dim.272), calls=%async_computation.2 | async-start | bytes 262144 | tf_op jit(solution)/shard_map/all_to_all | solution.py:232
  428.3 63.3 %slice-start.4 = ((s8[6291456]{0:T(1024)(128)(4,1)}), s8[2097152]{0:T(1024)(128)(4,1)S(1)}, s32[]{:S(2)}) async-start(s8[6291456]{0:T(1024)(128)(4,1)} %bitcast.259), calls=%async_computation.14 | async-start | bytes 4194304
  490.1 2.2 slice-start.5
  491.7 9.0 %copy-start.28 = (bf16[512,768]{1,0:T(8,128)(2,1)}, bf16[512,768]{1,0:T(8,128)(2,1)S(1)}, u32[]{:S(2)}) copy-start(bf16[512,768]{1,0:T(8,128)(2,1)S(1)} %get-tuple-element.101) | copy-start | bytes 2359300
  492.3 8.4 %copy-start.5 = (f32[512,768]{1,0:T(8,128)S(1)}, f32[512,768]{1,0:T(8,128)}, u32[]{:S(2)}) copy-start(f32[512,768]{1,0:T(8,128)} %copy-done.4) | copy-start | bytes 4718596
  500.7 6.4 copy-start.45
  508.1 0.9 copy-start.30
  516.6 4.4 copy-start.18
  516.6 4.4 copy-start.23
  516.6 4.4 copy-start.25
  521.9 1.1 copy-start.9
  523.0 2.1 copy-start.11
  531.1 2.1 copy-start.16
  532.9 1.4 copy-start.2
  533.0 1.5 copy-start.7
  533.0 1.5 copy-start.35
  533.0 1.4 copy-start.37
  533.0 1.4 copy-start.39
  534.4 5.4 copy-start.12
  534.4 5.4 copy-start.41
  542.4 11.0 %copy-start.13 = (bf16[512,2304]{0,1:T(8,128)(2,1)S(1)}, bf16[512,2304]{0,1:T(8,128)(2,1)}, u32[]{:S(2)}) copy-start(bf16[512,2304]{0,1:T(8,128)(2,1)} %copy-done.12) | copy-start | bytes 7077892
  544.2 28.8 %all-to-all-start.3 = ((bf16[4,128,768]{2,1,0:T(8,128)(2,1)}), bf16[4,128,768]{2,1,0:T(8,128)(2,1)S(1)}, u32[]{:S(2)}, u32[]{:S(2)}) async-start(bf16[4,128,768]{2,1,0:T(8,128)(2,1)} %bitcast.222), calls=%async_computation.3 | async-start | bytes 1572864 | tf_op jit(solution)/shard_map/all_to_all | solution.py:1333
  553.0 120.4 %reduce-scatter.2.cloned.1.call-start = ((), (), s32[]{:S(2)}) async-start(), calls=%async_computation.8 | async-start | bytes 16146432 | tf_op jit(solution)/shard_map/reduce_scatter | solution.py:1342
  553.4 5.1 copy-start.24
  553.4 5.1 copy-start.31
  553.4 6.9 copy-start.46
  558.5 1.8 copy-start.27
  560.3 4.4 copy-start.29
  560.3 4.4 copy-start.44
  616.5 32.6 %all-to-all-start.4 = ((f32[8,1,1344]{2,1,0:T(1,128)}), f32[8,1,1344]{2,1,0:T(1,128)S(1)}, u32[]{:S(2)}, u32[]{:S(2)}) async-start(f32[8,1,1344]{2,1,0:T(1,128)} %all_to_all.30), calls=%async_computation.5 | async-start | bytes 90112 | tf_op jit(solution)/shard_map/all_to_all | solution.py:1347
  675.9 46.7 %all-to-all-start.5 = ((bf16[4,292,768]{2,1,0:T(8,128)(2,1)}), bf16[4,292,768]{2,1,0:T(8,128)(2,1)S(1)}, u32[]{:S(2)}, u32[]{:S(2)}) async-start(bf16[4,292,768]{2,1,0:T(8,128)(2,1)} %reshape.787), calls=%async_computation.6 | async-start | bytes 3637248 | tf_op jit(solution)/shard_map/all_to_all | solution.py:1361
  725.5 18.6 %all-to-all-start.6 = ((f32[32,1,1344]{2,1,0:T(1,128)}), f32[32,1,1344]{2,1,0:T(1,128)S(1)}, u32[]{:S(2)}, u32[]{:S(2)}) async-start(f32[32,1,1344]{2,1,0:T(1,128)} %broadcast_in_dim.289), calls=%async_computation.7 | async-start | bytes 360448 | tf_op jit(solution)/shard_map/all_to_all | solution.py:232
  728.4 6.1 copy-start.3
  740.8 4.6 copy-start.32
  740.8 4.6 copy-start.33
Sparse Core Ops, SparseCore 1:
  573.1 100.2 reduce-scatter.1

commit v9 on v8

--- a/solution.py
+++ b/solution.py
@@ -296,6 +296,21 @@
     pl.semaphore_wait(barrier, len(peers))
 
 
+def greet_all(devices, members):
+    barrier = pltpu.get_barrier_semaphore()
+    me = lax.axis_index("grp") * members + lax.axis_index("cli")
+
+    def hello(j, carry):
+        other = lax.rem(me + j, devices)
+        pl.semaphore_signal(
+            barrier, inc=1, device_id=(lax.div(other, members), lax.rem(other, members)), device_id_type=MESH
+        )
+        return carry
+
+    lax.fori_loop(1, devices, hello, 0)
+    pl.semaphore_wait(barrier, devices - 1)
+
+
 def spread_sems(groups, members, pieces):
     xs, ys, items = groups // 4, 2, members * pieces
     dma = pltpu.SemaphoreType.DMA
@@ -657,13 +672,14 @@
     )(facts, table)
 
 
-def score_kernel(groups, members, share, pieces, src, table, target, out, stat, *rest):
-    part, pool, part_sem, out_sems = rest[:4]
-    sems = rest[4:]
+def score_kernel(groups, members, share, pieces, src, table, target, out, answer, *rest):
+    part, pool, stat, inbox, part_sem, out_sems, go_send, go_recv, back_send, back_recv = rest[:10]
+    sems = rest[10:]
+    devices = groups * members
     place = Place(groups, members)
     load_table = pltpu.make_async_copy(table, part, part_sem)
     load_table.start()
-    greet(place)
+    greet_all(devices, members)
     rows = pool.shape[1]
     size = rows // pieces
 
@@ -696,6 +712,49 @@
 
     spread_body(place, True, pieces, src, pool, sems, consume, load_table.wait)
 
+    me = place.block(0, 0, place.cli)
+
+    def device(index):
+        return (lax.div(index, members), lax.rem(index, members))
+
+    def ahead(j):
+        return lax.rem(me + j, devices)
+
+    def behind(j):
+        return lax.rem(me + devices - j, devices)
+
+    def go(j, source, target):
+        return pltpu.make_async_remote_copy(
+            src_ref=stat.at[source], dst_ref=inbox.at[target], send_sem=go_send.at[j], recv_sem=go_recv.at[j],
+            device_id=device(ahead(j)), device_id_type=MESH,
+        )
+
+    def back(j, source):
+        return pltpu.make_async_remote_copy(
+            src_ref=answer.at[source], dst_ref=answer.at[source], send_sem=back_send.at[j],
+            recv_sem=back_recv.at[j], device_id=device(ahead(j)), device_id_type=MESH,
+        )
+
+    def loop(step):
+        def run(j, carry):
+            step(j)
+            return carry
+
+        lax.fori_loop(1, devices, run, 0)
+
+    loop(lambda j: go(j, ahead(j), me).start())
+    inbox[me] = stat[me]
+    loop(lambda j: go(j, me, behind(j)).wait_recv())
+    logs = inbox[:, 0, :]
+    top = jnp.max(logs, axis=0, keepdims=True)
+    log_total = top + jnp.log(jnp.sum(jnp.exp(logs - top), axis=0, keepdims=True))
+    answer[me, 0:1, :] = log_total
+    answer[me, 1:2, :] = log_total - jnp.sum(inbox[:, 1, :], axis=0, keepdims=True)
+    loop(lambda j: back(j, me).start())
+    loop(lambda j: back(j, behind(j)).wait_recv())
+    loop(lambda j: go(j, ahead(j), me).wait_send())
+    loop(lambda j: back(j, me).wait_send())
+
     def close(block, carry):
         for piece in range(pieces):
             keep(block, piece).wait()
@@ -722,9 +781,12 @@
         scratch_shapes=[
             pltpu.VMEM(table_low.shape, table_low.dtype),
             pltpu.VMEM((blocks, rows, width), src.dtype),
+            pltpu.VMEM((blocks, 2, rows), jnp.float32),
+            pltpu.VMEM((blocks, 2, rows), jnp.float32),
             pltpu.SemaphoreType.DMA,
             pltpu.SemaphoreType.DMA((blocks, pieces)),
         ]
+        + [pltpu.SemaphoreType.DMA((blocks,))] * 4
         + spread_sems(groups, members, pieces),
         compiler_params=pltpu.CompilerParams(
             collective_id=collective_id, has_side_effects=True, vmem_limit_bytes=60 * MIB
@@ -929,12 +991,11 @@
     step = pl.program_id(0)
     owners, slab, width = pool_ref.shape
     weights_ref[...] = jnp.concatenate([pool_ref[j, :part] for j in range(owners)], axis=0)
-    columns = lax.broadcasted_iota(jnp.int32, (at_ref.shape[0], slab - start), 1) + start
-    found = jnp.zeros(rows_ref.shape, jnp.float32)
-    for j in range(owners):
-        at = at_ref[...] - (step * owners + j) * slab
-        hits = (columns == at).astype(jnp.float32).astype(jnp.bfloat16)
-        found = found + product(hits, pool_ref[j, start:])
+    count = slab - start
+    columns = lax.broadcasted_iota(jnp.int32, (1, count), 1) + start
+    columns = jnp.concatenate([columns + j * slab for j in range(owners)], axis=1)
+    hits = (columns == at_ref[...] - step * owners * slab).astype(jnp.float32).astype(jnp.bfloat16)
+    found = product(hits, jnp.concatenate([pool_ref[j, start:] for j in range(owners)], axis=0))
 
     @pl.when(step == 0)
     def begin():
@@ -947,7 +1008,7 @@
 
 def unpack(pool, part, at):
     devices, slab, width = pool.shape
-    owners = 8 // math.gcd(part, 8)
+    owners = max(4, 8 // math.gcd(part, 8))
     start = part // 16 * 16
     tokens = at.shape[0]
     return pl.pallas_call(
@@ -1243,16 +1304,16 @@
     target_local = jnp.where((target_local >= 0) & (target_local < block_rows), target_local, -1)
     target_blocks = target_local.reshape(groups * share, 1, local * seq_len)
     if devices * normed_out.size * 2 <= POOL_BYTES:
-        outs_all, stats = spread_score(
+        outs_all, everything = spread_score(
             normed_out[None], table_low, target_blocks, groups, members, share, 2
         )
     else:
         outs_all = spread(normed_out[None], groups, members, 2, True, 2)
         stats = head_stats(outs_all, table_low, target_blocks, groups, members, share)
-    shares = lax.all_to_all(stats, both, 0, 0, tiled=True)
-    log_total = jax.nn.logsumexp(shares[:, 0], axis=0)
-    token_loss = log_total - jnp.sum(shares[:, 1], axis=0)
-    everything = share_all(jnp.stack([log_total, token_loss]), both, devices)
+        shares = lax.all_to_all(stats, both, 0, 0, tiled=True)
+        log_total = jax.nn.logsumexp(shares[:, 0], axis=0)
+        token_loss = log_total - jnp.sum(shares[:, 1], axis=0)
+        everything = share_all(jnp.stack([log_total, token_loss]), both, devices)
     everything = (
         everything.reshape(groups, models, share, 2, local, seq_len)
         .transpose(3, 1, 0, 2, 4, 5)

time: 764 us -> 765 us (level)
  waiting for transfers between devices: 46.7 us -> 37.1 us
  Pallas kernels: 490 us -> 499 us
    pallas_call x1, Pallas kernels: 127 us -> 140 us  [spread_score(): pl.pallas_call(functools.partial(score_kernel, groups, members, share, pi...]
    unnamed x120 -> x143, local copies, waits for them, and re-layouts: 27.3 us -> 27.8 us
  transfers between devices with their start and end apart: 7 -> 5, of which waited for: 5 -> 3; matrix products, arithmetic and copies ran while one was open for 6% -> 5% of each run, Pallas kernels for 13% -> 13%
where the time goes in v9:
time: 765 us; the launch traced here: 755 us
  Pallas kernels  499 us (65%)
  matrix products  77.7 us (10%)
  local copies, waits for them, and re-layouts  67.3 us (9%)
  waiting for transfers between devices  37.1 us (5%)
  other arithmetic  36 us (5%)
  starting transfers between devices  19.3 us (3%)
  between operations  18.3 us (2%)
    pallas_call x1, Pallas kernels, spread_score(): pl.pallas_call(functools.partial(score_kernel, groups, members, share, pi...  140 us
    pallas_call x2, Pallas kernels, spread(): pl.pallas_call(functools.partial(spread_kernel, groups, members, chain, p...  139 us
    pallas_call x1, Pallas kernels, head_back(): pl.pallas_call(back_kernel, out_shape=(jax.ShapeDtypeStruct((2 * steps, s...  69.7 us
    pallas_call x1, Pallas kernels, collect(): pl.pallas_call(functools.partial(collect_kernel, groups, members), out_sh...  61.3 us
    pallas_call x2, Pallas kernels, finish_table(): pl.pallas_call(functools.partial(finish_kernel, first_model), out_shape=(...  59.5 us
    unnamed x143, local copies, waits for them, and re-layouts  27.8 us
    dot_general x6, matrix products, project(): lax.dot_general(inputs, matrix, (((1,), (1,)), ((), ())), preferred_eleme...  23.9 us
    reduce_scatter x1, waiting for transfers between devices, body(): lax.psum_scatter(stack_rows, 'grp', scatter_dimension=0, tiled=True)  23 us
  transfers between devices with their start and end apart: 5, of which 3 were waited for; matrix products, arithmetic and copies ran while one was open for 5% of the time, Pallas kernels for 13%

profile of v9, /device:TPU:0, one launch (start us, length us, event | category | flops | bytes accessed | tf_op | source)
XLA Modules:
  0.0 755.1 jit_solution(13708354960978502245)
XLA Ops:
  10.0 18.1 %shard_map.185 = (s32[32,1,512]{2,1,0:T(1,128)}, bf16[4,1600,768]{2,1,0:T(8,128)(2,1)}) custom-call(s32[1,512]{1,0:T(1,128)} %bitcast.237, f32[4,1600,768]{2,1,0:T(8,128)} %table_ref.5), custom_call_target="tpu_custom_call" | custom-call | bytes 29491200 | tf_op jit(solution)/shard_map/pallas_call | solution.py:660
  34.0 2.6 convert_element_type.237
  41.1 2.6 fusion.135
  46.8 5.3 fusion.44
  52.1 1.6 pad_maximum_fusion.src
  53.8 99.9 %shard_map.186.pool_ref = bf16[32,400,768]{2,1,0:T(8,128)(2,1)} custom-call(bf16[4,400,768]{2,1,0:T(8,128)(2,1)} %pad_maximum_fusion.src), custom_call_target="tpu_custom_call" | custom-call | bytes 39321600 | tf_op jit(solution)/shard_map/pallas_call | solution.py:579
  153.8 12.0 %shard_map.187 = (bf16[9344,768]{1,0:T(8,128)(2,1)S(1)}, f32[512,768]{1,0:T(8,128)S(1)}) custom-call(s32[512,1]{1,0:T(8,128)S(1)} %fusion.74.at_ref, bf16[32,400,768]{2,1,0:T(8,128)(2,1)} %shard_map.186.pool_ref), custom_call_target="tpu_custom_call" | custom-call | flops 2818572288 | bytes 39321600 | tf_op jit(solution)/shard_map/pallas_call | solution.py:1014
  165.8 5.3 copy-done
  173.3 1.6 fusion.98
  174.9 1.5 add_convert_fusion.4
  176.4 3.2 convolution_convert_fusion.6
  179.7 3.0 add_convert_fusion.2
  182.6 1.5 copy.256
  184.1 1.1 reshape.724
  185.2 3.0 add_convert_fusion.3
  188.2 1.4 copy.255
  189.6 1.1 reshape.723
  190.7 2.4 copy.257
  193.1 2.6 reshape.725
  195.9 2.1 fusion.65
  201.3 1.0 copy.349
  205.4 5.6 multiply_convert_fusion
  211.0 2.7 fusion.138
  214.9 1.2 fusion.54.src
  216.1 140.2 %shard_map.188 = (bf16[32,512,768]{2,1,0:T(8,128)(2,1)}, f32[32,2,512]{2,1,0:T(2,128)}) custom-call(bf16[1,512,768]{2,1,0:T(8,128)(2,1)} %fusion.54.src, bf16[4,1600,768]{2,1,0:T(8,128)(2,1)} %get-tuple-element.373, s32[8,1,512]{2,1,0:T(1,128)} %bitcast.218), custom_call_target="tpu_custom_call" | custom-call | flops 40265318400 | bytes 50331648 | tf_op jit(solution)/shard_map/pallas_call | solution.py:769
  356.3 1.0 reshape.727
  359.5 69.7 %shard_map.189 = (bf16[36,128,768]{2,1,0:T(8,128)(2,1)}, f32[4,1600,768]{2,1,0:T(8,128)}) custom-call(s32[18]{0:T(128)} %copy-done.53, s32[18]{0:T(128)} %add_convert_fusion.6.fresh_ref, s32[18]{0:T(128)} %slice.157.first_ref, s32[18]{0:T(128)} %slice.158.second_ref, s32[36]{0:T(128)} %get-tuple-element.268.place_ref, bf16[128,128,768]{2,1,0:T(8,128)(2,1)} %bitcast.243, ...), custom_call_target="tpu_custom_call" | custom-call | flops 33973862400 | bytes 43646976 | tf_op jit(solution)/shard_map/pallas_call | solution.py:1090
  429.2 61.3 %shard_map.190 = bf16[4,128,768]{2,1,0:T(8,128)(2,1)} custom-call(bf16[36,128,768]{2,1,0:T(8,128)(2,1)} %get-tuple-element.93.source), custom_call_target="tpu_custom_call" | custom-call | bytes 12582912 | tf_op jit(solution)/shard_map/pallas_call | solution.py:962
  490.5 1.5 fusion.127
  494.3 8.1 %convert_reduce_fusion = (f32[3072]{0:T(1024)S(1)}, bf16[512,3072]{1,0:T(8,128)(2,1)S(1)}) fusion(f32[512,3072]{1,0:T(8,128)S(1)} %bitcast.246, f32[3072]{0:T(1024)S(1)} %bitcast.235, bf16[512,768]{1,0:T(8,128)(2,1)S(1)} %get-tuple-element.101, bf16[9344,768]{1,0:T(8,128)(2,1)} %copy-done), kind=kOutput, calls=%fused_computation.32 | convolution fusion | flops 2452091904 | bytes 14966784 | tf_op jit(solution)/shard_map/dot_general | solution.py:37
  502.5 6.4 multiply_reduce_fusion.1
  509.6 1.1 copy-done.6
  511.9 2.9 convolution_convert_fusion.5
  514.8 2.3 copy.265
  517.1 2.6 reshape.733
  519.8 4.4 convert_reduce_fusion.3
  526.1 2.1 fusion.43
  528.2 1.4 convert_reduce_fusion.4
  529.8 2.7 copy.276
  532.5 1.8 copy.270
  534.3 1.8 copy.273
  537.1 5.3 multiply_reduce_fusion.2
  543.9 1.3 fusion.130
  545.3 8.1 %all-to-all-start.1 = ((bf16[4,128,768]{2,1,0:T(8,128)(2,1)}), bf16[4,128,768]{2,1,0:T(8,128)(2,1)S(1)}, u32[]{:S(2)}, u32[]{:S(2)}) async-start(bf16[4,128,768]{2,1,0:T(8,128)(2,1)} %bitcast.211), calls=%async_computation.1 | async-start | bytes 1572864 | tf_op jit(solution)/shard_map/all_to_all | solution.py:1394
  553.7 5.6 fusion.17
  559.3 1.8 fusion.37
  561.2 4.4 fusion.16
  565.6 4.4 fusion.15
  570.7 2.3 all-to-all-done.1
  574.9 1.3 fusion.119.start_ref
  577.0 38.7 %shard_map.191.d_ref = bf16[32,128,768]{2,1,0:T(8,128)(2,1)} custom-call(bf16[1,128,768]{2,1,0:T(8,128)(2,1)} %bitcast.220), custom_call_target="tpu_custom_call" | custom-call | bytes 12582912 | tf_op jit(solution)/shard_map/pallas_call | solution.py:579
  616.4 3.3 all-to-all-start.2
  619.8 30.6 %shard_map.192 = (f32[4,1600,768]{2,1,0:T(8,128)}, f32[4,1600,768]{2,1,0:T(8,128)}, f32[4,1600,768]{2,1,0:T(8,128)}) custom-call(s32[5]{0:T(128)} %fusion.119.start_ref, s32[18]{0:T(128)} %slice.153.first_ref, s32[18]{0:T(128)} %slice.154.second_ref, bf16[32,128,768]{2,1,0:T(8,128)(2,1)} %shard_map.191.d_ref, s32[18,1,256]{2,1,0:T(1,128)} %reshape.743.ids_ref, ...), custom_call_target="tpu_custom_call" | custom-call | flops 5033164800 | bytes 58982400 | tf_op jit(solution)/shard_map/pallas_call | solution.py:1152
  650.3 23.0 %reduce-scatter.2.cloned.1.call-done = bf16[1168,768]{1,0:T(8,128)(2,1)} async-done(((bf16[9344,768]{1,0:T(8,128)(2,1)}), bf16[1168,768]{1,0:T(8,128)(2,1)}) %reduce-scatter.2.cloned.1.call-update) | async-done | bytes 1794064 | tf_op jit(solution)/shard_map/reduce_scatter | solution.py:1403
  673.4 2.6 reshape.744
  675.9 4.6 all-to-all-start.3
  682.1 28.9 %shard_map.193 = (f32[4,1600,768]{2,1,0:T(8,128)}, f32[4,1600,768]{2,1,0:T(8,128)}, f32[4,1600,768]{2,1,0:T(8,128)}) custom-call(s32[5]{0:T(128)} %fusion.119.start_ref, s32[18]{0:T(128)} %slice.153.first_ref, s32[18]{0:T(128)} %slice.154.second_ref, ...), custom_call_target="tpu_custom_call", output_to_operand_aliasing={{0}: (8, {}), {1}: (9, {}), {2}: (10, {})} | custom-call | flops 5033164800 | bytes 58982400 | tf_op jit(solution)/shard_map/pallas_call | solution.py:1152
  710.9 11.7 %all-to-all-done.3 = bf16[4,292,768]{2,1,0:T(8,128)(2,1)S(1)} async-done(((bf16[4,292,768]{2,1,0:T(8,128)(2,1)}), bf16[4,292,768]{2,1,0:T(8,128)(2,1)S(1)}, u32[]{:S(2)}, u32[]{:S(2)}) %all-to-all-start.3) | async-done | bytes 1794080 | tf_op jit(solution)/shard_map/all_to_all | solution.py:1422
  722.7 2.0 convert_element_type.290
  725.5 3.0 all-to-all-start.4
  728.5 6.0 copy_subtract_fusion
  734.5 3.2 copy.282
  737.7 3.2 copy.284
  740.9 3.2 copy.283
  (278 shorter events, 44.3 us)
Async XLA Ops:
  29.1 1.5 copy-start.38
  30.4 1.2 copy-start.46
  30.5 7.0 copy-start.40
  30.6 8.8 %copy-start.42 = (pred[36]{0:T(512)(128)(4,1)}, pred[36]{0:T(512)(128)(4,1)S(1)}, u32[]{:S(2)}) copy-start(pred[36]{0:T(512)(128)(4,1)S(1)} %fusion.87) | copy-start | bytes 112
  30.7 5.9 copy-start.51
  30.8 6.8 copy-start.34
  30.9 8.5 %copy-start.48 = (pred[36]{0:T(512)(128)(4,1)}, pred[36]{0:T(512)(128)(4,1)S(1)}, u32[]{:S(2)}) copy-start(pred[36]{0:T(512)(128)(4,1)S(1)} %compare_and_fusion.3) | copy-start | bytes 112
  33.9 5.0 copy-start.16
  165.8 5.4 copy-start
  171.2 3.7 copy-start.8
  176.4 3.3 copy-start.18
  182.6 2.6 copy-start.19
  190.7 11.6 %slice-start = ((s8[14352384]{0:T(1024)(128)(4,1)}), s8[1769472]{0:T(1024)(128)(4,1)S(1)}, s32[]{:S(2)}) async-start(s8[14352384]{0:T(1024)(128)(4,1)} %bitcast.208), calls=%async_computation.8 | async-start | bytes 3538944
  195.9 6.4 slice-start.1
  198.1 4.3 slice-start.2
  199.0 1.7 copy-start.14
  199.2 3.9 slice-start.3
  200.7 3.1 copy-start.17
  200.7 3.1 copy-start.45
  204.7 6.3 copy-start.4
  205.4 5.7 copy-start.25
  205.4 5.7 copy-start.44
  211.0 2.7 copy-start.55
  213.8 1.1 copy-start.2
  216.1 142.0 %copy-start.43 = (pred[36]{0:T(512)(128)(4,1)S(1)}, pred[36]{0:T(512)(128)(4,1)}, u32[]{:S(2)}) copy-start(pred[36]{0:T(512)(128)(4,1)} %copy-done.42) | copy-start | bytes 112
  216.1 142.0 %copy-start.49 = (pred[36]{0:T(512)(128)(4,1)S(1)}, pred[36]{0:T(512)(128)(4,1)}, u32[]{:S(2)}) copy-start(pred[36]{0:T(512)(128)(4,1)} %copy-done.48) | copy-start | bytes 112
  216.1 142.2 %copy-start.54 = (pred[17]{0:T(512)(128)(4,1)S(1)}, pred[17]{0:T(512)(128)(4,1)}, u32[]{:S(2)}) copy-start(pred[17]{0:T(512)(128)(4,1)} %slice_compare_fusion.1) | copy-start | bytes 55
  429.2 61.3 %copy-start.50 = (pred[4]{0:T(512)(128)(4,1)S(1)}, pred[4]{0:T(512)(128)(4,1)}, u32[]{:S(2)}) copy-start(pred[4]{0:T(512)(128)(4,1)} %fusion.113) | copy-start | bytes 16
  429.2 64.5 %slice-start.4 = ((s8[6291456]{0:T(1024)(128)(4,1)}), s8[2097152]{0:T(1024)(128)(4,1)S(1)}, s32[]{:S(2)}) async-start(s8[6291456]{0:T(1024)(128)(4,1)} %bitcast.245), calls=%async_computation.12 | async-start | bytes 4194304
  490.5 1.6 copy-start.3
  492.2 2.2 slice-start.5
  493.7 8.8 %copy-start.27 = (bf16[512,768]{1,0:T(8,128)(2,1)}, bf16[512,768]{1,0:T(8,128)(2,1)S(1)}, u32[]{:S(2)}) copy-start(bf16[512,768]{1,0:T(8,128)(2,1)S(1)} %get-tuple-element.101) | copy-start | bytes 2359300
  494.3 8.1 %copy-start.5 = (f32[512,768]{1,0:T(8,128)S(1)}, f32[512,768]{1,0:T(8,128)}, u32[]{:S(2)}) copy-start(f32[512,768]{1,0:T(8,128)} %copy-done.4) | copy-start | bytes 4718596
  502.5 6.4 copy-start.57
  509.6 1.1 copy-start.6
  519.7 4.4 copy-start.15
  519.7 4.4 copy-start.23
  519.8 4.4 copy-start.24
  526.1 2.1 copy-start.11
  534.3 2.1 copy-start.13
  537.1 5.3 copy-start.12
  537.1 5.4 copy-start.37
  542.5 1.4 copy-start.7
  545.2 8.5 %copy-start.20 = (bf16[512,768]{1,0:T(8,128)(2,1)S(1)}, bf16[512,768]{1,0:T(8,128)(2,1)}, u32[]{:S(2)}) copy-start(bf16[512,768]{1,0:T(8,128)(2,1)} %copy-done.18) | copy-start | bytes 2359300
  545.3 27.7 %all-to-all-start.1 = ((bf16[4,128,768]{2,1,0:T(8,128)(2,1)}), bf16[4,128,768]{2,1,0:T(8,128)(2,1)S(1)}, u32[]{:S(2)}, u32[]{:S(2)}) async-start(bf16[4,128,768]{2,1,0:T(8,128)(2,1)} %bitcast.211), calls=%async_computation.1 | async-start | bytes 1572864 | tf_op jit(solution)/shard_map/all_to_all | solution.py:1394
  553.4 120.0 %reduce-scatter.2.cloned.1.call-start = ((), (), s32[]{:S(2)}) async-start(), calls=%async_computation.6 | async-start | bytes 16146432 | tf_op jit(solution)/shard_map/reduce_scatter | solution.py:1403
  553.7 5.6 copy-start.21
  553.7 5.6 copy-start.30
  553.7 7.4 copy-start.58
  559.3 1.8 copy-start.26
  561.1 4.4 copy-start.28
  561.1 4.4 copy-start.56
  570.7 2.4 copy-start.52
  570.7 3.6 copy-start.33
  570.7 4.2 copy-start.47
  616.4 33.9 %all-to-all-start.2 = ((f32[8,1,1344]{2,1,0:T(1,128)}), f32[8,1,1344]{2,1,0:T(1,128)S(1)}, u32[]{:S(2)}, u32[]{:S(2)}) async-start(f32[8,1,1344]{2,1,0:T(1,128)} %all_to_all.22), calls=%async_computation.3 | async-start | bytes 90112 | tf_op jit(solution)/shard_map/all_to_all | solution.py:1408
  675.9 4.6 copy-start.41
  675.9 4.8 copy-start.39
  675.9 5.5 copy-start.35
  675.9 46.7 %all-to-all-start.3 = ((bf16[4,292,768]{2,1,0:T(8,128)(2,1)}), bf16[4,292,768]{2,1,0:T(8,128)(2,1)S(1)}, u32[]{:S(2)}, u32[]{:S(2)}) async-start(bf16[4,292,768]{2,1,0:T(8,128)(2,1)} %reshape.744), calls=%async_computation.4 | async-start | bytes 3637248 | tf_op jit(solution)/shard_map/all_to_all | solution.py:1422
  725.5 18.6 %all-to-all-start.4 = ((f32[32,1,1344]{2,1,0:T(1,128)}), f32[32,1,1344]{2,1,0:T(1,128)S(1)}, u32[]{:S(2)}, u32[]{:S(2)}) async-start(f32[32,1,1344]{2,1,0:T(1,128)} %broadcast_in_dim.274), calls=%async_computation.5 | async-start | bytes 360448 | tf_op jit(solution)/shard_map/all_to_all | solution.py:232
  728.5 6.1 copy-start.1
  740.9 4.6 copy-start.31
  740.9 4.6 copy-start.32
  (6 other events, 5.7 us)
Sparse Core Ops, SparseCore 1:
  573.1 100.2 reduce-scatter.1

commit v10 on v9

--- a/solution.py
+++ b/solution.py
@@ -22,6 +22,7 @@
 SLAB_STEP = 16
 TILE = 400
 LANES = 128
+QUAD = 4
 MIB = 1 << 20
 POOL_BYTES = 32 * MIB
 MESH = pl.DeviceIdType.MESH
@@ -1036,93 +1037,102 @@
 
 
 def back_kernel(
-    model_ref, fresh_ref, first_ref, second_ref, place_ref, a_ref, b_ref, table_ref, info_ref, target_ref, d_outs_ref,
-    grad_ref, held, sems,
+    model_ref, fresh_ref, used_ref, piece_ref, place_ref, *rest
 ):
+    pieces = rest[:QUAD]
+    table_ref, info_ref, target_ref, d_outs_ref, grad_ref, held, sems = rest[QUAD:]
     step = pl.program_id(0)
-    steps = pl.num_programs(0)
-    seq_len = a_ref.shape[1]
+    seq_len = pieces[0].shape[1]
     slot = lax.rem(step, 2)
 
-    def leave(which, where, half):
-        return pltpu.make_async_copy(
-            held.at[which, half], d_outs_ref.at[where], sems.at[which, half]
-        )
-
-    @pl.when(step >= 2)
-    def reuse():
-        leave(slot, 0, 0).wait()
-        leave(slot, 0, 1).wait()
-    outs = jnp.concatenate([a_ref[0], b_ref[0]], axis=0)
-    @pl.when(fresh_ref[step] == 1)
-    def start():
-        grad_ref[...] = jnp.zeros_like(grad_ref)
-
-    part_rows = table_ref.shape[1]
-    size = tile_of(part_rows)
-    d_outs = jnp.zeros((2 * seq_len, outs.shape[1]), jnp.float32)
-    for first_row in range(0, part_rows, size):
-        here = pl.ds(first_row, size)
-        table_rows = table_ref[0, here]
-        logits = project(table_rows, outs)
-        rows = lax.broadcasted_iota(jnp.int32, logits.shape, 0) + first_row
-        soft = jnp.exp(logits - info_ref[0, 0:1, :])
-        soft = jnp.where(rows == target_ref[0], soft - 1.0, soft)
-        d_logits = (info_ref[0, 1:2, :] * soft).astype(jnp.bfloat16)
-        d_outs = d_outs + outer_rows(d_logits, table_rows)
-        grad_ref[0, here] += product(d_logits, outs)
-    held[slot, 0] = d_outs[:seq_len].astype(held.dtype)
-    held[slot, 1] = d_outs[seq_len:].astype(held.dtype)
-    leave(slot, place_ref[2 * step], 0).start()
-    leave(slot, place_ref[2 * step + 1], 1).start()
-
-    @pl.when(step == steps - 1)
-    def drain():
-        for which in range(2):
-            leave(which, 0, 0).wait()
-            leave(which, 0, 1).wait()
-
-
-def head_back(outs_pieces, table_low, model_of, fresh, first, second, place, info, target):
+    def leave(which, where, i):
+        return pltpu.make_async_copy(held.at[which, i], d_outs_ref.at[where], sems.at[which, i])
+
+    def settle(which):
+        for i in range(QUAD):
+            leave(which, 0, i).wait()
+
+    @pl.when(step < used_ref[0])
+    def work():
+        @pl.when(step >= 2)
+        def reuse():
+            settle(slot)
+
+        @pl.when(fresh_ref[step] == 1)
+        def start():
+            grad_ref[...] = jnp.zeros_like(grad_ref)
+
+        outs = jnp.concatenate([piece[0] for piece in pieces], axis=0)
+        part_rows = table_ref.shape[1]
+        size = tile_of(part_rows)
+        d_outs = jnp.zeros(outs.shape, jnp.float32)
+        for first_row in range(0, part_rows, size):
+            here = pl.ds(first_row, size)
+            table_rows = table_ref[0, here]
+            logits = project(table_rows, outs)
+            rows = lax.broadcasted_iota(jnp.int32, logits.shape, 0) + first_row
+            soft = jnp.exp(logits - info_ref[0, 0:1, :])
+            soft = jnp.where(rows == target_ref[0], soft - 1.0, soft)
+            d_logits = (info_ref[0, 1:2, :] * soft).astype(jnp.bfloat16)
+            d_outs = d_outs + outer_rows(d_logits, table_rows)
+            grad_ref[0, here] += product(d_logits, outs)
+        for i in range(QUAD):
+            held[slot, i] = d_outs[i * seq_len : (i + 1) * seq_len].astype(held.dtype)
+            leave(slot, place_ref[QUAD * step + i], i).start()
+
+        @pl.when(step == used_ref[0] - 1)
+        def drain():
+            settle(slot)
+
+            @pl.when(step >= 1)
+            def earlier():
+                settle(1 - slot)
+
+
+def head_back(outs_pieces, table_low, model_of, fresh, used, piece_at, place, info, target):
     steps = model_of.shape[0]
     models, part_rows, width = table_low.shape
     seq_len = outs_pieces.shape[1]
+    tokens = QUAD * seq_len
+
+    def piece(i):
+        return pl.BlockSpec((1, seq_len, width), lambda s, m, f, u, q, p: (q[QUAD * s + i], 0, 0))
+
     return pl.pallas_call(
         back_kernel,
         out_shape=(
-            jax.ShapeDtypeStruct((2 * steps, seq_len, width), jnp.bfloat16),
+            jax.ShapeDtypeStruct((QUAD * steps, seq_len, width), jnp.bfloat16),
             jax.ShapeDtypeStruct((models, part_rows, width), jnp.float32),
         ),
         grid_spec=pltpu.PrefetchScalarGridSpec(
             num_scalar_prefetch=5,
             grid=(steps,),
-            in_specs=[
-                pl.BlockSpec((1, seq_len, width), lambda s, m, f, a, b, p: (a[s], 0, 0)),
-                pl.BlockSpec((1, seq_len, width), lambda s, m, f, a, b, p: (b[s], 0, 0)),
-                pl.BlockSpec((1, part_rows, width), lambda s, m, f, a, b, p: (m[s], 0, 0)),
-                pl.BlockSpec((1, 2, 2 * seq_len), lambda s, m, f, a, b, p: (s, 0, 0)),
-                pl.BlockSpec((1, 1, 2 * seq_len), lambda s, m, f, a, b, p: (s, 0, 0)),
+            in_specs=[piece(i) for i in range(QUAD)]
+            + [
+                pl.BlockSpec((1, part_rows, width), lambda s, m, *_: (m[s], 0, 0)),
+                pl.BlockSpec((1, 2, tokens), lambda s, *_: (s, 0, 0)),
+                pl.BlockSpec((1, 1, tokens), lambda s, *_: (s, 0, 0)),
             ],
             out_specs=(
                 pl.BlockSpec(memory_space=pl.ANY),
-                pl.BlockSpec((1, part_rows, width), lambda s, m, f, a, b, p: (m[s], 0, 0)),
+                pl.BlockSpec((1, part_rows, width), lambda s, m, *_: (m[s], 0, 0)),
             ),
             scratch_shapes=[
-                pltpu.VMEM((2, 2, seq_len, width), jnp.bfloat16),
-                pltpu.SemaphoreType.DMA((2, 2)),
+                pltpu.VMEM((2, QUAD, seq_len, width), jnp.bfloat16),
+                pltpu.SemaphoreType.DMA((2, QUAD)),
             ],
         ),
         compiler_params=pltpu.CompilerParams(vmem_limit_bytes=56 * MIB),
         cost_estimate=pl.CostEstimate(
-            flops=12 * steps * seq_len * part_rows * width,
-            bytes_accessed=4 * steps * seq_len * width * 2 + 6 * table_low.size,
-            transcendentals=2 * steps * seq_len * part_rows,
-        ),
-    )(model_of, fresh, first, second, place, outs_pieces, outs_pieces, table_low, info, target)
+            flops=6 * steps * tokens * part_rows * width,
+            bytes_accessed=4 * steps * tokens * width + 6 * table_low.size,
+            transcendentals=steps * tokens * part_rows,
+        ),
+    )(model_of, fresh, used, piece_at, place, *([outs_pieces] * QUAD), table_low, info, target)
 
 
 def finish_kernel(
-    first_model, start_ref, first_ref, second_ref, d_ref, ids_ref, head_ref, table_ref, momentum_ref, *rest
+    first_model, start_ref, end_ref, first_ref, second_ref, d_ref, ids_ref, head_ref, table_ref, momentum_ref, *rest
 ):
     grad_ref, momentum_new_ref, table_new_ref = rest[-3:]
     model = pl.program_id(0) + first_model
@@ -1137,7 +1147,7 @@
         grad_ref[0] += product(hits, outs)
         return carry
 
-    lax.fori_loop(start_ref[model], start_ref[model + 1], pair, 0)
+    lax.fori_loop(start_ref[model], end_ref[model], pair, 0)
     renewed, fresh_table = update(table_ref[0], momentum_ref[0], grad_ref[0], table_rate)
     momentum_new_ref[0] = renewed
     table_new_ref[0] = fresh_table
@@ -1153,13 +1163,13 @@
         functools.partial(finish_kernel, first_model),
         out_shape=(state, state, state),
         grid_spec=pltpu.PrefetchScalarGridSpec(
-            num_scalar_prefetch=3,
+            num_scalar_prefetch=4,
             grid=(count, part_rows // tile_rows),
             in_specs=[whole, whole, piece, piece, piece]
             + [pl.BlockSpec(memory_space=pl.ANY)] * len(earlier),
             out_specs=(piece, piece, piece),
         ),
-        input_output_aliases={8 + i: i for i in range(len(earlier))},
+        input_output_aliases={9 + i: i for i in range(len(earlier))},
         compiler_params=pltpu.CompilerParams(vmem_limit_bytes=56 * MIB),
         cost_estimate=pl.CostEstimate(
             flops=2 * d_inputs.size * part_rows * count // models,
@@ -1327,7 +1337,7 @@
     chosen_total = jnp.sum(choice_table.T[:, :, None] * everything[0], axis=0)
 
     numbers = jnp.sum(choice_table, axis=0)
-    padded = 2.0 * jnp.ceil(numbers / 2.0)
+    padded = QUAD * jnp.ceil(numbers / QUAD)
     offsets = jnp.cumsum(padded) - padded
     earlier = (
         jnp.arange(devices)[None, :] < jnp.arange(devices)[:, None]
@@ -1335,14 +1345,16 @@
     slot_of = jnp.sum(choice_table * offsets[None, :], axis=1) + jnp.sum(
         earlier.astype(jnp.float32), axis=1
     )
-    slots = devices + models
-    steps = slots // 2
+    steps = (devices + (QUAD - 1) * models) // QUAD
+    slots = QUAD * steps
+    tokens_step = QUAD * seq_len
     at_slot = jnp.arange(slots)[:, None] == slot_of.astype(jnp.int32)[None, :]
     filled = jnp.any(at_slot, axis=1)
     client_at = jnp.sum(jnp.where(at_slot, jnp.arange(devices)[None, :], 0), axis=1).astype(
         jnp.int32
     )
-    step_start = 2.0 * jnp.arange(steps)
+    step_start = float(QUAD) * jnp.arange(steps)
+    used = (jnp.sum(padded) / QUAD).astype(jnp.int32)[None]
     model_of = (
         jnp.sum((step_start[:, None] >= offsets[None, :]).astype(jnp.int32), axis=1) - 1
     ).astype(jnp.int32)
@@ -1351,14 +1363,14 @@
     )
     within = client_at % members
     piece_at = (
-        (client_at // members * members + jnp.repeat(model_of, 2) * share + within // local) * local
+        (client_at // members * members + jnp.repeat(model_of, QUAD) * share + within // local) * local
         + within % local
     ).astype(jnp.int32)
     weight_rows = valid / total_of[:, None]
     slot_log = jnp.where(filled[:, None], jnp.take(chosen_total, client_at, axis=0), 1e30)
     slot_weight = jnp.where(filled[:, None], jnp.take(weight_rows, client_at, axis=0), 0.0)
     slot_info = jnp.stack(
-        [slot_log.reshape(steps, 2 * seq_len), slot_weight.reshape(steps, 2 * seq_len)], axis=1
+        [slot_log.reshape(steps, tokens_step), slot_weight.reshape(steps, tokens_step)], axis=1
     )
     slot_target = jnp.where(filled[:, None], jnp.take(target_local, client_at, axis=0), -1)
     spare = devices + jnp.cumsum(1 - filled.astype(jnp.int32)) - 1
@@ -1367,11 +1379,11 @@
         table_low,
         model_of,
         fresh,
-        piece_at[0::2],
-        piece_at[1::2],
+        used,
+        piece_at,
         jnp.where(filled, client_at, spare).astype(jnp.int32),
         slot_info,
-        slot_target.reshape(steps, 1, 2 * seq_len),
+        slot_target.reshape(steps, 1, tokens_step),
     )
     d_group = collect(d_outs, groups, members, 4)
     d_mine = lax.dynamic_slice(
@@ -1412,9 +1424,10 @@
     token_local = tokens - device_index * block_rows
     token_local = jnp.where((token_local >= 0) & (token_local < block_rows), token_local, -1)
     slot_token = jnp.where(filled[:, None], jnp.take(token_local, client_at, axis=0), -1)
-    pair_start = jnp.concatenate([offsets, jnp.sum(padded)[None]]) / 2.0
-    schedule = (pair_start.astype(jnp.int32), client_at[0::2], client_at[1::2])
-    slot_token = slot_token.reshape(steps, 1, 2 * seq_len)
+    pair_start = (offsets / 2.0).astype(jnp.int32)
+    pair_end = pair_start + jnp.ceil(numbers / 2.0).astype(jnp.int32)
+    schedule = (pair_start, pair_end, client_at[0::2], client_at[1::2])
+    slot_token = slot_token.reshape(slots // 2, 1, 2 * seq_len)
     lead = models // 2
 
     states = finish_table(d_all, head_grad, table, table_momentum, schedule, slot_token, 0, lead, ())

time: 765 us -> 747 us (0.976)
  Pallas kernels: 499 us -> 486 us
    pallas_call x1, Pallas kernels: 69.7 us -> 56.6 us  [head_back(): pl.pallas_call(back_kernel, out_shape=(jax.ShapeDtypeStruct((QUAD * steps...]
    unnamed x143 -> x177, local copies, waits for them, and re-layouts: 27.8 us -> 25.6 us
where the time goes in v10:
time: 747 us; the launch traced here: 735 us
  Pallas kernels  486 us (65%)
  matrix products  75.1 us (10%)
  local copies, waits for them, and re-layouts  59.9 us (8%)
  other arithmetic  38 us (5%)
  waiting for transfers between devices  37 us (5%)
  starting transfers between devices  19.8 us (3%)
  between operations  18.9 us (3%)
    pallas_call x2, Pallas kernels, spread(): pl.pallas_call(functools.partial(spread_kernel, groups, members, chain, p...  140 us
    pallas_call x1, Pallas kernels, spread_score(): pl.pallas_call(functools.partial(score_kernel, groups, members, share, pi...  139 us
    pallas_call x1, Pallas kernels, collect(): pl.pallas_call(functools.partial(collect_kernel, groups, members), out_sh...  61.3 us
    pallas_call x2, Pallas kernels, finish_table(): pl.pallas_call(functools.partial(finish_kernel, first_model), out_shape=(...  59.2 us
    pallas_call x1, Pallas kernels, head_back(): pl.pallas_call(back_kernel, out_shape=(jax.ShapeDtypeStruct((QUAD * steps...  56.6 us
    unnamed x177, local copies, waits for them, and re-layouts  25.6 us
    reduce_scatter x1, waiting for transfers between devices, body(): lax.psum_scatter(stack_rows, 'grp', scatter_dimension=0, tiled=True)  24.3 us
    dot_general x6, matrix products, project(): lax.dot_general(inputs, matrix, (((1,), (1,)), ((), ())), preferred_eleme...  22.8 us
  transfers between devices with their start and end apart: 5, of which 3 were waited for; matrix products, arithmetic and copies ran while one was open for 5% of the time, Pallas kernels for 13%

profile of v10, /device:TPU:0, one launch (start us, length us, event | category | flops | bytes accessed | tf_op | source)
XLA Modules:
  0.0 735.2 jit_solution(11898323676912942747)
XLA Ops:
  10.6 18.1 %shard_map.185 = (s32[32,1,512]{2,1,0:T(1,128)}, bf16[4,1600,768]{2,1,0:T(8,128)(2,1)}) custom-call(s32[1,512]{1,0:T(1,128)} %bitcast.238, f32[4,1600,768]{2,1,0:T(8,128)} %table_ref.5), custom_call_target="tpu_custom_call" | custom-call | bytes 29491200 | tf_op jit(solution)/shard_map/pallas_call | solution.py:661
  32.0 2.6 convert_element_type.243
  39.3 1.2 gather_fusion.2
  43.3 2.6 fusion.134
  48.9 5.3 fusion.44
  54.3 1.6 pad_maximum_fusion.src
  55.9 99.9 %shard_map.186.pool_ref = bf16[32,400,768]{2,1,0:T(8,128)(2,1)} custom-call(bf16[4,400,768]{2,1,0:T(8,128)(2,1)} %pad_maximum_fusion.src), custom_call_target="tpu_custom_call" | custom-call | bytes 39321600 | tf_op jit(solution)/shard_map/pallas_call | solution.py:580
  156.0 12.0 %shard_map.187 = (bf16[9344,768]{1,0:T(8,128)(2,1)S(1)}, f32[512,768]{1,0:T(8,128)S(1)}) custom-call(s32[512,1]{1,0:T(8,128)S(1)} %fusion.74.at_ref, bf16[32,400,768]{2,1,0:T(8,128)(2,1)} %shard_map.186.pool_ref), custom_call_target="tpu_custom_call" | custom-call | flops 2818572288 | bytes 39321600 | tf_op jit(solution)/shard_map/pallas_call | solution.py:1015
  168.0 5.3 copy-done
  174.8 1.4 constant_dynamic-slice_fusion.1
  176.2 1.5 fusion.98
  177.7 1.5 add_convert_fusion.4
  179.3 3.2 convolution_convert_fusion.6
  182.5 2.1 add_convert_fusion.2
  185.1 2.4 add_convert_fusion.3
  187.8 1.1 reshape.723
  188.8 1.2 copy.257
  190.0 2.1 reshape.725
  196.2 1.1 copy.349
  197.3 1.4 slice-done.3
  199.2 0.9 fusion.136
  200.9 5.6 multiply_convert_fusion
  206.6 2.7 fusion.137
  209.6 1.2 fusion.54.src
  210.9 139.5 %shard_map.188 = (bf16[32,512,768]{2,1,0:T(8,128)(2,1)}, f32[32,2,512]{2,1,0:T(2,128)}) custom-call(bf16[1,512,768]{2,1,0:T(8,128)(2,1)} %fusion.54.src, bf16[4,1600,768]{2,1,0:T(8,128)(2,1)} %get-tuple-element.375, s32[8,1,512]{2,1,0:T(1,128)} %bitcast.219), custom_call_target="tpu_custom_call" | custom-call | flops 40265318400 | bytes 50331648 | tf_op jit(solution)/shard_map/pallas_call | solution.py:770
  350.3 1.0 reshape.727
  353.7 56.6 %shard_map.189 = (bf16[44,128,768]{2,1,0:T(8,128)(2,1)}, f32[4,1600,768]{2,1,0:T(8,128)}) custom-call(s32[11]{0:T(128)} %copy-done.70, s32[11]{0:T(128)} %add_convert_fusion.6.fresh_ref, s32[1]{0:T(128)} %bitcast.23.used_ref, s32[44]{0:T(128)} %get-tuple-element.269.piece_ref, s32[44]{0:T(128)} %get-tuple-element.270.place_ref, ...), custom_call_target="tpu_custom_call" | custom-call | flops 41523609600 | bytes 46792704 | tf_op jit(solution)/shard_map/pallas_call | solution.py:1101
  410.3 61.3 %shard_map.190 = bf16[4,128,768]{2,1,0:T(8,128)(2,1)} custom-call(bf16[44,128,768]{2,1,0:T(8,128)(2,1)} %get-tuple-element.93.source), custom_call_target="tpu_custom_call" | custom-call | bytes 12582912 | tf_op jit(solution)/shard_map/pallas_call | solution.py:963
  471.6 1.6 fusion.126
  474.7 8.5 %convert_reduce_fusion = (f32[3072]{0:T(1024)S(1)}, bf16[512,3072]{1,0:T(8,128)(2,1)S(1)}) fusion(f32[512,3072]{1,0:T(8,128)S(1)} %bitcast.249, f32[3072]{0:T(1024)S(1)} %bitcast.236, bf16[512,768]{1,0:T(8,128)(2,1)S(1)} %get-tuple-element.101, bf16[9344,768]{1,0:T(8,128)(2,1)} %copy-done), kind=kOutput, calls=%fused_computation.32 | convolution fusion | flops 2452091904 | bytes 14966784 | tf_op jit(solution)/shard_map/dot_general | solution.py:38
  483.3 6.4 multiply_reduce_fusion.1
  491.5 2.9 convolution_convert_fusion.5
  494.5 2.3 copy.265
  496.8 2.4 reshape.733
  499.2 4.4 convert_reduce_fusion.3
  504.4 1.0 multiply_convert_fusion.1
  505.6 2.1 fusion.43
  507.6 1.4 convert_reduce_fusion.4
  509.2 2.6 copy.276
  511.9 1.8 copy.270
  513.7 1.8 copy.273
  515.9 1.0 copy-done.2
  517.0 5.3 multiply_reduce_fusion.2
  523.2 1.8 fusion.129
  525.1 8.6 %all-to-all-start.1 = ((bf16[4,128,768]{2,1,0:T(8,128)(2,1)}), bf16[4,128,768]{2,1,0:T(8,128)(2,1)S(1)}, u32[]{:S(2)}, u32[]{:S(2)}) async-start(bf16[4,128,768]{2,1,0:T(8,128)(2,1)} %bitcast.212), calls=%async_computation.1 | async-start | bytes 1572864 | tf_op jit(solution)/shard_map/all_to_all | solution.py:1406
  534.2 5.6 fusion.17
  539.8 1.8 fusion.37
  541.6 4.4 fusion.16
  546.0 4.4 fusion.15
  551.1 1.8 all-to-all-done.1
  556.2 39.7 %shard_map.191.d_ref = bf16[32,128,768]{2,1,0:T(8,128)(2,1)} custom-call(bf16[1,128,768]{2,1,0:T(8,128)(2,1)} %bitcast.221), custom_call_target="tpu_custom_call" | custom-call | bytes 12582912 | tf_op jit(solution)/shard_map/pallas_call | solution.py:580
  596.6 3.3 all-to-all-start.2
  599.9 29.5 %shard_map.192 = (f32[4,1600,768]{2,1,0:T(8,128)}, f32[4,1600,768]{2,1,0:T(8,128)}, f32[4,1600,768]{2,1,0:T(8,128)}) custom-call(s32[4]{0:T(128)} %multiply_convert_fusion.4.start_ref, s32[4]{0:T(128)} %get-tuple-element.240.end_ref, s32[22]{0:T(128)} %slice.147.first_ref, s32[22]{0:T(128)} %slice.148.second_ref, bf16[32,128,768]{2,1,0:T(8,128)(2,1)} %shard_map.191.d_ref, ...), custom_call_target="tpu_custom_call" | custom-call | flops 5033164800 | bytes 58982400 | tf_op jit(solution)/shard_map/pallas_call | solution.py:1162
  629.5 24.3 %reduce-scatter.2.cloned.1.call-done = bf16[1168,768]{1,0:T(8,128)(2,1)} async-done(((bf16[9344,768]{1,0:T(8,128)(2,1)}), bf16[1168,768]{1,0:T(8,128)(2,1)}) %reduce-scatter.2.cloned.1.call-update) | async-done | bytes 1794064 | tf_op jit(solution)/shard_map/reduce_scatter | solution.py:1415
  653.8 2.6 reshape.744
  656.3 4.6 all-to-all-start.3
  662.4 29.7 %shard_map.193 = (f32[4,1600,768]{2,1,0:T(8,128)}, f32[4,1600,768]{2,1,0:T(8,128)}, f32[4,1600,768]{2,1,0:T(8,128)}) custom-call(s32[4]{0:T(128)} %multiply_convert_fusion.4.start_ref, s32[4]{0:T(128)} %get-tuple-element.240.end_ref, s32[22]{0:T(128)} %slice.147.first_ref, ...), custom_call_target="tpu_custom_call", output_to_operand_aliasing={{0}: (9, {}), {1}: (10, {}), {2}: (11, {})} | custom-call | flops 5033164800 | bytes 58982400 | tf_op jit(solution)/shard_map/pallas_call | solution.py:1162
  692.2 10.9 %all-to-all-done.3 = bf16[4,292,768]{2,1,0:T(8,128)(2,1)S(1)} async-done(((bf16[4,292,768]{2,1,0:T(8,128)(2,1)}), bf16[4,292,768]{2,1,0:T(8,128)(2,1)S(1)}, u32[]{:S(2)}, u32[]{:S(2)}) %all-to-all-start.3) | async-done | bytes 1794080 | tf_op jit(solution)/shard_map/all_to_all | solution.py:1435
  703.1 2.0 convert_element_type.298
  705.9 2.9 all-to-all-start.4
  708.8 6.0 copy_subtract_fusion
  714.9 3.2 copy.282
  718.1 3.2 copy.284
  721.3 3.2 copy.283
  (310 shorter events, 40.7 us)
Async XLA Ops:
  31.5 4.7 copy-start.65
  31.5 5.5 copy-start.59
  31.7 9.9 %copy-start.55 = (pred[44]{0:T(512)(128)(4,1)}, pred[44]{0:T(512)(128)(4,1)S(1)}, u32[]{:S(2)}) copy-start(pred[44]{0:T(512)(128)(4,1)S(1)} %fusion.87) | copy-start | bytes 136
  31.8 6.3 copy-start.68
  31.8 5.3 copy-start.43
  31.9 9.1 %copy-start.17 = (s32[32,128]{1,0:T(8,128)}, s32[32,128]{1,0:T(8,128)S(1)}, u32[]{:S(2)}) copy-start(s32[32,128]{1,0:T(8,128)S(1)} %get-tuple-element.256) | copy-start | bytes 49156
  36.2 9.6 %copy-start.63 = (pred[44]{0:T(512)(128)(4,1)}, pred[44]{0:T(512)(128)(4,1)S(1)}, u32[]{:S(2)}) copy-start(pred[44]{0:T(512)(128)(4,1)S(1)} %compare_and_fusion.3) | copy-start | bytes 136
  38.6 7.2 copy-start.54
  168.0 5.4 copy-start
  173.4 4.4 copy-start.6
  173.6 5.6 copy-start.1
  173.8 5.4 copy-start.41
  174.2 8.3 %copy-start.46 = (f32[512]{0:T(512)}, f32[512]{0:T(512)S(1)}, u32[]{:S(2)}) copy-start(f32[512]{0:T(512)S(1)} %fusion.115) | copy-start | bytes 6148
  177.7 4.8 copy-start.38
  179.3 5.8 copy-start.19
  185.1 7.2 copy-start.8
  187.7 4.4 copy-start.37
  187.8 4.4 copy-start.48
  188.8 8.4 %slice-start = ((s8[14352384]{0:T(1024)(128)(4,1)}), s8[1769472]{0:T(1024)(128)(4,1)S(1)}, s32[]{:S(2)}) async-start(s8[14352384]{0:T(1024)(128)(4,1)} %bitcast.209), calls=%async_computation.8 | async-start | bytes 3538944
  192.3 5.0 slice-start.1
  193.0 4.3 slice-start.2
  194.6 4.2 slice-start.3
  195.6 3.6 copy-start.18
  195.6 3.6 copy-start.62
  200.2 6.4 copy-start.4
  200.9 5.7 copy-start.26
  200.9 5.7 copy-start.61
  206.6 3.1 copy-start.40
  206.6 3.1 copy-start.51
  210.8 140.5 %copy-start.36 = (f32[4,8,4]{2,0,1:T(4,128)S(1)}, f32[4,8,4]{2,0,1:T(4,128)}, u32[]{:S(2)}) copy-start(f32[4,8,4]{2,0,1:T(4,128)} %fusion.88) | copy-start | bytes 1540
  210.8 141.4 %copy-start.34 = (f32[44,128]{1,0:T(8,128)S(1)}, f32[44,128]{1,0:T(8,128)}, u32[]{:S(2)}) copy-start(f32[44,128]{1,0:T(8,128)} %gather_fusion.2) | copy-start | bytes 67588
  210.8 141.4 %copy-start.56 = (pred[44]{0:T(512)(128)(4,1)S(1)}, pred[44]{0:T(512)(128)(4,1)}, u32[]{:S(2)}) copy-start(pred[44]{0:T(512)(128)(4,1)} %copy-done.55) | copy-start | bytes 136
  210.8 141.5 %copy-start.64 = (pred[44]{0:T(512)(128)(4,1)S(1)}, pred[44]{0:T(512)(128)(4,1)}, u32[]{:S(2)}) copy-start(pred[44]{0:T(512)(128)(4,1)} %copy-done.63) | copy-start | bytes 136
  210.8 141.6 %copy-start.71 = (pred[10]{0:T(512)(128)(4,1)S(1)}, pred[10]{0:T(512)(128)(4,1)}, u32[]{:S(2)}) copy-start(pred[10]{0:T(512)(128)(4,1)} %slice_compare_fusion.1) | copy-start | bytes 34
  410.3 61.3 %copy-start.67 = (pred[4]{0:T(512)(128)(4,1)S(1)}, pred[4]{0:T(512)(128)(4,1)}, u32[]{:S(2)}) copy-start(pred[4]{0:T(512)(128)(4,1)} %fusion.113) | copy-start | bytes 16
  410.3 64.4 %slice-start.4 = ((s8[6291456]{0:T(1024)(128)(4,1)}), s8[2097152]{0:T(1024)(128)(4,1)S(1)}, s32[]{:S(2)}) async-start(s8[6291456]{0:T(1024)(128)(4,1)} %bitcast.248), calls=%async_computation.12 | async-start | bytes 4194304
  471.6 3.1 slice-start.5
  474.7 8.5 %copy-start.28 = (bf16[512,768]{1,0:T(8,128)(2,1)}, bf16[512,768]{1,0:T(8,128)(2,1)S(1)}, u32[]{:S(2)}) copy-start(bf16[512,768]{1,0:T(8,128)(2,1)S(1)} %get-tuple-element.101) | copy-start | bytes 2359300
  474.7 8.5 %copy-start.5 = (f32[512,768]{1,0:T(8,128)S(1)}, f32[512,768]{1,0:T(8,128)}, u32[]{:S(2)}) copy-start(f32[512,768]{1,0:T(8,128)} %copy-done.4) | copy-start | bytes 4718596
  483.2 6.4 copy-start.74
  499.2 4.4 copy-start.16
  499.2 4.4 copy-start.23
  499.2 4.4 copy-start.25
  517.0 5.4 copy-start.13
  517.0 5.4 copy-start.50
  525.0 9.1 %copy-start.12 = (f32[512,768]{1,0:T(8,128)S(1)}, f32[512,768]{1,0:T(8,128)}, u32[]{:S(2)}) copy-start(f32[512,768]{1,0:T(8,128)} %get-tuple-element.233) | copy-start | bytes 4718596
  525.0 9.2 %copy-start.20 = (bf16[512,768]{1,0:T(8,128)(2,1)S(1)}, bf16[512,768]{1,0:T(8,128)(2,1)}, u32[]{:S(2)}) copy-start(bf16[512,768]{1,0:T(8,128)(2,1)} %copy-done.19) | copy-start | bytes 2359300
  525.1 27.8 %all-to-all-start.1 = ((bf16[4,128,768]{2,1,0:T(8,128)(2,1)}), bf16[4,128,768]{2,1,0:T(8,128)(2,1)S(1)}, u32[]{:S(2)}, u32[]{:S(2)}) async-start(bf16[4,128,768]{2,1,0:T(8,128)(2,1)} %bitcast.212), calls=%async_computation.1 | async-start | bytes 1572864 | tf_op jit(solution)/shard_map/all_to_all | solution.py:1406
  533.7 120.1 %reduce-scatter.2.cloned.1.call-start = ((), (), s32[]{:S(2)}) async-start(), calls=%async_computation.6 | async-start | bytes 16146432 | tf_op jit(solution)/shard_map/reduce_scatter | solution.py:1415
  534.2 5.6 copy-start.21
  534.2 5.6 copy-start.31
  534.2 7.4 %copy-start.75 = (bf16[512,3072]{1,0:T(8,128)(2,1)S(1)}, bf16[512,3072]{1,0:T(8,128)(2,1)}, u32[]{:S(2)}) copy-start(bf16[512,3072]{1,0:T(8,128)(2,1)} %copy-done.74) | copy-start | bytes 9437188
  541.6 4.4 copy-start.29
  541.6 4.4 copy-start.73
  551.1 3.7 copy-start.66
  596.6 32.9 %all-to-all-start.2 = ((f32[8,1,1344]{2,1,0:T(1,128)}), f32[8,1,1344]{2,1,0:T(1,128)S(1)}, u32[]{:S(2)}, u32[]{:S(2)}) async-start(f32[8,1,1344]{2,1,0:T(1,128)} %all_to_all.22), calls=%async_computation.3 | async-start | bytes 90112 | tf_op jit(solution)/shard_map/all_to_all | solution.py:1420
  656.3 4.6 copy-start.60
  656.3 4.8 copy-start.58
  656.3 5.5 copy-start.44
  656.3 46.8 %all-to-all-start.3 = ((bf16[4,292,768]{2,1,0:T(8,128)(2,1)}), bf16[4,292,768]{2,1,0:T(8,128)(2,1)S(1)}, u32[]{:S(2)}, u32[]{:S(2)}) async-start(bf16[4,292,768]{2,1,0:T(8,128)(2,1)} %reshape.744), calls=%async_computation.4 | async-start | bytes 3637248 | tf_op jit(solution)/shard_map/all_to_all | solution.py:1435
  705.9 18.6 %all-to-all-start.4 = ((f32[32,1,1344]{2,1,0:T(1,128)}), f32[32,1,1344]{2,1,0:T(1,128)S(1)}, u32[]{:S(2)}, u32[]{:S(2)}) async-start(f32[32,1,1344]{2,1,0:T(1,128)} %broadcast_in_dim.274), calls=%async_computation.5 | async-start | bytes 360448 | tf_op jit(solution)/shard_map/all_to_all | solution.py:233
  708.8 6.1 copy-start.3
  721.3 4.6 copy-start.32
  721.3 4.6 copy-start.33
  (23 other events, 35.0 us)
Sparse Core Ops, SparseCore 1:
  553.0 100.7 reduce-scatter.1

commit v11 on v10

--- a/solution.py
+++ b/solution.py
@@ -1177,6 +1177,32 @@
             transcendentals=0,
         ),
     )(*schedule, d_inputs, ids, head_grad, table, momentum, *earlier)
+
+
+def stack_kernel(gradient_ref, weight_ref, momentum_ref, grad_ref, renewed_ref, fresh_ref):
+    for model in range(gradient_ref.shape[0]):
+        gradient = gradient_ref[model].astype(jnp.float32)
+        renewed, fresh = update(weight_ref[:, model, :], momentum_ref[:, model, :], gradient, stack_rate)
+        grad_ref[:, model, :] = gradient
+        renewed_ref[:, model, :] = renewed
+        fresh_ref[:, model, :] = fresh
+
+
+def update_stack(gradient, weight, momentum):
+    turn = functools.partial(jnp.transpose, axes=(1, 0, 2))
+    turned = jax.ShapeDtypeStruct(turn(weight).shape, jnp.float32)
+    whole = pl.BlockSpec(memory_space=pltpu.VMEM)
+    results = pl.pallas_call(
+        stack_kernel,
+        out_shape=(turned, turned, turned),
+        in_specs=[whole] * 3,
+        out_specs=(whole,) * 3,
+        compiler_params=pltpu.CompilerParams(vmem_limit_bytes=56 * MIB),
+        cost_estimate=pl.CostEstimate(
+            flops=6 * weight.size, bytes_accessed=22 * weight.size, transcendentals=0
+        ),
+    )(gradient, turn(weight), turn(momentum))
+    return tuple(turn(result) for result in results)
 
 
 def body(
@@ -1428,22 +1454,26 @@
     pair_end = pair_start + jnp.ceil(numbers / 2.0).astype(jnp.int32)
     schedule = (pair_start, pair_end, client_at[0::2], client_at[1::2])
     slot_token = slot_token.reshape(slots // 2, 1, 2 * seq_len)
-    lead = models // 2
+    lead = models - 1
 
     states = finish_table(d_all, head_grad, table, table_momentum, schedule, slot_token, 0, lead, ())
     stack_sum, states, vector_part = lax.optimization_barrier((stack_sum, states, vector_part))
     stack_back = lax.all_to_all(
         stack_sum.reshape(members, stack_part, model_width), "cli", 0, 0, tiled=True
-    ).astype(jnp.float32)
-    stack_grad = jnp.sum(stack_back.reshape(models, share, stack_part, model_width), axis=1)
-    table_grad, table_momentum_new, table_new = finish_table(
+    )
+    if share > 1:
+        stack_back = jnp.sum(
+            stack_back.astype(jnp.float32).reshape(models, share, stack_part, model_width), axis=1
+        )
+    states = finish_table(
         d_all, head_grad, table, table_momentum, schedule, slot_token, lead, models - lead, states
     )
-    stack_grad, vector_part = lax.optimization_barrier((stack_grad, vector_part))
+    stack_back, vector_part, states = lax.optimization_barrier((stack_back, vector_part, states))
+    table_grad, table_momentum_new, table_new = states
     vector_parts = share_all(jnp.sum(vector_part, axis=0), both, devices)
     vector_grad = jnp.sum(vector_parts.reshape(groups, models, share, vector_piece), axis=2)
     vector_grad = vector_grad.transpose(1, 0, 2).reshape(vectors.shape)
-    stack_momentum_new, stack_new = update(stack, stack_momentum, stack_grad, stack_rate)
+    stack_grad, stack_momentum_new, stack_new = update_stack(stack_back, stack, stack_momentum)
     vector_momentum_new, vector_new = update(vectors, vector_momentum, vector_grad, vector_rate)
     return (
         loss,

time: 747 us -> 757 us (1.013)
  Pallas kernels: 486 us -> 501 us
  matrix products: 75.1 us -> 84.7 us
  local copies, waits for them, and re-layouts: 59.9 us -> 51.9 us
    all_to_all x1, waiting for transfers between devices: 10.9 us -> 26.2 us  [body(): lax.all_to_all(stack_sum.reshape(members, stack_part, model_width), 'cli'...]
    reduce_scatter x1, waiting for transfers between devices: 24.3 us -> 10.9 us  [body(): lax.psum_scatter(stack_rows, 'grp', scatter_dimension=0, tiled=True)]
    unnamed x177 -> x192, local copies, waits for them, and re-layouts: 25.6 us -> 14.5 us
    pallas_call x0 -> x1, Pallas kernels: none -> 10.7 us  [update_stack(): pl.pallas_call(stack_kernel, out_shape=(turned, turned, turned), in_specs...]
  transfers between devices with their start and end apart: 5 -> 5, of which waited for: 3 -> 3; matrix products, arithmetic and copies ran while one was open for 5% -> 3% of each run, Pallas kernels for 13% -> 14%
where the time goes in v11:
time: 757 us; the launch traced here: 750 us
  Pallas kernels  501 us (66%)
  matrix products  84.7 us (11%)
  local copies, waits for them, and re-layouts  51.9 us (7%)
  waiting for transfers between devices  39.4 us (5%)
  other arithmetic  34.2 us (5%)
  starting transfers between devices  19.6 us (3%)
  between operations  19.2 us (3%)
    pallas_call x1, Pallas kernels, spread_score(): pl.pallas_call(functools.partial(score_kernel, groups, members, share, pi...  139 us
    pallas_call x2, Pallas kernels, spread(): pl.pallas_call(functools.partial(spread_kernel, groups, members, chain, p...  139 us
    pallas_call x1, Pallas kernels, head_back(): pl.pallas_call(back_kernel, out_shape=(jax.ShapeDtypeStruct((QUAD * steps...  61.5 us
    pallas_call x1, Pallas kernels, collect(): pl.pallas_call(functools.partial(collect_kernel, groups, members), out_sh...  61.4 us
    pallas_call x2, Pallas kernels, finish_table(): pl.pallas_call(functools.partial(finish_kernel, first_model), out_shape=(...  58.7 us
    dot_general x6, matrix products, project(): lax.dot_general(inputs, matrix, (((1,), (1,)), ((), ())), preferred_eleme...  28.9 us
    all_to_all x1, waiting for transfers between devices, body(): lax.all_to_all(stack_sum.reshape(members, stack_part, model_width), 'cli'...  26.2 us
    dot_general x6, matrix products, product(): return jnp.dot(inputs, matrix, preferred_element_type=jnp.float32)  23.2 us
  transfers between devices with their start and end apart: 5, of which 3 were waited for; matrix products, arithmetic and copies ran while one was open for 3% of the time, Pallas kernels for 14%

profile of v11, /device:TPU:0, one launch (start us, length us, event | category | flops | bytes accessed | tf_op | source)
XLA Modules:
  0.0 750.1 jit_solution(17149319794562967063)
XLA Ops:
  9.9 18.1 %shard_map.185 = (s32[32,1,512]{2,1,0:T(1,128)}, bf16[4,1600,768]{2,1,0:T(8,128)(2,1)}) custom-call(s32[1,512]{1,0:T(1,128)} %bitcast.243, f32[4,1600,768]{2,1,0:T(8,128)} %table_ref.5), custom_call_target="tpu_custom_call" | custom-call | bytes 29491200 | tf_op jit(solution)/shard_map/pallas_call | solution.py:661
  38.0 2.6 fusion.133
  43.3 2.6 convert_element_type.240
  46.2 5.3 fusion.43
  51.5 1.6 pad_maximum_fusion.src
  53.2 99.9 %shard_map.186.pool_ref = bf16[32,400,768]{2,1,0:T(8,128)(2,1)} custom-call(bf16[4,400,768]{2,1,0:T(8,128)(2,1)} %pad_maximum_fusion.src), custom_call_target="tpu_custom_call" | custom-call | bytes 39321600 | tf_op jit(solution)/shard_map/pallas_call | solution.py:580
  154.4 12.0 %shard_map.187 = (bf16[9344,768]{1,0:T(8,128)(2,1)S(1)}, f32[512,768]{1,0:T(8,128)S(1)}) custom-call(s32[512,1]{1,0:T(8,128)S(1)} %fusion.73.at_ref, bf16[32,400,768]{2,1,0:T(8,128)(2,1)} %shard_map.186.pool_ref), custom_call_target="tpu_custom_call" | custom-call | flops 2818572288 | bytes 39321600 | tf_op jit(solution)/shard_map/pallas_call | solution.py:1015
  166.5 5.3 copy-done
  173.2 1.5 fusion.97
  174.8 1.5 add_convert_fusion.4
  176.3 3.2 convolution_convert_fusion.6
  179.5 2.1 add_convert_fusion.2
  182.1 1.7 copy.231
  184.0 3.2 add_convert_fusion.3
  187.3 1.4 copy.229
  189.7 1.1 fusion.134
  191.5 1.0 copy-done.17
  193.4 2.2 fusion.135
  197.2 9.0 %multiply_convert_fusion = (bf16[512,3072]{1,0:T(8,128)(2,1)S(1)}, f32[512,3072]{1,0:T(8,128)}) fusion(f32[3072]{0:T(1024)S(1)} %bitcast.240, bf16[512,768]{1,0:T(8,128)(2,1)S(1)} %add_convert_fusion.1, bf16[9344,768]{1,0:T(8,128)(2,1)} %copy-done), kind=kOutput, calls=%fused_computation.33 | convolution fusion | flops 2431647744 | bytes 14954496 | tf_op jit(solution)/shard_map/dot_general | solution.py:38
  206.2 6.2 fusion.136
  212.8 1.2 fusion.53.src
  214.0 139.5 %shard_map.188 = (bf16[32,512,768]{2,1,0:T(8,128)(2,1)}, f32[32,2,512]{2,1,0:T(2,128)}) custom-call(bf16[1,512,768]{2,1,0:T(8,128)(2,1)} %fusion.53.src, bf16[4,1600,768]{2,1,0:T(8,128)(2,1)} %get-tuple-element.385, s32[8,1,512]{2,1,0:T(1,128)} %bitcast.224), custom_call_target="tpu_custom_call" | custom-call | flops 40265318400 | bytes 50331648 | tf_op jit(solution)/shard_map/pallas_call | solution.py:770
  353.5 1.0 reshape.724
  358.3 61.5 %shard_map.189 = (bf16[44,128,768]{2,1,0:T(8,128)(2,1)}, f32[4,1600,768]{2,1,0:T(8,128)}) custom-call(s32[11]{0:T(128)} %copy-done.83, s32[11]{0:T(128)} %add_convert_fusion.6.fresh_ref, s32[1]{0:T(128)} %bitcast.23.used_ref, s32[44]{0:T(128)} %get-tuple-element.280.piece_ref, s32[44]{0:T(128)} %get-tuple-element.279.place_ref, ...), custom_call_target="tpu_custom_call" | custom-call | flops 41523609600 | bytes 46792704 | tf_op jit(solution)/shard_map/pallas_call | solution.py:1101
  419.8 61.4 %shard_map.190 = bf16[4,128,768]{2,1,0:T(8,128)(2,1)} custom-call(bf16[44,128,768]{2,1,0:T(8,128)(2,1)} %get-tuple-element.99.source), custom_call_target="tpu_custom_call" | custom-call | bytes 12582912 | tf_op jit(solution)/shard_map/pallas_call | solution.py:963
  482.0 2.2 fusion.125
  484.2 1.2 fusion.32
  486.8 9.1 %convert_reduce_fusion = (f32[3072]{0:T(1024)}, bf16[512,3072]{1,0:T(8,128)(2,1)S(1)}) fusion(f32[512,3072]{1,0:T(8,128)S(1)} %bitcast.257, f32[3072]{0:T(1024)S(1)} %bitcast.241, bf16[512,768]{1,0:T(8,128)(2,1)S(1)} %get-tuple-element.107, bf16[9344,768]{1,0:T(8,128)(2,1)} %copy-done), kind=kOutput, calls=%fused_computation.32 | convolution fusion | flops 2452091904 | bytes 14966784 | tf_op jit(solution)/shard_map/dot_general | solution.py:38
  495.9 7.0 multiply_reduce_fusion.1
  503.6 1.1 convert_reduce_fusion.2
  505.6 2.0 convolution_convert_fusion.5
  508.1 3.9 convert_reduce_fusion.3
  514.1 1.2 fusion.42
  515.3 1.2 convert_reduce_fusion.4
  516.5 1.0 copy.312
  519.8 1.1 copy-done.2
  521.0 7.1 multiply_reduce_fusion.2
  529.3 1.4 stack.23
  530.7 1.4 stack.22
  532.0 1.3 stack.24
  533.3 1.3 reshape.733
  534.6 1.3 reshape.734
  535.8 1.3 reshape.737
  537.1 1.3 stack.25
  538.4 1.3 reshape.735
  539.7 1.3 reshape.736
  541.7 2.2 fusion.129
  544.0 1.3 fusion.128
  545.5 8.5 %all-to-all-start.1 = ((bf16[4,128,768]{2,1,0:T(8,128)(2,1)}), bf16[4,128,768]{2,1,0:T(8,128)(2,1)S(1)}, u32[]{:S(2)}, u32[]{:S(2)}) async-start(bf16[4,128,768]{2,1,0:T(8,128)(2,1)} %bitcast.217), calls=%async_computation.1 | async-start | bytes 1572864 | tf_op jit(solution)/shard_map/all_to_all | solution.py:1432
  554.2 5.6 fusion.17
  559.8 1.8 fusion.36
  561.6 4.4 fusion.16
  566.0 4.4 fusion.15
  571.1 2.2 all-to-all-done.1
  576.6 39.2 %shard_map.191.d_ref = bf16[32,128,768]{2,1,0:T(8,128)(2,1)} custom-call(bf16[1,128,768]{2,1,0:T(8,128)(2,1)} %bitcast.226), custom_call_target="tpu_custom_call" | custom-call | bytes 12582912 | tf_op jit(solution)/shard_map/pallas_call | solution.py:580
  616.5 3.3 all-to-all-start.2
  619.9 42.9 %shard_map.192 = (f32[4,1600,768]{2,1,0:T(8,128)}, f32[4,1600,768]{2,1,0:T(8,128)}, f32[4,1600,768]{2,1,0:T(8,128)}) custom-call(s32[4]{0:T(128)} %multiply_convert_fusion.4.start_ref, s32[4]{0:T(128)} %get-tuple-element.240.end_ref, s32[22]{0:T(128)} %slice.151.first_ref, s32[22]{0:T(128)} %slice.152.second_ref, bf16[32,128,768]{2,1,0:T(8,128)(2,1)} %shard_map.191.d_ref, ...), custom_call_target="tpu_custom_call" | custom-call | flops 7549747200 | bytes 88473600 | tf_op jit(solution)/shard_map/pallas_call | solution.py:1162
  662.8 10.9 %reduce-scatter.2.cloned.1.call-done = bf16[1168,768]{1,0:T(8,128)(2,1)} async-done(((bf16[9344,768]{1,0:T(8,128)(2,1)}), bf16[1168,768]{1,0:T(8,128)(2,1)}) %reduce-scatter.2.cloned.1.call-update) | async-done | bytes 1794064 | tf_op jit(solution)/shard_map/reduce_scatter | solution.py:1441
  673.8 2.6 reshape.741
  676.3 4.7 all-to-all-start.3
  681.2 15.7 %shard_map.193 = (f32[4,1600,768]{2,1,0:T(8,128)}, f32[4,1600,768]{2,1,0:T(8,128)}, f32[4,1600,768]{2,1,0:T(8,128)}) custom-call(s32[4]{0:T(128)} %multiply_convert_fusion.4.start_ref, s32[4]{0:T(128)} %get-tuple-element.240.end_ref, s32[22]{0:T(128)} %slice.151.first_ref, ...), custom_call_target="tpu_custom_call", output_to_operand_aliasing={{0}: (9, {}), {1}: (10, {}), {2}: (11, {})} | custom-call | flops 2516582400 | bytes 29491200 | tf_op jit(solution)/shard_map/pallas_call | solution.py:1162
  697.0 26.2 %all-to-all-done.3.gradient_ref = bf16[4,292,768]{2,1,0:T(8,128)(2,1)S(1)} async-done(((bf16[4,292,768]{2,1,0:T(8,128)(2,1)}), bf16[4,292,768]{2,1,0:T(8,128)(2,1)S(1)}, u32[]{:S(2)}, u32[]{:S(2)}) %all-to-all-start.3) | async-done | bytes 1794080 | tf_op jit(solution)/shard_map/all_to_all | solution.py:1461
  724.1 3.0 all-to-all-start.4
  728.4 10.7 %shard_map.194 = (f32[292,4,768]{2,1,0:T(4,128)}, f32[292,4,768]{2,1,0:T(4,128)}, f32[292,4,768]{2,1,0:T(4,128)}) custom-call(bf16[4,292,768]{2,1,0:T(8,128)(2,1)} %copy-done.9, f32[292,4,768]{2,1,0:T(4,128)} %bitcast.214, f32[292,4,768]{2,1,0:T(4,128)} %bitcast.216), custom_call_target="tpu_custom_call" | custom-call | flops 5382144 | bytes 19734528 | tf_op jit(solution)/shard_map/pallas_call | solution.py:1195
  (323 shorter events, 44.8 us)
Async XLA Ops:
  29.6 10.9 %copy-start.36 = (pred[32,127]{1,0:T(8,128)(4,1)}, pred[32,127]{1,0:T(8,128)(4,1)S(1)}, u32[]{:S(2)}) copy-start(pred[32,127]{1,0:T(8,128)(4,1)S(1)} %slice_compare_fusion) | copy-start | bytes 12196
  29.8 6.3 copy-start.70
  31.4 3.4 copy-start.79
  32.2 8.4 %copy-start.68 = (pred[44]{0:T(512)(128)(4,1)}, pred[44]{0:T(512)(128)(4,1)S(1)}, u32[]{:S(2)}) copy-start(pred[44]{0:T(512)(128)(4,1)S(1)} %fusion.86) | copy-start | bytes 136
  32.3 8.3 %copy-start.81 = (s32[44]{0:T(128)}, s32[44]{0:T(128)S(1)}, u32[]{:S(2)}) copy-start(s32[44]{0:T(128)S(1)} %select_reduce_fusion.1) | copy-start | bytes 532
  32.3 8.2 %copy-start.19 = (s32[32,128]{1,0:T(8,128)}, s32[32,128]{1,0:T(8,128)S(1)}, u32[]{:S(2)}) copy-start(s32[32,128]{1,0:T(8,128)S(1)} %get-tuple-element.266) | copy-start | bytes 49156
  34.9 5.7 copy-start.77
  166.4 5.4 copy-start
  171.8 2.9 copy-start.7
  172.0 2.7 copy-start.1
  172.2 4.0 copy-start.41
  172.6 3.7 copy-start.49
  176.3 7.7 %copy-start.21 = (bf16[512,768]{1,0:T(8,128)(2,1)}, bf16[512,768]{1,0:T(8,128)(2,1)S(1)}, u32[]{:S(2)}) copy-start(bf16[512,768]{1,0:T(8,128)(2,1)S(1)} %get-tuple-element.101) | copy-start | bytes 2359300
  182.1 6.8 copy-start.10
  184.0 4.9 copy-start.12
  188.9 2.0 copy-start.23
  190.8 2.5 copy-start.20
  190.9 2.5 copy-start.75
  193.1 2.5 copy-start.15
  193.4 3.4 copy-start.46
  193.4 3.5 copy-start.56
  195.6 10.6 %copy-start.3 = (f32[512,768]{1,0:T(8,128)}, f32[512,768]{1,0:T(8,128)S(1)}, u32[]{:S(2)}) copy-start(f32[512,768]{1,0:T(8,128)S(1)} %get-tuple-element.289) | copy-start | bytes 4718596
  197.2 9.0 %copy-start.26 = (bf16[512,768]{1,0:T(8,128)(2,1)}, bf16[512,768]{1,0:T(8,128)(2,1)S(1)}, u32[]{:S(2)}) copy-start(bf16[512,768]{1,0:T(8,128)(2,1)S(1)} %add_convert_fusion.1) | copy-start | bytes 2359300
  197.2 9.0 %copy-start.74 = (f32[768]{0:T(1024)S(1)}, f32[768]{0:T(1024)}, u32[]{:S(2)}) copy-start(f32[768]{0:T(1024)} %get-tuple-element.209) | copy-start | bytes 9220
  206.2 6.2 copy-start.85
  206.2 6.5 copy-start.40
  206.2 6.5 copy-start.55
  214.0 140.6 %copy-start.44 = (s32[8,4]{1,0:T(8,128)S(1)}, s32[8,4]{1,0:T(8,128)}, u32[]{:S(2)}) copy-start(s32[8,4]{1,0:T(8,128)} %eq.178) | copy-start | bytes 388
  214.0 140.6 %copy-start.35 = (f32[32,128]{1,0:T(8,128)S(1)}, f32[32,128]{1,0:T(8,128)}, u32[]{:S(2)}) copy-start(f32[32,128]{1,0:T(8,128)} %pad_convert_fusion) | copy-start | bytes 49156
  214.0 141.5 %copy-start.37 = (pred[32,127]{1,0:T(8,128)(4,1)S(1)}, pred[32,127]{1,0:T(8,128)(4,1)}, u32[]{:S(2)}) copy-start(pred[32,127]{1,0:T(8,128)(4,1)} %copy-done.36) | copy-start | bytes 12196
  214.0 141.5 %copy-start.72 = (f32[32]{0:T(128)S(1)}, f32[32]{0:T(128)}, u32[]{:S(2)}) copy-start(f32[32]{0:T(128)} %get-tuple-element.221) | copy-start | bytes 388
  214.0 142.3 %copy-start.69 = (pred[44]{0:T(512)(128)(4,1)S(1)}, pred[44]{0:T(512)(128)(4,1)}, u32[]{:S(2)}) copy-start(pred[44]{0:T(512)(128)(4,1)} %copy-done.68) | copy-start | bytes 136
  214.0 142.3 %copy-start.78 = (pred[44]{0:T(512)(128)(4,1)S(1)}, pred[44]{0:T(512)(128)(4,1)}, u32[]{:S(2)}) copy-start(pred[44]{0:T(512)(128)(4,1)} %copy-done.77) | copy-start | bytes 136
  214.0 143.7 %copy-start.84 = (pred[10]{0:T(512)(128)(4,1)S(1)}, pred[10]{0:T(512)(128)(4,1)}, u32[]{:S(2)}) copy-start(pred[10]{0:T(512)(128)(4,1)} %slice_compare_fusion.1) | copy-start | bytes 34
  419.8 67.0 %slice-start = ((s8[6291456]{0:T(1024)(128)(4,1)}), s8[2097152]{0:T(1024)(128)(4,1)S(1)}, s32[]{:S(2)}) async-start(s8[6291456]{0:T(1024)(128)(4,1)} %bitcast.256), calls=%async_computation.8 | async-start | bytes 4194304
  482.0 4.8 slice-start.1
  486.0 17.6 %copy-start.47 = (f32[512]{0:T(512)}, f32[512]{0:T(512)S(1)}, u32[]{:S(2)}) copy-start(f32[512]{0:T(512)S(1)} %negate_multiply_fusion.2) | copy-start | bytes 6148
  486.8 9.1 %copy-start.28 = (bf16[512,768]{1,0:T(8,128)(2,1)}, bf16[512,768]{1,0:T(8,128)(2,1)S(1)}, u32[]{:S(2)}) copy-start(bf16[512,768]{1,0:T(8,128)(2,1)S(1)} %get-tuple-element.107) | copy-start | bytes 2359300
  486.8 9.1 %copy-start.4 = (f32[512,768]{1,0:T(8,128)S(1)}, f32[512,768]{1,0:T(8,128)}, u32[]{:S(2)}) copy-start(f32[512,768]{1,0:T(8,128)} %copy-done.3) | copy-start | bytes 4718596
  495.9 7.0 copy-start.87
  508.1 3.9 copy-start.18
  508.1 3.9 copy-start.24
  521.0 7.1 copy-start.14
  541.6 2.3 copy-start.6
  541.6 2.3 copy-start.48
  541.7 2.3 copy-start.52
  545.4 8.7 %copy-start.22 = (bf16[512,768]{1,0:T(8,128)(2,1)S(1)}, bf16[512,768]{1,0:T(8,128)(2,1)}, u32[]{:S(2)}) copy-start(bf16[512,768]{1,0:T(8,128)(2,1)} %copy-done.21) | copy-start | bytes 2359300
  545.5 27.8 %all-to-all-start.1 = ((bf16[4,128,768]{2,1,0:T(8,128)(2,1)}), bf16[4,128,768]{2,1,0:T(8,128)(2,1)S(1)}, u32[]{:S(2)}, u32[]{:S(2)}) async-start(bf16[4,128,768]{2,1,0:T(8,128)(2,1)} %bitcast.217), calls=%async_computation.1 | async-start | bytes 1572864 | tf_op jit(solution)/shard_map/all_to_all | solution.py:1432
  554.1 119.7 %reduce-scatter.2.cloned.1.call-start = ((), (), s32[]{:S(2)}) async-start(), calls=%async_computation.6 | async-start | bytes 16146432 | tf_op jit(solution)/shard_map/reduce_scatter | solution.py:1441
  554.2 5.6 copy-start.25
  554.2 5.6 copy-start.31
  554.2 7.4 copy-start.88
  561.6 4.4 copy-start.29
  561.6 4.4 copy-start.86
  571.1 2.2 copy-start.82
  571.1 3.5 copy-start.34
  571.1 4.1 copy-start.80
  616.5 46.3 %all-to-all-start.2 = ((f32[8,1,1344]{2,1,0:T(1,128)}), f32[8,1,1344]{2,1,0:T(1,128)S(1)}, u32[]{:S(2)}, u32[]{:S(2)}) async-start(f32[8,1,1344]{2,1,0:T(1,128)} %all_to_all.22), calls=%async_computation.3 | async-start | bytes 90112 | tf_op jit(solution)/shard_map/all_to_all | solution.py:1446
  676.3 4.7 copy-start.73
  676.3 46.9 %all-to-all-start.3 = ((bf16[4,292,768]{2,1,0:T(8,128)(2,1)}), bf16[4,292,768]{2,1,0:T(8,128)(2,1)S(1)}, u32[]{:S(2)}, u32[]{:S(2)}) async-start(bf16[4,292,768]{2,1,0:T(8,128)(2,1)} %reshape.741), calls=%async_computation.4 | async-start | bytes 3637248 | tf_op jit(solution)/shard_map/all_to_all | solution.py:1461
  681.2 45.9 %copy-start.71 = (f32[32]{0:T(128)S(1)}, f32[32]{0:T(128)}, u32[]{:S(2)}) copy-start(f32[32]{0:T(128)} %copy-done.70) | copy-start | bytes 388
  681.2 46.6 %copy-start.45 = (s32[8,4]{1,0:T(8,128)S(1)}, s32[8,4]{1,0:T(8,128)}, u32[]{:S(2)}) copy-start(s32[8,4]{1,0:T(8,128)} %eq.178) | copy-start | bytes 388
  723.2 5.2 copy-start.9
  724.1 15.0 %all-to-all-start.4 = ((f32[32,1,1344]{2,1,0:T(1,128)}), f32[32,1,1344]{2,1,0:T(1,128)S(1)}, u32[]{:S(2)}, u32[]{:S(2)}) async-start(f32[32,1,1344]{2,1,0:T(1,128)} %broadcast_in_dim.274), calls=%async_computation.5 | async-start | bytes 360448 | tf_op jit(solution)/shard_map/all_to_all | solution.py:233
  (32 other events, 41.5 us)
Sparse Core Ops, SparseCore 1:
  573.4 100.3 reduce-scatter.1

commit v12 on v11

--- a/solution.py
+++ b/solution.py
@@ -1428,7 +1428,7 @@
             d_wide,
             (part_own * local * seq_len, 0),
         )
-    d_wide, pairs, vector_rows = lax.optimization_barrier((d_wide, pairs, vector_rows))
+    d_wide, pairs = lax.optimization_barrier((d_wide, pairs))
     d_turned = lax.all_to_all(
         d_wide.reshape(members, seq_len, model_width), "cli", 0, 0, tiled=True
     )
@@ -1441,12 +1441,6 @@
     stack_sum = lax.psum_scatter(stack_rows, "grp", scatter_dimension=0, tiled=True)
     d_client = jnp.sum(d_turned.astype(jnp.float32), axis=0, keepdims=True).astype(jnp.bfloat16)
     d_all = spread(d_client, groups, members, 3, True, 2)
-    d_all, vector_rows = lax.optimization_barrier((d_all, vector_rows))
-    vector_piece = vector_rows.size // groups
-    vector_part = lax.all_to_all(
-        vector_rows.reshape(groups, vector_piece), "grp", 0, 0, tiled=True
-    )
-
     token_local = tokens - device_index * block_rows
     token_local = jnp.where((token_local >= 0) & (token_local < block_rows), token_local, -1)
     slot_token = jnp.where(filled[:, None], jnp.take(token_local, client_at, axis=0), -1)
@@ -1457,6 +1451,11 @@
     lead = models - 1
 
     states = finish_table(d_all, head_grad, table, table_momentum, schedule, slot_token, 0, lead, ())
+    states, vector_rows = lax.optimization_barrier((states, vector_rows))
+    vector_piece = vector_rows.size // groups
+    vector_part = lax.all_to_all(
+        vector_rows.reshape(groups, vector_piece), "grp", 0, 0, tiled=True
+    )
     stack_sum, states, vector_part = lax.optimization_barrier((stack_sum, states, vector_part))
     stack_back = lax.all_to_all(
         stack_sum.reshape(members, stack_part, model_width), "cli", 0, 0, tiled=True

time: 757 us -> 739 us (0.976)
  blocking collectives: 0 us -> 9.11 us
  local copies, waits for them, and re-layouts: 51.9 us -> 43.4 us
    all_to_all x0 -> x1, blocking collectives: none -> 9.11 us  [body(): lax.all_to_all(vector_rows.reshape(groups, vector_piece), 'grp', 0, 0, ti...]
  transfers between devices with their start and end apart: 5 -> 4, of which waited for: 3 -> 3; matrix products, arithmetic and copies ran while one was open for 3% -> 3% of each run, Pallas kernels for 14% -> 15%
where the time goes in v12:
time: 739 us; the launch traced here: 730 us
  Pallas kernels  495 us (67%)
  matrix products  81.6 us (11%)
  local copies, waits for them, and re-layouts  43.4 us (6%)
  waiting for transfers between devices  35.2 us (5%)
  other arithmetic  30.3 us (4%)
  between operations  18.9 us (3%)
  starting transfers between devices  16.3 us (2%)
  blocking collectives  9.11 us (1%)
    pallas_call x2, Pallas kernels, spread(): pl.pallas_call(functools.partial(spread_kernel, groups, members, chain, p...  140 us
    pallas_call x1, Pallas kernels, spread_score(): pl.pallas_call(functools.partial(score_kernel, groups, members, share, pi...  139 us
    pallas_call x1, Pallas kernels, collect(): pl.pallas_call(functools.partial(collect_kernel, groups, members), out_sh...  61.3 us
    pallas_call x2, Pallas kernels, finish_table(): pl.pallas_call(functools.partial(finish_kernel, first_model), out_shape=(...  57.2 us
    pallas_call x1, Pallas kernels, head_back(): pl.pallas_call(back_kernel, out_shape=(jax.ShapeDtypeStruct((QUAD * steps...  56.6 us
    dot_general x6, matrix products, project(): lax.dot_general(inputs, matrix, (((1,), (1,)), ((), ())), preferred_eleme...  28.3 us
    all_to_all x1, waiting for transfers between devices, body(): lax.all_to_all(stack_sum.reshape(members, stack_part, model_width), 'cli'...  26.2 us
    dot_general x6, matrix products, product(): return jnp.dot(inputs, matrix, preferred_element_type=jnp.float32)  21.7 us
  transfers between devices with their start and end apart: 4, of which 3 were waited for; matrix products, arithmetic and copies ran while one was open for 3% of the time, Pallas kernels for 15%

profile of v12, /device:TPU:0, one launch (start us, length us, event | category | flops | bytes accessed | tf_op | source)
XLA Modules:
  0.0 729.9 jit_solution(17401050597298856787)
XLA Ops:
  9.9 18.1 %shard_map.185 = (s32[32,1,512]{2,1,0:T(1,128)}, bf16[4,1600,768]{2,1,0:T(8,128)(2,1)}) custom-call(s32[1,512]{1,0:T(1,128)} %bitcast.243, f32[4,1600,768]{2,1,0:T(8,128)} %table_ref.5), custom_call_target="tpu_custom_call" | custom-call | bytes 29491200 | tf_op jit(solution)/shard_map/pallas_call | solution.py:661
  28.0 0.8 copy.313
  38.0 2.6 fusion.133
  43.3 2.6 convert_element_type.240
  46.2 5.3 fusion.43
  51.5 1.6 pad_maximum_fusion.src
  53.2 99.9 %shard_map.186.pool_ref = bf16[32,400,768]{2,1,0:T(8,128)(2,1)} custom-call(bf16[4,400,768]{2,1,0:T(8,128)(2,1)} %pad_maximum_fusion.src), custom_call_target="tpu_custom_call" | custom-call | bytes 39321600 | tf_op jit(solution)/shard_map/pallas_call | solution.py:580
  154.4 12.0 %shard_map.187 = (bf16[9344,768]{1,0:T(8,128)(2,1)S(1)}, f32[512,768]{1,0:T(8,128)S(1)}) custom-call(s32[512,1]{1,0:T(8,128)S(1)} %fusion.73.at_ref, bf16[32,400,768]{2,1,0:T(8,128)(2,1)} %shard_map.186.pool_ref), custom_call_target="tpu_custom_call" | custom-call | flops 2818572288 | bytes 39321600 | tf_op jit(solution)/shard_map/pallas_call | solution.py:1015
  166.5 5.3 copy-done
  173.2 1.5 fusion.97
  174.8 1.5 add_convert_fusion.4
  176.3 3.2 convolution_convert_fusion.6
  179.6 2.1 add_convert_fusion.2
  182.2 1.7 copy.231
  184.1 3.2 add_convert_fusion.3
  187.3 1.4 copy.229
  189.8 1.3 fusion.134
  191.8 1.0 copy-done.16
  193.7 2.2 fusion.135
  196.3 0.9 constant_dynamic-slice_fusion.1
  197.5 9.0 %multiply_convert_fusion = (bf16[512,3072]{1,0:T(8,128)(2,1)S(1)}, f32[512,3072]{1,0:T(8,128)}) fusion(f32[3072]{0:T(1024)S(1)} %bitcast.240, bf16[512,768]{1,0:T(8,128)(2,1)S(1)} %add_convert_fusion.1, bf16[9344,768]{1,0:T(8,128)(2,1)} %copy-done), kind=kOutput, calls=%fused_computation.33 | convolution fusion | flops 2431647744 | bytes 14954496 | tf_op jit(solution)/shard_map/dot_general | solution.py:38
  206.6 6.2 fusion.136
  213.1 1.2 fusion.53.src
  214.4 139.5 %shard_map.188 = (bf16[32,512,768]{2,1,0:T(8,128)(2,1)}, f32[32,2,512]{2,1,0:T(2,128)}) custom-call(bf16[1,512,768]{2,1,0:T(8,128)(2,1)} %fusion.53.src, bf16[4,1600,768]{2,1,0:T(8,128)(2,1)} %get-tuple-element.387, s32[8,1,512]{2,1,0:T(1,128)} %bitcast.224), custom_call_target="tpu_custom_call" | custom-call | flops 40265318400 | bytes 50331648 | tf_op jit(solution)/shard_map/pallas_call | solution.py:770
  353.9 1.0 reshape.724
  358.6 56.6 %shard_map.189 = (bf16[44,128,768]{2,1,0:T(8,128)(2,1)}, f32[4,1600,768]{2,1,0:T(8,128)}) custom-call(s32[11]{0:T(128)} %copy-done.68, s32[11]{0:T(128)} %add_convert_fusion.6.fresh_ref, s32[1]{0:T(128)} %bitcast.23.used_ref, s32[44]{0:T(128)} %get-tuple-element.282.piece_ref, s32[44]{0:T(128)} %get-tuple-element.281.place_ref, ...), custom_call_target="tpu_custom_call" | custom-call | flops 41523609600 | bytes 46792704 | tf_op jit(solution)/shard_map/pallas_call | solution.py:1101
  415.2 61.3 %shard_map.190 = bf16[4,128,768]{2,1,0:T(8,128)(2,1)} custom-call(bf16[44,128,768]{2,1,0:T(8,128)(2,1)} %get-tuple-element.100.source), custom_call_target="tpu_custom_call" | custom-call | bytes 12582912 | tf_op jit(solution)/shard_map/pallas_call | solution.py:963
  476.5 0.8 fusion.112
  477.3 1.6 fusion.125
  480.4 8.5 %convert_reduce_fusion = (f32[3072]{0:T(1024)S(1)}, bf16[512,3072]{1,0:T(8,128)(2,1)S(1)}) fusion(f32[512,3072]{1,0:T(8,128)S(1)} %bitcast.257, f32[3072]{0:T(1024)S(1)} %bitcast.241, bf16[512,768]{1,0:T(8,128)(2,1)S(1)} %get-tuple-element.108, bf16[9344,768]{1,0:T(8,128)(2,1)} %copy-done), kind=kOutput, calls=%fused_computation.32 | convolution fusion | flops 2452091904 | bytes 14966784 | tf_op jit(solution)/shard_map/dot_general | solution.py:38
  488.9 6.4 multiply_reduce_fusion.1
  496.4 0.9 copy-done.30
  497.2 2.9 convolution_convert_fusion.5
  500.2 2.3 copy.239
  502.4 2.4 reshape.730
  504.9 3.6 convert_reduce_fusion.3
  508.5 0.8 multiply_reduce_fusion
  509.3 1.0 multiply_convert_fusion.1
  510.5 1.2 fusion.42
  512.8 1.0 copy.312
  516.1 1.1 copy-done.2
  517.3 5.3 multiply_reduce_fusion.2
  523.4 1.8 fusion.128
  525.3 8.5 %all-to-all-start.1 = ((bf16[4,128,768]{2,1,0:T(8,128)(2,1)}), bf16[4,128,768]{2,1,0:T(8,128)(2,1)S(1)}, u32[]{:S(2)}, u32[]{:S(2)}) async-start(bf16[4,128,768]{2,1,0:T(8,128)(2,1)} %bitcast.217), calls=%async_computation.1 | async-start | bytes 1572864 | tf_op jit(solution)/shard_map/all_to_all | solution.py:1432
  534.3 5.6 fusion.17
  539.9 1.8 fusion.36
  541.7 4.4 fusion.16
  546.1 4.4 fusion.15
  551.2 1.7 all-to-all-done.1
  555.7 0.8 reduce_sum.514
  556.5 39.6 %shard_map.191.d_ref = bf16[32,128,768]{2,1,0:T(8,128)(2,1)} custom-call(bf16[1,128,768]{2,1,0:T(8,128)(2,1)} %bitcast.226), custom_call_target="tpu_custom_call" | custom-call | bytes 12582912 | tf_op jit(solution)/shard_map/pallas_call | solution.py:580
  596.2 41.5 %shard_map.192 = (f32[4,1600,768]{2,1,0:T(8,128)}, f32[4,1600,768]{2,1,0:T(8,128)}, f32[4,1600,768]{2,1,0:T(8,128)}) custom-call(s32[4]{0:T(128)} %multiply_convert_fusion.4.start_ref, s32[4]{0:T(128)} %get-tuple-element.246.end_ref, s32[22]{0:T(128)} %slice.151.first_ref, s32[22]{0:T(128)} %slice.152.second_ref, bf16[32,128,768]{2,1,0:T(8,128)(2,1)} %shard_map.191.d_ref, ...), custom_call_target="tpu_custom_call" | custom-call | flops 7549747200 | bytes 88473600 | tf_op jit(solution)/shard_map/pallas_call | solution.py:1162
  637.7 9.1 %all_to_all.34 = f32[8,1,1344]{2,1,0:T(1,128)S(1)} all-to-all(f32[8,1,1344]{2,1,0:T(1,128)S(1)} %all_to_all.22), channel_id=1, replica_groups=mesh['grp'=8,'cli'=4] {'grp'}, dimensions={0} | all-to-all | bytes 86016 | tf_op jit(solution)/shard_map/all_to_all | solution.py:1456
  646.8 7.2 reduce-scatter.2.cloned.1.call-done
  654.1 2.6 reshape.741
  656.6 4.6 all-to-all-start.3
  661.4 15.7 %shard_map.193 = (f32[4,1600,768]{2,1,0:T(8,128)}, f32[4,1600,768]{2,1,0:T(8,128)}, f32[4,1600,768]{2,1,0:T(8,128)}) custom-call(s32[4]{0:T(128)} %multiply_convert_fusion.4.start_ref, s32[4]{0:T(128)} %get-tuple-element.246.end_ref, s32[22]{0:T(128)} %slice.151.first_ref, ...), custom_call_target="tpu_custom_call", output_to_operand_aliasing={{0}: (9, {}), {1}: (10, {}), {2}: (11, {})} | custom-call | flops 2516582400 | bytes 29491200 | tf_op jit(solution)/shard_map/pallas_call | solution.py:1162
  677.1 26.2 %all-to-all-done.3.gradient_ref = bf16[4,292,768]{2,1,0:T(8,128)(2,1)S(1)} async-done(((bf16[4,292,768]{2,1,0:T(8,128)(2,1)}), bf16[4,292,768]{2,1,0:T(8,128)(2,1)S(1)}, u32[]{:S(2)}, u32[]{:S(2)}) %all-to-all-start.3) | async-done | bytes 1794080 | tf_op jit(solution)/shard_map/all_to_all | solution.py:1460
  703.4 0.9 broadcast_in_dim.274
  704.3 2.9 all-to-all-start.4
  708.5 10.7 %shard_map.194 = (f32[292,4,768]{2,1,0:T(4,128)}, f32[292,4,768]{2,1,0:T(4,128)}, f32[292,4,768]{2,1,0:T(4,128)}) custom-call(bf16[4,292,768]{2,1,0:T(8,128)(2,1)} %copy-done.7, f32[292,4,768]{2,1,0:T(4,128)} %bitcast.214, f32[292,4,768]{2,1,0:T(4,128)} %bitcast.216), custom_call_target="tpu_custom_call" | custom-call | flops 5382144 | bytes 19734528 | tf_op jit(solution)/shard_map/pallas_call | solution.py:1195
  719.8 0.8 copy.254
  720.7 0.8 copy.255
  721.5 0.8 copy.256
  (292 shorter events, 35.6 us)
Async XLA Ops:
  29.6 10.9 %copy-start.35 = (pred[32,127]{1,0:T(8,128)(4,1)}, pred[32,127]{1,0:T(8,128)(4,1)S(1)}, u32[]{:S(2)}) copy-start(pred[32,127]{1,0:T(8,128)(4,1)S(1)} %slice_compare_fusion) | copy-start | bytes 12196
  29.8 6.3 copy-start.56
  31.4 3.4 copy-start.64
  32.2 8.4 %copy-start.54 = (pred[44]{0:T(512)(128)(4,1)}, pred[44]{0:T(512)(128)(4,1)S(1)}, u32[]{:S(2)}) copy-start(pred[44]{0:T(512)(128)(4,1)S(1)} %fusion.86) | copy-start | bytes 136
  32.3 8.3 %copy-start.66 = (s32[44]{0:T(128)}, s32[44]{0:T(128)S(1)}, u32[]{:S(2)}) copy-start(s32[44]{0:T(128)S(1)} %select_reduce_fusion.1) | copy-start | bytes 532
  32.3 8.2 %copy-start.18 = (s32[32,128]{1,0:T(8,128)}, s32[32,128]{1,0:T(8,128)S(1)}, u32[]{:S(2)}) copy-start(s32[32,128]{1,0:T(8,128)S(1)} %get-tuple-element.268) | copy-start | bytes 49156
  34.9 5.7 copy-start.62
  166.5 5.4 copy-start
  171.8 3.0 copy-start.5
  172.1 2.7 copy-start.1
  172.3 4.0 copy-start.41
  172.7 3.7 copy-start.46
  174.8 1.5 copy-start.38
  176.3 7.7 %copy-start.20 = (bf16[512,768]{1,0:T(8,128)(2,1)}, bf16[512,768]{1,0:T(8,128)(2,1)S(1)}, u32[]{:S(2)}) copy-start(bf16[512,768]{1,0:T(8,128)(2,1)S(1)} %get-tuple-element.102) | copy-start | bytes 2359300
  182.1 6.8 copy-start.8
  182.1 1.9 copy-start.61
  184.0 4.9 copy-start.10
  188.9 2.2 copy-start.22
  191.2 1.7 copy-start.16
  191.2 2.5 copy-start.19
  191.2 2.5 copy-start.60
  193.4 2.5 copy-start.14
  193.7 3.4 copy-start.45
  193.7 3.5 copy-start.52
  196.0 10.6 %copy-start.3 = (f32[512,768]{1,0:T(8,128)}, f32[512,768]{1,0:T(8,128)S(1)}, u32[]{:S(2)}) copy-start(f32[512,768]{1,0:T(8,128)S(1)} %get-tuple-element.291) | copy-start | bytes 4718596
  197.5 9.1 %copy-start.26 = (bf16[512,768]{1,0:T(8,128)(2,1)}, bf16[512,768]{1,0:T(8,128)(2,1)S(1)}, u32[]{:S(2)}) copy-start(bf16[512,768]{1,0:T(8,128)(2,1)S(1)} %add_convert_fusion.1) | copy-start | bytes 2359300
  197.5 9.1 %copy-start.59 = (f32[768]{0:T(1024)S(1)}, f32[768]{0:T(1024)}, u32[]{:S(2)}) copy-start(f32[768]{0:T(1024)} %get-tuple-element.211) | copy-start | bytes 9220
  206.6 6.2 copy-start.70
  206.6 6.5 copy-start.40
  206.6 6.5 copy-start.51
  214.3 140.6 %copy-start.43 = (s32[8,4]{1,0:T(8,128)S(1)}, s32[8,4]{1,0:T(8,128)}, u32[]{:S(2)}) copy-start(s32[8,4]{1,0:T(8,128)} %eq.178) | copy-start | bytes 388
  214.3 141.5 %copy-start.36 = (pred[32,127]{1,0:T(8,128)(4,1)S(1)}, pred[32,127]{1,0:T(8,128)(4,1)}, u32[]{:S(2)}) copy-start(pred[32,127]{1,0:T(8,128)(4,1)} %copy-done.35) | copy-start | bytes 12196
  214.3 141.5 %copy-start.58 = (f32[32]{0:T(128)S(1)}, f32[32]{0:T(128)}, u32[]{:S(2)}) copy-start(f32[32]{0:T(128)} %get-tuple-element.223) | copy-start | bytes 388
  214.3 142.3 %copy-start.55 = (pred[44]{0:T(512)(128)(4,1)S(1)}, pred[44]{0:T(512)(128)(4,1)}, u32[]{:S(2)}) copy-start(pred[44]{0:T(512)(128)(4,1)} %copy-done.54) | copy-start | bytes 136
  214.3 142.3 %copy-start.63 = (pred[44]{0:T(512)(128)(4,1)S(1)}, pred[44]{0:T(512)(128)(4,1)}, u32[]{:S(2)}) copy-start(pred[44]{0:T(512)(128)(4,1)} %copy-done.62) | copy-start | bytes 136
  214.4 143.6 %copy-start.69 = (pred[10]{0:T(512)(128)(4,1)S(1)}, pred[10]{0:T(512)(128)(4,1)}, u32[]{:S(2)}) copy-start(pred[10]{0:T(512)(128)(4,1)} %slice_compare_fusion.1) | copy-start | bytes 34
  415.2 65.2 %slice-start = ((s8[6291456]{0:T(1024)(128)(4,1)}), s8[2097152]{0:T(1024)(128)(4,1)S(1)}, s32[]{:S(2)}) async-start(s8[6291456]{0:T(1024)(128)(4,1)} %bitcast.256), calls=%async_computation.8 | async-start | bytes 4194304
  477.3 3.1 slice-start.1
  480.4 8.6 %copy-start.28 = (bf16[512,768]{1,0:T(8,128)(2,1)}, bf16[512,768]{1,0:T(8,128)(2,1)S(1)}, u32[]{:S(2)}) copy-start(bf16[512,768]{1,0:T(8,128)(2,1)S(1)} %get-tuple-element.108) | copy-start | bytes 2359300
  480.4 8.5 %copy-start.4 = (f32[512,768]{1,0:T(8,128)S(1)}, f32[512,768]{1,0:T(8,128)}, u32[]{:S(2)}) copy-start(f32[512,768]{1,0:T(8,128)} %copy-done.3) | copy-start | bytes 4718596
  488.9 6.4 copy-start.72
  504.9 3.6 copy-start.17
  504.9 3.6 copy-start.23
  504.9 3.6 copy-start.25
  517.3 5.4 copy-start.13
  517.3 5.4 copy-start.50
  525.3 8.9 %copy-start.12 = (f32[512,768]{1,0:T(8,128)S(1)}, f32[512,768]{1,0:T(8,128)}, u32[]{:S(2)}) copy-start(f32[512,768]{1,0:T(8,128)} %get-tuple-element.249) | copy-start | bytes 4718596
  525.3 9.0 %copy-start.21 = (bf16[512,768]{1,0:T(8,128)(2,1)S(1)}, bf16[512,768]{1,0:T(8,128)(2,1)}, u32[]{:S(2)}) copy-start(bf16[512,768]{1,0:T(8,128)(2,1)} %copy-done.20) | copy-start | bytes 2359300
  525.3 27.7 %all-to-all-start.1 = ((bf16[4,128,768]{2,1,0:T(8,128)(2,1)}), bf16[4,128,768]{2,1,0:T(8,128)(2,1)S(1)}, u32[]{:S(2)}, u32[]{:S(2)}) async-start(bf16[4,128,768]{2,1,0:T(8,128)(2,1)} %bitcast.217), calls=%async_computation.1 | async-start | bytes 1572864 | tf_op jit(solution)/shard_map/all_to_all | solution.py:1432
  533.7 120.3 %reduce-scatter.2.cloned.1.call-start = ((), (), s32[]{:S(2)}) async-start(), calls=%async_computation.6 | async-start | bytes 16146432 | tf_op jit(solution)/shard_map/reduce_scatter | solution.py:1441
  534.3 5.6 copy-start.24
  534.3 5.6 copy-start.31
  534.3 7.4 %copy-start.73 = (bf16[512,3072]{1,0:T(8,128)(2,1)S(1)}, bf16[512,3072]{1,0:T(8,128)(2,1)}, u32[]{:S(2)}) copy-start(bf16[512,3072]{1,0:T(8,128)(2,1)} %copy-done.72) | copy-start | bytes 9437188
  539.9 1.8 copy-start.27
  541.7 4.4 copy-start.29
  541.7 4.4 copy-start.71
  551.2 1.8 copy-start.67
  551.2 3.3 copy-start.34
  551.2 4.0 copy-start.65
  656.6 46.7 %all-to-all-start.3 = ((bf16[4,292,768]{2,1,0:T(8,128)(2,1)}), bf16[4,292,768]{2,1,0:T(8,128)(2,1)S(1)}, u32[]{:S(2)}, u32[]{:S(2)}) async-start(bf16[4,292,768]{2,1,0:T(8,128)(2,1)} %reshape.741), calls=%async_computation.4 | async-start | bytes 3637248 | tf_op jit(solution)/shard_map/all_to_all | solution.py:1460
  661.4 45.8 %copy-start.57 = (f32[32]{0:T(128)S(1)}, f32[32]{0:T(128)}, u32[]{:S(2)}) copy-start(f32[32]{0:T(128)} %copy-done.56) | copy-start | bytes 388
  661.4 46.5 %copy-start.44 = (s32[8,4]{1,0:T(8,128)S(1)}, s32[8,4]{1,0:T(8,128)}, u32[]{:S(2)}) copy-start(s32[8,4]{1,0:T(8,128)} %eq.178) | copy-start | bytes 388
  703.4 5.1 copy-start.7
  704.3 14.9 %all-to-all-start.4 = ((f32[32,1,1344]{2,1,0:T(1,128)}), f32[32,1,1344]{2,1,0:T(1,128)S(1)}, u32[]{:S(2)}, u32[]{:S(2)}) async-start(f32[32,1,1344]{2,1,0:T(1,128)} %broadcast_in_dim.274), calls=%async_computation.5 | async-start | bytes 360448 | tf_op jit(solution)/shard_map/all_to_all | solution.py:233
  (16 other events, 17.7 us)
Sparse Core Ops, SparseCore 1:
  553.1 100.9 reduce-scatter.1

commit v13 on v12

--- a/solution.py
+++ b/solution.py
@@ -590,8 +590,8 @@
     )(src)
 
 
-def tile_of(part_rows):
-    return TILE if part_rows % TILE == 0 else part_rows
+def tile_of(part_rows, size=TILE):
+    return size if part_rows % size == 0 else part_rows
 
 
 def opening_kernel(groups, members, facts_ref, table_ref, facts_out, low_ref, own_sem, send_sems, recv_sems):
@@ -626,7 +626,7 @@
         own.start()
         lax.fori_loop(1, devices, hello, 0)
 
-    @pl.when(step == last // 2)
+    @pl.when(step == last // 4)
     def exchange():
         def start(j, carry):
             give(j).start()
@@ -1064,7 +1064,7 @@
 
         outs = jnp.concatenate([piece[0] for piece in pieces], axis=0)
         part_rows = table_ref.shape[1]
-        size = tile_of(part_rows)
+        size = tile_of(part_rows, 2 * TILE)
         d_outs = jnp.zeros(outs.shape, jnp.float32)
         for first_row in range(0, part_rows, size):
             here = pl.ds(first_row, size)

time: 739 us -> 741 us (level)
    pallas_call x2, Pallas kernels: 140 us -> 131 us  [spread(): pl.pallas_call(functools.partial(spread_kernel, groups, members, chain, p...]
where the time goes in v13:
time: 741 us; the launch traced here: 729 us
  Pallas kernels  497 us (67%)
  matrix products  81.6 us (11%)
  local copies, waits for them, and re-layouts  43.4 us (6%)
  waiting for transfers between devices  34 us (5%)
  other arithmetic  30.3 us (4%)
  between operations  18.9 us (3%)
  starting transfers between devices  15.8 us (2%)
  blocking collectives  8.39 us (1%)
    pallas_call x1, Pallas kernels, spread_score(): pl.pallas_call(functools.partial(score_kernel, groups, members, share, pi...  142 us
    pallas_call x2, Pallas kernels, spread(): pl.pallas_call(functools.partial(spread_kernel, groups, members, chain, p...  131 us
    pallas_call x1, Pallas kernels, collect(): pl.pallas_call(functools.partial(collect_kernel, groups, members), out_sh...  61.3 us
    pallas_call x2, Pallas kernels, finish_table(): pl.pallas_call(functools.partial(finish_kernel, first_model), out_shape=(...  59.5 us
    pallas_call x1, Pallas kernels, head_back(): pl.pallas_call(back_kernel, out_shape=(jax.ShapeDtypeStruct((QUAD * steps...  58.9 us
    dot_general x6, matrix products, project(): lax.dot_general(inputs, matrix, (((1,), (1,)), ((), ())), preferred_eleme...  28.3 us
    all_to_all x1, waiting for transfers between devices, body(): lax.all_to_all(stack_sum.reshape(members, stack_part, model_width), 'cli'...  25.1 us
    dot_general x6, matrix products, product(): return jnp.dot(inputs, matrix, preferred_element_type=jnp.float32)  21.7 us
  transfers between devices with their start and end apart: 4, of which 3 were waited for; matrix products, arithmetic and copies ran while one was open for 3% of the time, Pallas kernels for 15%

profile of v13, /device:TPU:0, one launch (start us, length us, event | category | flops | bytes accessed | tf_op | source)
XLA Modules:
  0.0 729.2 jit_solution(9428467125340068397)
XLA Ops:
  9.9 21.4 %shard_map.185 = (s32[32,1,512]{2,1,0:T(1,128)}, bf16[4,1600,768]{2,1,0:T(8,128)(2,1)}) custom-call(s32[1,512]{1,0:T(1,128)} %bitcast.243, f32[4,1600,768]{2,1,0:T(8,128)} %table_ref.5), custom_call_target="tpu_custom_call" | custom-call | bytes 29491200 | tf_op jit(solution)/shard_map/pallas_call | solution.py:661
  31.3 0.8 copy.313
  41.3 2.6 fusion.133
  46.6 2.6 convert_element_type.240
  49.5 5.3 fusion.43
  54.9 1.6 pad_maximum_fusion.src
  56.5 91.3 %shard_map.186.pool_ref = bf16[32,400,768]{2,1,0:T(8,128)(2,1)} custom-call(bf16[4,400,768]{2,1,0:T(8,128)(2,1)} %pad_maximum_fusion.src), custom_call_target="tpu_custom_call" | custom-call | bytes 39321600 | tf_op jit(solution)/shard_map/pallas_call | solution.py:580
  149.2 12.0 %shard_map.187 = (bf16[9344,768]{1,0:T(8,128)(2,1)S(1)}, f32[512,768]{1,0:T(8,128)S(1)}) custom-call(s32[512,1]{1,0:T(8,128)S(1)} %fusion.73.at_ref, bf16[32,400,768]{2,1,0:T(8,128)(2,1)} %shard_map.186.pool_ref), custom_call_target="tpu_custom_call" | custom-call | flops 2818572288 | bytes 39321600 | tf_op jit(solution)/shard_map/pallas_call | solution.py:1015
  161.2 5.3 copy-done
  168.0 1.5 fusion.97
  169.6 1.5 add_convert_fusion.4
  171.1 3.2 convolution_convert_fusion.6
  174.3 2.1 add_convert_fusion.2
  176.9 1.7 copy.231
  178.8 3.2 add_convert_fusion.3
  182.1 1.4 copy.229
  184.6 1.3 fusion.134
  186.6 1.0 copy-done.16
  188.5 2.2 fusion.135
  191.1 0.9 constant_dynamic-slice_fusion.1
  192.3 9.0 %multiply_convert_fusion = (bf16[512,3072]{1,0:T(8,128)(2,1)S(1)}, f32[512,3072]{1,0:T(8,128)}) fusion(f32[3072]{0:T(1024)S(1)} %bitcast.240, bf16[512,768]{1,0:T(8,128)(2,1)S(1)} %add_convert_fusion.1, bf16[9344,768]{1,0:T(8,128)(2,1)} %copy-done), kind=kOutput, calls=%fused_computation.33 | convolution fusion | flops 2431647744 | bytes 14954496 | tf_op jit(solution)/shard_map/dot_general | solution.py:38
  201.4 6.2 fusion.136
  207.9 1.2 fusion.53.src
  209.1 142.3 %shard_map.188 = (bf16[32,512,768]{2,1,0:T(8,128)(2,1)}, f32[32,2,512]{2,1,0:T(2,128)}) custom-call(bf16[1,512,768]{2,1,0:T(8,128)(2,1)} %fusion.53.src, bf16[4,1600,768]{2,1,0:T(8,128)(2,1)} %get-tuple-element.387, s32[8,1,512]{2,1,0:T(1,128)} %bitcast.224), custom_call_target="tpu_custom_call" | custom-call | flops 40265318400 | bytes 50331648 | tf_op jit(solution)/shard_map/pallas_call | solution.py:770
  351.4 1.0 reshape.724
  356.1 58.9 %shard_map.189 = (bf16[44,128,768]{2,1,0:T(8,128)(2,1)}, f32[4,1600,768]{2,1,0:T(8,128)}) custom-call(s32[11]{0:T(128)} %copy-done.68, s32[11]{0:T(128)} %add_convert_fusion.6.fresh_ref, s32[1]{0:T(128)} %bitcast.23.used_ref, s32[44]{0:T(128)} %get-tuple-element.282.piece_ref, s32[44]{0:T(128)} %get-tuple-element.281.place_ref, ...), custom_call_target="tpu_custom_call" | custom-call | flops 41523609600 | bytes 46792704 | tf_op jit(solution)/shard_map/pallas_call | solution.py:1101
  415.1 61.3 %shard_map.190 = bf16[4,128,768]{2,1,0:T(8,128)(2,1)} custom-call(bf16[44,128,768]{2,1,0:T(8,128)(2,1)} %get-tuple-element.100.source), custom_call_target="tpu_custom_call" | custom-call | bytes 12582912 | tf_op jit(solution)/shard_map/pallas_call | solution.py:963
  476.4 0.8 fusion.112
  477.2 1.6 fusion.125
  480.3 8.5 %convert_reduce_fusion = (f32[3072]{0:T(1024)S(1)}, bf16[512,3072]{1,0:T(8,128)(2,1)S(1)}) fusion(f32[512,3072]{1,0:T(8,128)S(1)} %bitcast.257, f32[3072]{0:T(1024)S(1)} %bitcast.241, bf16[512,768]{1,0:T(8,128)(2,1)S(1)} %get-tuple-element.108, bf16[9344,768]{1,0:T(8,128)(2,1)} %copy-done), kind=kOutput, calls=%fused_computation.32 | convolution fusion | flops 2452091904 | bytes 14966784 | tf_op jit(solution)/shard_map/dot_general | solution.py:38
  488.8 6.4 multiply_reduce_fusion.1
  496.2 0.9 copy-done.30
  497.1 2.9 convolution_convert_fusion.5
  500.0 2.3 copy.239
  502.3 2.4 reshape.730
  504.8 3.6 convert_reduce_fusion.3
  508.4 0.8 multiply_reduce_fusion
  509.2 1.0 multiply_convert_fusion.1
  510.4 1.2 fusion.42
  512.7 1.0 copy.312
  516.0 1.1 copy-done.2
  517.2 5.3 multiply_reduce_fusion.2
  523.3 1.8 fusion.128
  525.1 7.9 %all-to-all-start.1 = ((bf16[4,128,768]{2,1,0:T(8,128)(2,1)}), bf16[4,128,768]{2,1,0:T(8,128)(2,1)S(1)}, u32[]{:S(2)}, u32[]{:S(2)}) async-start(bf16[4,128,768]{2,1,0:T(8,128)(2,1)} %bitcast.217), calls=%async_computation.1 | async-start | bytes 1572864 | tf_op jit(solution)/shard_map/all_to_all | solution.py:1432
  533.6 5.6 fusion.17
  539.2 1.8 fusion.36
  541.1 4.4 fusion.16
  545.5 4.4 fusion.15
  550.6 2.2 all-to-all-done.1
  555.6 0.8 reduce_sum.514
  556.4 39.2 %shard_map.191.d_ref = bf16[32,128,768]{2,1,0:T(8,128)(2,1)} custom-call(bf16[1,128,768]{2,1,0:T(8,128)(2,1)} %bitcast.226), custom_call_target="tpu_custom_call" | custom-call | bytes 12582912 | tf_op jit(solution)/shard_map/pallas_call | solution.py:580
  595.6 42.6 %shard_map.192 = (f32[4,1600,768]{2,1,0:T(8,128)}, f32[4,1600,768]{2,1,0:T(8,128)}, f32[4,1600,768]{2,1,0:T(8,128)}) custom-call(s32[4]{0:T(128)} %multiply_convert_fusion.4.start_ref, s32[4]{0:T(128)} %get-tuple-element.246.end_ref, s32[22]{0:T(128)} %slice.151.first_ref, s32[22]{0:T(128)} %slice.152.second_ref, bf16[32,128,768]{2,1,0:T(8,128)(2,1)} %shard_map.191.d_ref, ...), custom_call_target="tpu_custom_call" | custom-call | flops 7549747200 | bytes 88473600 | tf_op jit(solution)/shard_map/pallas_call | solution.py:1162
  638.3 8.4 %all_to_all.34 = f32[8,1,1344]{2,1,0:T(1,128)S(1)} all-to-all(f32[8,1,1344]{2,1,0:T(1,128)S(1)} %all_to_all.22), channel_id=1, replica_groups=mesh['grp'=8,'cli'=4] {'grp'}, dimensions={0} | all-to-all | bytes 86016 | tf_op jit(solution)/shard_map/all_to_all | solution.py:1456
  646.7 6.6 reduce-scatter.2.cloned.1.call-done
  653.3 2.6 reshape.741
  655.9 4.6 all-to-all-start.3
  660.7 16.9 %shard_map.193 = (f32[4,1600,768]{2,1,0:T(8,128)}, f32[4,1600,768]{2,1,0:T(8,128)}, f32[4,1600,768]{2,1,0:T(8,128)}) custom-call(s32[4]{0:T(128)} %multiply_convert_fusion.4.start_ref, s32[4]{0:T(128)} %get-tuple-element.246.end_ref, s32[22]{0:T(128)} %slice.151.first_ref, ...), custom_call_target="tpu_custom_call", output_to_operand_aliasing={{0}: (9, {}), {1}: (10, {}), {2}: (11, {})} | custom-call | flops 2516582400 | bytes 29491200 | tf_op jit(solution)/shard_map/pallas_call | solution.py:1162
  677.5 25.1 %all-to-all-done.3.gradient_ref = bf16[4,292,768]{2,1,0:T(8,128)(2,1)S(1)} async-done(((bf16[4,292,768]{2,1,0:T(8,128)(2,1)}), bf16[4,292,768]{2,1,0:T(8,128)(2,1)S(1)}, u32[]{:S(2)}, u32[]{:S(2)}) %all-to-all-start.3) | async-done | bytes 1794080 | tf_op jit(solution)/shard_map/all_to_all | solution.py:1460
  702.7 0.9 broadcast_in_dim.274
  703.5 2.9 all-to-all-start.4
  707.8 10.7 %shard_map.194 = (f32[292,4,768]{2,1,0:T(4,128)}, f32[292,4,768]{2,1,0:T(4,128)}, f32[292,4,768]{2,1,0:T(4,128)}) custom-call(bf16[4,292,768]{2,1,0:T(8,128)(2,1)} %copy-done.7, f32[292,4,768]{2,1,0:T(4,128)} %bitcast.214, f32[292,4,768]{2,1,0:T(4,128)} %bitcast.216), custom_call_target="tpu_custom_call" | custom-call | flops 5382144 | bytes 19734528 | tf_op jit(solution)/shard_map/pallas_call | solution.py:1195
  719.1 0.8 copy.254
  720.0 0.8 copy.255
  720.8 0.8 copy.256
  (292 shorter events, 35.6 us)
Async XLA Ops:
  33.0 10.9 %copy-start.35 = (pred[32,127]{1,0:T(8,128)(4,1)}, pred[32,127]{1,0:T(8,128)(4,1)S(1)}, u32[]{:S(2)}) copy-start(pred[32,127]{1,0:T(8,128)(4,1)S(1)} %slice_compare_fusion) | copy-start | bytes 12196
  33.1 6.3 copy-start.56
  34.7 3.4 copy-start.64
  35.5 8.4 %copy-start.54 = (pred[44]{0:T(512)(128)(4,1)}, pred[44]{0:T(512)(128)(4,1)S(1)}, u32[]{:S(2)}) copy-start(pred[44]{0:T(512)(128)(4,1)S(1)} %fusion.86) | copy-start | bytes 136
  35.6 8.3 %copy-start.66 = (s32[44]{0:T(128)}, s32[44]{0:T(128)S(1)}, u32[]{:S(2)}) copy-start(s32[44]{0:T(128)S(1)} %select_reduce_fusion.1) | copy-start | bytes 532
  35.7 8.2 %copy-start.18 = (s32[32,128]{1,0:T(8,128)}, s32[32,128]{1,0:T(8,128)S(1)}, u32[]{:S(2)}) copy-start(s32[32,128]{1,0:T(8,128)S(1)} %get-tuple-element.268) | copy-start | bytes 49156
  38.2 5.7 copy-start.62
  161.2 5.4 copy-start
  166.6 3.0 copy-start.5
  166.9 2.7 copy-start.1
  167.1 4.0 copy-start.41
  167.4 3.7 copy-start.46
  169.6 1.5 copy-start.38
  171.1 7.7 %copy-start.20 = (bf16[512,768]{1,0:T(8,128)(2,1)}, bf16[512,768]{1,0:T(8,128)(2,1)S(1)}, u32[]{:S(2)}) copy-start(bf16[512,768]{1,0:T(8,128)(2,1)S(1)} %get-tuple-element.102) | copy-start | bytes 2359300
  176.9 6.8 copy-start.8
  176.9 1.9 copy-start.61
  178.8 4.9 copy-start.10
  183.7 2.2 copy-start.22
  185.9 1.7 copy-start.16
  185.9 2.5 copy-start.19
  186.0 2.5 copy-start.60
  188.2 2.5 copy-start.14
  188.5 3.4 copy-start.45
  188.5 3.5 copy-start.52
  190.7 10.6 %copy-start.3 = (f32[512,768]{1,0:T(8,128)}, f32[512,768]{1,0:T(8,128)S(1)}, u32[]{:S(2)}) copy-start(f32[512,768]{1,0:T(8,128)S(1)} %get-tuple-element.291) | copy-start | bytes 4718596
  192.3 9.1 %copy-start.26 = (bf16[512,768]{1,0:T(8,128)(2,1)}, bf16[512,768]{1,0:T(8,128)(2,1)S(1)}, u32[]{:S(2)}) copy-start(bf16[512,768]{1,0:T(8,128)(2,1)S(1)} %add_convert_fusion.1) | copy-start | bytes 2359300
  192.3 9.1 %copy-start.59 = (f32[768]{0:T(1024)S(1)}, f32[768]{0:T(1024)}, u32[]{:S(2)}) copy-start(f32[768]{0:T(1024)} %get-tuple-element.211) | copy-start | bytes 9220
  201.3 6.2 copy-start.70
  201.3 6.5 copy-start.40
  201.4 6.5 copy-start.51
  209.1 143.3 %copy-start.43 = (s32[8,4]{1,0:T(8,128)S(1)}, s32[8,4]{1,0:T(8,128)}, u32[]{:S(2)}) copy-start(s32[8,4]{1,0:T(8,128)} %eq.178) | copy-start | bytes 388
  209.1 144.3 %copy-start.36 = (pred[32,127]{1,0:T(8,128)(4,1)S(1)}, pred[32,127]{1,0:T(8,128)(4,1)}, u32[]{:S(2)}) copy-start(pred[32,127]{1,0:T(8,128)(4,1)} %copy-done.35) | copy-start | bytes 12196
  209.1 144.3 %copy-start.58 = (f32[32]{0:T(128)S(1)}, f32[32]{0:T(128)}, u32[]{:S(2)}) copy-start(f32[32]{0:T(128)} %get-tuple-element.223) | copy-start | bytes 388
  209.1 145.1 %copy-start.55 = (pred[44]{0:T(512)(128)(4,1)S(1)}, pred[44]{0:T(512)(128)(4,1)}, u32[]{:S(2)}) copy-start(pred[44]{0:T(512)(128)(4,1)} %copy-done.54) | copy-start | bytes 136
  209.1 145.1 %copy-start.63 = (pred[44]{0:T(512)(128)(4,1)S(1)}, pred[44]{0:T(512)(128)(4,1)}, u32[]{:S(2)}) copy-start(pred[44]{0:T(512)(128)(4,1)} %copy-done.62) | copy-start | bytes 136
  209.1 146.4 %copy-start.69 = (pred[10]{0:T(512)(128)(4,1)S(1)}, pred[10]{0:T(512)(128)(4,1)}, u32[]{:S(2)}) copy-start(pred[10]{0:T(512)(128)(4,1)} %slice_compare_fusion.1) | copy-start | bytes 34
  415.1 65.2 %slice-start = ((s8[6291456]{0:T(1024)(128)(4,1)}), s8[2097152]{0:T(1024)(128)(4,1)S(1)}, s32[]{:S(2)}) async-start(s8[6291456]{0:T(1024)(128)(4,1)} %bitcast.256), calls=%async_computation.8 | async-start | bytes 4194304
  477.2 3.1 slice-start.1
  480.2 8.6 %copy-start.28 = (bf16[512,768]{1,0:T(8,128)(2,1)}, bf16[512,768]{1,0:T(8,128)(2,1)S(1)}, u32[]{:S(2)}) copy-start(bf16[512,768]{1,0:T(8,128)(2,1)S(1)} %get-tuple-element.108) | copy-start | bytes 2359300
  480.3 8.5 %copy-start.4 = (f32[512,768]{1,0:T(8,128)S(1)}, f32[512,768]{1,0:T(8,128)}, u32[]{:S(2)}) copy-start(f32[512,768]{1,0:T(8,128)} %copy-done.3) | copy-start | bytes 4718596
  488.8 6.4 copy-start.72
  504.8 3.6 copy-start.17
  504.8 3.6 copy-start.23
  504.8 3.6 copy-start.25
  517.2 5.4 copy-start.13
  517.2 5.4 copy-start.50
  525.1 8.4 %copy-start.12 = (f32[512,768]{1,0:T(8,128)S(1)}, f32[512,768]{1,0:T(8,128)}, u32[]{:S(2)}) copy-start(f32[512,768]{1,0:T(8,128)} %get-tuple-element.249) | copy-start | bytes 4718596
  525.1 8.5 %copy-start.21 = (bf16[512,768]{1,0:T(8,128)(2,1)S(1)}, bf16[512,768]{1,0:T(8,128)(2,1)}, u32[]{:S(2)}) copy-start(bf16[512,768]{1,0:T(8,128)(2,1)} %copy-done.20) | copy-start | bytes 2359300
  525.1 27.7 %all-to-all-start.1 = ((bf16[4,128,768]{2,1,0:T(8,128)(2,1)}), bf16[4,128,768]{2,1,0:T(8,128)(2,1)S(1)}, u32[]{:S(2)}, u32[]{:S(2)}) async-start(bf16[4,128,768]{2,1,0:T(8,128)(2,1)} %bitcast.217), calls=%async_computation.1 | async-start | bytes 1572864 | tf_op jit(solution)/shard_map/all_to_all | solution.py:1432
  533.1 120.2 %reduce-scatter.2.cloned.1.call-start = ((), (), s32[]{:S(2)}) async-start(), calls=%async_computation.6 | async-start | bytes 16146432 | tf_op jit(solution)/shard_map/reduce_scatter | solution.py:1441
  533.6 5.6 copy-start.24
  533.6 5.6 copy-start.31
  533.6 7.4 %copy-start.73 = (bf16[512,3072]{1,0:T(8,128)(2,1)S(1)}, bf16[512,3072]{1,0:T(8,128)(2,1)}, u32[]{:S(2)}) copy-start(bf16[512,3072]{1,0:T(8,128)(2,1)} %copy-done.72) | copy-start | bytes 9437188
  539.2 1.8 copy-start.27
  541.1 4.4 copy-start.29
  541.1 4.4 copy-start.71
  550.6 2.3 copy-start.67
  550.6 3.7 copy-start.34
  550.6 4.4 copy-start.65
  655.9 46.7 %all-to-all-start.3 = ((bf16[4,292,768]{2,1,0:T(8,128)(2,1)}), bf16[4,292,768]{2,1,0:T(8,128)(2,1)S(1)}, u32[]{:S(2)}, u32[]{:S(2)}) async-start(bf16[4,292,768]{2,1,0:T(8,128)(2,1)} %reshape.741), calls=%async_computation.4 | async-start | bytes 3637248 | tf_op jit(solution)/shard_map/all_to_all | solution.py:1460
  660.7 45.8 %copy-start.57 = (f32[32]{0:T(128)S(1)}, f32[32]{0:T(128)}, u32[]{:S(2)}) copy-start(f32[32]{0:T(128)} %copy-done.56) | copy-start | bytes 388
  660.7 46.5 %copy-start.44 = (s32[8,4]{1,0:T(8,128)S(1)}, s32[8,4]{1,0:T(8,128)}, u32[]{:S(2)}) copy-start(s32[8,4]{1,0:T(8,128)} %eq.178) | copy-start | bytes 388
  702.6 5.1 copy-start.7
  703.5 14.9 %all-to-all-start.4 = ((f32[32,1,1344]{2,1,0:T(1,128)}), f32[32,1,1344]{2,1,0:T(1,128)S(1)}, u32[]{:S(2)}, u32[]{:S(2)}) async-start(f32[32,1,1344]{2,1,0:T(1,128)} %broadcast_in_dim.274), calls=%async_computation.5 | async-start | bytes 360448 | tf_op jit(solution)/shard_map/all_to_all | solution.py:233
  (16 other events, 17.7 us)
Sparse Core Ops, SparseCore 1:
  552.9 100.4 reduce-scatter.1
